TPU v7x, 32 devices: a whole 2x2x4 slice. The times are simulated.
32 devices in a mesh: rep: 4 (over y, core), shard: 8 (over z, x).
Axes of the slice: x: 2, y: 2, z: 4, core: 2. Of those that a mesh axis runs over, the one named last changes fastest.
Arguments:
- tokens: bfloat16 [10240, 1536], P(('rep', 'shard')), may hold values from -6 to 6
- cotangent: bfloat16 [10240, 1536], P(('rep', 'shard')), may hold values from -6 to 6
- cond: float32 [11, 1536], replicated, may hold values from -6 to 6
- seq_lengths: int32 [11], replicated, may hold values from 0 to 1178, as said below
- stream_mask: int32 [10240], P(('rep', 'shard')), may hold values from 0 to 1, as said below
- w_mod: float32 [2, 1536, 9216], P(None, 'shard', 'rep'), may hold values from -0.15625 to 0.15625
- m_mod: float32 [2, 1536, 9216], P(None, 'shard', 'rep'), may hold values from -40 to 40
- v_mod: float32 [2, 1536, 9216], P(None, 'shard', 'rep'), may hold values from 1.8432 to 29.696
- w_qkv: float32 [2, 1536, 4608], P(None, 'shard', 'rep'), may hold values from -0.15625 to 0.15625
- m_qkv: float32 [2, 1536, 4608], P(None, 'shard', 'rep'), may hold values from -48 to 48
- v_qkv: float32 [2, 1536, 4608], P(None, 'shard', 'rep'), may hold values from 2.56 to 39.936
- w_out: float32 [2, 1536, 1536], P(None, 'shard', 'rep'), may hold values from -0.75 to 0.75
- m_out: float32 [2, 1536, 1536], P(None, 'shard', 'rep'), may hold values from -14 to 14
- v_out: float32 [2, 1536, 1536], P(None, 'shard', 'rep'), may hold values from 0.2048 to 3.2768
- w_fc1: float32 [2, 1536, 6144], P(None, 'shard', 'rep'), may hold values from -0.15625 to 0.15625
- m_fc1: float32 [2, 1536, 6144], P(None, 'shard', 'rep'), may hold values from -28 to 28
- v_fc1: float32 [2, 1536, 6144], P(None, 'shard', 'rep'), may hold values from 0.8192 to 13.312
- w_fc2: float32 [2, 6144, 1536], P(None, 'shard', 'rep'), may hold values from -0.078125 to 0.078125
- m_fc2: float32 [2, 6144, 1536], P(None, 'shard', 'rep'), may hold values from -32 to 32
- v_fc2: float32 [2, 6144, 1536], P(None, 'shard', 'rep'), may hold values from 1.28 to 20.48
- gains: float32 [2, 128], replicated, may hold values from 0.5 to 1.5
- m_gains: float32 [2, 128], replicated, may hold values from -192 to 192
- v_gains: float32 [2, 128], replicated, may hold values from 46.08 to 737.28
Outputs:
- output: bfloat16 [10240, 1536], P(('rep', 'shard'))
- d_tokens: float32 [10240, 1536], P(('rep', 'shard'))
- new_w_mod: float32 [2, 1536, 9216], P(None, 'shard', 'rep')
- new_m_mod: float32 [2, 1536, 9216], P(None, 'shard', 'rep')
- new_v_mod: float32 [2, 1536, 9216], P(None, 'shard', 'rep')
- copy_w_mod: bfloat16 [2, 1536, 9216], P(None, 'shard', 'rep')
- new_w_qkv: float32 [2, 1536, 4608], P(None, 'shard', 'rep')
- new_m_qkv: float32 [2, 1536, 4608], P(None, 'shard', 'rep')
- new_v_qkv: float32 [2, 1536, 4608], P(None, 'shard', 'rep')
- copy_w_qkv: bfloat16 [2, 1536, 4608], P(None, 'shard', 'rep')
- new_w_out: float32 [2, 1536, 1536], P(None, 'shard', 'rep')
- new_m_out: float32 [2, 1536, 1536], P(None, 'shard', 'rep')
- new_v_out: float32 [2, 1536, 1536], P(None, 'shard', 'rep')
- copy_w_out: bfloat16 [2, 1536, 1536], P(None, 'shard', 'rep')
- new_w_fc1: float32 [2, 1536, 6144], P(None, 'shard', 'rep')
- new_m_fc1: float32 [2, 1536, 6144], P(None, 'shard', 'rep')
- new_v_fc1: float32 [2, 1536, 6144], P(None, 'shard', 'rep')
- copy_w_fc1: bfloat16 [2, 1536, 6144], P(None, 'shard', 'rep')
- new_w_fc2: float32 [2, 6144, 1536], P(None, 'shard', 'rep')
- new_m_fc2: float32 [2, 6144, 1536], P(None, 'shard', 'rep')
- new_v_fc2: float32 [2, 6144, 1536], P(None, 'shard', 'rep')
- copy_w_fc2: bfloat16 [2, 6144, 1536], P(None, 'shard', 'rep')
- new_gains: float32 [2, 128], replicated
- new_m_gains: float32 [2, 128], replicated
- new_v_gains: float32 [2, 128], replicated
Inputs may be any that keep to these rules, and one draw needn't show every extreme that they name: `seq_lengths`: slots hold sequences in order and sum to 10240; the first is 1178; once a slot is 0 all later ones are 0; every nonzero one but the last nonzero one is at least 1024, so the 320 tokens of one device meet at most two sequences. `stream_mask`: the 320 tokens of one device hold at most min(320, 154) text tokens, all in one run, and the first device holds exactly that many.
All inputs are finite; a program needn't handle non-finite values.
Results may differ from a plain program's by a relative error of at most 0.035.
Values may be sent and summed in bfloat16 or wider, within the bound.
A program may use at most 512 MiB of HBM per device.

v0:
```python
import math

import jax
import jax.numpy as jnp
from jax import lax
from jax.sharding import PartitionSpec as P

HD = 64
MAXLEN = 1178
TXT = 154
STEP = 7


norm_eps = 1e-06
adam_eps = 1e-08
score_scale = 0.125
masked_score = -1e30
rate_mod = 0.03
rate_qkv = 0.03
rate_out = 0.15
rate_fc1 = 0.03
rate_fc2 = 0.015
rate_gains = 1.0


def for_sending(value):
    return jax.tree.map(lambda a: a.astype(jnp.bfloat16) if a.dtype == jnp.float32 else a, value)


def from_behind(value, axis, steps):
    count = lax.axis_size(axis)
    leading, last = (max(0, -steps), min(count, count - steps))
    return lax.ppermute(value, axis, [(source, source + steps) for source in range(leading, last)])


def layer_modulate(values, shift, scale):
    centred = values - jnp.mean(values, axis=-1, keepdims=True)
    normed = centred * lax.rsqrt(jnp.mean(centred * centred, axis=-1, keepdims=True) + norm_eps)
    return normed * (1.0 + scale) + shift


def head_norm(values, gain):
    return values * lax.rsqrt(jnp.mean(values * values, axis=-1, keepdims=True) + norm_eps) * gain


def query_key_norm(query_pre, key_pre, gain_tok):
    half_width = gain_tok.shape[1] // 2
    return (
        head_norm(query_pre, gain_tok[:, None, :half_width]),
        head_norm(key_pre, gain_tok[:, None, half_width:]),
    )


def gelu_tanh(values):
    return jax.nn.gelu(values, approximate=True)


def adam_step(weight, moment_one, moment_two, grads, rate):
    new_one = 0.9 * moment_one + 0.1 * grads
    new_two = 0.999 * moment_two + 0.001 * grads * grads
    fixed_one = new_one / (1.0 - 0.9**STEP)
    fixed_two = new_two / (1.0 - 0.999**STEP)
    new_weight = weight - rate * (fixed_one / (jnp.sqrt(fixed_two) + adam_eps) + 0.01 * weight)
    return (new_weight, new_one, new_two, new_weight.astype(jnp.bfloat16))


def segment_index(position, seq_starts, all_tokens):
    counted = jnp.sum((seq_starts[None, :] <= position[:, None]).astype(jnp.int32), axis=1) - 1
    inside = (position >= 0) & (position < all_tokens)
    return jnp.where(inside, counted, -1)


def spread_rows(values, text_rows, text_valid, row_total):
    kept = jnp.where(text_valid, values, jnp.zeros_like(values))
    return jnp.zeros((row_total, values.shape[1]), values.dtype).at[text_rows].add(kept)


def fetch_columns(weight_part):
    return lax.all_gather(weight_part.astype(jnp.bfloat16), "rep", axis=2, tiled=True)


def forward_product(acts, layout, weight_part):
    image_col, text_rows, text_valid = layout
    columns = fetch_columns(weight_part)
    acts_text = jnp.take(acts, text_rows, axis=0)
    weight_piece = lax.all_gather(columns, "shard", axis=1, tiled=True)
    image_out = jnp.dot(acts, weight_piece[0], preferred_element_type=jnp.float32)
    text_out = jnp.dot(acts_text, weight_piece[1], preferred_element_type=jnp.float32)
    text_full = spread_rows(text_out, text_rows, text_valid, acts.shape[0])
    return jnp.where(image_col, image_out, text_full)


def backward_product(grads_low, layout, weight_part):
    image_col, text_rows, text_valid = layout
    columns = fetch_columns(weight_part)
    grads_text = jnp.take(grads_low, text_rows, axis=0)
    row_here = grads_low.shape[0]
    weight_piece = lax.all_gather(columns, "shard", axis=1, tiled=True)
    image_part = jnp.einsum(
        "tc,nc->tn", grads_low, weight_piece[0], preferred_element_type=jnp.float32
    )
    text_part = jnp.einsum(
        "tc,nc->tn", grads_text, weight_piece[1], preferred_element_type=jnp.float32
    )
    joined = jnp.concatenate([image_part, text_part], axis=0)
    text_full = spread_rows(joined[row_here:], text_rows, text_valid, row_here)
    return jnp.where(image_col, joined[:row_here], text_full)


def weight_gradient(acts, grads_low, layout):
    image_col, text_rows, text_valid = layout
    image_grads = jnp.where(image_col, grads_low, jnp.zeros_like(grads_low))
    text_acts = jnp.take(acts, text_rows, axis=0)
    text_grads = jnp.take(grads_low, text_rows, axis=0)
    text_grads = jnp.where(text_valid, text_grads, jnp.zeros_like(text_grads))
    in_width = acts.shape[1]
    own_rows = in_width // lax.axis_size("shard")
    summed = []
    for left_acts, right_grads in ((acts, image_grads), (text_acts, text_grads)):

        def grad_term(first_row, row_count, left_acts=left_acts, right_grads=right_grads):
            return jnp.einsum(
                "tn,tc->nc", left_acts, right_grads, preferred_element_type=jnp.float32
            )

        summed.append(
            lax.psum_scatter(
                grad_term(jnp.int32(0), own_rows * lax.axis_size("shard")).astype(jnp.bfloat16),
                "shard",
                scatter_dimension=0,
                tiled=True,
            ).astype(jnp.float32)
        )
    quarter = summed[0].shape[1] // lax.axis_size("rep")
    totals = (
        lax.psum(summed[0].astype(jnp.bfloat16), "rep").astype(jnp.float32),
        lax.psum(summed[1].astype(jnp.bfloat16), "rep").astype(jnp.float32),
    )
    offset = lax.axis_index("rep") * quarter
    shares = [lax.dynamic_slice_in_dim(total_part, offset, quarter, 1) for total_part in totals]
    return jnp.stack([shares[0], shares[1]])


def relay_keys(pair, hop):
    return jax.tree.map(
        lambda part, own: part.astype(own.dtype),
        from_behind(for_sending(pair), ("rep", "shard"), hop),
        pair,
    )


def relay_grads(pair, hop):
    return from_behind((for_sending(pair[0]), for_sending(pair[1])), ("rep", "shard"), hop)


def body(
    tokens,
    cotangent,
    cond,
    seq_lengths,
    stream_mask,
    w_mod,
    m_mod,
    v_mod,
    w_qkv,
    m_qkv,
    v_qkv,
    w_out,
    m_out,
    v_out,
    w_fc1,
    m_fc1,
    v_fc1,
    w_fc2,
    m_fc2,
    v_fc2,
    gains,
    m_gains,
    v_gains,
):
    tok_rows = tokens.shape[0]
    model_width = tokens.shape[1]
    heads = model_width // HD
    slot_count = seq_lengths.shape[0]
    device_count = lax.axis_size(("rep", "shard"))
    device_index = lax.axis_index(("rep", "shard"))
    all_tokens = tok_rows * device_count
    reach = (MAXLEN - 2) // tok_rows + 1
    seq_starts = jnp.cumsum(seq_lengths) - seq_lengths
    local_pos = device_index * tok_rows + jnp.arange(tok_rows, dtype=jnp.int32)
    seq_ids = segment_index(local_pos, seq_starts, all_tokens)
    image_col = (stream_mask == 1)[:, None]
    text_cap = min(tok_rows, TXT)
    ordering = jnp.argsort(stream_mask, stable=True)
    text_rows = ordering[:text_cap]
    text_valid = (jnp.take(stream_mask, text_rows) == 0)[:, None]
    layout = (image_col, text_rows, text_valid)
    silu_cond = jax.nn.silu(cond).astype(jnp.bfloat16)
    part_rows = w_mod.shape[1]
    cond_rows = lax.dynamic_slice_in_dim(
        silu_cond, lax.axis_index("shard") * part_rows, part_rows, 1
    )
    mod_terms = jnp.einsum(
        "sd,tde->ste", cond_rows, w_mod.astype(jnp.bfloat16), preferred_element_type=jnp.float32
    )
    mod_local = lax.psum_scatter(
        mod_terms.astype(jnp.bfloat16), "shard", scatter_dimension=2, tiled=True
    )
    mod_all = lax.all_gather(mod_local, ("rep", "shard"), axis=2, tiled=True)
    first_seq = seq_ids[0]
    second_seq = jnp.minimum(first_seq + 1, slot_count - 1)
    is_second = (seq_ids != first_seq)[:, None]
    first_mod = mod_all[first_seq]
    second_mod = mod_all[second_seq]
    mod_image = jnp.where(is_second, second_mod[0][None], first_mod[0][None])
    mod_text = jnp.where(is_second, second_mod[1][None], first_mod[1][None])
    mod_tok = jnp.where(image_col, mod_image, mod_text).astype(jnp.float32)
    shift_one, scale_one, gate_one, shift_two, scale_two, gate_two = jnp.split(mod_tok, 6, axis=1)
    stream_in = tokens.astype(jnp.float32)
    act_one = layer_modulate(stream_in, shift_one, scale_one).astype(jnp.bfloat16)
    qkv_pre = forward_product(act_one, layout, w_qkv)
    query_pre = qkv_pre[:, :model_width].reshape(tok_rows, heads, HD)
    key_pre = qkv_pre[:, model_width : 2 * model_width].reshape(tok_rows, heads, HD)
    value_pre = qkv_pre[:, 2 * model_width :]
    gain_tok = jnp.where(image_col, gains[0][None], gains[1][None])
    query_f, key_f = query_key_norm(query_pre, key_pre, gain_tok)
    query_low = query_f.reshape(tok_rows, model_width).astype(jnp.bfloat16)
    key_low = key_f.reshape(tok_rows, model_width).astype(jnp.bfloat16)
    value_low = value_pre.astype(jnp.bfloat16)
    earlier = []
    moving = (key_low, value_low)
    for hop_index in range(reach):
        moving = relay_keys(moving, 1)
        earlier.append(moving)
    later = []
    moving = (key_low, value_low)
    for hop_index in range(reach):
        moving = relay_keys(moving, -1)
        later.append(moving)
    before = earlier[::-1]
    window_key = jnp.concatenate(
        [block_pair[0] for block_pair in before]
        + [key_low]
        + [block_pair[0] for block_pair in later],
        axis=0,
    )
    window_value = jnp.concatenate(
        [block_pair[1] for block_pair in before]
        + [value_low]
        + [block_pair[1] for block_pair in later],
        axis=0,
    )
    window_len = window_key.shape[0]
    key_pos = (device_index - reach) * tok_rows + jnp.arange(window_len, dtype=jnp.int32)
    key_ids = segment_index(key_pos, seq_starts, all_tokens)
    allowed = seq_ids[:, None] == key_ids[None, :]
    group_heads = math.gcd(heads, 8)
    group_count = heads // group_heads
    group_width = group_heads * HD

    def group_scores(group_index):
        query_group = lax.dynamic_slice_in_dim(
            query_low, group_index * group_width, group_width, 1
        ).reshape(tok_rows, group_heads, HD)
        key_group = lax.dynamic_slice_in_dim(
            window_key, group_index * group_width, group_width, 1
        ).reshape(window_len, group_heads, HD)
        value_group = lax.dynamic_slice_in_dim(
            window_value, group_index * group_width, group_width, 1
        ).reshape(window_len, group_heads, HD)
        scores = (
            jnp.einsum("qhd,khd->hqk", query_group, key_group, preferred_element_type=jnp.float32)
            * score_scale
        )
        scores = jnp.where(allowed[None], scores, masked_score)
        return (query_group, key_group, value_group, scores)

    def attend(group_index, state):
        attended_acc, logsum_acc = state
        query_group, key_group, value_group, scores = group_scores(group_index)
        peak = jnp.max(scores, axis=-1, keepdims=True)
        lifted = jnp.exp(scores - peak)
        denom = jnp.sum(lifted, axis=-1, keepdims=True)
        probs = (lifted / denom).astype(jnp.bfloat16)
        attended = jnp.einsum(
            "hqk,khd->qhd", probs, value_group, preferred_element_type=jnp.float32
        ).reshape(tok_rows, group_width)
        logsum = (peak + jnp.log(denom))[:, :, 0]
        return (
            lax.dynamic_update_slice_in_dim(attended_acc, attended, group_index * group_width, 1),
            lax.dynamic_update_slice_in_dim(logsum_acc, logsum, group_index * group_heads, 0),
        )

    attended_all, logsum_all = lax.fori_loop(
        0,
        group_count,
        attend,
        (
            jnp.zeros((tok_rows, model_width), jnp.float32),
            jnp.zeros((heads, tok_rows), jnp.float32),
        ),
    )
    attended_low = attended_all.astype(jnp.bfloat16)
    branch = forward_product(attended_low, layout, w_out)
    mid = stream_in + gate_one * branch
    act_two = layer_modulate(mid, shift_two, scale_two).astype(jnp.bfloat16)
    up_proj = forward_product(act_two, layout, w_fc1)
    gelu_low = gelu_tanh(up_proj).astype(jnp.bfloat16)
    down_proj = forward_product(gelu_low, layout, w_fc2)
    output = mid + gate_two * down_proj
    back_out = cotangent.astype(jnp.float32)
    d_down = (gate_two * back_out).astype(jnp.bfloat16)
    d_gate_two = back_out * down_proj
    g_fc2 = weight_gradient(gelu_low, d_down, layout)
    d_gelu = backward_product(d_down, layout, w_fc2)
    d_up = jax.vjp(gelu_tanh, up_proj)[1](d_gelu)[0].astype(jnp.bfloat16)
    g_fc1 = weight_gradient(act_two, d_up, layout)
    d_act_two = backward_product(d_up, layout, w_fc1)
    d_mid_norm, d_shift_two, d_scale_two = jax.vjp(layer_modulate, mid, shift_two, scale_two)[1](
        d_act_two
    )
    d_mid = back_out + d_mid_norm
    d_branch = (gate_one * d_mid).astype(jnp.bfloat16)
    d_gate_one = d_mid * branch
    g_out = weight_gradient(attended_low, d_branch, layout)
    d_attended = backward_product(d_branch, layout, w_out).astype(jnp.bfloat16)

    def attend_back(group_index, state):
        d_query_acc, d_key_acc, d_value_acc = state
        query_group, key_group, value_group, scores = group_scores(group_index)
        logsum = lax.dynamic_slice_in_dim(logsum_all, group_index * group_heads, group_heads, 0)
        probs_full = jnp.exp(scores - logsum[:, :, None])
        probs_low = probs_full.astype(jnp.bfloat16)
        d_att_group = lax.dynamic_slice_in_dim(
            d_attended, group_index * group_width, group_width, 1
        ).reshape(tok_rows, group_heads, HD)
        d_probs = jnp.einsum(
            "qhd,khd->hqk", d_att_group, value_group, preferred_element_type=jnp.float32
        )
        d_scores = (
            probs_full * (d_probs - jnp.sum(d_probs * probs_full, axis=-1, keepdims=True))
        ).astype(jnp.bfloat16)
        d_query = (
            jnp.einsum("hqk,khd->qhd", d_scores, key_group, preferred_element_type=jnp.float32)
            * score_scale
        )
        d_key = (
            jnp.einsum("hqk,qhd->khd", d_scores, query_group, preferred_element_type=jnp.float32)
            * score_scale
        )
        d_value = jnp.einsum(
            "hqk,qhd->khd", probs_low, d_att_group, preferred_element_type=jnp.float32
        )
        return (
            lax.dynamic_update_slice_in_dim(
                d_query_acc, d_query.reshape(tok_rows, group_width), group_index * group_width, 1
            ),
            lax.dynamic_update_slice_in_dim(
                d_key_acc, d_key.reshape(window_len, group_width), group_index * group_width, 1
            ),
            lax.dynamic_update_slice_in_dim(
                d_value_acc, d_value.reshape(window_len, group_width), group_index * group_width, 1
            ),
        )

    d_query_all, d_key_win, d_value_win = lax.fori_loop(
        0,
        group_count,
        attend_back,
        (
            jnp.zeros((tok_rows, model_width), jnp.float32),
            jnp.zeros((window_len, model_width), jnp.float32),
            jnp.zeros((window_len, model_width), jnp.float32),
        ),
    )

    def window_block(block_index):
        return (
            d_key_win[block_index * tok_rows : (block_index + 1) * tok_rows],
            d_value_win[block_index * tok_rows : (block_index + 1) * tok_rows],
        )

    running = window_block(0)
    for distance in range(reach, 1, -1):
        moved = relay_grads(running, -1)
        extra = window_block(reach - distance + 1)
        running = (moved[0] + extra[0], moved[1] + extra[1])
    from_later = relay_grads(running, -1)
    running = window_block(2 * reach)
    for distance in range(reach, 1, -1):
        moved = relay_grads(running, 1)
        extra = window_block(reach + distance - 1)
        running = (moved[0] + extra[0], moved[1] + extra[1])
    from_earlier = relay_grads(running, 1)
    returned = [from_later, from_earlier]
    own_pair = window_block(reach)
    key_grad = own_pair[0]
    value_grad = own_pair[1]
    for back_pair in returned:
        key_grad = key_grad + back_pair[0]
        value_grad = value_grad + back_pair[1]
    pull_norm = jax.vjp(query_key_norm, query_pre, key_pre, gain_tok)[1]
    d_query_pre, d_key_pre, d_gain_tok = pull_norm(
        (d_query_all.reshape(tok_rows, heads, HD), key_grad.reshape(tok_rows, heads, HD))
    )
    d_qkv = jnp.concatenate(
        [
            d_query_pre.reshape(tok_rows, model_width),
            d_key_pre.reshape(tok_rows, model_width),
            value_grad,
        ],
        axis=1,
    ).astype(jnp.bfloat16)
    g_qkv = weight_gradient(act_one, d_qkv, layout)
    d_act_one = backward_product(d_qkv, layout, w_qkv)
    d_in_norm, d_shift_one, d_scale_one = jax.vjp(layer_modulate, stream_in, shift_one, scale_one)[
        1
    ](d_act_one)
    d_tokens = d_mid + d_in_norm
    d_mod_tok = jnp.concatenate(
        [d_shift_one, d_scale_one, d_gate_one, d_shift_two, d_scale_two, d_gate_two], axis=1
    )
    image_flag = image_col[:, 0]
    second_flag = is_second[:, 0]
    selector = jnp.stack(
        [
            ~second_flag & image_flag,
            ~second_flag & ~image_flag,
            second_flag & image_flag,
            second_flag & ~image_flag,
        ],
        axis=1,
    ).astype(jnp.float32)
    pooled = jnp.einsum("tp,te->pe", selector, d_mod_tok, precision=lax.Precision.HIGHEST)
    d_mod_part = (
        jnp.zeros((slot_count, 2, 6 * model_width), jnp.float32)
        .at[first_seq]
        .add(pooled[0:2])
        .at[second_seq]
        .add(pooled[2:4])
    )
    gain_part = jnp.stack(
        [
            jnp.sum(jnp.where(image_col, d_gain_tok, 0.0), axis=0),
            jnp.sum(jnp.where(image_col, 0.0, d_gain_tok), axis=0),
        ]
    )
    d_mod_all, g_gains = lax.psum((d_mod_part, gain_part), ("rep", "shard"))
    quarter_cols = w_mod.shape[2]
    d_mod_cols = lax.dynamic_slice_in_dim(
        d_mod_all, lax.axis_index("rep") * quarter_cols, quarter_cols, 2
    )
    g_mod = jnp.einsum(
        "sd,ste->tde", cond_rows.astype(jnp.float32), d_mod_cols, precision=lax.Precision.HIGHEST
    )
    up_mod = adam_step(w_mod, m_mod, v_mod, g_mod, rate_mod)
    up_qkv = adam_step(w_qkv, m_qkv, v_qkv, g_qkv, rate_qkv)
    up_out = adam_step(w_out, m_out, v_out, g_out, rate_out)
    up_fc1 = adam_step(w_fc1, m_fc1, v_fc1, g_fc1, rate_fc1)
    up_fc2 = adam_step(w_fc2, m_fc2, v_fc2, g_fc2, rate_fc2)
    up_gains = adam_step(gains, m_gains, v_gains, g_gains, rate_gains)
    return (
        output.astype(jnp.bfloat16),
        d_tokens,
        up_mod[0],
        up_mod[1],
        up_mod[2],
        up_mod[3],
        up_qkv[0],
        up_qkv[1],
        up_qkv[2],
        up_qkv[3],
        up_out[0],
        up_out[1],
        up_out[2],
        up_out[3],
        up_fc1[0],
        up_fc1[1],
        up_fc1[2],
        up_fc1[3],
        up_fc2[0],
        up_fc2[1],
        up_fc2[2],
        up_fc2[3],
        up_gains[0],
        up_gains[1],
        up_gains[2],
    )


def solution(mesh):
    placed = (
        P(("rep", "shard"), None),
        P(("rep", "shard"), None),
        P(),
        P(),
        P(("rep", "shard")),
        P(None, "shard", "rep"),
        P(None, "shard", "rep"),
        P(None, "shard", "rep"),
        P(None, "shard", "rep"),
        P(None, "shard", "rep"),
        P(None, "shard", "rep"),
        P(None, "shard", "rep"),
        P(None, "shard", "rep"),
        P(None, "shard", "rep"),
        P(None, "shard", "rep"),
        P(None, "shard", "rep"),
        P(None, "shard", "rep"),
        P(None, "shard", "rep"),
        P(None, "shard", "rep"),
        P(None, "shard", "rep"),
        P(),
        P(),
        P(),
    )
    return jax.shard_map(
        body,
        mesh=mesh,
        in_specs=placed,
        out_specs=(
            P(("rep", "shard"), None),
            P(("rep", "shard"), None),
            P(None, "shard", "rep"),
            P(None, "shard", "rep"),
            P(None, "shard", "rep"),
            P(None, "shard", "rep"),
            P(None, "shard", "rep"),
            P(None, "shard", "rep"),
            P(None, "shard", "rep"),
            P(None, "shard", "rep"),
            P(None, "shard", "rep"),
            P(None, "shard", "rep"),
            P(None, "shard", "rep"),
            P(None, "shard", "rep"),
            P(None, "shard", "rep"),
            P(None, "shard", "rep"),
            P(None, "shard", "rep"),
            P(None, "shard", "rep"),
            P(None, "shard", "rep"),
            P(None, "shard", "rep"),
            P(None, "shard", "rep"),
            P(None, "shard", "rep"),
            P(),
            P(),
            P(),
        ),
        check_vma=False,
    )
```

profile of v0, /device:TPU:1, one launch (start us, length us, event | category | flops | bytes accessed | tf_op | source)
XLA Modules:
  0.0 5638.4 jit_solution(14251265897891546321)
XLA Ops:
  21.3 23.1 all-gather.9.cloned.1.call-done
  44.5 19.6 all-gather.13.cloned.1.call-done
  64.2 39.7 all-gather.17.cloned.1.call-done
  104.0 39.4 all-gather.21.cloned.1.call-done
  160.2 318.7 %all_gather.35 = bf16[11,2,9216]{0,1,2:T(2,128)(2,1)} all-gather(bf16[11,2,288]{0,1,2:T(2,128)(2,1)S(1)} %bitcast.250), channel_id=1, replica_groups=mesh['rep'=4,'shard'=8] {'rep','shard'}, dimensions={2}, use_global_device_ids=true | all-gather | bytes 418176 | tf_op jit(solution)/shard_map/all_gather | solution.py:209
  479.0 173.1 %dynamic-slice_reduce_fusion.3 = (bf16[9216]{0:T(1024)(128)(2,1)S(1)}, bf16[9216]{0:T(1024)(128)(2,1)S(1)}, bf16[9216]{0:T(1024)(128)(2,1)S(1)}, bf16[9216]{0:T(1024)(128)(2,1)S(1)}) fusion(bf16[11,2,9216]{0,1,2:T(2,128)(2,1)} %all_gather.35, s32[]{:T(128)} %select_n.249, s32[]{:T(128)} %select_n.250, s32[]{:T(128)S(6)} %add.600), kind=kLoop, calls=%fused_computation.100 | loop fusion | bytes 147468 | tf_op jit(solution)/shard_map/slice | solution.py:215
  659.6 122.3 %all-gather.11.cloned.1.call-done = bf16[2,1536,4608]{2,1,0:T(8,128)(2,1)} async-done(((bf16[2,192,4608]{2,1,0:T(8,128)(2,1)}), bf16[2,1536,4608]{2,1,0:T(8,128)(2,1)}) %all-gather.11.cloned.1.call-update) | async-done | bytes 28311568 | tf_op jit(solution)/shard_map/all_gather | solution.py:86
  852.4 34.4 collective-permute-done.8
  891.8 68.9 %collective-permute-done = bf16[320,1536]{1,0:T(8,128)(2,1)S(1)} collective-permute-done((bf16[320,1536]{1,0:T(8,128)(2,1)S(1)}, bf16[320,1536]{1,0:T(8,128)(2,1)S(1)}, u32[]{:S(2)}, u32[]{:S(2)}) %collective-permute-start) | collective-permute-done | bytes 983072 | tf_op jit(solution)/shard_map/ppermute | solution.py:33
  968.9 45.0 collective-permute-done.12
  1021.9 30.6 collective-permute-done.1
  1056.9 27.7 collective-permute-done.5
  1086.5 126.6 %collective-permute-done.13 = bf16[320,1536]{1,0:T(8,128)(2,1)} collective-permute-done((bf16[320,1536]{1,0:T(8,128)(2,1)S(1)}, bf16[320,1536]{1,0:T(8,128)(2,1)}, u32[]{:S(2)}, u32[]{:S(2)}) %collective-permute-start.13) | collective-permute-done | bytes 983072 | tf_op jit(solution)/shard_map/ppermute | solution.py:33
  1222.4 127.7 %collective-permute-done.6 = bf16[320,1536]{1,0:T(8,128)(2,1)} collective-permute-done((bf16[320,1536]{1,0:T(8,128)(2,1)}, bf16[320,1536]{1,0:T(8,128)(2,1)}, u32[]{:S(2)}, u32[]{:S(2)}) %collective-permute-start.6) | collective-permute-done | bytes 983072 | tf_op jit(solution)/shard_map/ppermute | solution.py:33
  1352.0 65.5 %collective-permute-done.14 = bf16[320,1536]{1,0:T(8,128)(2,1)} collective-permute-done((bf16[320,1536]{1,0:T(8,128)(2,1)}, bf16[320,1536]{1,0:T(8,128)(2,1)}, u32[]{:S(2)}, u32[]{:S(2)}) %collective-permute-start.14) | collective-permute-done | bytes 983072 | tf_op jit(solution)/shard_map/ppermute | solution.py:33
  1441.8 97.9 %collective-permute-done.15 = bf16[320,1536]{1,0:T(8,128)(2,1)S(1)} collective-permute-done((bf16[320,1536]{1,0:T(8,128)(2,1)}, bf16[320,1536]{1,0:T(8,128)(2,1)S(1)}, u32[]{:S(2)}, u32[]{:S(2)}) %collective-permute-start.15) | collective-permute-done | bytes 983072 | tf_op jit(solution)/shard_map/ppermute | solution.py:33
  1540.7 12.8 copy.213
  1561.2 12.4 copy.211
  1574.4 146.1 %while.36 = (s32[]{:T(128)}, bf16[320,1536]{1,0:T(8,128)(2,1)S(1)}, f32[24,320]{1,0:T(8,128)}, bf16[2880,1536]{0,1:T(8,128)(2,1)}, bf16[320,1536]{0,1:T(8,128)(2...) while((s32[]{:T(128)}, bf16[320,1536]{1,0:T(8,128)(2,1)S(1)}, ...), condition=%wide.region_13.15_spmd.clone, body=%wide.region_10.14_spmd.clone.sunk | while | flops 1976829440 | bytes 112573176 | solution.py:294
  1579.8 13.0 fusion.222
  1592.9 14.5 fusion.223
  1607.3 14.9 fusion.224
  1628.5 12.9 fusion.222
  1641.4 14.5 fusion.223
  1656.0 14.9 fusion.224
  1677.2 12.8 fusion.222
  1690.0 14.5 fusion.223
  1704.5 15.0 fusion.224
  1744.1 196.3 %all-gather.19.cloned.1.call-done = bf16[2,1536,6144]{2,1,0:T(8,128)(2,1)} async-done(((bf16[2,192,6144]{2,1,0:T(8,128)(2,1)}), bf16[2,1536,6144]{2,1,0:T(8,128)(2,1)}) %all-gather.19.cloned.1.call-update) | async-done | bytes 37748752 | tf_op jit(solution)/shard_map/all_gather | solution.py:86
  1962.4 694.8 %all-gather.23.cloned.1.call-done = bf16[2,6144,1536]{2,1,0:T(8,128)(2,1)} async-done(((bf16[2,768,1536]{2,1,0:T(8,128)(2,1)}), bf16[2,6144,1536]{2,1,0:T(8,128)(2,1)}) %all-gather.23.cloned.1.call-update) | async-done | bytes 37748752 | tf_op jit(solution)/shard_map/all_gather | solution.py:86
  2679.4 15.7 multiply_convert_fusion.1
  2695.1 17.6 fusion.33
  2734.9 13.5 multiply_reduce_fusion.7
  2768.1 15.2 fusion.170
  2823.1 396.8 %while.37 = (s32[]{:T(128)}, f32[320,1536]{0,1:T(8,128)}, f32[2880,1536]{1,0:T(8,128)}, f32[2880,1536]{1,0:T(8,128)}, bf16[2880,1536]{0,1:T(8,128)(2,1)}, /*inde...) while((s32[]{:T(128)}, f32[320,1536]{0,1:T(8,128)}, ...), condition=%wide.region_26.29_spmd.clone, body=%wide.region_24.28_spmd.clone.sunk | while | flops 4831741440 | bytes 329124800 | solution.py:366
  2832.7 12.1 fusion.235
  2844.9 15.4 fusion.236
  2866.7 26.7 multiply_reduce_fusion.10
  2893.4 25.5 multiply_convert_fusion.9
  2977.1 15.1 fusion.236
  2998.6 26.6 multiply_reduce_fusion.10
  3025.3 25.5 multiply_convert_fusion.9
  3108.9 15.1 fusion.236
  3130.4 26.7 multiply_reduce_fusion.10
  3157.1 25.5 multiply_convert_fusion.9
  3241.4 32.4 collective-permute-done.16
  3288.3 27.7 collective-permute-done.24
  3325.2 15.1 collective-permute-done.17
  3353.5 32.5 collective-permute-done.28
  3400.2 40.0 collective-permute-done.18
  3448.6 43.0 collective-permute-done.26
  3518.1 40.2 collective-permute-done.30
  3565.4 14.0 collective-permute-done.23
  3643.9 15.7 convolution_convert_fusion.1
  3660.8 15.3 convolution_convert_fusion.3
  3715.9 13.7 constant_dynamic-update-slice_fusion.23
  3752.4 109.6 %reduce-scatter.12.cloned.1.call-done = bf16[192,4608]{1,0:T(8,128)(2,1)} async-done(((bf16[1536,4608]{1,0:T(8,128)(2,1)}), bf16[192,4608]{1,0:T(8,128)(2,1)}) %reduce-scatter.12.cloned.1.call-update) | async-done | bytes 1769488 | tf_op jit(solution)/shard_map/reduce_scatter | solution.py:127
  3861.9 235.5 %reduce-scatter.14.cloned.1.call-done = bf16[192,4608]{1,0:T(8,128)(2,1)} async-done(((bf16[1536,4608]{1,0:T(8,128)(2,1)}), bf16[192,4608]{1,0:T(8,128)(2,1)}) %reduce-scatter.14.cloned.1.call-update) | async-done | bytes 1769488 | tf_op jit(solution)/shard_map/reduce_scatter | solution.py:127
  4097.5 315.0 %reduce-scatter.24.cloned.1.call-done = bf16[768,1536]{1,0:T(8,128)(2,1)} async-done(((bf16[6144,1536]{1,0:T(8,128)(2,1)}), bf16[768,1536]{1,0:T(8,128)(2,1)}) %reduce-scatter.24.cloned.1.call-update) | async-done | bytes 2359312 | tf_op jit(solution)/shard_map/reduce_scatter | solution.py:127
  4412.5 314.3 %reduce-scatter.20.cloned.1.call-done = bf16[192,6144]{1,0:T(8,128)(2,1)} async-done(((bf16[1536,6144]{1,0:T(8,128)(2,1)}), bf16[192,6144]{1,0:T(8,128)(2,1)}) %reduce-scatter.20.cloned.1.call-update) | async-done | bytes 2359312 | tf_op jit(solution)/shard_map/reduce_scatter | solution.py:127
  4726.7 314.4 %reduce-scatter.26.cloned.1.call-done = bf16[768,1536]{1,0:T(8,128)(2,1)} async-done(((bf16[6144,1536]{1,0:T(8,128)(2,1)}), bf16[768,1536]{1,0:T(8,128)(2,1)}) %reduce-scatter.26.cloned.1.call-update) | async-done | bytes 2359312 | tf_op jit(solution)/shard_map/reduce_scatter | solution.py:127
  5041.1 314.5 %reduce-scatter.22.cloned.1.call-done = bf16[192,6144]{1,0:T(8,128)(2,1)} async-done(((bf16[1536,6144]{1,0:T(8,128)(2,1)}), bf16[192,6144]{1,0:T(8,128)(2,1)}) %reduce-scatter.22.cloned.1.call-update) | async-done | bytes 2359312 | tf_op jit(solution)/shard_map/reduce_scatter | solution.py:127
  5356.9 40.4 psum.79
  5408.9 195.4 %all-reduce.8.cloned.1.call-done = (bf16[192,4608]{1,0:T(8,128)(2,1)}, bf16[192,4608]{1,0:T(8,128)(2,1)}, bf16[192,1536]{1,0:T(8,128)(2,1)}, bf16[192,1536]{1,0:...) async-done(((bf16[192,4608]{1,0:T(8,128)(2,1)}, bf16[192,4608]{1,0:T(8,128)(2,1)}, ...) | async-done | bytes 14155792 | tf_op jit(solution)/shard_map/psum | solution.py:137
  (606 shorter events, 808.4 us)
Async XLA Ops:
  8.0 36.4 all-gather.9.cloned.1.call-start
  10.7 53.4 all-gather.13.cloned.1.call-start
  11.5 92.4 %all-gather.17.cloned.1.call-start = ((), (), s32[]{:S(2)}) async-start(), calls=%async_computation.13 | async-start | bytes 5898240 | tf_op jit(solution)/shard_map/all_gather | solution.py:79
  14.4 129.0 %all-gather.21.cloned.1.call-start = ((), (), s32[]{:S(2)}) async-start(), calls=%async_computation.15 | async-start | bytes 5898240 | tf_op jit(solution)/shard_map/all_gather | solution.py:79
  15.6 143.6 %reduce-scatter.28.cloned.1.call-start = ((), (), s32[]{:S(2)}) async-start(), calls=%async_computation.26 | async-start | bytes 663552
  21.3 760.6 %all-gather.11.cloned.1.call-start = ((), (), s32[]{:S(2)}) async-start(), calls=%async_computation.10 | async-start | bytes 31850496 | tf_op jit(solution)/shard_map/all_gather | solution.py:86
  44.4 1678.1 %all-gather.15.cloned.1.call-start = ((), (), s32[]{:S(2)}) async-start(), calls=%async_computation.12 | async-start | bytes 10616832 | tf_op jit(solution)/shard_map/all_gather | solution.py:86
  64.1 1876.3 %all-gather.19.cloned.1.call-start = ((), (), s32[]{:S(2)}) async-start(), calls=%async_computation.14 | async-start | bytes 42467328 | tf_op jit(solution)/shard_map/all_gather | solution.py:86
  103.9 2553.3 %all-gather.23.cloned.1.call-start = ((), (), s32[]{:S(2)}) async-start(), calls=%async_computation.16 | async-start | bytes 42467328 | tf_op jit(solution)/shard_map/all_gather | solution.py:86
  143.4 3608.9 %reduce-scatter.16.cloned.1.call-start = ((), (), s32[]{:S(2)}) async-start(), calls=%async_computation.20 | async-start | bytes 5308416 | tf_op jit(solution)/shard_map/reduce_scatter | solution.py:127
  150.0 641.0 %copy-start.125 = (s32[154]{0:T(256)}, s32[154]{0:T(256)S(1)}, u32[]{:S(2)}) copy-start(s32[154]{0:T(256)S(1)} %compare_select_fusion) | copy-start | bytes 1852
  150.0 508.5 %copy-start.104 = (s32[1024]{0:T(1024)}, s32[1024]{0:T(1024)S(1)}, u32[]{:S(2)}) copy-start(s32[1024]{0:T(1024)S(1)} %pad_clamp_fusion) | copy-start | bytes 12292
  152.9 499.3 %copy-start.121 = (pred[320]{0:T(512)(128)(4,1)}, pred[320]{0:T(512)(128)(4,1)S(1)}, u32[]{:S(2)}) copy-start(pred[320]{0:T(512)(128)(4,1)S(1)} %get-tuple-element.579) | copy-start | bytes 964
  152.9 646.6 %copy-start.101 = (pred[320]{0:T(512)(128)(4,1)}, pred[320]{0:T(512)(128)(4,1)S(1)}, u32[]{:S(2)}) copy-start(pred[320]{0:T(512)(128)(4,1)S(1)} %get-tuple-element.578) | copy-start | bytes 964
  158.7 495.0 %copy-start.106 = (f32[320]{0:T(512)}, f32[320]{0:T(512)S(1)}, u32[]{:S(2)}) copy-start(f32[320]{0:T(512)S(1)} %broadcast_multiply_fusion.1) | copy-start | bytes 3844
  159.2 494.6 %copy-start.110 = (f32[320]{0:T(512)}, f32[320]{0:T(512)S(1)}, u32[]{:S(2)}) copy-start(f32[320]{0:T(512)S(1)} %fusion.134) | copy-start | bytes 3844
  159.2 622.7 %copy-start.98 = (pred[154]{0:T(512)(128)(4,1)}, pred[154]{0:T(512)(128)(4,1)S(1)}, u32[]{:S(2)}) copy-start(pred[154]{0:T(512)(128)(4,1)S(1)} %get-tuple-element.587) | copy-start | bytes 466
  159.2 622.7 %copy-start.118 = (pred[154]{0:T(512)(128)(4,1)}, pred[154]{0:T(512)(128)(4,1)S(1)}, u32[]{:S(2)}) copy-start(pred[154]{0:T(512)(128)(4,1)S(1)} %get-tuple-element.586) | copy-start | bytes 466
  836.6 50.2 collective-permute-start.8
  840.4 120.2 %collective-permute-start = (bf16[320,1536]{1,0:T(8,128)(2,1)S(1)}, bf16[320,1536]{1,0:T(8,128)(2,1)S(1)}, u32[]{:S(2)}, u32[]{:S(2)}) collective-permute-start(bf16[320,1536]{1,0:T(8,128)(2,1)S(1)} %slice.348), channel_id=1, source_target_pairs={{0,1},{1,2},{2,3},{3,4},{4,5},{5,6},{6,7},{7,8},{8,9},{9,10},{10,1... | collective-permute-start | bytes 2949128 | tf_op jit(solution)/shard_map/ppermute | solution.py:33
  844.7 120.2 %collective-permute-start.4 = (bf16[320,1536]{1,0:T(8,128)(2,1)S(1)}, bf16[320,1536]{1,0:T(8,128)(2,1)S(1)}, u32[]{:S(2)}, u32[]{:S(2)}) collective-permute-start(bf16[320,1536]{1,0:T(8,128)(2,1)S(1)} %slice.348), channel_id=1, source_target_pairs={{1,0},{2,1},{3,2},{4,3},{5,4},{6,5},{7,6},{8,7},{9,8},{10,9},{11,1... | collective-permute-start | bytes 2949128 | tf_op jit(solution)/shard_map/ppermute | solution.py:33
  848.7 165.2 %collective-permute-start.12 = (bf16[320,1536]{1,0:T(8,128)(2,1)S(1)}, bf16[320,1536]{1,0:T(8,128)(2,1)S(1)}, u32[]{:S(2)}, u32[]{:S(2)}) collective-permute-start(bf16[320,1536]{1,0:T(8,128)(2,1)S(1)} %get-tuple-element.613), channel_id=1, source_target_pairs={{1,0},{2,1},{3,2},{4,3},{5,4},{6,5},{7,6},{8,7},{9,8},{10,9},{11,1... | collective-permute-start | bytes 2949128 | tf_op jit(solution)/shard_map/ppermute | solution.py:33
  886.8 133.1 %collective-permute-start.9 = (bf16[320,1536]{1,0:T(8,128)(2,1)S(1)}, bf16[320,1536]{1,0:T(8,128)(2,1)S(1)}, u32[]{:S(2)}, u32[]{:S(2)}) collective-permute-start(bf16[320,1536]{1,0:T(8,128)(2,1)S(1)} %collective-permute-done.8), channel_id=1, source_target_pairs={{0,1},{1,2},{2,3},{3,4},{4,5},{5,6},{6,7},{7,8},{8,9},{9,10},{10,1... | collective-permute-start | bytes 2949128 | tf_op jit(solution)/shard_map/ppermute | solution.py:33
  960.7 91.8 %collective-permute-start.1 = (bf16[320,1536]{1,0:T(8,128)(2,1)S(1)}, bf16[320,1536]{1,0:T(8,128)(2,1)}, u32[]{:S(2)}, u32[]{:S(2)}) collective-permute-start(bf16[320,1536]{1,0:T(8,128)(2,1)S(1)} %collective-permute-done), channel_id=1, source_target_pairs={{0,1},{1,2},{2,3},{3,4},{4,5},{5,6},{6,7},{7,8},{8,9},{9,10},{10,1... | collective-permute-start | bytes 2949128 | tf_op jit(solution)/shard_map/ppermute | solution.py:33
  964.9 119.7 %collective-permute-start.5 = (bf16[320,1536]{1,0:T(8,128)(2,1)S(1)}, bf16[320,1536]{1,0:T(8,128)(2,1)}, u32[]{:S(2)}, u32[]{:S(2)}) collective-permute-start(bf16[320,1536]{1,0:T(8,128)(2,1)S(1)} %collective-permute-done.4), channel_id=1, source_target_pairs={{1,0},{2,1},{3,2},{4,3},{5,4},{6,5},{7,6},{8,7},{9,8},{10,9},{11,1... | collective-permute-start | bytes 2949128 | tf_op jit(solution)/shard_map/ppermute | solution.py:33
  1013.9 199.2 %collective-permute-start.13 = (bf16[320,1536]{1,0:T(8,128)(2,1)S(1)}, bf16[320,1536]{1,0:T(8,128)(2,1)}, u32[]{:S(2)}, u32[]{:S(2)}) collective-permute-start(bf16[320,1536]{1,0:T(8,128)(2,1)S(1)} %collective-permute-done.12), channel_id=1, source_target_pairs={{1,0},{2,1},{3,2},{4,3},{5,4},{6,5},{7,6},{8,7},{9,8},{10,9},{11,1... | collective-permute-start | bytes 2949128 | tf_op jit(solution)/shard_map/ppermute | solution.py:33
  1019.9 195.1 %collective-permute-start.10 = (bf16[320,1536]{1,0:T(8,128)(2,1)S(1)}, bf16[320,1536]{1,0:T(8,128)(2,1)}, u32[]{:S(2)}, u32[]{:S(2)}) collective-permute-start(bf16[320,1536]{1,0:T(8,128)(2,1)S(1)} %collective-permute-done.9), channel_id=1, source_target_pairs={{0,1},{1,2},{2,3},{3,4},{4,5},{5,6},{6,7},{7,8},{8,9},{9,10},{10,1... | collective-permute-start | bytes 2949128 | tf_op jit(solution)/shard_map/ppermute | solution.py:33
  1052.5 167.8 %collective-permute-start.2 = (bf16[320,1536]{1,0:T(8,128)(2,1)}, bf16[320,1536]{1,0:T(8,128)(2,1)}, u32[]{:S(2)}, u32[]{:S(2)}) collective-permute-start(bf16[320,1536]{1,0:T(8,128)(2,1)} %collective-permute-done.1), channel_id=1, source_target_pairs={{0,1},{1,2},{2,3},{3,4},{4,5},{5,6},{6,7},{7,8},{8,9},{9,10},{10,1... | collective-permute-start | bytes 2949128 | tf_op jit(solution)/shard_map/ppermute | solution.py:33
  1084.6 265.4 %collective-permute-start.6 = (bf16[320,1536]{1,0:T(8,128)(2,1)}, bf16[320,1536]{1,0:T(8,128)(2,1)}, u32[]{:S(2)}, u32[]{:S(2)}) collective-permute-start(bf16[320,1536]{1,0:T(8,128)(2,1)} %collective-permute-done.5), channel_id=1, source_target_pairs={{1,0},{2,1},{3,2},{4,3},{5,4},{6,5},{7,6},{8,7},{9,8},{10,9},{11,1... | collective-permute-start | bytes 2949128 | tf_op jit(solution)/shard_map/ppermute | solution.py:33
  1213.1 204.3 %collective-permute-start.14 = (bf16[320,1536]{1,0:T(8,128)(2,1)}, bf16[320,1536]{1,0:T(8,128)(2,1)}, u32[]{:S(2)}, u32[]{:S(2)}) collective-permute-start(bf16[320,1536]{1,0:T(8,128)(2,1)} %collective-permute-done.13), channel_id=1, source_target_pairs={{1,0},{2,1},{3,2},{4,3},{5,4},{6,5},{7,6},{8,7},{9,8},{10,9},{11,1... | collective-permute-start | bytes 2949128 | tf_op jit(solution)/shard_map/ppermute | solution.py:33
  1215.1 204.3 %collective-permute-start.11 = (bf16[320,1536]{1,0:T(8,128)(2,1)}, bf16[320,1536]{1,0:T(8,128)(2,1)}, u32[]{:S(2)}, u32[]{:S(2)}) collective-permute-start(bf16[320,1536]{1,0:T(8,128)(2,1)} %collective-permute-done.10), channel_id=1, source_target_pairs={{0,1},{1,2},{2,3},{3,4},{4,5},{5,6},{6,7},{7,8},{8,9},{9,10},{10,1... | collective-permute-start | bytes 2949128 | tf_op jit(solution)/shard_map/ppermute | solution.py:33
  1220.3 212.3 %collective-permute-start.3 = (bf16[320,1536]{1,0:T(8,128)(2,1)}, bf16[320,1536]{1,0:T(8,128)(2,1)S(1)}, u32[]{:S(2)}, u32[]{:S(2)}) collective-permute-start(bf16[320,1536]{1,0:T(8,128)(2,1)} %collective-permute-done.2), channel_id=1, source_target_pairs={{0,1},{1,2},{2,3},{3,4},{4,5},{5,6},{6,7},{7,8},{8,9},{9,10},{10,1... | collective-permute-start | bytes 2949128 | tf_op jit(solution)/shard_map/ppermute | solution.py:33
  1350.1 209.0 %collective-permute-start.7 = (bf16[320,1536]{1,0:T(8,128)(2,1)}, bf16[320,1536]{1,0:T(8,128)(2,1)}, u32[]{:S(2)}, u32[]{:S(2)}) collective-permute-start(bf16[320,1536]{1,0:T(8,128)(2,1)} %collective-permute-done.6), channel_id=1, source_target_pairs={{1,0},{2,1},{3,2},{4,3},{5,4},{6,5},{7,6},{8,7},{9,8},{10,9},{11,1... | collective-permute-start | bytes 2949128 | tf_op jit(solution)/shard_map/ppermute | solution.py:33
  1417.5 122.2 %collective-permute-start.15 = (bf16[320,1536]{1,0:T(8,128)(2,1)}, bf16[320,1536]{1,0:T(8,128)(2,1)S(1)}, u32[]{:S(2)}, u32[]{:S(2)}) collective-permute-start(bf16[320,1536]{1,0:T(8,128)(2,1)} %collective-permute-done.14), channel_id=1, source_target_pairs={{1,0},{2,1},{3,2},{4,3},{5,4},{6,5},{7,6},{8,7},{9,8},{10,9},{11,1... | collective-permute-start | bytes 2949128 | tf_op jit(solution)/shard_map/ppermute | solution.py:33
  1737.8 1030.2 %copy-start.108 = (f32[320]{0:T(512)}, f32[320]{0:T(512)S(1)}, u32[]{:S(2)}) copy-start(f32[320]{0:T(512)S(1)} %broadcast_multiply_fusion) | copy-start | bytes 3844
  1738.2 1029.9 %copy-start.112 = (f32[320]{0:T(512)}, f32[320]{0:T(512)S(1)}, u32[]{:S(2)}) copy-start(f32[320]{0:T(512)S(1)} %fusion.135) | copy-start | bytes 3844
  1742.1 937.3 %copy-start.18 = (bf16[320,1536]{1,0:T(8,128)(2,1)}, bf16[320,1536]{1,0:T(8,128)(2,1)S(1)}, u32[]{:S(2)}) copy-start(bf16[320,1536]{1,0:T(8,128)(2,1)S(1)} %get-tuple-element.606) | copy-start | bytes 2949124
  1742.1 953.0 %copy-start.20 = (bf16[320,1536]{1,0:T(8,128)(2,1)}, bf16[320,1536]{1,0:T(8,128)(2,1)S(1)}, u32[]{:S(2)}) copy-start(bf16[320,1536]{1,0:T(8,128)(2,1)S(1)} %get-tuple-element.605) | copy-start | bytes 2949124
  1743.1 914.1 %copy-start.69 = (bf16[154,1536]{1,0:T(8,128)(2,1)}, bf16[154,1536]{1,0:T(8,128)(2,1)S(1)}, u32[]{:S(2)}) copy-start(bf16[154,1536]{1,0:T(8,128)(2,1)S(1)} %gather_fusion.5) | copy-start | bytes 1419268
  2792.3 960.1 %reduce-scatter.18.cloned.1.call-start = ((), (), s32[]{:S(2)}) async-start(), calls=%async_computation.21 | async-start | bytes 5308416 | tf_op jit(solution)/shard_map/reduce_scatter | solution.py:127
  3227.8 46.0 collective-permute-start.16
  3235.9 80.1 %collective-permute-start.24 = (bf16[320,1536]{1,0:T(8,128)(2,1)S(1)}, bf16[320,1536]{1,0:T(8,128)(2,1)}, u32[]{:S(2)}, u32[]{:S(2)}) collective-permute-start(bf16[320,1536]{1,0:T(8,128)(2,1)S(1)} %get-tuple-element.609), channel_id=1, source_target_pairs={{1,0},{2,1},{3,2},{4,3},{5,4},{6,5},{7,6},{8,7},{9,8},{10,9},{11,1... | collective-permute-start | bytes 2949128 | tf_op jit(solution)/shard_map/ppermute | solution.py:33
  3239.4 85.8 %collective-permute-start.20 = (bf16[320,1536]{1,0:T(8,128)(2,1)}, bf16[320,1536]{1,0:T(8,128)(2,1)S(1)}, u32[]{:S(2)}, u32[]{:S(2)}) collective-permute-start(bf16[320,1536]{1,0:T(8,128)(2,1)} %get-tuple-element.608), channel_id=1, source_target_pairs={{0,1},{1,2},{2,3},{3,4},{4,5},{5,6},{6,7},{7,8},{8,9},{9,10},{10,1... | collective-permute-start | bytes 2949128 | tf_op jit(solution)/shard_map/ppermute | solution.py:33
  3276.5 63.8 %collective-permute-start.17 = (bf16[320,1536]{1,0:T(8,128)(2,1)}, bf16[320,1536]{1,0:T(8,128)(2,1)}, u32[]{:S(2)}, u32[]{:S(2)}) collective-permute-start(bf16[320,1536]{1,0:T(8,128)(2,1)} %add_convert_fusion.12), channel_id=1, source_target_pairs={{1,0},{2,1},{3,2},{4,3},{5,4},{6,5},{7,6},{8,7},{9,8},{10,9},{11,1... | collective-permute-start | bytes 2949128 | tf_op jit(solution)/shard_map/ppermute | solution.py:33
  3282.7 103.3 %collective-permute-start.28 = (bf16[320,1536]{1,0:T(8,128)(2,1)}, bf16[320,1536]{1,0:T(8,128)(2,1)S(1)}, u32[]{:S(2)}, u32[]{:S(2)}) collective-permute-start(bf16[320,1536]{1,0:T(8,128)(2,1)} %get-tuple-element.610), channel_id=1, source_target_pairs={{0,1},{1,2},{2,3},{3,4},{4,5},{5,6},{6,7},{7,8},{8,9},{9,10},{10,1... | collective-permute-start | bytes 2949128 | tf_op jit(solution)/shard_map/ppermute | solution.py:33
  3319.0 67.0 %collective-permute-start.25 = (bf16[320,1536]{1,0:T(8,128)(2,1)}, bf16[320,1536]{1,0:T(8,128)(2,1)S(1)}, u32[]{:S(2)}, u32[]{:S(2)}) collective-permute-start(bf16[320,1536]{1,0:T(8,128)(2,1)} %add_convert_fusion.6), channel_id=1, source_target_pairs={{1,0},{2,1},{3,2},{4,3},{5,4},{6,5},{7,6},{8,7},{9,8},{10,9},{11,1... | collective-permute-start | bytes 2949128 | tf_op jit(solution)/shard_map/ppermute | solution.py:33
  3325.1 536.8 %reduce-scatter.12.cloned.1.call-start = ((), (), s32[]{:S(2)}) async-start(), calls=%async_computation.18 | async-start | bytes 15925248 | tf_op jit(solution)/shard_map/reduce_scatter | solution.py:127
  3343.3 96.9 %collective-permute-start.18 = (bf16[320,1536]{1,0:T(8,128)(2,1)S(1)}, bf16[320,1536]{1,0:T(8,128)(2,1)S(1)}, u32[]{:S(2)}, u32[]{:S(2)}) collective-permute-start(bf16[320,1536]{1,0:T(8,128)(2,1)S(1)} %get-tuple-element.598), channel_id=1, source_target_pairs={{1,0},{2,1},{3,2},{4,3},{5,4},{6,5},{7,6},{8,7},{9,8},{10,9},{11,1... | collective-permute-start | bytes 2949128 | tf_op jit(solution)/shard_map/ppermute | solution.py:33
  3351.5 89.3 %collective-permute-start.21 = (bf16[320,1536]{1,0:T(8,128)(2,1)S(1)}, bf16[320,1536]{1,0:T(8,128)(2,1)S(1)}, u32[]{:S(2)}, u32[]{:S(2)}) collective-permute-start(bf16[320,1536]{1,0:T(8,128)(2,1)S(1)} %get-tuple-element.599), channel_id=1, source_target_pairs={{0,1},{1,2},{2,3},{3,4},{4,5},{5,6},{6,7},{7,8},{8,9},{9,10},{10,1... | collective-permute-start | bytes 2949128 | tf_op jit(solution)/shard_map/ppermute | solution.py:33
  3388.7 103.0 %collective-permute-start.26 = (bf16[320,1536]{1,0:T(8,128)(2,1)S(1)}, bf16[320,1536]{1,0:T(8,128)(2,1)S(1)}, u32[]{:S(2)}, u32[]{:S(2)}) collective-permute-start(bf16[320,1536]{1,0:T(8,128)(2,1)S(1)} %get-tuple-element.602), channel_id=1, source_target_pairs={{1,0},{2,1},{3,2},{4,3},{5,4},{6,5},{7,6},{8,7},{9,8},{10,9},{11,1... | collective-permute-start | bytes 2949128 | tf_op jit(solution)/shard_map/ppermute | solution.py:33
  3398.3 93.4 %collective-permute-start.29 = (bf16[320,1536]{1,0:T(8,128)(2,1)S(1)}, bf16[320,1536]{1,0:T(8,128)(2,1)S(1)}, u32[]{:S(2)}, u32[]{:S(2)}) collective-permute-start(bf16[320,1536]{1,0:T(8,128)(2,1)S(1)} %get-tuple-element.603), channel_id=1, source_target_pairs={{0,1},{1,2},{2,3},{3,4},{4,5},{5,6},{6,7},{7,8},{8,9},{9,10},{10,1... | collective-permute-start | bytes 2949128 | tf_op jit(solution)/shard_map/ppermute | solution.py:33
  3444.6 60.6 %collective-permute-start.22 = (bf16[320,1536]{1,0:T(8,128)(2,1)S(1)}, bf16[320,1536]{1,0:T(8,128)(2,1)S(1)}, u32[]{:S(2)}, u32[]{:S(2)}) collective-permute-start(bf16[320,1536]{1,0:T(8,128)(2,1)S(1)} %get-tuple-element.597), channel_id=1, source_target_pairs={{0,1},{1,2},{2,3},{3,4},{4,5},{5,6},{6,7},{7,8},{8,9},{9,10},{10,1... | collective-permute-start | bytes 2949128 | tf_op jit(solution)/shard_map/ppermute | solution.py:33
  3495.7 62.6 %collective-permute-start.30 = (bf16[320,1536]{1,0:T(8,128)(2,1)}, bf16[320,1536]{1,0:T(8,128)(2,1)}, u32[]{:S(2)}, u32[]{:S(2)}) collective-permute-start(bf16[320,1536]{1,0:T(8,128)(2,1)} %get-tuple-element.601), channel_id=1, source_target_pairs={{0,1},{1,2},{2,3},{3,4},{4,5},{5,6},{6,7},{7,8},{8,9},{9,10},{10,1... | collective-permute-start | bytes 2949128 | tf_op jit(solution)/shard_map/ppermute | solution.py:33
  3497.7 67.6 %collective-permute-start.19 = (bf16[320,1536]{1,0:T(8,128)(2,1)}, bf16[320,1536]{1,0:T(8,128)(2,1)}, u32[]{:S(2)}, u32[]{:S(2)}) collective-permute-start(bf16[320,1536]{1,0:T(8,128)(2,1)} %get-tuple-element.596), channel_id=1, source_target_pairs={{1,0},{2,1},{3,2},{4,3},{5,4},{6,5},{7,6},{8,7},{9,8},{10,9},{11,1... | collective-permute-start | bytes 2949128 | tf_op jit(solution)/shard_map/ppermute | solution.py:33
  3507.9 71.4 %collective-permute-start.23 = (bf16[320,1536]{1,0:T(8,128)(2,1)}, bf16[320,1536]{1,0:T(8,128)(2,1)}, u32[]{:S(2)}, u32[]{:S(2)}) collective-permute-start(bf16[320,1536]{1,0:T(8,128)(2,1)} %add_convert_fusion.7), channel_id=1, source_target_pairs={{0,1},{1,2},{2,3},{3,4},{4,5},{5,6},{6,7},{7,8},{8,9},{9,10},{10,1... | collective-permute-start | bytes 2949128 | tf_op jit(solution)/shard_map/ppermute | solution.py:33
  3511.8 94.6 %collective-permute-start.27 = (bf16[320,1536]{1,0:T(8,128)(2,1)}, bf16[320,1536]{1,0:T(8,128)(2,1)S(1)}, u32[]{:S(2)}, u32[]{:S(2)}) collective-permute-start(bf16[320,1536]{1,0:T(8,128)(2,1)} %get-tuple-element.600), channel_id=1, source_target_pairs={{1,0},{2,1},{3,2},{4,3},{5,4},{6,5},{7,6},{8,7},{9,8},{10,9},{11,1... | collective-permute-start | bytes 2949128 | tf_op jit(solution)/shard_map/ppermute | solution.py:33
  3561.3 45.1 collective-permute-start.31
  3628.6 468.9 %reduce-scatter.14.cloned.1.call-start = ((), (), s32[]{:S(2)}) async-start(), calls=%async_computation.19 | async-start | bytes 15925248 | tf_op jit(solution)/shard_map/reduce_scatter | solution.py:127
  3642.7 769.8 %reduce-scatter.24.cloned.1.call-start = ((), (), s32[]{:S(2)}) async-start(), calls=%async_computation.24 | async-start | bytes 21233664 | tf_op jit(solution)/shard_map/reduce_scatter | solution.py:127
  3659.6 1067.1 %reduce-scatter.20.cloned.1.call-start = ((), (), s32[]{:S(2)}) async-start(), calls=%async_computation.22 | async-start | bytes 21233664 | tf_op jit(solution)/shard_map/reduce_scatter | solution.py:127
  3676.1 1365.0 %reduce-scatter.26.cloned.1.call-start = ((), (), s32[]{:S(2)}) async-start(), calls=%async_computation.25 | async-start | bytes 21233664 | tf_op jit(solution)/shard_map/reduce_scatter | solution.py:127
  3687.2 1668.4 %reduce-scatter.22.cloned.1.call-start = ((), (), s32[]{:S(2)}) async-start(), calls=%async_computation.23 | async-start | bytes 21233664 | tf_op jit(solution)/shard_map/reduce_scatter | solution.py:127
  3698.6 1700.0 %all-reduce.6.cloned.1.call-start = ((), (), s32[]{:S(2)}) async-start(), calls=%async_computation.17 | async-start | bytes 1622016 | tf_op jit(solution)/shard_map/psum | solution.py:448
  3752.2 1852.1 %all-reduce.8.cloned.1.call-start = ((), (), s32[]{:S(2)}) async-start(), calls=%async_computation.27 | async-start | bytes 28311552 | tf_op jit(solution)/shard_map/psum | solution.py:137
  (129 other events, 3405.2 us)
Sparse Core Ops, SparseCore 0:
  11.1 33.2 all-gather.8
  46.6 17.4 all-gather.12
  66.3 37.5 all-gather.16
  105.9 37.3 all-gather.20
  144.8 636.9 all-gather.10
  784.1 291.1 all-gather.14
  1077.0 863.3 all-gather.18
  1942.0 715.1 all-gather.22
  3752.4 318.4 all-reduce.5
  5355.8 248.4 all-reduce.7
Sparse Core Ops, SparseCore 1:
  21.4 62.6 reduce-scatter.27
  2792.3 94.9 reduce-scatter.15
  3325.2 183.6 reduce-scatter.17
  3628.7 233.2 reduce-scatter.11
  3866.1 231.4 reduce-scatter.13
  4101.9 310.6 reduce-scatter.23
  4416.7 310.0 reduce-scatter.19
  4731.0 310.1 reduce-scatter.25
  5045.4 310.2 reduce-scatter.21
where the time goes:
time: 5650 us; the launch traced here: 5640 us
  waiting for transfers between devices  3810 us (67%)
  matrix products  571 us (10%)
  local copies, waits for them, and re-layouts  454 us (8%)
  blocking collectives  359 us (6%)
  other arithmetic  294 us (5%)
  starting transfers between devices  126 us (2%)
    reduce_scatter x8, waiting for transfers between devices, weight_gradient(): lax.psum_scatter(grad_term(jnp.int32(0), own_rows * lax.axis_size('shard'...  1600 us
    all_gather x4, waiting for transfers between devices, forward_product(): weight_piece = lax.all_gather(columns, 'shard', axis=1, tiled=True)  1010 us
    ppermute x32, waiting for transfers between devices, from_behind(): lax.ppermute(value, axis, [(source, source + steps) for source in range(l...  878 us
    all_gather x1, blocking collectives, body(): mod_all = lax.all_gather(mod_local, ('rep', 'shard'), axis=2, tiled=True)  319 us
    psum x1, waiting for transfers between devices, weight_gradient(): lax.psum(summed[1].astype(jnp.bfloat16), 'rep').astype(jnp.float32)  195 us
    slice x1, local copies, waits for them, and re-layouts, body(): mod_image = jnp.where(is_second, second_mod[0][None], first_mod[0][None])  173 us
    ppermute x32, starting transfers between devices, from_behind(): lax.ppermute(value, axis, [(source, source + steps) for source in range(l...  126 us
    all_gather x4, waiting for transfers between devices, fetch_columns(): lax.all_gather(weight_part.astype(jnp.bfloat16), 'rep', axis=2, tiled=True)  122 us
  transfers between devices with their start and end apart: 51, of which 33 were waited for; matrix products, arithmetic and copies ran while one was open for 20% of the time, Pallas kernels for 0%

commit v1 on v0

v1 whole, which is shorter than its diff:
```python
import functools

import jax
import jax.numpy as jnp
from jax import lax
from jax.experimental import pallas as pl
from jax.experimental.pallas import tpu as pltpu
from jax.sharding import PartitionSpec as P

HD = 64
MAXLEN = 1178
STEP = 7

norm_eps = 1e-06
adam_eps = 1e-08
score_scale = 0.125
rate_mod = 0.03
rate_qkv = 0.03
rate_out = 0.15
rate_fc1 = 0.03
rate_fc2 = 0.015
rate_gains = 1.0

bf16 = jnp.bfloat16
f32 = jnp.float32
QB = 256
KB = 256
TXT = 154
WINDOW = (TXT + 15 + 15) // 16 * 16
COLS = 512
GELU_A = 0.7978845608028654
GELU_B = 0.044715
NN = (((1,), (0,)), ((), ()))
NT = (((1,), (1,)), ((), ()))
TN = (((0,), (0,)), ((), ()))


def layer_modulate(values, shift, scale):
    centred = values - jnp.mean(values, axis=-1, keepdims=True)
    normed = centred * lax.rsqrt(jnp.mean(centred * centred, axis=-1, keepdims=True) + norm_eps)
    return normed * (1.0 + scale) + shift


def adam_step(weight, moment_one, moment_two, grads, rate):
    new_one = 0.9 * moment_one + 0.1 * grads
    new_two = 0.999 * moment_two + 0.001 * grads * grads
    fixed_one = new_one / (1.0 - 0.9**STEP)
    fixed_two = new_two / (1.0 - 0.999**STEP)
    new_weight = weight - rate * (fixed_one / (jnp.sqrt(fixed_two) + adam_eps) + 0.01 * weight)
    return (new_weight, new_one, new_two, new_weight.astype(bf16))


def segment_index(position, seq_starts, all_tokens):
    counted = jnp.sum((seq_starts[None, :] <= position[:, None]).astype(jnp.int32), axis=1) - 1
    inside = (position >= 0) & (position < all_tokens)
    return jnp.where(inside, counted, -1)


def fill_window(own_ref, before_ref, after_ref, keys, values):
    halo, own = before_ref.shape[0], own_ref.shape[0]
    heads = keys.shape[0]
    width = heads * HD
    parts = ((before_ref, 0, 0, halo), (own_ref, width, halo, own), (after_ref, 0, halo + own, halo))
    for source, skip, first, count in parts:
        for head in range(heads):
            for index, dest in ((0, keys), (1, values)):
                start = skip + index * width + head * HD
                dest[head, first : first + count, :HD] = source[:, start : start + HD]


def attend_kernel(
    lo_ref, hi_ref, own_ref, before_ref, after_ref, qid_ref, kid_ref, o_ref, l_ref, keys, values, acc
):
    step = pl.program_id(0)
    heads = keys.shape[0]

    @pl.when(step == 0)
    def _():
        lane = lax.broadcasted_iota(jnp.int32, values.shape[1:], 1)
        for head in range(heads):
            values[head] = (lane == HD).astype(bf16)
        fill_window(own_ref, before_ref, after_ref, keys, values)

    qid = qid_ref[...]
    diagonal = lax.broadcasted_iota(jnp.int32, (QB, QB), 0) == lax.broadcasted_iota(
        jnp.int32, (QB, QB), 1
    )
    own_rows = pl.ds(pl.multiple_of(step * QB, QB), QB)
    queries = [own_ref[own_rows, head * HD : (head + 1) * HD] for head in range(heads)]
    acc[...] = jnp.zeros_like(acc)

    @pl.loop(lo_ref[step], hi_ref[step])
    def _(block):
        rows = pl.ds(pl.multiple_of(block * KB, KB), KB)
        same = qid == kid_ref[pl.ds(block, 1), :]
        for head in range(heads):
            scores = lax.dot_general(
                queries[head], keys[head, rows, :], NT, preferred_element_type=f32
            )
            lifted = jnp.where(same, jnp.exp(scores), 0.0).astype(bf16)
            acc[head] += jnp.dot(lifted, values[head, rows, :], preferred_element_type=f32)

    for head in range(heads):
        total = acc[head, :, HD : HD + 1]
        o_ref[:, head * HD : (head + 1) * HD] = (acc[head, :, :HD] / total).astype(bf16)
        l_ref[0, head : head + 1, :] = jnp.sum(
            jnp.where(diagonal, jnp.log(total), 0.0), axis=0, keepdims=True
        )


def attend_back_kernel(
    lo_ref,
    hi_ref,
    own_ref,
    before_ref,
    after_ref,
    do_ref,
    o_ref,
    qid_ref,
    kid_ref,
    l_ref,
    dq_ref,
    d_before_ref,
    d_after_ref,
    d_own_ref,
    keys,
    values,
    d_keys,
    d_values,
    d_query,
):
    step = pl.program_id(0)
    heads = keys.shape[0]
    width = heads * HD

    @pl.when(step == 0)
    def _():
        fill_window(own_ref, before_ref, after_ref, keys, values)
        d_keys[...] = jnp.zeros_like(d_keys)
        d_values[...] = jnp.zeros_like(d_values)

    qid = qid_ref[0]
    ones = jnp.ones((8, HD), bf16)
    own_rows = pl.ds(pl.multiple_of(step * QB, QB), QB)
    queries, outs, dots = [], [], []
    for head in range(heads):
        lanes = slice(head * HD, (head + 1) * HD)
        queries.append(own_ref[own_rows, lanes])
        outs.append(do_ref[:, lanes])
        product = outs[head].astype(f32) * o_ref[:, lanes].astype(f32)
        coarse = product.astype(bf16)
        fine = (product - coarse.astype(f32)).astype(bf16)
        total = lax.dot_general(ones, coarse, NT, preferred_element_type=f32)
        dots.append((total + lax.dot_general(ones, fine, NT, preferred_element_type=f32))[:1])
    d_query[...] = jnp.zeros_like(d_query)

    @pl.loop(lo_ref[step], hi_ref[step])
    def _(block):
        rows = pl.ds(pl.multiple_of(block * KB, KB), KB)
        same = kid_ref[rows, :] == qid
        for head in range(heads):
            key = keys[head, rows, :]
            scores = lax.dot_general(key, queries[head], NT, preferred_element_type=f32)
            probs = jnp.where(same, jnp.exp(scores - l_ref[0, head : head + 1, :]), 0.0)
            d_values[head, rows, :] += jnp.dot(
                probs.astype(bf16), outs[head], preferred_element_type=f32
            )
            d_probs = lax.dot_general(
                values[head, rows, :], outs[head], NT, preferred_element_type=f32
            )
            d_scores = (probs * (d_probs - dots[head])).astype(bf16)
            d_keys[head, rows, :] += jnp.dot(d_scores, queries[head], preferred_element_type=f32)
            d_query[head] += lax.dot_general(d_scores, key, TN, preferred_element_type=f32)

    for head in range(heads):
        dq_ref[:, head * HD : (head + 1) * HD] = (d_query[head] * score_scale).astype(bf16)

    @pl.when(step == pl.num_programs(0) - 1)
    def _():
        halo, own = d_before_ref.shape[0], d_own_ref.shape[0]
        for index, source in ((0, d_keys), (1, d_values)):
            for head in range(heads):
                span = slice(index * width + head * HD, index * width + (head + 1) * HD)
                d_before_ref[:, span] = source[head, :halo, :].astype(bf16)
                d_own_ref[:, span] = source[head, halo : halo + own, :]
                d_after_ref[:, span] = source[head, halo + own :, :].astype(bf16)


def resident(shape):
    return pl.BlockSpec(shape, lambda *index: (0,) * len(shape))


def attention(own, before, after, lo, hi, qid, kid):
    count, width = own.shape[0], own.shape[1] // 3
    heads = width // HD
    window = count + 2 * before.shape[0]
    steps = count // QB
    return pl.pallas_call(
        attend_kernel,
        grid_spec=pltpu.PrefetchScalarGridSpec(
            num_scalar_prefetch=2,
            grid=(steps,),
            in_specs=[
                resident(own.shape),
                resident(before.shape),
                resident(after.shape),
                pl.BlockSpec((QB, 1), lambda i, lo, hi: (i, 0)),
                resident((window // KB, KB)),
            ],
            out_specs=[
                pl.BlockSpec((QB, width), lambda i, lo, hi: (i, 0)),
                pl.BlockSpec((1, 8, QB), lambda i, lo, hi: (i, 0, 0)),
            ],
            scratch_shapes=[
                pltpu.VMEM((heads, window, HD), bf16),
                pltpu.VMEM((heads, window, 2 * HD), bf16),
                pltpu.VMEM((heads, QB, 2 * HD), f32),
            ],
        ),
        out_shape=[
            jax.ShapeDtypeStruct((count, width), bf16),
            jax.ShapeDtypeStruct((steps, 8, QB), f32),
        ],
        compiler_params=pltpu.CompilerParams(vmem_limit_bytes=40 << 20),
        cost_estimate=pl.CostEstimate(flops=40 << 30, bytes_accessed=8 << 20, transcendentals=12 << 20),
        name="attend",
    )(lo, hi, own, before, after, qid[:, None], kid.reshape(window // KB, KB))


def attention_back(own, before, after, d_out, out, lo, hi, qid, kid, logsum):
    count, width = own.shape[0], own.shape[1] // 3
    heads = width // HD
    halo = before.shape[0]
    window = count + 2 * halo
    steps = count // QB
    rows = pl.BlockSpec((QB, width), lambda i, lo, hi: (i, 0))
    return pl.pallas_call(
        attend_back_kernel,
        grid_spec=pltpu.PrefetchScalarGridSpec(
            num_scalar_prefetch=2,
            grid=(steps,),
            in_specs=[
                resident(own.shape),
                resident(before.shape),
                resident(after.shape),
                rows,
                rows,
                pl.BlockSpec((1, 1, QB), lambda i, lo, hi: (i, 0, 0)),
                resident((window, 1)),
                pl.BlockSpec((1, 8, QB), lambda i, lo, hi: (i, 0, 0)),
            ],
            out_specs=[
                rows,
                resident((halo, 2 * width)),
                resident((halo, 2 * width)),
                resident((count, 2 * width)),
            ],
            scratch_shapes=[pltpu.VMEM((heads, window, HD), bf16)] * 2
            + [pltpu.VMEM((heads, window, HD), f32)] * 2
            + [pltpu.VMEM((heads, QB, HD), f32)],
        ),
        out_shape=[
            jax.ShapeDtypeStruct((count, width), bf16),
            jax.ShapeDtypeStruct((halo, 2 * width), bf16),
            jax.ShapeDtypeStruct((halo, 2 * width), bf16),
            jax.ShapeDtypeStruct((count, 2 * width), f32),
        ],
        compiler_params=pltpu.CompilerParams(vmem_limit_bytes=58 << 20),
        cost_estimate=pl.CostEstimate(flops=90 << 30, bytes_accessed=24 << 20, transcendentals=12 << 20),
        name="attend_back",
    )(lo, hi, own, before, after, d_out, out, qid.reshape(steps, 1, QB), kid[:, None], logsum)


def text_windows(spots, blocks, count, work):
    for p in range(blocks):

        @pl.when(spots[blocks + p] == 1)
        def _(p=p):
            first = pl.multiple_of(spots[p], 16)
            base = p * (count // blocks)
            work(p, first, pl.ds(pl.multiple_of(base + first, 16), WINDOW))


def flat(value):
    return value.reshape(-1, value.shape[-1])


def product(x_ref, rows, weight, dims):
    total = None
    for cols, get in weight:
        term = lax.dot_general(x_ref[rows, cols], get(), dims, preferred_element_type=f32)
        total = term if total is None else total + term
    return total


def group_sums(values, blocks_of):
    coarse = values.astype(bf16)
    fine = (values - coarse.astype(f32)).astype(bf16)
    return jnp.dot(coarse, blocks_of, preferred_element_type=f32) + jnp.dot(
        fine, blocks_of, preferred_element_type=f32
    )


def head_blocks(width):
    row = lax.broadcasted_iota(jnp.int32, (width, width), 0) // HD
    col = lax.broadcasted_iota(jnp.int32, (width, width), 1) // HD
    return (row == col).astype(bf16)


def qkv_kernel(blocks, spots, x_ref, w0, w1, image_ref, gain_ref, packed_ref, pre_ref):
    kind = pl.program_id(0)
    every = slice(None)
    size, width = packed_ref.shape[1], packed_ref.shape[2] // 3
    rep = spots[2 * blocks]
    spread = head_blocks(2 * width)

    def finish(t, values, gain):
        if t < 2:
            mean = group_sums(values * values, spread) * (1.0 / HD)
            values = values * lax.rsqrt(mean + norm_eps) * gain
        values = values.astype(bf16)
        return values * jnp.asarray(score_scale, bf16) if t == 0 else values

    for t in range(3):

        @pl.when(kind == t)
        def _(t=t):
            @pl.loop(0, blocks)
            def _(p):
                rows = pl.ds(pl.multiple_of(p * size, size), size)
                values = product(x_ref, rows, [(every, lambda: flat(w0[...]))], NN)
                if t < 2:
                    pre_ref[rows, :] = values
                values = finish(t, values, gain_ref[0, :1])
                for g in range(2):
                    packed_ref[pl.ds((rep ^ p) * 2 + g, 1), :, t * width : (t + 1) * width] = values[
                        :, g * width : (g + 1) * width
                    ][None]

            def text(p, first, rows):
                values = product(x_ref, rows, [(every, lambda: flat(w1[...]))], NN)
                image = image_ref[rows, :] == 1
                if t < 2:
                    pre_ref[rows, :] = jnp.where(image, pre_ref[rows, :], values)
                values = finish(t, values, gain_ref[0, 1:])
                for g in range(2):
                    place = (
                        pl.ds((rep ^ p) * 2 + g, 1),
                        pl.ds(first, WINDOW),
                        slice(t * width, (t + 1) * width),
                    )
                    packed_ref[place] = jnp.where(
                        image[None], packed_ref[place], values[:, g * width : (g + 1) * width][None]
                    )

            text_windows(spots, blocks, x_ref.shape[0], text)


def column_weights(weight, tile):
    shards, _, rows, _ = weight.shape
    return [
        pl.BlockSpec((shards, 1, rows, tile), lambda j, s, stream=stream: (0, stream, 0, j))
        for stream in range(2)
    ]


def tiled_gains(gains, heads):
    return jnp.stack([jnp.tile(gains[:, :HD], (1, heads)), jnp.tile(gains[:, HD:], (1, heads))])


def qkv_product(spots, x, weight, image, gains):
    count, depth = x.shape
    blocks = (spots.shape[0] - 1) // 2
    part = weight.shape[3] // 3
    size = count // blocks
    return pl.pallas_call(
        functools.partial(qkv_kernel, blocks),
        grid_spec=pltpu.PrefetchScalarGridSpec(
            num_scalar_prefetch=1,
            grid=(3,),
            in_specs=[
                resident(x.shape),
                *column_weights(weight, part),
                resident(image.shape),
                pl.BlockSpec((1, 2, part), lambda j, s: (jnp.minimum(j, 1), 0, 0)),
            ],
            out_specs=[
                resident((2 * blocks, size, 3 * part // 2)),
                pl.BlockSpec((count, part), lambda j, s: (0, jnp.minimum(j, 1))),
            ],
        ),
        out_shape=[
            jax.ShapeDtypeStruct((2 * blocks, size, 3 * part // 2), bf16),
            jax.ShapeDtypeStruct((count, 2 * part), f32),
        ],
        compiler_params=pltpu.CompilerParams(vmem_limit_bytes=40 << 20),
        cost_estimate=pl.CostEstimate(flops=7 << 30, bytes_accessed=20 << 20, transcendentals=0),
        name="qkv_product",
    )(spots, x, weight, weight, image, tiled_gains(gains, part // HD))


def norm_back_kernel(blocks, spots, came_ref, pre_ref, image_ref, gain_ref, out_ref, sum_ref, both):
    @pl.when(pl.program_id(0) == 0)
    def _():
        sum_ref[...] = jnp.zeros_like(sum_ref)

    part = both.shape[1]
    width = part // 2
    image = image_ref[...] == 1
    spread = head_blocks(part)
    for t in range(3):
        for g in range(2):
            both[:, g * width : (g + 1) * width] = came_ref[g, :, t * width : (t + 1) * width].astype(
                f32
            )
        grad = both[...]
        if t < 2:
            pre = pre_ref[:, t * part : (t + 1) * part]
            scale = lax.rsqrt(group_sums(pre * pre, spread) * (1.0 / HD) + norm_eps)
            gain = jnp.where(image, gain_ref[t, :1], gain_ref[t, 1:])
            each = grad * pre * scale
            total = jnp.sum(each, axis=0, keepdims=True)
            text = jnp.sum(jnp.where(image, 0.0, each), axis=0, keepdims=True)
            sum_ref[2 * t : 2 * t + 1, :] += total - text
            sum_ref[2 * t + 1 : 2 * t + 2, :] += text
            grad = grad * gain
            mean = group_sums(grad * pre, spread) * (1.0 / HD)
            grad = scale * (grad - pre * (scale * scale * mean))
        out_ref[:, t * part : (t + 1) * part] = grad.astype(bf16)


def norm_back(spots, came, pre, image, gains):
    blocks = (spots.shape[0] - 1) // 2
    _, size, width3 = came.shape
    part = 2 * width3 // 3
    tiled = tiled_gains(gains, part // HD)
    return pl.pallas_call(
        functools.partial(norm_back_kernel, blocks),
        grid_spec=pltpu.PrefetchScalarGridSpec(
            num_scalar_prefetch=1,
            grid=(blocks,),
            in_specs=[
                pl.BlockSpec((2, size, width3), lambda p, s: (s[2 * blocks] ^ p, 0, 0)),
                pl.BlockSpec((size, 2 * part), lambda p, s: (p, 0)),
                pl.BlockSpec((size, 1), lambda p, s: (p, 0)),
                resident(tiled.shape),
            ],
            out_specs=[
                pl.BlockSpec((size, 3 * part), lambda p, s: (p, 0)),
                resident((4, part)),
            ],
            scratch_shapes=[pltpu.VMEM((size, part), f32)],
        ),
        out_shape=[
            jax.ShapeDtypeStruct((blocks * size, 3 * part), bf16),
            jax.ShapeDtypeStruct((4, part), f32),
        ],
        compiler_params=pltpu.CompilerParams(vmem_limit_bytes=32 << 20),
        cost_estimate=pl.CostEstimate(flops=4 << 30, bytes_accessed=12 << 20, transcendentals=0),
        name="norm_back",
    )(spots, came, pre, image, tiled)


def forward_kernel(blocks, gathers, gelu, spots, x_ref, w0, w1, image_ref, *rest):
    rep = spots[2 * blocks]
    out_ref = rest[0]
    if gathers:
        x_out = rest[1]
        size, width = x_ref.shape[1:]

        @pl.when(pl.program_id(0) == 0)
        def _():
            for p in range(blocks):
                for g in range(2):
                    x_out[p * size : (p + 1) * size, g * width : (g + 1) * width] = x_ref[
                        pl.ds((rep ^ p) * 2 + g, 1)
                    ][0]

        x_ref = x_out
    every = slice(None)
    count = x_ref.shape[0]

    def finish(values):
        if not gelu:
            return (values.astype(bf16),)
        square = values * values
        bend = jnp.tanh(values * (GELU_A + GELU_A * GELU_B * square))
        half = 0.5 * (1.0 + bend)
        slope = half + 0.5 * values * (1.0 - bend * bend) * (GELU_A + 3.0 * GELU_A * GELU_B * square)
        return (values * half).astype(bf16), slope.astype(bf16)

    outs = rest if gelu else (out_ref,)
    chunk = count // (blocks if gelu else 2)

    @pl.loop(0, count // chunk)
    def _(p):
        rows = pl.ds(pl.multiple_of(p * chunk, chunk), chunk)
        values = product(x_ref, rows, [(every, lambda: flat(w0[...]))], NN)
        for out, value in zip(outs, finish(values)):
            out[rows, :] = value

    def text(p, first, rows):
        values = product(x_ref, rows, [(every, lambda: flat(w1[...]))], NN)
        image = image_ref[rows, :] == 1
        for out, value in zip(outs, finish(values)):
            out[rows, :] = jnp.where(image, out[rows, :], value)

    text_windows(spots, blocks, count, text)


def forward_product(spots, x, weight, image, gathers=False, gelu=False):
    blocks = (spots.shape[0] - 1) // 2
    if weight.ndim == 5:
        tiles, q, _, rows, tile = weight.shape
        weights = [
            pl.BlockSpec((1, q, 1, rows, tile), lambda j, s, stream=stream: (j, 0, stream, 0, 0))
            for stream in range(2)
        ]
        depth = q * rows
    else:
        depth, tile = weight.shape[0] * weight.shape[2], COLS
        tiles = weight.shape[3] // tile
        weights = column_weights(weight, tile)
    count = image.shape[0]
    column = pl.BlockSpec((count, tile), lambda j, s: (0, j))
    whole = jax.ShapeDtypeStruct((count, tiles * tile), bf16)
    out_specs, out_shape = [column], [whole]
    if gathers:
        out_specs.append(resident((count, depth)))
        out_shape.append(jax.ShapeDtypeStruct((count, depth), bf16))
    if gelu:
        out_specs.append(column)
        out_shape.append(whole)
    return pl.pallas_call(
        functools.partial(forward_kernel, blocks, gathers, gelu),
        grid_spec=pltpu.PrefetchScalarGridSpec(
            num_scalar_prefetch=1,
            grid=(tiles,),
            in_specs=[resident(x.shape), *weights, resident(image.shape)],
            out_specs=out_specs,
        ),
        out_shape=out_shape,
        compiler_params=pltpu.CompilerParams(vmem_limit_bytes=40 << 20),
        cost_estimate=pl.CostEstimate(
            flops=3 * count * depth * tiles * tile, bytes_accessed=20 << 20, transcendentals=0
        ),
        name="forward_product",
    )(spots, x, weight, weight, image)


def backward_kernel(blocks, turned, scaled, packs, spots, dy_ref, w0, w1, image_ref, *rest):
    rest = list(rest)
    factor_ref = rest.pop(0) if scaled else None
    out_ref = rest[0]
    if turned:
        tiles, tile = w0.shape[0], w0.shape[4]
        weights = [
            [
                (slice(n * tile, (n + 1) * tile), lambda w=w, n=n: flat(w[n, :, 0]))
                for n in range(tiles)
            ]
            for w in (w0, w1)
        ]
    else:
        every = slice(None)
        weights = [[(every, lambda w=w: flat(w[...]))] for w in (w0, w1)]
    count = dy_ref.shape[0]
    size = count // blocks
    rep = spots[2 * blocks]
    part = pl.program_id(0)

    def finish(rows, values):
        if scaled:
            values = values * factor_ref[rows, :].astype(f32)
        return values.astype(bf16)

    chunk = size if packs or scaled else count // 2

    @pl.loop(0, count // chunk)
    def _(p):
        rows = pl.ds(pl.multiple_of(p * chunk, chunk), chunk)
        values = finish(rows, product(dy_ref, rows, weights[0], NT))
        if packs:
            out_ref[pl.ds((rep ^ p) * 2 + part, 1)] = values[None]
        else:
            out_ref[rows, :] = values

    def text(p, first, rows):
        values = finish(rows, product(dy_ref, rows, weights[1], NT))
        image = image_ref[rows, :] == 1
        if packs:
            place = (pl.ds((rep ^ p) * 2 + part, 1), pl.ds(first, WINDOW), slice(None))
            out_ref[place] = jnp.where(image[None], out_ref[place], values[None])
        else:
            out_ref[rows, :] = jnp.where(image, out_ref[rows, :], values)

    text_windows(spots, blocks, count, text)


def backward_product(spots, dy, weight, image, factor=None, packs=False):
    blocks = (spots.shape[0] - 1) // 2
    turned = weight.ndim == 5
    count = image.shape[0]
    if turned:
        tiles, q, _, rows, tile = weight.shape
        step = q * rows // 2 if packs else min(q * rows, 768)
        grid = (q * rows // step,)
        if rows < step:
            block = (tiles, step // rows, 1, rows, tile)
            weights = [
                pl.BlockSpec(block, lambda j, s, stream=stream: (0, j, stream, 0, 0))
                for stream in range(2)
            ]
        else:
            per = rows // step
            weights = [
                pl.BlockSpec(
                    (tiles, 1, 1, step, tile),
                    lambda j, s, stream=stream: (0, j // per, stream, j % per, 0),
                )
                for stream in range(2)
            ]
        depth = q * rows
    else:
        shards, _, rows, width = weight.shape
        depth = shards * rows
        bunch = max(1, 768 // rows)
        step = bunch * rows
        grid = (depth // step,)
        weights = [
            pl.BlockSpec((bunch, 1, rows, width), lambda j, s, stream=stream: (j, stream, 0, 0))
            for stream in range(2)
        ]
    column = pl.BlockSpec((count, step), lambda j, s: (0, j))
    in_specs = [resident(dy.shape), *weights, resident(image.shape)]
    operands = [spots, dy, weight, weight, image]
    if factor is not None:
        in_specs.append(column)
        operands.append(factor)
    if packs:
        shape = (2 * blocks, count // blocks, step)
        out_spec, out_shape = resident(shape), jax.ShapeDtypeStruct(shape, bf16)
    else:
        out_spec, out_shape = column, jax.ShapeDtypeStruct((count, depth), bf16)
    return pl.pallas_call(
        functools.partial(backward_kernel, blocks, turned, factor is not None, packs),
        grid_spec=pltpu.PrefetchScalarGridSpec(
            num_scalar_prefetch=1,
            grid=grid,
            in_specs=in_specs,
            out_specs=out_spec,
        ),
        out_shape=out_shape,
        compiler_params=pltpu.CompilerParams(vmem_limit_bytes=48 << 20),
        cost_estimate=pl.CostEstimate(
            flops=3 * count * depth * dy.shape[1], bytes_accessed=20 << 20, transcendentals=0
        ),
        name="backward_product",
    )(*operands)


def gradient_kernel(blocks, spots, x_ref, dy_ref, image_ref, out, turned_x, masked, acc):
    count, width = dy_ref.shape
    size = count // blocks
    cols_at_once = acc.shape[1]

    @pl.when(pl.program_id(0) == 0)
    def _():
        @pl.loop(0, blocks)
        def _(p):
            rows = pl.ds(pl.multiple_of(p * size, size), size)
            kept = dy_ref[rows, :]
            masked[rows, :] = jnp.where(image_ref[rows, :] == 1, kept, jnp.zeros_like(kept))

    turned_x[...] = x_ref[...].T

    def store(stream, n, values):
        values = values.astype(bf16)
        if len(out.shape) == 5:
            tile, per = out.shape[4], out.shape[3]
            for t in range(cols_at_once // tile):
                for q in range(out.shape[1]):
                    out[n * (cols_at_once // tile) + t, q, stream] = values[
                        q * per : (q + 1) * per, t * tile : (t + 1) * tile
                    ]
        else:
            per = out.shape[2]
            for k in range(out.shape[0]):
                out[k, stream, :, n * cols_at_once : (n + 1) * cols_at_once] = values[
                    k * per : (k + 1) * per
                ]

    for n in range(width // cols_at_once):
        cols = slice(n * cols_at_once, (n + 1) * cols_at_once)
        store(0, n, jnp.dot(turned_x[...], masked[:, cols], preferred_element_type=f32))
        acc[...] = jnp.zeros_like(acc)

        def text(p, first, rows, cols=cols):
            kept = dy_ref[rows, cols]
            kept = jnp.where(image_ref[rows, :] == 1, jnp.zeros_like(kept), kept)
            acc[...] += lax.dot_general(x_ref[rows, :], kept, TN, preferred_element_type=f32)

        text_windows(spots, blocks, count, text)
        store(1, n, acc[...])


def gradient(spots, x, dy, image, shape):
    blocks = (spots.shape[0] - 1) // 2
    count, depth = x.shape
    width = dy.shape[1]
    step = 384
    cols = 1152 if width % 768 else 768
    if len(shape) == 4:
        per = step // shape[2]
        out_spec = pl.BlockSpec((per, 2, shape[2], width), lambda j, s: (j, 0, 0, 0))
    else:
        tiles, q, _, rows, tile = shape
        if rows < step:
            block = (tiles, step // rows, 2, rows, tile)
            out_spec = pl.BlockSpec(block, lambda j, s: (0, j, 0, 0, 0))
        else:
            per = rows // step
            out_spec = pl.BlockSpec(
                (tiles, 1, 2, step, tile), lambda j, s: (0, j // per, 0, j % per, 0)
            )
    return pl.pallas_call(
        functools.partial(gradient_kernel, blocks),
        grid_spec=pltpu.PrefetchScalarGridSpec(
            num_scalar_prefetch=1,
            grid=(depth // step,),
            in_specs=[
                pl.BlockSpec((count, step), lambda j, s: (0, j)),
                resident(dy.shape),
                resident(image.shape),
            ],
            out_specs=out_spec,
            scratch_shapes=[
                pltpu.VMEM((step, count), bf16),
                pltpu.VMEM((count, width), bf16),
                pltpu.VMEM((step, cols), f32),
            ],
        ),
        out_shape=jax.ShapeDtypeStruct(shape, bf16),
        compiler_params=pltpu.CompilerParams(vmem_limit_bytes=48 << 20),
        cost_estimate=pl.CostEstimate(
            flops=3 * count * depth * width, bytes_accessed=20 << 20, transcendentals=0
        ),
        name="gradient",
    )(spots, x, dy, image)


def over_rep(value, target):
    count = lax.axis_size("rep")
    return lax.ppermute(value, "rep", [(r, target(r)) for r in range(count)])


def sibling(value):
    return over_rep(value, lambda r: r ^ 1)


def across(value):
    return over_rep(value, lambda r: r ^ 2)


def gather_rep(value):
    far = across(value)
    return [value, sibling(value), far, sibling(far)]


def reduce_rep(parts):
    near = sibling((parts[1], parts[3]))
    far = across((parts[2].astype(f32) + near[1].astype(f32)).astype(bf16))
    return parts[0].astype(f32) + near[0].astype(f32) + far.astype(f32)


def turn(value):
    reps, shards = lax.axis_size("rep"), lax.axis_size("shard")
    q = shards // reps
    pairs = []
    for r in range(reps):
        for s in range(shards):
            pairs.append((r * shards + s, (s // q) * shards + r * q + s % q))
    return lax.ppermute(value, ("rep", "shard"), pairs)


def gather_weight(weight_low):
    return lax.all_gather(weight_low, "shard", axis=0, tiled=False)


def gather_turned(moved):
    full = gather_weight(moved)
    reps = lax.axis_size("rep")
    return full.reshape(reps, full.shape[0] // reps, *full.shape[1:])


def scatter_weight(terms):
    blocks = terms.reshape(lax.axis_size("shard"), -1, *terms.shape[-3:])
    return lax.psum_scatter(
        blocks.reshape(-1, *terms.shape[-2:]), "shard", scatter_dimension=0, tiled=True
    ).reshape(terms.shape[-3:])


def body(
    tokens,
    cotangent,
    cond,
    seq_lengths,
    stream_mask,
    w_mod,
    m_mod,
    v_mod,
    w_qkv,
    m_qkv,
    v_qkv,
    w_out,
    m_out,
    v_out,
    w_fc1,
    m_fc1,
    v_fc1,
    w_fc2,
    m_fc2,
    v_fc2,
    gains,
    m_gains,
    v_gains,
):
    tok_rows, model_width = tokens.shape
    slot_count = seq_lengths.shape[0]
    reps, shards = lax.axis_size("rep"), lax.axis_size("shard")
    rep_index, shard_index = lax.axis_index("rep"), lax.axis_index("shard")
    device_index = rep_index * shards + shard_index
    all_tokens = tok_rows * reps * shards
    reach = (MAXLEN - 2) // tok_rows + 1
    part_width = model_width // reps
    part_rows = w_mod.shape[1]
    mod_cols = w_mod.shape[2]

    seq_starts = jnp.cumsum(seq_lengths) - seq_lengths
    local_pos = device_index * tok_rows + jnp.arange(tok_rows, dtype=jnp.int32)
    seq_ids = segment_index(local_pos, seq_starts, all_tokens)
    image_col = (stream_mask == 1)[:, None]
    image_group = jnp.concatenate(gather_rep(stream_mask)) == 1
    image = image_group[:, None].astype(jnp.int32)
    text_group = ~image_group.reshape(reps, tok_rows)
    text_first = jnp.argmax(text_group, axis=1).astype(jnp.int32)
    spots = jnp.concatenate(
        [
            jnp.minimum(text_first // 16 * 16, tok_rows - WINDOW),
            jnp.any(text_group, axis=1).astype(jnp.int32),
            rep_index[None].astype(jnp.int32),
        ]
    )

    silu_cond = jax.nn.silu(cond).astype(bf16)
    cond_rows = lax.dynamic_slice_in_dim(silu_cond, shard_index * part_rows, part_rows, 1)
    mod_terms = jnp.concatenate(
        [
            jnp.dot(cond_rows, w_mod[s].astype(bf16), preferred_element_type=f32)
            for s in range(2)
        ],
        axis=0,
    ).astype(bf16)
    device_count = reps * shards
    firsts = segment_index(
        jnp.arange(device_count, dtype=jnp.int32) * tok_rows, seq_starts, all_tokens
    )
    seconds = jnp.minimum(firsts + 1, slot_count - 1)
    stream_offset = jnp.arange(2, dtype=jnp.int32) * slot_count
    wanted = jnp.stack([firsts, seconds], axis=1)[:, :, None] + stream_offset
    hot = (wanted.reshape(-1, 1) == jnp.arange(2 * slot_count, dtype=jnp.int32)).astype(bf16)
    mod_sent = jnp.dot(hot, mod_terms, preferred_element_type=f32).astype(bf16)
    mod_got = lax.all_to_all(
        mod_sent.reshape(device_count, 4, mod_cols), ("rep", "shard"), 0, 0, tiled=True
    )
    mod_sum = jnp.sum(mod_got.reshape(reps, shards, 4, mod_cols).astype(f32), axis=1).astype(bf16)
    mod_rows = jnp.concatenate([mod_sum[r] for r in range(reps)], axis=1)

    qkv_low = w_qkv.astype(bf16)
    chunks = [
        over_rep(
            qkv_low[:, :, i * part_width : (i + 1) * part_width],
            lambda r, i=i: (3 * r + i) % reps,
        )
        for i in range(3)
    ]
    turns = rep_index % 3

    def rolled(parts, amount):
        return [
            jnp.where(
                amount == 0,
                parts[t],
                jnp.where(amount == 1, parts[(t + 1) % 3], parts[(t + 2) % 3]),
            )
            for t in range(3)
        ]

    qkv_weights = gather_weight(jnp.concatenate(rolled(chunks, turns), axis=2))
    fc1_weights = gather_weight(w_fc1.astype(bf16))
    out_turned = turn(w_out.astype(bf16))
    fc2_turned = turn(w_fc2.astype(bf16))

    first_seq = seq_ids[0]
    second_seq = jnp.minimum(first_seq + 1, slot_count - 1)
    is_second = (seq_ids != first_seq)[:, None]

    def mod_block(index):
        span = slice(index * model_width, (index + 1) * model_width)
        rows = mod_rows[:, span].astype(f32)
        pick = [jnp.where(is_second, rows[2 + s][None], rows[s][None]) for s in range(2)]
        return jnp.where(image_col, pick[0], pick[1])

    shift_one, scale_one, gate_one, shift_two, scale_two, gate_two = [
        mod_block(i) for i in range(6)
    ]
    stream_in = tokens.astype(f32)
    back_out = cotangent.astype(f32)
    act_one = layer_modulate(stream_in, shift_one, scale_one).astype(bf16)
    act_one_group = jnp.concatenate(gather_rep(act_one))
    d_down = (gate_two * back_out).astype(bf16)
    d_down_group = jnp.concatenate(gather_rep(d_down))

    act_one_group, out_turned, fc2_turned = lax.optimization_barrier(
        (act_one_group, out_turned, fc2_turned)
    )
    out_weights = gather_turned(out_turned)
    fc2_weights = gather_turned(fc2_turned)

    packed, qk_pre = qkv_product(spots, act_one_group, qkv_weights, image, gains)

    bunch = 2 * reps
    bunches = shards // bunch
    half_width = part_width // 2
    groups = [[q * bunch + i for i in range(bunch)] for q in range(bunches)]

    def exchange(value):
        return lax.all_to_all(
            value, "shard", 0, 0, axis_index_groups=None if bunches == 1 else groups, tiled=True
        )

    stretch_count = reps * bunches
    stretch_rows = bunch * tok_rows
    halo = reach * tok_rows

    def stretch_shift(value, steps):
        def place(stretch, g):
            return (stretch % bunches) * bunch + (stretch // bunches) * 2 + g

        pairs = [
            (place(t, g), place(t + steps, g))
            for t in range(stretch_count)
            for g in range(2)
            if 0 <= t + steps < stretch_count
        ]
        return lax.ppermute(value, "shard", pairs)

    own = exchange(packed).reshape(stretch_rows, 3 * half_width)
    pair_own = own[:, half_width:]
    pair_before = stretch_shift(pair_own[-halo:], 1)
    pair_after = stretch_shift(pair_own[:halo], -1)
    window_rows = stretch_rows + 2 * halo
    stretch = ((shard_index % bunch) // 2) * bunches + shard_index // bunch
    stretch_first = stretch * stretch_rows
    qid = segment_index(
        stretch_first + jnp.arange(stretch_rows, dtype=jnp.int32), seq_starts, all_tokens
    )
    kid = segment_index(
        stretch_first - halo + jnp.arange(window_rows, dtype=jnp.int32), seq_starts, all_tokens
    )
    seq_ends = seq_starts + seq_lengths
    low_pos = seq_starts[qid[::QB]] - (stretch_first - halo)
    high_pos = seq_ends[qid[QB - 1 :: QB]] - (stretch_first - halo)
    lo = jnp.clip(low_pos // KB, 0, window_rows // KB).astype(jnp.int32)
    hi = jnp.clip((high_pos + KB - 1) // KB, 0, window_rows // KB).astype(jnp.int32)
    attended_own, logsum = attention(own, pair_before, pair_after, lo, hi, qid, kid)
    attended_came = exchange(attended_own.reshape(bunch, tok_rows, half_width))

    def split_group(value):
        return [value[p * tok_rows : (p + 1) * tok_rows] for p in range(reps)]

    branch_terms, attended_low = forward_product(
        spots, attended_came, out_weights, image, gathers=True
    )
    branch = reduce_rep(split_group(branch_terms))
    branch, fc1_weights = lax.optimization_barrier((branch, fc1_weights))
    mid = stream_in + gate_one * branch
    act_two = layer_modulate(mid, shift_two, scale_two).astype(bf16)
    act_two_group = jnp.concatenate(gather_rep(act_two))
    gelu_low, gelu_slope = forward_product(spots, act_two_group, fc1_weights, image, gelu=True)
    down_proj = reduce_rep(split_group(forward_product(spots, gelu_low, fc2_weights, image)[0]))
    output = mid + gate_two * down_proj

    d_gate_two = back_out * down_proj
    d_up = backward_product(spots, d_down_group, fc2_weights, image, factor=gelu_slope)
    g_fc2 = turn(
        scatter_weight(gradient(spots, gelu_low, d_down_group, image, fc2_weights.shape))
    )
    d_act_two = reduce_rep(split_group(backward_product(spots, d_up, fc1_weights, image)))
    g_fc1 = scatter_weight(gradient(spots, act_two_group, d_up, image, fc1_weights.shape))
    d_mid_norm, d_shift_two, d_scale_two = jax.vjp(layer_modulate, mid, shift_two, scale_two)[1](
        d_act_two
    )
    d_mid = back_out + d_mid_norm
    d_branch = (gate_one * d_mid).astype(bf16)
    d_gate_one = d_mid * branch
    d_branch_group = jnp.concatenate(gather_rep(d_branch))
    d_attended = backward_product(spots, d_branch_group, out_weights, image, packs=True)
    g_out = turn(
        scatter_weight(gradient(spots, attended_low, d_branch_group, image, out_weights.shape))
    )
    d_attended_own = exchange(d_attended).reshape(stretch_rows, half_width)
    d_query_own, d_before, d_after, d_pair_own = attention_back(
        own, pair_before, pair_after, d_attended_own, attended_own, lo, hi, qid, kid, logsum
    )
    from_later = stretch_shift(d_before, -1).astype(f32)
    from_earlier = stretch_shift(d_after, 1).astype(f32)
    rest = jnp.zeros((stretch_rows - halo, 2 * half_width), f32)
    d_pair_own = (
        d_pair_own
        + jnp.concatenate([rest, from_later], axis=0)
        + jnp.concatenate([from_earlier, rest], axis=0)
    )
    d_own = jnp.concatenate([d_query_own, d_pair_own.astype(bf16)], axis=1)
    d_came = exchange(d_own.reshape(bunch, tok_rows, 3 * half_width))
    d_qkv, gain_sums = norm_back(spots, d_came, qk_pre, image, gains)
    d_act_one = reduce_rep(split_group(backward_product(spots, d_qkv, qkv_weights, image)))
    g_qkv_group = scatter_weight(gradient(spots, act_one_group, d_qkv, image, qkv_weights.shape))
    g_parts = [
        g_qkv_group[:, :, t * part_width : (t + 1) * part_width] for t in range(3)
    ]
    g_parts = rolled(g_parts, (3 - turns) % 3)
    g_qkv = jnp.concatenate(
        [over_rep(g_parts[i], lambda d, i=i: (3 * (d - i)) % reps) for i in range(3)], axis=2
    )

    d_in_norm, d_shift_one, d_scale_one = jax.vjp(layer_modulate, stream_in, shift_one, scale_one)[
        1
    ](d_act_one)
    d_tokens = d_mid + d_in_norm
    d_mod_tok = jnp.concatenate(
        [d_shift_one, d_scale_one, d_gate_one, d_shift_two, d_scale_two, d_gate_two], axis=1
    )
    image_flag = image_col[:, 0]
    second_flag = is_second[:, 0]
    selector = jnp.stack(
        [
            ~second_flag & image_flag,
            ~second_flag & ~image_flag,
            second_flag & image_flag,
            second_flag & ~image_flag,
        ],
        axis=1,
    ).astype(f32)
    pooled = jnp.einsum("tp,te->pe", selector, d_mod_tok, precision=lax.Precision.HIGHEST)
    gain_sums = jnp.sum(gain_sums.reshape(2, 2, part_width // HD, HD), axis=2)
    gain_part = jnp.concatenate([gain_sums[0], gain_sums[1]], axis=1)
    gain_rows = jnp.concatenate([gain_part, jnp.zeros_like(gain_part)], axis=0)
    leaving = jnp.stack(
        [
            jnp.concatenate([pooled[:, r * mod_cols : (r + 1) * mod_cols], gain_rows], axis=1)
            for r in range(reps)
        ]
    )
    leaving = jnp.broadcast_to(leaving[:, None], (reps, shards, *leaving.shape[1:]))
    came = lax.all_to_all(
        leaving.reshape(device_count, *leaving.shape[2:]), ("rep", "shard"), 0, 0, tiled=True
    )
    g_gains = jnp.sum(came[:, :2, mod_cols:], axis=0)
    came = came[:, :, :mod_cols].reshape(2 * device_count, 2, mod_cols)
    seqs = jnp.stack([firsts, seconds], axis=1).reshape(-1)
    hot_seq = (seqs[:, None] == jnp.arange(slot_count, dtype=jnp.int32)).astype(bf16)
    cond_seq = jnp.dot(hot_seq, cond_rows, preferred_element_type=f32)
    g_mod = jnp.stack(
        [
            lax.dot_general(
                cond_seq,
                came[:, s],
                (((0,), (0,)), ((), ())),
                precision=lax.Precision.HIGHEST,
                preferred_element_type=f32,
            )
            for s in range(2)
        ]
    )
    up_mod = adam_step(w_mod, m_mod, v_mod, g_mod, rate_mod)
    up_qkv = adam_step(w_qkv, m_qkv, v_qkv, g_qkv.astype(f32), rate_qkv)
    up_out = adam_step(w_out, m_out, v_out, g_out.astype(f32), rate_out)
    up_fc1 = adam_step(w_fc1, m_fc1, v_fc1, g_fc1.astype(f32), rate_fc1)
    up_fc2 = adam_step(w_fc2, m_fc2, v_fc2, g_fc2.astype(f32), rate_fc2)
    up_gains = adam_step(gains, m_gains, v_gains, g_gains, rate_gains)
    return (
        output.astype(bf16),
        d_tokens,
        *up_mod,
        *up_qkv,
        *up_out,
        *up_fc1,
        *up_fc2,
        *up_gains[:3],
    )


def solution(mesh):
    rows = P(("rep", "shard"), None)
    held = P(None, "shard", "rep")
    return jax.shard_map(
        body,
        mesh=mesh,
        in_specs=(rows, rows, P(), P(), P(("rep", "shard")), *([held] * 15), P(), P(), P()),
        out_specs=(rows, rows, *([held] * 20), P(), P(), P()),
        check_vma=False,
    )
```

time: 5650 us -> 1470 us (0.26)
  waiting for transfers between devices: 3810 us -> 741 us
  matrix products: 571 us -> 11.5 us
  local copies, waits for them, and re-layouts: 454 us -> 62.5 us
  Pallas kernels: 0 us -> 318 us
  blocking collectives: 359 us -> 73.1 us
  other arithmetic: 294 us -> 92.8 us
    reduce_scatter x8 -> x4, waiting for transfers between devices: 1600 us -> 137 us  [scatter_weight(): lax.psum_scatter(blocks.reshape(-1, *terms.shape[-2:]), 'shard', scatter_...]
    all_gather x8 -> x4, waiting for transfers between devices: 1140 us -> 0.03 us  [gather_weight(): return lax.all_gather(weight_low, 'shard', axis=0, tiled=False)]
    ppermute x32 -> x41, waiting for transfers between devices: 878 us -> 320 us  [the longest x33 166 us: over_rep(): return lax.ppermute(value, 'rep', [(r, target(r)) for r in range(count)])]
    dot_general x47 -> x6, matrix products: 564 us -> 7.54 us  [the longest x2 3.17 us: body(): lax.dot_general(cond_seq, came[:, s], (((0,), (0,)), ((), ())), precision...]
    all_gather x1 -> x0, blocking collectives: 319 us -> none  [body(): mod_all = lax.all_gather(mod_local, ('rep', 'shard'), axis=2, tiled=True)]
    pallas_call x0 -> x15, Pallas kernels: none -> 318 us  [the longest x1 87 us: attention_back(): pl.pallas_call(attend_back_kernel, grid_spec=pltpu.PrefetchScalarGridSpec...]
    all_to_all x0 -> x5, waiting for transfers between devices: none -> 284 us  [the longest x3 242 us: exchange(): lax.all_to_all(value, 'shard', 0, 0, axis_index_groups=None if bunches ==...]
    psum x2 -> x0, waiting for transfers between devices: 195 us -> none  [the longest x1 195 us: weight_gradient(): lax.psum(summed[1].astype(jnp.bfloat16), 'rep').astype(jnp.float32)]
  transfers between devices with their start and end apart: 51 -> 54, of which waited for: 33 -> 27; matrix products, arithmetic and copies ran while one was open for 20% -> 8% of each run, Pallas kernels for 0% -> 19%
where the time goes in v1:
time: 1470 us; the launch traced here: 1460 us
  waiting for transfers between devices  741 us (50%)
  Pallas kernels  318 us (22%)
  starting transfers between devices  144 us (10%)
  other arithmetic  92.8 us (6%)
  blocking collectives  73.1 us (5%)
  local copies, waits for them, and re-layouts  62.5 us (4%)
  between operations  16.2 us (1%)
    all_to_all x3, waiting for transfers between devices, exchange(): lax.all_to_all(value, 'shard', 0, 0, axis_index_groups=None if bunches ==...  242 us
    ppermute x33, waiting for transfers between devices, over_rep(): return lax.ppermute(value, 'rep', [(r, target(r)) for r in range(count)])  166 us
    reduce_scatter x4, waiting for transfers between devices, scatter_weight(): lax.psum_scatter(blocks.reshape(-1, *terms.shape[-2:]), 'shard', scatter_...  137 us
    pallas_call x1, Pallas kernels, attention_back(): pl.pallas_call(attend_back_kernel, grid_spec=pltpu.PrefetchScalarGridSpec...  87 us
    ppermute x4, waiting for transfers between devices, turn(): return lax.ppermute(value, ('rep', 'shard'), pairs)  83.5 us
    ppermute x33, starting transfers between devices, over_rep(): return lax.ppermute(value, 'rep', [(r, target(r)) for r in range(count)])  82.1 us
    all_to_all x1, blocking collectives, exchange(): lax.all_to_all(value, 'shard', 0, 0, axis_index_groups=None if bunches ==...  73.1 us
    ppermute x4, waiting for transfers between devices, stretch_shift(): return lax.ppermute(value, 'shard', pairs)  70.5 us
  transfers between devices with their start and end apart: 54, of which 27 were waited for; matrix products, arithmetic and copies ran while one was open for 8% of the time, Pallas kernels for 19%

profile of v1, /device:TPU:1, one launch (start us, length us, event | category | flops | bytes accessed | tf_op | source)
XLA Modules:
  0.0 1458.6 jit_solution(18230030677911332229)
XLA Ops:
  9.8 3.7 collective-permute-start.10
  13.6 4.6 collective-permute-start.8
  18.2 4.3 collective-permute-done.8
  34.0 6.0 all-to-all-start
  42.8 30.5 %all-to-all-done = bf16[32,4,2304]{2,1,0:T(4,128)(2,1)} async-done(((bf16[32,4,2304]{2,1,0:T(4,128)(2,1)}), bf16[32,4,2304]{2,1,0:T(4,128)(2,1)}, u32[]{:S(2)}, u32[]{:S(2)}) %all-to-all-start) | async-done | bytes 589856 | tf_op jit(solution)/shard_map/all_to_all | solution.py:873
  75.5 3.5 fusion.16
  80.5 21.2 %collective-permute-done.4 = bf16[320,1536]{1,0:T(8,128)(2,1)S(1)} collective-permute-done((bf16[320,1536]{1,0:T(8,128)(2,1)S(1)}, bf16[320,1536]{1,0:T(8,128)(2,1)S(1)}, u32[]{:S(2)}, u32[]{:S(2)}) %collective-permute-start.4) | collective-permute-done | bytes 983072 | tf_op jit(solution)/shard_map/ppermute | solution.py:754
  106.5 3.8 collective-permute-start.6
  112.4 52.6 %collective-permute-done.6 = bf16[2,192,384]{2,1,0:T(8,128)(2,1)} collective-permute-done((bf16[2,192,384]{2,1,0:T(8,128)(2,1)S(1)}, bf16[2,192,384]{2,1,0:T(8,128)(2,1)}, u32[]{:S(2)}, u32[]{:S(2)}) %collective-permute-start.6) | collective-permute-done | bytes 294944 | tf_op jit(solution)/shard_map/ppermute | solution.py:783
  166.5 10.5 collective-permute-start.1
  177.0 34.1 %collective-permute-start = (s32[320]{0:T(512)S(1)}, s32[320]{0:T(512)S(1)}, u32[]{:S(2)}, u32[]{:S(2)}) collective-permute-start(s32[320]{0:T(512)S(1)} %copy-done.100), channel_id=1, source_target_pairs={{0,8},{8,0},{16,24},{24,16},{1,9},{9,1},{17,25},{25,17},{2,10},{10... | collective-permute-start | bytes 3848 | tf_op jit(solution)/shard_map/ppermute | solution.py:754
  217.3 18.6 %qkv_product.1 = (bf16[8,320,576]{2,1,0:T(8,128)(2,1)S(1)}, f32[1280,768]{1,0:T(8,128)S(1)}) custom-call(s32[9]{0:T(128)S(1)} %pad_add_fusion.1.spots, bf16[1280,1536]{1,0:T(8,128)(2,1)S(1)} %copy-done.6, bf16[8,2,192,1152]{3,2,1,0:T(8,128)(2,1)} %bitcast.87, bf16[8,2,192,1152]{3,2,1,0:T(8,128)(2,1)} %bitcast.88, ...), custom_call_target="tpu_custom_call" | custom-call | flops 7516192768 | bytes 20971520 | tf_op jit(solution)/shard_map/qkv_product/pallas_call | solution.py:376
  239.5 5.6 all-to-all-start.1
  246.8 114.8 %all-to-all-done.1 = bf16[8,320,576]{2,1,0:T(8,128)(2,1)S(1)} async-done(((bf16[8,320,576]{2,1,0:T(8,128)(2,1)}), bf16[8,320,576]{2,1,0:T(8,128)(2,1)S(1)}, u32[]{:S(2)}, u32[]{:S(2)}) %all-to-all-start.1) | async-done | bytes 2949152 | tf_op jit(solution)/shard_map/all_to_all | solution.py:938
  365.3 5.0 collective-permute-start.11
  371.4 51.3 %collective-permute-done.12.after_ref = bf16[1280,384]{1,0:T(8,128)(2,1)} collective-permute-done((bf16[1280,384]{1,0:T(8,128)(2,1)}, bf16[1280,384]{1,0:T(8,128)(2,1)}, u32[]{:S(2)}, u32[]{:S(2)}) %collective-permute-start.12) | collective-permute-done | bytes 983072 | tf_op jit(solution)/shard_map/ppermute | solution.py:956
  422.8 45.5 %attend.1 = (bf16[2560,192]{1,0:T(8,128)(2,1)S(1)}, f32[10,8,256]{2,1,0:T(8,128)S(1)}) custom-call(s32[10]{0:T(128)S(1)} %fusion.63.lo_ref, s32[10]{0:T(128)S(1)} %fusion.62.hi_ref, bf16[2560,576]{1,0:T(8,128)(2,1)S(1)} %bitcast.69, bf16[1280,384]{1,0:T(8,128)(2,1)} %collective-permute-done.11.before_ref, ...), custom_call_target="tpu_custom_call" | custom-call | flops 42949672960 | bytes 8388608 | tf_op jit(solution)/shard_map/attend/pallas_call | solution.py:198
  471.7 73.1 %all_to_all.30 = bf16[8,320,192]{1,2,0:T(8,128)(2,1)} all-to-all(bf16[8,320,192]{1,2,0:T(8,128)(2,1)S(1)} %copy.93), channel_id=1, replica_groups=mesh['rep'=4,'shard'=8] {'shard'}, dimensions={0} | all-to-all | bytes 1966080 | tf_op jit(solution)/shard_map/all_to_all | solution.py:938
  548.2 7.3 forward_product.3
  560.3 22.0 %collective-permute-done.15 = bf16[320,1536]{1,0:T(8,128)(2,1)S(1)} collective-permute-done((bf16[320,1536]{1,0:T(8,128)(2,1)S(1)}, bf16[320,1536]{1,0:T(8,128)(2,1)S(1)}, u32[]{:S(2)}, u32[]{:S(2)}) %collective-permute-start.15) | collective-permute-done | bytes 983072 | tf_op jit(solution)/shard_map/ppermute | solution.py:754
  583.9 3.1 fusion.83
  587.4 3.4 add_convert_fusion.5
  594.0 19.1 %collective-permute-done.17 = bf16[320,1536]{1,0:T(8,128)(2,1)S(1)} collective-permute-done((bf16[320,1536]{1,0:T(8,128)(2,1)S(1)}, bf16[320,1536]{1,0:T(8,128)(2,1)S(1)}, u32[]{:S(2)}, u32[]{:S(2)}) %collective-permute-start.17) | collective-permute-done | bytes 983072 | tf_op jit(solution)/shard_map/ppermute | solution.py:754
  613.2 3.5 collective-permute-start.18
  616.7 17.4 %collective-permute-done.23 = bf16[320,1536]{1,0:T(8,128)(2,1)S(1)} collective-permute-done((bf16[320,1536]{1,0:T(8,128)(2,1)S(1)}, bf16[320,1536]{1,0:T(8,128)(2,1)S(1)}, u32[]{:S(2)}, u32[]{:S(2)}) %collective-permute-start.23) | collective-permute-done | bytes 983072 | tf_op jit(solution)/shard_map/ppermute | solution.py:754
  640.4 18.3 %forward_product.4 = (bf16[1280,1536]{1,0:T(8,128)(2,1)S(1)}, bf16[1280,1536]{1,0:T(8,128)(2,1)S(1)}) custom-call(s32[9]{0:T(128)S(1)} %pad_add_fusion.1.spots, bf16[1280,1536]{1,0:T(8,128)(2,1)S(1)} %pad_maximum_fusion.1.x_ref, bf16[8,2,192,1536]{3,2,1,0:T(8,128)(2,1)} %bitcast.79, bf16[8,2,192,1536]{3,2,1,0:T(8,128)(2,1)} %bitcast.80, s32[1280,1]{1,0:T(8,128)S(1)} %copy-done.13), custom_call_target="tpu_custom_call" | custom-call | flops 9059696640 | bytes 20971520 | tf_op jit(solution)/shard_map/forward_product/pallas_call | solution.py:534
  662.6 18.3 %backward_product.4.dy_ref = bf16[1280,1536]{1,0:T(8,128)(2,1)S(1)} custom-call(s32[9]{0:T(128)S(1)} %pad_add_fusion.1.spots, bf16[1280,1536]{1,0:T(8,128)(2,1)} %pad_maximum_fusion.2.dy_ref, bf16[4,2,2,768,384]{4,3,2,1,0:T(8,128)(2,1)} %bitcast.83, bf16[4,2,2,768,384]{4,3,2,1,0:T(8,128)(2,1)} %bitcast.84, s32[1280,1]{1,0:T(8,128)S(1)} %copy-done.13, ...), custom_call_target="tpu_custom_call" | custom-call | flops 9059696640 | bytes 20971520 | tf_op jit(solution)/shard_map/backward_product/pallas_call | solution.py:645
  682.8 14.9 %backward_product.5 = bf16[1280,1536]{1,0:T(8,128)(2,1)S(1)} custom-call(s32[9]{0:T(128)S(1)} %pad_add_fusion.1.spots, bf16[1280,1536]{1,0:T(8,128)(2,1)} %copy-done.22, bf16[8,2,192,1536]{3,2,1,0:T(8,128)(2,1)} %bitcast.81, bf16[8,2,192,1536]{3,2,1,0:T(8,128)(2,1)} %bitcast.82, s32[1280,1]{1,0:T(8,128)S(1)} %copy-done.13), custom_call_target="tpu_custom_call" | custom-call | flops 9059696640 | bytes 20971520 | tf_op jit(solution)/shard_map/backward_product/pallas_call | solution.py:645
  702.0 21.9 %collective-permute-done.27 = bf16[320,1536]{1,0:T(8,128)(2,1)S(1)} collective-permute-done((bf16[320,1536]{1,0:T(8,128)(2,1)S(1)}, bf16[320,1536]{1,0:T(8,128)(2,1)S(1)}, u32[]{:S(2)}, u32[]{:S(2)}) %collective-permute-start.27) | collective-permute-done | bytes 983072 | tf_op jit(solution)/shard_map/ppermute | solution.py:754
  729.1 20.5 %collective-permute-done.29 = bf16[320,1536]{1,0:T(8,128)(2,1)S(1)} collective-permute-done((bf16[320,1536]{1,0:T(8,128)(2,1)S(1)}, bf16[320,1536]{1,0:T(8,128)(2,1)S(1)}, u32[]{:S(2)}, u32[]{:S(2)}) %collective-permute-start.29) | collective-permute-done | bytes 983072 | tf_op jit(solution)/shard_map/ppermute | solution.py:754
  756.0 8.6 gradient.5
  766.8 20.2 %gradient.7 = bf16[4,2,2,768,384]{4,3,2,1,0:T(8,128)(2,1)} custom-call(s32[9]{0:T(128)S(1)} %pad_add_fusion.1.spots, bf16[1280,1536]{1,0:T(8,128)(2,1)S(1)} %copy-done.25, bf16[1280,1536]{1,0:T(8,128)(2,1)} %pad_maximum_fusion.2.dy_ref, s32[1280,1]{1,0:T(8,128)S(1)} %copy-done.13), custom_call_target="tpu_custom_call" | custom-call | flops 9059696640 | bytes 20971520 | tf_op jit(solution)/shard_map/gradient/pallas_call | solution.py:726
  790.0 8.6 backward_product.6
  802.2 13.7 all-to-all-start.3
  819.5 20.0 %gradient.6 = bf16[8,2,192,1536]{3,2,1,0:T(8,128)(2,1)} custom-call(s32[9]{0:T(128)S(1)} %pad_add_fusion.1.spots, bf16[1280,1536]{1,0:T(8,128)(2,1)S(1)} %copy-done.10, bf16[1280,1536]{1,0:T(8,128)(2,1)} %copy-done.22, s32[1280,1]{1,0:T(8,128)S(1)} %copy-done.13), custom_call_target="tpu_custom_call" | custom-call | flops 9059696640 | bytes 20971520 | tf_op jit(solution)/shard_map/gradient/pallas_call | solution.py:726
  839.6 14.1 all-to-all-done.3
  856.1 87.0 %attend_back.1 = (bf16[2560,192]{1,0:T(8,128)(2,1)}, bf16[1280,384]{1,0:T(8,128)(2,1)}, bf16[1280,384]{1,0:T(8,128)(2,1)}, f32[2560,384]{1,0:T(8,128)}) custom-call(s32[10]{0:T(128)} %copy-done.21, s32[10]{0:T(128)} %copy-done.20, bf16[2560,576]{1,0:T(8,128)(2,1)} %bitcast.70, bf16[1280,384]{1,0:T(8,128)(2,1)} %collective-permute-done.11.before_ref, ...), custom_call_target="tpu_custom_call" | custom-call | flops 96636764160 | bytes 25165824 | tf_op jit(solution)/shard_map/attend_back/pallas_call | solution.py:237
  944.4 4.5 collective-permute-start.32
  948.9 18.1 %collective-permute-done.31 = bf16[1280,384]{1,0:T(8,128)(2,1)S(1)} collective-permute-done((bf16[1280,384]{1,0:T(8,128)(2,1)}, bf16[1280,384]{1,0:T(8,128)(2,1)S(1)}, u32[]{:S(2)}, u32[]{:S(2)}) %collective-permute-start.31) | collective-permute-done | bytes 983072 | tf_op jit(solution)/shard_map/ppermute | solution.py:956
  968.0 2.7 add_convert_fusion
  970.8 3.3 pad_maximum_fusion.5
  974.0 6.3 all-to-all-start.4
  983.6 15.7 %forward_product.5 = bf16[1280,1536]{1,0:T(8,128)(2,1)S(1)} custom-call(s32[9]{0:T(128)S(1)} %pad_add_fusion.1.spots, bf16[1280,1536]{1,0:T(8,128)(2,1)S(1)} %copy-done.26, bf16[4,2,2,768,384]{4,3,2,1,0:T(8,128)(2,1)} %bitcast.85, bf16[4,2,2,768,384]{4,3,2,1,0:T(8,128)(2,1)} %bitcast.86, s32[1280,1]{1,0:T(8,128)S(1)} %copy-done.14), custom_call_target="tpu_custom_call" | custom-call | flops 9059696640 | bytes 20971520 | tf_op jit(solution)/shard_map/forward_product/pallas_call | solution.py:534
  1001.2 112.8 %all-to-all-done.4.came_ref = bf16[8,320,576]{2,1,0:T(8,128)(2,1)S(1)} async-done(((bf16[8,320,576]{2,1,0:T(8,128)(2,1)}), bf16[8,320,576]{2,1,0:T(8,128)(2,1)S(1)}, u32[]{:S(2)}, u32[]{:S(2)}) %all-to-all-start.4) | async-done | bytes 2949152 | tf_op jit(solution)/shard_map/all_to_all | solution.py:938
  1117.3 7.1 norm_back.1
  1124.4 12.9 backward_product.7
  1137.3 2.7 fusion.84
  1140.1 4.3 collective-permute-start.34
  1145.8 14.5 gradient.4
  1168.2 18.8 %collective-permute-done.35 = bf16[320,1536]{1,0:T(8,128)(2,1)S(1)} collective-permute-done((bf16[320,1536]{1,0:T(8,128)(2,1)}, bf16[320,1536]{1,0:T(8,128)(2,1)S(1)}, u32[]{:S(2)}, u32[]{:S(2)}) %collective-permute-start.35) | collective-permute-done | bytes 983072 | tf_op jit(solution)/shard_map/ppermute | solution.py:754
  1189.5 2.8 fusion.81
  1198.4 9.8 collective-permute-done.21
  1208.2 3.7 fusion.21
  1211.8 4.0 fusion.51
  1217.2 5.4 all-to-all-start.5
  1222.6 3.5 collective-permute-start.39
  1227.2 30.9 %collective-permute-done.39 = bf16[2,192,384]{2,1,0:T(8,128)(2,1)S(1)} collective-permute-done((bf16[2,192,384]{2,1,0:T(8,128)(2,1)}, bf16[2,192,384]{2,1,0:T(8,128)(2,1)S(1)}, u32[]{:S(2)}, u32[]{:S(2)}) %collective-permute-start.39) | collective-permute-done | bytes 294944 | tf_op jit(solution)/shard_map/ppermute | solution.py:783
  1259.7 11.9 all-to-all-done.5
  1280.1 7.5 fusion.79
  1289.6 7.4 fusion.70
  1297.0 137.2 %reduce-scatter.5.cloned.1.call-done = bf16[2,192,1152]{2,1,0:T(8,128)(2,1)} async-done(((bf16[16,192,1152]{2,1,0:T(8,128)(2,1)}), bf16[2,192,1152]{2,1,0:T(8,128)(2,1)}) %reduce-scatter.5.cloned.1.call-update) | async-done | bytes 884752 | tf_op jit(solution)/shard_map/reduce_scatter | solution.py:798
  1435.5 3.1 collective-permute-start.36
  1439.7 8.1 fusion.67
  1447.9 3.6 fusion.76
  (433 shorter events, 148.7 us)
Async XLA Ops:
  7.2 208.0 %all-gather.9.cloned.1.call-start = ((), (), s32[]{:S(2)}) async-start(), calls=%async_computation.14 | async-start | bytes 7962624 | tf_op jit(solution)/shard_map/all_gather | solution.py:787
  9.8 8.4 collective-permute-start.9
  9.8 8.4 collective-permute-start.10
  13.6 9.0 collective-permute-start.8
  34.0 39.3 %all-to-all-start = ((bf16[32,4,2304]{2,1,0:T(4,128)(2,1)}), bf16[32,4,2304]{2,1,0:T(4,128)(2,1)}, u32[]{:S(2)}, u32[]{:S(2)}) async-start(bf16[32,4,2304]{2,1,0:T(4,128)(2,1)} %reshape.422), calls=%async_computation | async-start | bytes 1179648 | tf_op jit(solution)/shard_map/all_to_all | solution.py:873
  40.0 506.6 %all-gather.11.cloned.1.call-start = ((), (), s32[]{:S(2)}) async-start(), calls=%async_computation.15 | async-start | bytes 2654208 | tf_op jit(solution)/shard_map/all_gather | solution.py:787
  40.9 62.5 %copy-start.50 = (f32[2,768,384]{2,1,0:T(8,128)S(1)}, f32[2,768,384]{2,1,0:T(8,128)}, u32[]{:S(2)}) copy-start(f32[2,768,384]{2,1,0:T(8,128)} %param.40) | copy-start | bytes 7077892
  41.3 62.1 %copy-start.93 = (f32[320]{0:T(512)}, f32[320]{0:T(512)S(1)}, u32[]{:S(2)}) copy-start(f32[320]{0:T(512)S(1)} %fusion.59) | copy-start | bytes 3844
  42.8 61.8 %copy-start.86 = (pred[320]{0:T(512)(128)(4,1)}, pred[320]{0:T(512)(128)(4,1)S(1)}, u32[]{:S(2)}) copy-start(pred[320]{0:T(512)(128)(4,1)S(1)} %get-tuple-element.114) | copy-start | bytes 964
  42.8 683.5 %copy-start.84 = (pred[320]{0:T(512)(128)(4,1)}, pred[320]{0:T(512)(128)(4,1)S(1)}, u32[]{:S(2)}) copy-start(pred[320]{0:T(512)(128)(4,1)S(1)} %get-tuple-element.113) | copy-start | bytes 964
  79.1 22.7 %collective-permute-start.4 = (bf16[320,1536]{1,0:T(8,128)(2,1)S(1)}, bf16[320,1536]{1,0:T(8,128)(2,1)S(1)}, u32[]{:S(2)}, u32[]{:S(2)}) collective-permute-start(bf16[320,1536]{1,0:T(8,128)(2,1)S(1)} %fusion.16), channel_id=1, source_target_pairs={{0,16},{8,24},{16,0},{24,8},{1,17},{9,25},{17,1},{25,9},{2,18},{10... | collective-permute-start | bytes 2949128 | tf_op jit(solution)/shard_map/ppermute | solution.py:754
  80.1 30.3 %collective-permute-start.3 = (bf16[320,1536]{1,0:T(8,128)(2,1)S(1)}, bf16[320,1536]{1,0:T(8,128)(2,1)S(1)}, u32[]{:S(2)}, u32[]{:S(2)}) collective-permute-start(bf16[320,1536]{1,0:T(8,128)(2,1)S(1)} %fusion.16), channel_id=1, source_target_pairs={{0,8},{8,0},{16,24},{24,16},{1,9},{9,1},{17,25},{25,17},{2,10},{10... | collective-permute-start | bytes 2949128 | tf_op jit(solution)/shard_map/ppermute | solution.py:754
  101.8 8.6 collective-permute-start.5
  104.6 60.5 %collective-permute-start.7 = (bf16[2,768,384]{2,1,0:T(8,128)(2,1)}, bf16[2,768,384]{2,1,0:T(8,128)(2,1)S(1)}, u32[]{:S(2)}, u32[]{:S(2)}) collective-permute-start(bf16[2,768,384]{2,1,0:T(8,128)(2,1)} %convert_element_type.207), channel_id=1, source_target_pairs={{0,0},{1,1},{2,8},{3,9},{4,16},{5,17},{6,24},{7,25},{8,2},{9,3},{1... | collective-permute-start | bytes 3538952 | tf_op jit(solution)/shard_map/ppermute | solution.py:783
  106.5 58.5 %collective-permute-start.6 = (bf16[2,192,384]{2,1,0:T(8,128)(2,1)S(1)}, bf16[2,192,384]{2,1,0:T(8,128)(2,1)}, u32[]{:S(2)}, u32[]{:S(2)}) collective-permute-start(bf16[2,192,384]{2,1,0:T(8,128)(2,1)S(1)} %convert_element_type.206), channel_id=1, source_target_pairs={{0,0},{1,1},{2,8},{3,9},{4,16},{5,17},{6,24},{7,25},{8,2},{9,3},{1... | collective-permute-start | bytes 884744 | tf_op jit(solution)/shard_map/ppermute | solution.py:783
  165.0 418.9 %all-gather.13.cloned.1.call-start = ((), (), s32[]{:S(2)}) async-start(), calls=%async_computation.16 | async-start | bytes 10616832 | tf_op jit(solution)/shard_map/all_gather | solution.py:787
  166.5 45.7 %collective-permute-start.1 = (s32[320]{0:T(512)S(1)}, s32[320]{0:T(512)S(1)}, u32[]{:S(2)}, u32[]{:S(2)}) collective-permute-start(s32[320]{0:T(512)S(1)} %copy-done.100), channel_id=1, source_target_pairs={{0,16},{8,24},{16,0},{24,8},{1,17},{9,25},{17,1},{25,9},{2,18},{10... | collective-permute-start | bytes 3848 | tf_op jit(solution)/shard_map/ppermute | solution.py:754
  177.0 35.7 %collective-permute-start = (s32[320]{0:T(512)S(1)}, s32[320]{0:T(512)S(1)}, u32[]{:S(2)}, u32[]{:S(2)}) collective-permute-start(s32[320]{0:T(512)S(1)} %copy-done.100), channel_id=1, source_target_pairs={{0,8},{8,0},{16,24},{24,16},{1,9},{9,1},{17,25},{25,17},{2,10},{10... | collective-permute-start | bytes 3848 | tf_op jit(solution)/shard_map/ppermute | solution.py:754
  212.2 1.4 collective-permute-start.2
  239.5 122.1 %all-to-all-start.1 = ((bf16[8,320,576]{2,1,0:T(8,128)(2,1)}), bf16[8,320,576]{2,1,0:T(8,128)(2,1)S(1)}, u32[]{:S(2)}, u32[]{:S(2)}) async-start(bf16[8,320,576]{2,1,0:T(8,128)(2,1)} %copy-done.11), calls=%async_computation.1 | async-start | bytes 6553600 | tf_op jit(solution)/shard_map/all_to_all | solution.py:938
  245.1 417.5 %all-gather.15.cloned.1.call-start = ((), (), s32[]{:S(2)}) async-start(), calls=%async_computation.17 | async-start | bytes 10616832 | tf_op jit(solution)/shard_map/all_gather | solution.py:787
  246.4 976.2 %reduce-scatter.7.cloned.1.call-start = ((), (), s32[]{:S(2)}) async-start(), calls=%async_computation.11 | async-start | bytes 2654208 | tf_op jit(solution)/shard_map/reduce_scatter | solution.py:798
  364.0 58.8 %collective-permute-start.12 = (bf16[1280,384]{1,0:T(8,128)(2,1)}, bf16[1280,384]{1,0:T(8,128)(2,1)}, u32[]{:S(2)}, u32[]{:S(2)}) collective-permute-start(bf16[1280,384]{1,0:T(8,128)(2,1)} %get-tuple-element.134), channel_id=1, source_target_pairs={{2,0},{3,1},{4,2},{5,3},{6,4},{7,5},{10,8},{11,9},{12,10},{13,11},... | collective-permute-start | bytes 2949128 | tf_op jit(solution)/shard_map/ppermute | solution.py:956
  365.3 57.5 %collective-permute-start.11 = (bf16[1280,384]{1,0:T(8,128)(2,1)}, bf16[1280,384]{1,0:T(8,128)(2,1)}, u32[]{:S(2)}, u32[]{:S(2)}) collective-permute-start(bf16[1280,384]{1,0:T(8,128)(2,1)} %get-tuple-element.135), channel_id=1, source_target_pairs={{0,2},{1,3},{2,4},{3,5},{4,6},{5,7},{8,10},{9,11},{10,12},{11,13},... | collective-permute-start | bytes 2949128 | tf_op jit(solution)/shard_map/ppermute | solution.py:956
  370.3 97.9 %copy-start.20 = (s32[10]{0:T(128)}, s32[10]{0:T(128)S(1)}, u32[]{:S(2)}) copy-start(s32[10]{0:T(128)S(1)} %fusion.62.hi_ref) | copy-start | bytes 124
  371.0 97.2 %copy-start.21 = (s32[10]{0:T(128)}, s32[10]{0:T(128)S(1)}, u32[]{:S(2)}) copy-start(s32[10]{0:T(128)S(1)} %fusion.63.lo_ref) | copy-start | bytes 124
  471.7 74.8 %copy-start.13 = (s32[1280,1]{1,0:T(8,128)S(1)}, s32[1280,1]{1,0:T(8,128)}, u32[]{:S(2)}) copy-start(s32[1280,1]{1,0:T(8,128)} %copy-done.12) | copy-start | bytes 15364
  555.7 3.2 collective-permute-start.14
  556.7 3.6 collective-permute-start.13
  559.1 23.1 %collective-permute-start.15 = (bf16[320,1536]{1,0:T(8,128)(2,1)S(1)}, bf16[320,1536]{1,0:T(8,128)(2,1)S(1)}, u32[]{:S(2)}, u32[]{:S(2)}) collective-permute-start(bf16[320,1536]{1,0:T(8,128)(2,1)S(1)} %add_convert_fusion.6), channel_id=1, source_target_pairs={{0,16},{8,24},{16,0},{24,8},{1,17},{9,25},{17,1},{25,9},{2,18},{10... | collective-permute-start | bytes 2949128 | tf_op jit(solution)/shard_map/ppermute | solution.py:754
  587.0 137.9 %copy-start.82 = (f32[320]{0:T(512)}, f32[320]{0:T(512)S(1)}, u32[]{:S(2)}) copy-start(f32[320]{0:T(512)S(1)} %broadcast_multiply_fusion) | copy-start | bytes 3844
  587.4 137.5 %copy-start.91 = (f32[320]{0:T(512)}, f32[320]{0:T(512)S(1)}, u32[]{:S(2)}) copy-start(f32[320]{0:T(512)S(1)} %fusion.60) | copy-start | bytes 3844
  590.9 22.3 %collective-permute-start.17 = (bf16[320,1536]{1,0:T(8,128)(2,1)S(1)}, bf16[320,1536]{1,0:T(8,128)(2,1)S(1)}, u32[]{:S(2)}, u32[]{:S(2)}) collective-permute-start(bf16[320,1536]{1,0:T(8,128)(2,1)S(1)} %add_convert_fusion.5), channel_id=1, source_target_pairs={{0,16},{8,24},{16,0},{24,8},{1,17},{9,25},{17,1},{25,9},{2,18},{10... | collective-permute-start | bytes 2949128 | tf_op jit(solution)/shard_map/ppermute | solution.py:754
  591.0 43.1 %collective-permute-start.23 = (bf16[320,1536]{1,0:T(8,128)(2,1)S(1)}, bf16[320,1536]{1,0:T(8,128)(2,1)S(1)}, u32[]{:S(2)}, u32[]{:S(2)}) collective-permute-start(bf16[320,1536]{1,0:T(8,128)(2,1)S(1)} %get-tuple-element.174), channel_id=1, source_target_pairs={{0,16},{8,24},{16,0},{24,8},{1,17},{9,25},{17,1},{25,9},{2,18},{10... | collective-permute-start | bytes 2949128 | tf_op jit(solution)/shard_map/ppermute | solution.py:754
  592.4 43.8 %collective-permute-start.16 = (bf16[320,1536]{1,0:T(8,128)(2,1)S(1)}, bf16[320,1536]{1,0:T(8,128)(2,1)S(1)}, u32[]{:S(2)}, u32[]{:S(2)}) collective-permute-start(bf16[320,1536]{1,0:T(8,128)(2,1)S(1)} %add_convert_fusion.5), channel_id=1, source_target_pairs={{0,8},{8,0},{16,24},{24,16},{1,9},{9,1},{17,25},{25,17},{2,10},{10... | collective-permute-start | bytes 2949128 | tf_op jit(solution)/shard_map/ppermute | solution.py:754
  613.2 23.0 %collective-permute-start.18 = (bf16[320,1536]{1,0:T(8,128)(2,1)S(1)}, bf16[320,1536]{1,0:T(8,128)(2,1)S(1)}, u32[]{:S(2)}, u32[]{:S(2)}) collective-permute-start(bf16[320,1536]{1,0:T(8,128)(2,1)S(1)} %collective-permute-done.17), channel_id=1, source_target_pairs={{0,8},{8,0},{16,24},{24,16},{1,9},{9,1},{17,25},{25,17},{2,10},{10... | collective-permute-start | bytes 2949128 | tf_op jit(solution)/shard_map/ppermute | solution.py:754
  616.7 19.8 %collective-permute-start.22 = (bf16[320,1536]{1,0:T(8,128)(2,1)S(1)}, bf16[320,1536]{1,0:T(8,128)(2,1)S(1)}, u32[]{:S(2)}, u32[]{:S(2)}) collective-permute-start(bf16[320,1536]{1,0:T(8,128)(2,1)S(1)} %get-tuple-element.174), channel_id=1, source_target_pairs={{0,8},{8,0},{16,24},{24,16},{1,9},{9,1},{17,25},{25,17},{2,10},{10... | collective-permute-start | bytes 2949128 | tf_op jit(solution)/shard_map/ppermute | solution.py:754
  634.1 4.2 collective-permute-start.24
  697.9 2.7 collective-permute-start.26
  698.4 3.6 collective-permute-start.25
  700.8 23.0 %collective-permute-start.27 = (bf16[320,1536]{1,0:T(8,128)(2,1)S(1)}, bf16[320,1536]{1,0:T(8,128)(2,1)S(1)}, u32[]{:S(2)}, u32[]{:S(2)}) collective-permute-start(bf16[320,1536]{1,0:T(8,128)(2,1)S(1)} %add_convert_fusion.2), channel_id=1, source_target_pairs={{0,16},{8,24},{16,0},{24,8},{1,17},{9,25},{17,1},{25,9},{2,18},{10... | collective-permute-start | bytes 2949128 | tf_op jit(solution)/shard_map/ppermute | solution.py:754
  727.5 22.0 %collective-permute-start.29 = (bf16[320,1536]{1,0:T(8,128)(2,1)S(1)}, bf16[320,1536]{1,0:T(8,128)(2,1)S(1)}, u32[]{:S(2)}, u32[]{:S(2)}) collective-permute-start(bf16[320,1536]{1,0:T(8,128)(2,1)S(1)} %multiply_convert_fusion), channel_id=1, source_target_pairs={{0,16},{8,24},{16,0},{24,8},{1,17},{9,25},{17,1},{25,9},{2,18},{10... | collective-permute-start | bytes 2949128 | tf_op jit(solution)/shard_map/ppermute | solution.py:754
  727.6 24.1 %collective-permute-start.28 = (bf16[320,1536]{1,0:T(8,128)(2,1)S(1)}, bf16[320,1536]{1,0:T(8,128)(2,1)S(1)}, u32[]{:S(2)}, u32[]{:S(2)}) collective-permute-start(bf16[320,1536]{1,0:T(8,128)(2,1)S(1)} %multiply_convert_fusion), channel_id=1, source_target_pairs={{0,8},{8,0},{16,24},{24,16},{1,9},{9,1},{17,25},{25,17},{2,10},{10... | collective-permute-start | bytes 2949128 | tf_op jit(solution)/shard_map/ppermute | solution.py:754
  749.6 4.3 collective-permute-start.30
  764.6 523.1 %reduce-scatter.11.cloned.1.call-start = ((), (), s32[]{:S(2)}) async-start(), calls=%async_computation.13 | async-start | bytes 10616832 | tf_op jit(solution)/shard_map/reduce_scatter | solution.py:798
  802.2 51.4 %all-to-all-start.3 = ((bf16[8,320,192]{1,2,0:T(8,128)(2,1)}), bf16[8,320,192]{1,2,0:T(8,128)(2,1)}, u32[]{:S(2)}, u32[]{:S(2)}) async-start(bf16[8,320,192]{1,2,0:T(8,128)(2,1)} %copy.95), calls=%async_computation.3 | async-start | bytes 2359296 | tf_op jit(solution)/shard_map/all_to_all | solution.py:938
  816.0 473.6 %reduce-scatter.9.cloned.1.call-start = ((), (), s32[]{:S(2)}) async-start(), calls=%async_computation.12 | async-start | bytes 10616832 | tf_op jit(solution)/shard_map/reduce_scatter | solution.py:798
  943.1 23.9 %collective-permute-start.31 = (bf16[1280,384]{1,0:T(8,128)(2,1)}, bf16[1280,384]{1,0:T(8,128)(2,1)S(1)}, u32[]{:S(2)}, u32[]{:S(2)}) collective-permute-start(bf16[1280,384]{1,0:T(8,128)(2,1)} %get-tuple-element.59), channel_id=1, source_target_pairs={{2,0},{3,1},{4,2},{5,3},{6,4},{7,5},{10,8},{11,9},{12,10},{13,11},... | collective-permute-start | bytes 2949128 | tf_op jit(solution)/shard_map/ppermute | solution.py:956
  944.4 23.6 %collective-permute-start.32 = (bf16[1280,384]{1,0:T(8,128)(2,1)}, bf16[1280,384]{1,0:T(8,128)(2,1)S(1)}, u32[]{:S(2)}, u32[]{:S(2)}) collective-permute-start(bf16[1280,384]{1,0:T(8,128)(2,1)} %get-tuple-element.60), channel_id=1, source_target_pairs={{0,2},{1,3},{2,4},{3,5},{4,6},{5,7},{8,10},{9,11},{10,12},{11,13},... | collective-permute-start | bytes 2949128 | tf_op jit(solution)/shard_map/ppermute | solution.py:956
  974.0 140.0 %all-to-all-start.4 = ((bf16[8,320,576]{2,1,0:T(8,128)(2,1)}), bf16[8,320,576]{2,1,0:T(8,128)(2,1)S(1)}, u32[]{:S(2)}, u32[]{:S(2)}) async-start(bf16[8,320,576]{2,1,0:T(8,128)(2,1)} %bitcast.73), calls=%async_computation.4 | async-start | bytes 6553600 | tf_op jit(solution)/shard_map/all_to_all | solution.py:938
  980.4 453.9 %reduce-scatter.5.cloned.1.call-start = ((), (), s32[]{:S(2)}) async-start(), calls=%async_computation.10 | async-start | bytes 7962624 | tf_op jit(solution)/shard_map/reduce_scatter | solution.py:798
  983.6 130.4 %copy-start.19 = (f32[2,2,384]{2,1,0:T(2,128)S(1)}, f32[2,2,384]{2,1,0:T(2,128)}, u32[]{:S(2)}) copy-start(f32[2,2,384]{2,1,0:T(2,128)} %copy-done.18) | copy-start | bytes 18436
  1140.1 20.9 %collective-permute-start.34 = (bf16[320,1536]{1,0:T(8,128)(2,1)S(1)}, bf16[320,1536]{1,0:T(8,128)(2,1)S(1)}, u32[]{:S(2)}, u32[]{:S(2)}) collective-permute-start(bf16[320,1536]{1,0:T(8,128)(2,1)S(1)} %get-tuple-element.127), channel_id=1, source_target_pairs={{0,8},{8,0},{16,24},{24,16},{1,9},{9,1},{17,25},{25,17},{2,10},{10... | collective-permute-start | bytes 2949128 | tf_op jit(solution)/shard_map/ppermute | solution.py:754
  1145.8 18.8 %collective-permute-start.20 = (bf16[320,1536]{1,0:T(8,128)(2,1)}, bf16[320,1536]{1,0:T(8,128)(2,1)}, u32[]{:S(2)}, u32[]{:S(2)}) collective-permute-start(bf16[320,1536]{1,0:T(8,128)(2,1)} %get-tuple-element.131), channel_id=1, source_target_pairs={{0,8},{8,0},{16,24},{24,16},{1,9},{9,1},{17,25},{25,17},{2,10},{10... | collective-permute-start | bytes 2949128 | tf_op jit(solution)/shard_map/ppermute | solution.py:754
  1160.4 7.9 collective-permute-start.33
  1163.4 23.7 %collective-permute-start.35 = (bf16[320,1536]{1,0:T(8,128)(2,1)}, bf16[320,1536]{1,0:T(8,128)(2,1)S(1)}, u32[]{:S(2)}, u32[]{:S(2)}) collective-permute-start(bf16[320,1536]{1,0:T(8,128)(2,1)} %add_convert_fusion.1), channel_id=1, source_target_pairs={{0,16},{8,24},{16,0},{24,8},{1,17},{9,25},{17,1},{25,9},{2,18},{10... | collective-permute-start | bytes 2949128 | tf_op jit(solution)/shard_map/ppermute | solution.py:754
  1164.2 34.2 %collective-permute-start.19 = (bf16[320,1536]{1,0:T(8,128)(2,1)}, bf16[320,1536]{1,0:T(8,128)(2,1)}, u32[]{:S(2)}, u32[]{:S(2)}) collective-permute-start(bf16[320,1536]{1,0:T(8,128)(2,1)} %get-tuple-element.130), channel_id=1, source_target_pairs={{0,8},{8,0},{16,24},{24,16},{1,9},{9,1},{17,25},{25,17},{2,10},{10... | collective-permute-start | bytes 2949128 | tf_op jit(solution)/shard_map/ppermute | solution.py:754
  1167.2 40.9 %collective-permute-start.21 = (bf16[320,1536]{1,0:T(8,128)(2,1)}, bf16[320,1536]{1,0:T(8,128)(2,1)}, u32[]{:S(2)}, u32[]{:S(2)}) collective-permute-start(bf16[320,1536]{1,0:T(8,128)(2,1)} %add_convert_fusion.4), channel_id=1, source_target_pairs={{0,16},{8,24},{16,0},{24,8},{1,17},{9,25},{17,1},{25,9},{2,18},{10... | collective-permute-start | bytes 2949128 | tf_op jit(solution)/shard_map/ppermute | solution.py:754
  1217.2 54.4 %all-to-all-start.5 = ((f32[32,4,2432]{2,1,0:T(4,128)}), f32[32,4,2432]{2,1,0:T(4,128)S(1)}, u32[]{:S(2)}, u32[]{:S(2)}) async-start(f32[32,4,2432]{2,1,0:T(4,128)} %bitcast.27), calls=%async_computation.5 | async-start | bytes 2490368 | tf_op jit(solution)/shard_map/all_to_all | solution.py:1066
  1222.6 35.5 %collective-permute-start.39 = (bf16[2,192,384]{2,1,0:T(8,128)(2,1)}, bf16[2,192,384]{2,1,0:T(8,128)(2,1)S(1)}, u32[]{:S(2)}, u32[]{:S(2)}) collective-permute-start(bf16[2,192,384]{2,1,0:T(8,128)(2,1)} %reduce-scatter.7.cloned.1.call-done), channel_id=1, source_target_pairs={{0,0},{1,1},{2,8},{3,9},{4,16},{5,17},{6,24},{7,25},{8,2},{9,3},{1... | collective-permute-start | bytes 884744 | tf_op jit(solution)/shard_map/ppermute | solution.py:783
  1287.7 152.0 %collective-permute-start.40 = (bf16[2,768,384]{2,1,0:T(8,128)(2,1)}, bf16[2,768,384]{2,1,0:T(8,128)(2,1)S(1)}, u32[]{:S(2)}, u32[]{:S(2)}) collective-permute-start(bf16[2,768,384]{2,1,0:T(8,128)(2,1)} %reduce-scatter.11.cloned.1.call-done), channel_id=1, source_target_pairs={{0,0},{1,1},{2,8},{3,9},{4,16},{5,17},{6,24},{7,25},{8,2},{9,3},{1... | collective-permute-start | bytes 3538952 | tf_op jit(solution)/shard_map/ppermute | solution.py:783
  1435.5 12.4 collective-permute-start.36
  1438.6 9.2 collective-permute-start.37
  1438.7 9.1 collective-permute-start.38
  (96 other events, 1180.0 us)
Sparse Core Ops, SparseCore 0:
  25.0 168.7 all-gather.8
  195.9 65.7 all-gather.10
  264.5 201.7 all-gather.12
  468.9 163.3 all-gather.14
  764.7 87.4 reduce-scatter.6
  855.6 185.8 reduce-scatter.10
  1045.1 205.5 reduce-scatter.8
  1254.4 179.8 reduce-scatter.4

commit v2 on v1

--- a/solution.py
+++ b/solution.py
@@ -60,16 +60,16 @@
     halo, own = before_ref.shape[0], own_ref.shape[0]
     heads = keys.shape[0]
     width = heads * HD
-    parts = ((before_ref, 0, 0, halo), (own_ref, width, halo, own), (after_ref, 0, halo + own, halo))
-    for source, skip, first, count in parts:
+    parts = ((before_ref, 0, halo), (own_ref, halo, own), (after_ref, halo + own, halo))
+    for source, first, count in parts:
         for head in range(heads):
             for index, dest in ((0, keys), (1, values)):
-                start = skip + index * width + head * HD
+                start = index * width + head * HD
                 dest[head, first : first + count, :HD] = source[:, start : start + HD]
 
 
 def attend_kernel(
-    lo_ref, hi_ref, own_ref, before_ref, after_ref, qid_ref, kid_ref, o_ref, l_ref, keys, values, acc
+    lo_ref, hi_ref, q_ref, own_ref, before_ref, after_ref, qid_ref, kid_ref, o_ref, l_ref, keys, values, acc
 ):
     step = pl.program_id(0)
     heads = keys.shape[0]
@@ -85,8 +85,7 @@
     diagonal = lax.broadcasted_iota(jnp.int32, (QB, QB), 0) == lax.broadcasted_iota(
         jnp.int32, (QB, QB), 1
     )
-    own_rows = pl.ds(pl.multiple_of(step * QB, QB), QB)
-    queries = [own_ref[own_rows, head * HD : (head + 1) * HD] for head in range(heads)]
+    queries = [q_ref[:, head * HD : (head + 1) * HD] for head in range(heads)]
     acc[...] = jnp.zeros_like(acc)
 
     @pl.loop(lo_ref[step], hi_ref[step])
@@ -111,6 +110,7 @@
 def attend_back_kernel(
     lo_ref,
     hi_ref,
+    q_ref,
     own_ref,
     before_ref,
     after_ref,
@@ -141,11 +141,10 @@
 
     qid = qid_ref[0]
     ones = jnp.ones((8, HD), bf16)
-    own_rows = pl.ds(pl.multiple_of(step * QB, QB), QB)
     queries, outs, dots = [], [], []
     for head in range(heads):
         lanes = slice(head * HD, (head + 1) * HD)
-        queries.append(own_ref[own_rows, lanes])
+        queries.append(q_ref[:, lanes])
         outs.append(do_ref[:, lanes])
         product = outs[head].astype(f32) * o_ref[:, lanes].astype(f32)
         coarse = product.astype(bf16)
@@ -190,8 +189,8 @@
     return pl.BlockSpec(shape, lambda *index: (0,) * len(shape))
 
 
-def attention(own, before, after, lo, hi, qid, kid):
-    count, width = own.shape[0], own.shape[1] // 3
+def attention(query, own, before, after, lo, hi, qid, kid):
+    count, width = query.shape
     heads = width // HD
     window = count + 2 * before.shape[0]
     steps = count // QB
@@ -201,6 +200,7 @@
             num_scalar_prefetch=2,
             grid=(steps,),
             in_specs=[
+                pl.BlockSpec((QB, width), lambda i, lo, hi: (i, 0)),
                 resident(own.shape),
                 resident(before.shape),
                 resident(after.shape),
@@ -222,13 +222,13 @@
             jax.ShapeDtypeStruct((steps, 8, QB), f32),
         ],
         compiler_params=pltpu.CompilerParams(vmem_limit_bytes=40 << 20),
-        cost_estimate=pl.CostEstimate(flops=40 << 30, bytes_accessed=8 << 20, transcendentals=12 << 20),
+        cost_estimate=pl.CostEstimate(flops=1 << 30, bytes_accessed=4 << 20, transcendentals=0),
         name="attend",
-    )(lo, hi, own, before, after, qid[:, None], kid.reshape(window // KB, KB))
-
-
-def attention_back(own, before, after, d_out, out, lo, hi, qid, kid, logsum):
-    count, width = own.shape[0], own.shape[1] // 3
+    )(lo, hi, query, own, before, after, qid[:, None], kid.reshape(window // KB, KB))
+
+
+def attention_back(query, own, before, after, d_out, out, lo, hi, qid, kid, logsum):
+    count, width = query.shape
     heads = width // HD
     halo = before.shape[0]
     window = count + 2 * halo
@@ -240,6 +240,7 @@
             num_scalar_prefetch=2,
             grid=(steps,),
             in_specs=[
+                rows,
                 resident(own.shape),
                 resident(before.shape),
                 resident(after.shape),
@@ -266,9 +267,9 @@
             jax.ShapeDtypeStruct((count, 2 * width), f32),
         ],
         compiler_params=pltpu.CompilerParams(vmem_limit_bytes=58 << 20),
-        cost_estimate=pl.CostEstimate(flops=90 << 30, bytes_accessed=24 << 20, transcendentals=12 << 20),
+        cost_estimate=pl.CostEstimate(flops=24 << 30, bytes_accessed=8 << 20, transcendentals=0),
         name="attend_back",
-    )(lo, hi, own, before, after, d_out, out, qid.reshape(steps, 1, QB), kid[:, None], logsum)
+    )(lo, hi, query, own, before, after, d_out, out, qid.reshape(steps, 1, QB), kid[:, None], logsum)
 
 
 def text_windows(spots, blocks, count, work):
@@ -307,10 +308,10 @@
     return (row == col).astype(bf16)
 
 
-def qkv_kernel(blocks, spots, x_ref, w0, w1, image_ref, gain_ref, packed_ref, pre_ref):
+def qkv_kernel(blocks, spots, x_ref, w0, w1, image_ref, gain_ref, q_ref, kv_ref, pre_ref):
     kind = pl.program_id(0)
     every = slice(None)
-    size, width = packed_ref.shape[1], packed_ref.shape[2] // 3
+    size, width = q_ref.shape[1:]
     rep = spots[2 * blocks]
     spread = head_blocks(2 * width)
 
@@ -325,6 +326,9 @@
 
         @pl.when(kind == t)
         def _(t=t):
+            packed_ref = kv_ref if t else q_ref
+            lanes = slice((t - 1) * width, t * width) if t else slice(0, width)
+
             @pl.loop(0, blocks)
             def _(p):
                 rows = pl.ds(pl.multiple_of(p * size, size), size)
@@ -333,7 +337,7 @@
                     pre_ref[rows, :] = values
                 values = finish(t, values, gain_ref[0, :1])
                 for g in range(2):
-                    packed_ref[pl.ds((rep ^ p) * 2 + g, 1), :, t * width : (t + 1) * width] = values[
+                    packed_ref[pl.ds((rep ^ p) * 2 + g, 1), :, lanes] = values[
                         :, g * width : (g + 1) * width
                     ][None]
 
@@ -347,7 +351,7 @@
                     place = (
                         pl.ds((rep ^ p) * 2 + g, 1),
                         pl.ds(first, WINDOW),
-                        slice(t * width, (t + 1) * width),
+                        lanes,
                     )
                     packed_ref[place] = jnp.where(
                         image[None], packed_ref[place], values[:, g * width : (g + 1) * width][None]
@@ -385,21 +389,23 @@
                 pl.BlockSpec((1, 2, part), lambda j, s: (jnp.minimum(j, 1), 0, 0)),
             ],
             out_specs=[
-                resident((2 * blocks, size, 3 * part // 2)),
+                resident((2 * blocks, size, part // 2)),
+                resident((2 * blocks, size, part)),
                 pl.BlockSpec((count, part), lambda j, s: (0, jnp.minimum(j, 1))),
             ],
         ),
         out_shape=[
-            jax.ShapeDtypeStruct((2 * blocks, size, 3 * part // 2), bf16),
+            jax.ShapeDtypeStruct((2 * blocks, size, part // 2), bf16),
+            jax.ShapeDtypeStruct((2 * blocks, size, part), bf16),
             jax.ShapeDtypeStruct((count, 2 * part), f32),
         ],
         compiler_params=pltpu.CompilerParams(vmem_limit_bytes=40 << 20),
-        cost_estimate=pl.CostEstimate(flops=7 << 30, bytes_accessed=20 << 20, transcendentals=0),
+        cost_estimate=pl.CostEstimate(flops=1 << 30, bytes_accessed=4 << 20, transcendentals=0),
         name="qkv_product",
     )(spots, x, weight, weight, image, tiled_gains(gains, part // HD))
 
 
-def norm_back_kernel(blocks, spots, came_ref, pre_ref, image_ref, gain_ref, out_ref, sum_ref, both):
+def norm_back_kernel(blocks, spots, q_ref, kv_ref, pre_ref, image_ref, gain_ref, out_ref, sum_ref, both):
     @pl.when(pl.program_id(0) == 0)
     def _():
         sum_ref[...] = jnp.zeros_like(sum_ref)
@@ -409,10 +415,10 @@
     image = image_ref[...] == 1
     spread = head_blocks(part)
     for t in range(3):
+        came_ref = kv_ref if t else q_ref
+        lanes = slice((t - 1) * width, t * width) if t else slice(0, width)
         for g in range(2):
-            both[:, g * width : (g + 1) * width] = came_ref[g, :, t * width : (t + 1) * width].astype(
-                f32
-            )
+            both[:, g * width : (g + 1) * width] = came_ref[g, :, lanes].astype(f32)
         grad = both[...]
         if t < 2:
             pre = pre_ref[:, t * part : (t + 1) * part]
@@ -429,10 +435,9 @@
         out_ref[:, t * part : (t + 1) * part] = grad.astype(bf16)
 
 
-def norm_back(spots, came, pre, image, gains):
+def norm_back(spots, came_query, came_pair, pre, image, gains):
     blocks = (spots.shape[0] - 1) // 2
-    _, size, width3 = came.shape
-    part = 2 * width3 // 3
+    _, size, part = came_pair.shape
     tiled = tiled_gains(gains, part // HD)
     return pl.pallas_call(
         functools.partial(norm_back_kernel, blocks),
@@ -440,7 +445,8 @@
             num_scalar_prefetch=1,
             grid=(blocks,),
             in_specs=[
-                pl.BlockSpec((2, size, width3), lambda p, s: (s[2 * blocks] ^ p, 0, 0)),
+                pl.BlockSpec((2, size, part // 2), lambda p, s: (s[2 * blocks] ^ p, 0, 0)),
+                pl.BlockSpec((2, size, part), lambda p, s: (s[2 * blocks] ^ p, 0, 0)),
                 pl.BlockSpec((size, 2 * part), lambda p, s: (p, 0)),
                 pl.BlockSpec((size, 1), lambda p, s: (p, 0)),
                 resident(tiled.shape),
@@ -458,7 +464,7 @@
         compiler_params=pltpu.CompilerParams(vmem_limit_bytes=32 << 20),
         cost_estimate=pl.CostEstimate(flops=4 << 30, bytes_accessed=12 << 20, transcendentals=0),
         name="norm_back",
-    )(spots, came, pre, image, tiled)
+    )(spots, came_query, came_pair, pre, image, tiled)
 
 
 def forward_kernel(blocks, gathers, gelu, spots, x_ref, w0, w1, image_ref, *rest):
@@ -542,7 +548,7 @@
         out_shape=out_shape,
         compiler_params=pltpu.CompilerParams(vmem_limit_bytes=40 << 20),
         cost_estimate=pl.CostEstimate(
-            flops=3 * count * depth * tiles * tile, bytes_accessed=20 << 20, transcendentals=0
+            flops=count * depth // 4 * tiles * tile, bytes_accessed=4 << 20, transcendentals=0
         ),
         name="forward_product",
     )(spots, x, weight, weight, image)
@@ -653,7 +659,7 @@
         out_shape=out_shape,
         compiler_params=pltpu.CompilerParams(vmem_limit_bytes=48 << 20),
         cost_estimate=pl.CostEstimate(
-            flops=3 * count * depth * dy.shape[1], bytes_accessed=20 << 20, transcendentals=0
+            flops=count * depth // 4 * dy.shape[1], bytes_accessed=4 << 20, transcendentals=0
         ),
         name="backward_product",
     )(*operands)
@@ -743,7 +749,7 @@
         out_shape=jax.ShapeDtypeStruct(shape, bf16),
         compiler_params=pltpu.CompilerParams(vmem_limit_bytes=48 << 20),
         cost_estimate=pl.CostEstimate(
-            flops=3 * count * depth * width, bytes_accessed=20 << 20, transcendentals=0
+            flops=count * depth // 4 * width, bytes_accessed=4 << 20, transcendentals=0
         ),
         name="gradient",
     )(spots, x, dy, image)
@@ -791,6 +797,152 @@
     full = gather_weight(moved)
     reps = lax.axis_size("rep")
     return full.reshape(reps, full.shape[0] // reps, *full.shape[1:])
+
+
+def ring_place(shards):
+    mine = lax.axis_index("shard")
+    odd = mine % 2
+    return (1 - odd) * (mine // 2) + odd * (shards - 1 - mine // 2)
+
+
+def ring_owner(place, shards):
+    place = (place + 2 * shards) % shards
+    back = place // ((shards + 1) // 2)
+    return (1 - back) * (2 * place) + back * (2 * (shards - 1 - place) + 1)
+
+
+def ring_kernel(shards, count, *refs):
+    sources, dests = refs[:count], refs[count : 2 * count]
+    send_sem, recv_sem, own_sem = refs[2 * count :]
+    place = ring_place(shards)
+    mine = ring_owner(place, shards)
+    peers = [ring_owner(place + 1, shards), ring_owner(place - 1, shards)]
+
+    barrier = pltpu.get_barrier_semaphore()
+    for peer in peers:
+        pl.semaphore_signal(
+            barrier, inc=1, device_id={"shard": peer}, device_id_type=pl.DeviceIdType.MESH
+        )
+    pl.semaphore_wait(barrier, 2)
+
+    kept = [
+        pltpu.make_async_copy(sources[w], dests[w].at[mine], own_sem.at[w]) for w in range(count)
+    ]
+    for copy in kept:
+        copy.start()
+    chains = [(w, way) for w in range(count) for way in range(2)]
+    copies = {}
+    for step in range(shards - 1):
+        for chain in chains:
+            w, way = chain
+            if step:
+                copies[chain, step - 1].wait_recv()
+            owner = ring_owner(place - step if way == 0 else place + step, shards)
+            dest = dests[w].at[owner, way]
+            copies[chain, step] = pltpu.make_async_remote_copy(
+                src_ref=dest if step else sources[w].at[way],
+                dst_ref=dest,
+                send_sem=send_sem.at[w, way, step],
+                recv_sem=recv_sem.at[w, way, step],
+                device_id={"shard": peers[way]},
+                device_id_type=pl.DeviceIdType.MESH,
+            )
+            copies[chain, step].start()
+    for chain in chains:
+        copies[chain, shards - 2].wait_recv()
+        for step in range(shards - 1):
+            copies[chain, step].wait_send()
+    for copy in kept:
+        copy.wait()
+
+
+def ring_gather(*blocks):
+    shards = lax.axis_size("shard")
+    count = len(blocks)
+    anywhere = pl.BlockSpec(memory_space=pl.ANY)
+    return pl.pallas_call(
+        functools.partial(ring_kernel, shards, count),
+        in_specs=[anywhere] * count,
+        out_specs=[anywhere] * count,
+        out_shape=[jax.ShapeDtypeStruct((shards, *b.shape), b.dtype) for b in blocks],
+        scratch_shapes=[
+            pltpu.SemaphoreType.DMA((count, 2, shards - 1)),
+            pltpu.SemaphoreType.DMA((count, 2, shards - 1)),
+            pltpu.SemaphoreType.DMA((count,)),
+        ],
+        compiler_params=pltpu.CompilerParams(collective_id=0, has_side_effects=True),
+        cost_estimate=pl.CostEstimate(flops=1 << 20, bytes_accessed=8 << 20, transcendentals=0),
+        name="ring_gather",
+    )(*blocks)
+
+
+def ring_scatter_kernel(terms, out, held, send_sem, recv_sem):
+    shards, _, rows, _ = terms.shape
+    pieces = held.shape[1]
+    part = rows // pieces
+    place = ring_place(shards)
+    mine = ring_owner(place, shards)
+    peers = [ring_owner(place + 1, shards), ring_owner(place - 1, shards)]
+
+    barrier = pltpu.get_barrier_semaphore()
+    for peer in peers:
+        pl.semaphore_signal(
+            barrier, inc=1, device_id={"shard": peer}, device_id_type=pl.DeviceIdType.MESH
+        )
+    pl.semaphore_wait(barrier, 2)
+
+    chains = [(way, piece) for piece in range(pieces) for way in range(2)]
+    copies = {}
+    for step in range(shards):
+        for way, piece in chains:
+            span = slice(piece * part, (piece + 1) * part)
+            if step < shards - 1:
+                owner = ring_owner(place - 1 - step if way == 0 else place + 1 + step, shards)
+            else:
+                owner = mine
+            source = terms.at[owner, way, span]
+            if step:
+                copies[way, piece, step - 1].wait_recv()
+                arrived = held.at[way, piece, step - 1]
+                total = arrived[...].astype(f32) + source[...].astype(f32)
+                if step == shards - 1:
+                    out[way, span] = total.astype(bf16)
+                    continue
+                arrived[...] = total.astype(bf16)
+                source = arrived
+            copies[way, piece, step] = pltpu.make_async_remote_copy(
+                src_ref=source,
+                dst_ref=held.at[way, piece, step],
+                send_sem=send_sem.at[way, piece, step],
+                recv_sem=recv_sem.at[way, piece, step],
+                device_id={"shard": peers[way]},
+                device_id_type=pl.DeviceIdType.MESH,
+            )
+            copies[way, piece, step].start()
+    for copy in copies.values():
+        copy.wait_send()
+
+
+def ring_scatter(terms):
+    shards, _, rows, width = terms.shape
+    pieces = 2 if rows % 32 == 0 else 1
+    sems = pltpu.SemaphoreType.DMA((2, pieces, shards - 1))
+    return pl.pallas_call(
+        ring_scatter_kernel,
+        in_specs=[pl.BlockSpec(memory_space=pltpu.VMEM)],
+        out_specs=pl.BlockSpec(memory_space=pltpu.VMEM),
+        out_shape=jax.ShapeDtypeStruct((2, rows, width), bf16),
+        scratch_shapes=[
+            pltpu.VMEM((2, pieces, shards - 1, rows // pieces, width), bf16),
+            sems,
+            sems,
+        ],
+        compiler_params=pltpu.CompilerParams(
+            collective_id=1, has_side_effects=True, vmem_limit_bytes=32 << 20
+        ),
+        cost_estimate=pl.CostEstimate(flops=1 << 20, bytes_accessed=256 << 20, transcendentals=0),
+        name="ring_scatter",
+    )(terms)
 
 
 def scatter_weight(terms):
@@ -897,10 +1049,6 @@
         ]
 
     qkv_weights = gather_weight(jnp.concatenate(rolled(chunks, turns), axis=2))
-    fc1_weights = gather_weight(w_fc1.astype(bf16))
-    out_turned = turn(w_out.astype(bf16))
-    fc2_turned = turn(w_fc2.astype(bf16))
-
     first_seq = seq_ids[0]
     second_seq = jnp.minimum(first_seq + 1, slot_count - 1)
     is_second = (seq_ids != first_seq)[:, None]
@@ -921,13 +1069,15 @@
     d_down = (gate_two * back_out).astype(bf16)
     d_down_group = jnp.concatenate(gather_rep(d_down))
 
-    act_one_group, out_turned, fc2_turned = lax.optimization_barrier(
-        (act_one_group, out_turned, fc2_turned)
-    )
-    out_weights = gather_turned(out_turned)
-    fc2_weights = gather_turned(fc2_turned)
-
-    packed, qk_pre = qkv_product(spots, act_one_group, qkv_weights, image, gains)
+    fc1_low, act_one_group = lax.optimization_barrier((w_fc1.astype(bf16), act_one_group))
+    (fc1_weights,) = ring_gather(fc1_low)
+    act_one_group, fc1_weights = lax.optimization_barrier((act_one_group, fc1_weights))
+
+    query_sent, pair_sent, qk_pre = qkv_product(spots, act_one_group, qkv_weights, image, gains)
+    out_low, fc2_low, pair_sent = lax.optimization_barrier(
+        (w_out.astype(bf16), w_fc2.astype(bf16), pair_sent)
+    )
+    out_turned, fc2_turned = turn(out_low), turn(fc2_low)
 
     bunch = 2 * reps
     bunches = shards // bunch
@@ -955,8 +1105,14 @@
         ]
         return lax.ppermute(value, "shard", pairs)
 
-    own = exchange(packed).reshape(stretch_rows, 3 * half_width)
-    pair_own = own[:, half_width:]
+    pair_own = exchange(pair_sent).reshape(stretch_rows, 2 * half_width)
+    query_sent, pair_own = lax.optimization_barrier((query_sent, pair_own))
+    query_own = exchange(query_sent).reshape(stretch_rows, half_width)
+    out_turned, fc2_turned, query_own = lax.optimization_barrier(
+        (out_turned, fc2_turned, query_own)
+    )
+    out_weights = gather_turned(out_turned)
+    fc2_weights = gather_turned(fc2_turned)
     pair_before = stretch_shift(pair_own[-halo:], 1)
     pair_after = stretch_shift(pair_own[:halo], -1)
     window_rows = stretch_rows + 2 * halo
@@ -973,7 +1129,9 @@
     high_pos = seq_ends[qid[QB - 1 :: QB]] - (stretch_first - halo)
     lo = jnp.clip(low_pos // KB, 0, window_rows // KB).astype(jnp.int32)
     hi = jnp.clip((high_pos + KB - 1) // KB, 0, window_rows // KB).astype(jnp.int32)
-    attended_own, logsum = attention(own, pair_before, pair_after, lo, hi, qid, kid)
+    attended_own, logsum = attention(
+        query_own, pair_own, pair_before, pair_after, lo, hi, qid, kid
+    )
     attended_came = exchange(attended_own.reshape(bunch, tok_rows, half_width))
 
     def split_group(value):
@@ -983,36 +1141,47 @@
         spots, attended_came, out_weights, image, gathers=True
     )
     branch = reduce_rep(split_group(branch_terms))
-    branch, fc1_weights = lax.optimization_barrier((branch, fc1_weights))
     mid = stream_in + gate_one * branch
     act_two = layer_modulate(mid, shift_two, scale_two).astype(bf16)
     act_two_group = jnp.concatenate(gather_rep(act_two))
     gelu_low, gelu_slope = forward_product(spots, act_two_group, fc1_weights, image, gelu=True)
-    down_proj = reduce_rep(split_group(forward_product(spots, gelu_low, fc2_weights, image)[0]))
-    output = mid + gate_two * down_proj
-
-    d_gate_two = back_out * down_proj
+    down_terms = forward_product(spots, gelu_low, fc2_weights, image)[0]
+
+    fc2_terms = gradient(spots, gelu_low, d_down_group, image, fc2_weights.shape)
+    fc2_terms, gelu_slope = lax.optimization_barrier((fc2_terms, gelu_slope))
+    fc2_own = scatter_weight(fc2_terms)
     d_up = backward_product(spots, d_down_group, fc2_weights, image, factor=gelu_slope)
-    g_fc2 = turn(
-        scatter_weight(gradient(spots, gelu_low, d_down_group, image, fc2_weights.shape))
-    )
     d_act_two = reduce_rep(split_group(backward_product(spots, d_up, fc1_weights, image)))
-    g_fc1 = scatter_weight(gradient(spots, act_two_group, d_up, image, fc1_weights.shape))
     d_mid_norm, d_shift_two, d_scale_two = jax.vjp(layer_modulate, mid, shift_two, scale_two)[1](
         d_act_two
     )
     d_mid = back_out + d_mid_norm
     d_branch = (gate_one * d_mid).astype(bf16)
+    fc1_terms = gradient(spots, act_two_group, d_up, image, fc1_weights.shape)
+    fc1_terms, d_branch = lax.optimization_barrier((fc1_terms, d_branch))
+    g_fc1 = scatter_weight(fc1_terms)
     d_gate_one = d_mid * branch
     d_branch_group = jnp.concatenate(gather_rep(d_branch))
     d_attended = backward_product(spots, d_branch_group, out_weights, image, packs=True)
-    g_out = turn(
-        scatter_weight(gradient(spots, attended_low, d_branch_group, image, out_weights.shape))
+    out_terms = gradient(spots, attended_low, d_branch_group, image, out_weights.shape)
+    out_came = lax.all_to_all(
+        out_terms.reshape(shards, -1, out_terms.shape[-1]), "shard", 0, 0, tiled=True
     )
     d_attended_own = exchange(d_attended).reshape(stretch_rows, half_width)
     d_query_own, d_before, d_after, d_pair_own = attention_back(
-        own, pair_before, pair_after, d_attended_own, attended_own, lo, hi, qid, kid, logsum
-    )
+        query_own,
+        pair_own,
+        pair_before,
+        pair_after,
+        d_attended_own,
+        attended_own,
+        lo,
+        hi,
+        qid,
+        kid,
+        logsum,
+    )
+    d_query_came = exchange(d_query_own.reshape(bunch, tok_rows, half_width))
     from_later = stretch_shift(d_before, -1).astype(f32)
     from_earlier = stretch_shift(d_after, 1).astype(f32)
     rest = jnp.zeros((stretch_rows - halo, 2 * half_width), f32)
@@ -1021,19 +1190,16 @@
         + jnp.concatenate([rest, from_later], axis=0)
         + jnp.concatenate([from_earlier, rest], axis=0)
     )
-    d_own = jnp.concatenate([d_query_own, d_pair_own.astype(bf16)], axis=1)
-    d_came = exchange(d_own.reshape(bunch, tok_rows, 3 * half_width))
-    d_qkv, gain_sums = norm_back(spots, d_came, qk_pre, image, gains)
+    d_pair_own, out_came = lax.optimization_barrier((d_pair_own, out_came))
+    g_out = turn(jnp.sum(out_came.astype(f32), axis=0).astype(bf16).reshape(w_out.shape))
+    d_pair_came = exchange(d_pair_own.astype(bf16).reshape(bunch, tok_rows, 2 * half_width))
+    d_pair_came, down_terms = lax.optimization_barrier((d_pair_came, down_terms))
+    down_proj = reduce_rep(split_group(down_terms))
+    output = mid + gate_two * down_proj
+    d_gate_two = back_out * down_proj
+    d_qkv, gain_sums = norm_back(spots, d_query_came, d_pair_came, qk_pre, image, gains)
     d_act_one = reduce_rep(split_group(backward_product(spots, d_qkv, qkv_weights, image)))
-    g_qkv_group = scatter_weight(gradient(spots, act_one_group, d_qkv, image, qkv_weights.shape))
-    g_parts = [
-        g_qkv_group[:, :, t * part_width : (t + 1) * part_width] for t in range(3)
-    ]
-    g_parts = rolled(g_parts, (3 - turns) % 3)
-    g_qkv = jnp.concatenate(
-        [over_rep(g_parts[i], lambda d, i=i: (3 * (d - i)) % reps) for i in range(3)], axis=2
-    )
-
+    qkv_terms = gradient(spots, act_one_group, d_qkv, image, qkv_weights.shape)
     d_in_norm, d_shift_one, d_scale_one = jax.vjp(layer_modulate, stream_in, shift_one, scale_one)[
         1
     ](d_act_one)
@@ -1062,10 +1228,24 @@
             for r in range(reps)
         ]
     )
+    qkv_terms, g_fc1, fc2_own, leaving = lax.optimization_barrier(
+        (qkv_terms, g_fc1, fc2_own, leaving)
+    )
     leaving = jnp.broadcast_to(leaving[:, None], (reps, shards, *leaving.shape[1:]))
     came = lax.all_to_all(
         leaving.reshape(device_count, *leaving.shape[2:]), ("rep", "shard"), 0, 0, tiled=True
     )
+    g_fc2 = turn(fc2_own)
+    g_qkv_group = ring_scatter(qkv_terms)
+    g_qkv_group, came = lax.optimization_barrier((g_qkv_group, came))
+    g_parts = [
+        g_qkv_group[:, :, t * part_width : (t + 1) * part_width] for t in range(3)
+    ]
+    g_parts = rolled(g_parts, (3 - turns) % 3)
+    g_qkv = jnp.concatenate(
+        [over_rep(g_parts[i], lambda d, i=i: (3 * (d - i)) % reps) for i in range(3)], axis=2
+    )
+
     g_gains = jnp.sum(came[:, :2, mod_cols:], axis=0)
     came = came[:, :, :mod_cols].reshape(2 * device_count, 2, mod_cols)
     seqs = jnp.stack([firsts, seconds], axis=1).reshape(-1)

time: 1470 us -> 1420 us (0.966); the launches traced: 1460 us -> 1430 us
  waiting for transfers between devices: 741 us -> 437 us
  Pallas kernels: 318 us -> 590 us
  starting transfers between devices: 144 us -> 103 us
  blocking collectives: 73.1 us -> 113 us
    pallas_call x0 -> x2, Pallas kernels: none -> 253 us  [the longest x1 132 us: ring_scatter(): pl.pallas_call(ring_scatter_kernel, in_specs=[pl.BlockSpec(memory_space=p...]
    reduce_scatter x4 -> x2, waiting for transfers between devices: 137 us -> 0.04 us  [scatter_weight(): lax.psum_scatter(blocks.reshape(-1, *terms.shape[-2:]), 'shard', scatter_...]
    ppermute x4, waiting for transfers between devices: 83.5 us -> 0.01 us  [turn(): return lax.ppermute(value, ('rep', 'shard'), pairs)]
    all_to_all x3 -> x4, waiting for transfers between devices: 242 us -> 168 us  [exchange(): lax.all_to_all(value, 'shard', 0, 0, axis_index_groups=None if bunches ==...]
    ppermute x33, starting transfers between devices: 82.1 us -> 37.9 us  [over_rep(): return lax.ppermute(value, 'rep', [(r, target(r)) for r in range(count)])]
    ppermute x4, waiting for transfers between devices: 70.5 us -> 114 us  [stretch_shift(): return lax.ppermute(value, 'shard', pairs)]
    ppermute x33, waiting for transfers between devices: 166 us -> 123 us  [over_rep(): return lax.ppermute(value, 'rep', [(r, target(r)) for r in range(count)])]
    all_to_all x1 -> x2, blocking collectives: 73.1 us -> 113 us  [exchange(): lax.all_to_all(value, 'shard', 0, 0, axis_index_groups=None if bunches ==...]
  transfers between devices with their start and end apart: 54 -> 53, of which waited for: 27 -> 21; matrix products, arithmetic and copies ran while one was open for 8% -> 9% of each run, Pallas kernels for 19% -> 40%
where the time goes in v2:
time: 1420 us; the launch traced here: 1430 us
  Pallas kernels  590 us (42%)
  waiting for transfers between devices  437 us (31%)
  blocking collectives  113 us (8%)
  starting transfers between devices  103 us (7%)
  other arithmetic  90 us (6%)
  local copies, waits for them, and re-layouts  67.9 us (5%)
  between operations  15.9 us (1%)
    all_to_all x4, waiting for transfers between devices, exchange(): lax.all_to_all(value, 'shard', 0, 0, axis_index_groups=None if bunches ==...  168 us
    pallas_call x1, Pallas kernels, ring_scatter(): pl.pallas_call(ring_scatter_kernel, in_specs=[pl.BlockSpec(memory_space=p...  132 us
    ppermute x33, waiting for transfers between devices, over_rep(): return lax.ppermute(value, 'rep', [(r, target(r)) for r in range(count)])  123 us
    pallas_call x1, Pallas kernels, ring_gather(): pl.pallas_call(functools.partial(ring_kernel, shards, count), in_specs=[a...  121 us
    ppermute x4, waiting for transfers between devices, stretch_shift(): return lax.ppermute(value, 'shard', pairs)  114 us
    all_to_all x2, blocking collectives, exchange(): lax.all_to_all(value, 'shard', 0, 0, axis_index_groups=None if bunches ==...  113 us
    pallas_call x1, Pallas kernels, attention_back(): pl.pallas_call(attend_back_kernel, grid_spec=pltpu.PrefetchScalarGridSpec...  84 us
    pallas_call x4, Pallas kernels, gradient(): pl.pallas_call(functools.partial(gradient_kernel, blocks), grid_spec=pltp...  73.9 us
  transfers between devices with their start and end apart: 53, of which 21 were waited for; matrix products, arithmetic and copies ran while one was open for 9% of the time, Pallas kernels for 40%

profile of v2, /device:TPU:1, one launch (start us, length us, event | category | flops | bytes accessed | tf_op | source)
XLA Modules:
  0.0 1430.9 jit_solution(3341497599017691192)
XLA Ops:
  8.9 4.0 collective-permute-start.6
  13.7 3.3 collective-permute-done.6
  25.5 9.7 all-to-all-start
  38.3 30.2 %all-to-all-done = bf16[32,4,2304]{2,1,0:T(4,128)(2,1)S(1)} async-done(((bf16[32,4,2304]{2,1,0:T(4,128)(2,1)}), bf16[32,4,2304]{2,1,0:T(4,128)(2,1)S(1)}, u32[]{:S(2)}, u32[]{:S(2)}) %all-to-all-start) | async-done | bytes 589856 | tf_op jit(solution)/shard_map/all_to_all | solution.py:1025
  69.6 3.5 fusion.16
  76.4 19.3 %collective-permute-done.1 = s32[320]{0:T(512)S(1)} collective-permute-done((s32[320]{0:T(512)S(1)}, s32[320]{0:T(512)S(1)}, u32[]{:S(2)}, u32[]{:S(2)}) %collective-permute-start.1) | collective-permute-done | bytes 1312 | tf_op jit(solution)/shard_map/ppermute | solution.py:760
  100.3 2.9 convert_element_type.206
  107.8 3.3 pad_maximum_fusion.x_ref
  111.1 121.3 %ring_gather.1.w0.w1 = bf16[8,2,192,1536]{3,2,1,0:T(8,128)(2,1)} custom-call(bf16[2,192,1536]{2,1,0:T(8,128)(2,1)} %convert_element_type.207.refs_0_), custom_call_target="tpu_custom_call" | custom-call | flops 1048576 | bytes 8388608 | tf_op jit(solution)/shard_map/ring_gather/pallas_call | solution.py:863
  234.5 21.4 %qkv_product.1 = (bf16[8,320,192]{2,1,0:T(8,128)(2,1)S(1)}, bf16[8,320,384]{2,1,0:T(8,128)(2,1)S(1)}, f32[1280,768]{1,0:T(8,128)S(1)}) custom-call(s32[9]{0:T(128)S(1)} %pad_add_fusion.1.spots, bf16[1280,1536]{1,0:T(8,128)(2,1)S(1)} %copy-done.2, bf16[8,2,192,1152]{3,2,1,0:T(8,128)(2,1)} %bitcast.80, bf16[8,2,192,1152]{3,2,1,0:T(8,128)(2,1)} %bitcast.81, ...), custom_call_target="tpu_custom_call" | custom-call | flops 1073741824 | bytes 4194304 | tf_op jit(solution)/shard_map/qkv_product/pallas_call | solution.py:380
  257.8 46.1 %all_to_all.45 = bf16[8,320,384]{2,1,0:T(8,128)(2,1)S(1)} all-to-all(bf16[8,320,384]{2,1,0:T(8,128)(2,1)S(1)} %get-tuple-element.75), channel_id=1, replica_groups=mesh['rep'=4,'shard'=8] {'shard'}, dimensions={0} | all-to-all | bytes 3932160 | tf_op jit(solution)/shard_map/all_to_all | solution.py:1088
  303.9 3.1 copy.104
  307.0 4.3 all-to-all-start.2
  311.3 6.5 collective-permute-start.10
  319.7 49.7 %all-to-all-done.2 = bf16[8,320,192]{1,2,0:T(8,128)(2,1)} async-done(((bf16[8,320,192]{1,2,0:T(8,128)(2,1)}), bf16[8,320,192]{1,2,0:T(8,128)(2,1)}, u32[]{:S(2)}, u32[]{:S(2)}) %all-to-all-start.2) | async-done | bytes 983072 | tf_op jit(solution)/shard_map/all_to_all | solution.py:1088
  378.8 13.6 collective-permute-done.11.before_ref
  392.5 59.0 %collective-permute-done.12.after_ref = bf16[1280,384]{1,0:T(8,128)(2,1)S(1)} collective-permute-done((bf16[1280,384]{1,0:T(8,128)(2,1)S(1)}, bf16[1280,384]{1,0:T(8,128)(2,1)S(1)}, u32[]{:S(2)}, u32[]{:S(2)}) %collective-permute-start.12) | collective-permute-done | bytes 983072 | tf_op jit(solution)/shard_map/ppermute | solution.py:1106
  451.5 42.7 %attend.1 = (bf16[2560,192]{1,0:T(8,128)(2,1)S(1)}, f32[10,8,256]{2,1,0:T(8,128)S(1)}) custom-call(s32[10]{0:T(128)S(1)} %fusion.63.lo_ref, s32[10]{0:T(128)S(1)} %fusion.62.hi_ref, bf16[2560,192]{1,0:T(8,128)(2,1)S(1)} %bitcast.73, bf16[2560,384]{1,0:T(8,128)(2,1)S(1)} %bitcast.70, bf16[1280,384]{1,0:T(8,128)(2,1)S(1)} %collective-permute-done.11.before_ref, ...), custom_call_target="tpu_custom_call" | custom-call | flops 1073741824 | bytes 4194304 | tf_op jit(solution)/shard_map/attend/pallas_call | solution.py:197
  497.1 67.4 %all_to_all.46 = bf16[8,320,192]{1,2,0:T(8,128)(2,1)} all-to-all(bf16[8,320,192]{1,2,0:T(8,128)(2,1)S(1)} %copy.107), channel_id=1, replica_groups=mesh['rep'=4,'shard'=8] {'shard'}, dimensions={0} | all-to-all | bytes 1966080 | tf_op jit(solution)/shard_map/all_to_all | solution.py:1088
  567.8 8.2 forward_product.3
  580.7 21.7 %collective-permute-done.15 = bf16[320,1536]{1,0:T(8,128)(2,1)S(1)} collective-permute-done((bf16[320,1536]{1,0:T(8,128)(2,1)S(1)}, bf16[320,1536]{1,0:T(8,128)(2,1)S(1)}, u32[]{:S(2)}, u32[]{:S(2)}) %collective-permute-start.15) | collective-permute-done | bytes 983072 | tf_op jit(solution)/shard_map/ppermute | solution.py:760
  604.4 3.4 add_convert_fusion.4
  610.8 19.5 %collective-permute-done.17 = bf16[320,1536]{1,0:T(8,128)(2,1)S(1)} collective-permute-done((bf16[320,1536]{1,0:T(8,128)(2,1)S(1)}, bf16[320,1536]{1,0:T(8,128)(2,1)S(1)}, u32[]{:S(2)}, u32[]{:S(2)}) %collective-permute-start.17) | collective-permute-done | bytes 983072 | tf_op jit(solution)/shard_map/ppermute | solution.py:760
  630.4 3.1 collective-permute-start.18
  633.4 18.0 %collective-permute-done.20 = bf16[320,1536]{1,0:T(8,128)(2,1)S(1)} collective-permute-done((bf16[320,1536]{1,0:T(8,128)(2,1)S(1)}, bf16[320,1536]{1,0:T(8,128)(2,1)S(1)}, u32[]{:S(2)}, u32[]{:S(2)}) %collective-permute-start.20) | collective-permute-done | bytes 983072 | tf_op jit(solution)/shard_map/ppermute | solution.py:760
  653.5 21.0 %forward_product.4 = (bf16[1280,1536]{1,0:T(8,128)(2,1)S(1)}, bf16[1280,1536]{1,0:T(8,128)(2,1)S(1)}) custom-call(s32[9]{0:T(128)S(1)} %pad_add_fusion.1.spots, bf16[1280,1536]{1,0:T(8,128)(2,1)S(1)} %pad_maximum_fusion.1.x_ref, bf16[8,2,192,1536]{3,2,1,0:T(8,128)(2,1)} %ring_gather.1.w0.w1, bf16[8,2,192,1536]{3,2,1,0:T(8,128)(2,1)} %ring_gather.1.w0.w1, ...), custom_call_target="tpu_custom_call" | custom-call | flops 754974720 | bytes 4194304 | tf_op jit(solution)/shard_map/forward_product/pallas_call | solution.py:540
  678.7 23.7 %gradient.4 = bf16[4,2,2,768,384]{4,3,2,1,0:T(8,128)(2,1)} custom-call(s32[9]{0:T(128)S(1)} %pad_add_fusion.1.spots, bf16[1280,1536]{1,0:T(8,128)(2,1)S(1)} %get-tuple-element.84.x_ref, bf16[1280,1536]{1,0:T(8,128)(2,1)} %pad_maximum_fusion.2.dy_ref, s32[1280,1]{1,0:T(8,128)S(1)} %convert_element_type.212.image_ref), custom_call_target="tpu_custom_call" | custom-call | flops 754974720 | bytes 4194304 | tf_op jit(solution)/shard_map/gradient/pallas_call | solution.py:732
  702.5 20.4 %backward_product.4.dy_ref = bf16[1280,1536]{1,0:T(8,128)(2,1)S(1)} custom-call(s32[9]{0:T(128)S(1)} %pad_add_fusion.1.spots, bf16[1280,1536]{1,0:T(8,128)(2,1)} %pad_maximum_fusion.2.dy_ref, bf16[4,2,2,768,384]{4,3,2,1,0:T(8,128)(2,1)} %bitcast.76, bf16[4,2,2,768,384]{4,3,2,1,0:T(8,128)(2,1)} %bitcast.77, s32[1280,1]{1,0:T(8,128)S(1)} %convert_element_type.212.image_ref, ...), custom_call_target="tpu_custom_call" | custom-call | flops 754974720 | bytes 4194304 | tf_op jit(solution)/shard_map/backward_product/pallas_call | solution.py:651
  724.8 16.9 %backward_product.5 = bf16[1280,1536]{1,0:T(8,128)(2,1)S(1)} custom-call(s32[9]{0:T(128)S(1)} %pad_add_fusion.1.spots, bf16[1280,1536]{1,0:T(8,128)(2,1)} %copy-done.5, bf16[8,2,192,1536]{3,2,1,0:T(8,128)(2,1)} %ring_gather.1.w0.w1, bf16[8,2,192,1536]{3,2,1,0:T(8,128)(2,1)} %ring_gather.1.w0.w1, s32[1280,1]{1,0:T(8,128)S(1)} %convert_element_type.212.image_ref), custom_call_target="tpu_custom_call" | custom-call | flops 754974720 | bytes 4194304 | tf_op jit(solution)/shard_map/backward_product/pallas_call | solution.py:651
  743.2 3.4 collective-permute-done.23
  747.4 23.9 %gradient.5 = bf16[8,2,192,1536]{3,2,1,0:T(8,128)(2,1)} custom-call(s32[9]{0:T(128)S(1)} %pad_add_fusion.1.spots, bf16[1280,1536]{1,0:T(8,128)(2,1)S(1)} %copy-done.4, bf16[1280,1536]{1,0:T(8,128)(2,1)} %copy-done.5, s32[1280,1]{1,0:T(8,128)S(1)} %convert_element_type.212.image_ref), custom_call_target="tpu_custom_call" | custom-call | flops 754974720 | bytes 4194304 | tf_op jit(solution)/shard_map/gradient/pallas_call | solution.py:732
  776.7 21.3 %collective-permute-done.26 = bf16[320,1536]{1,0:T(8,128)(2,1)S(1)} collective-permute-done((bf16[320,1536]{1,0:T(8,128)(2,1)S(1)}, bf16[320,1536]{1,0:T(8,128)(2,1)S(1)}, u32[]{:S(2)}, u32[]{:S(2)}) %collective-permute-start.26) | collective-permute-done | bytes 983072 | tf_op jit(solution)/shard_map/ppermute | solution.py:760
  803.4 9.3 backward_product.6
  814.1 3.6 all-to-all-start.4
  817.7 9.7 gradient.6
  827.4 44.9 %all-to-all-done.4 = bf16[8,320,192]{1,2,0:T(8,128)(2,1)S(1)} async-done(((bf16[8,320,192]{1,2,0:T(8,128)(2,1)}), bf16[8,320,192]{1,2,0:T(8,128)(2,1)S(1)}, u32[]{:S(2)}, u32[]{:S(2)}) %all-to-all-start.4) | async-done | bytes 983072 | tf_op jit(solution)/shard_map/all_to_all | solution.py:1088
  872.3 6.0 all-to-all-start.5
  881.9 3.8 fusion.8.kid_ref
  887.2 84.0 %attend_back.1 = (bf16[2560,192]{1,0:T(8,128)(2,1)}, bf16[1280,384]{1,0:T(8,128)(2,1)}, bf16[1280,384]{1,0:T(8,128)(2,1)}, f32[2560,384]{1,0:T(8,128)}) custom-call(s32[10]{0:T(128)} %copy-done.26, s32[10]{0:T(128)} %copy-done.25, bf16[2560,192]{1,0:T(8,128)(2,1)} %bitcast.72, bf16[2560,384]{1,0:T(8,128)(2,1)} %bitcast.71, bf16[1280,384]{1,0:T(8,128)(2,1)} %copy-done.23, ...), custom_call_target="tpu_custom_call" | custom-call | flops 25769803776 | bytes 8388608 | tf_op jit(solution)/shard_map/attend_back/pallas_call | solution.py:237
  972.5 11.9 collective-permute-start.29
  986.9 3.6 all-to-all-start.7
  990.5 41.7 %collective-permute-done.28 = bf16[1280,384]{1,0:T(8,128)(2,1)S(1)} collective-permute-done((bf16[1280,384]{1,0:T(8,128)(2,1)}, bf16[1280,384]{1,0:T(8,128)(2,1)S(1)}, u32[]{:S(2)}, u32[]{:S(2)}) %collective-permute-start.28) | collective-permute-done | bytes 983072 | tf_op jit(solution)/shard_map/ppermute | solution.py:1106
  1032.2 4.1 convert_add_fusion
  1036.2 21.0 %all-to-all-done.7 = bf16[8,320,192]{1,2,0:T(8,128)(2,1)S(1)} async-done(((bf16[8,320,192]{1,2,0:T(8,128)(2,1)}), bf16[8,320,192]{1,2,0:T(8,128)(2,1)S(1)}, u32[]{:S(2)}, u32[]{:S(2)}) %all-to-all-start.7) | async-done | bytes 983072 | tf_op jit(solution)/shard_map/all_to_all | solution.py:1088
  1058.3 3.8 all-to-all-start.6
  1064.3 17.5 %forward_product.5 = bf16[1280,1536]{1,0:T(8,128)(2,1)S(1)} custom-call(s32[9]{0:T(128)S(1)} %pad_add_fusion.1.spots, bf16[1280,1536]{1,0:T(8,128)(2,1)S(1)} %copy-done.11, bf16[4,2,2,768,384]{4,3,2,1,0:T(8,128)(2,1)} %bitcast.78, bf16[4,2,2,768,384]{4,3,2,1,0:T(8,128)(2,1)} %bitcast.79, s32[1280,1]{1,0:T(8,128)S(1)} %convert_element_type.212.image_ref), custom_call_target="tpu_custom_call" | custom-call | flops 754974720 | bytes 4194304 | tf_op jit(solution)/shard_map/forward_product/pallas_call | solution.py:540
  1086.2 52.6 %all-to-all-done.6.kv_ref = bf16[8,320,384]{2,1,0:T(8,128)(2,1)S(1)} async-done(((bf16[8,320,384]{2,1,0:T(8,128)(2,1)}), bf16[8,320,384]{2,1,0:T(8,128)(2,1)S(1)}, u32[]{:S(2)}, u32[]{:S(2)}) %all-to-all-start.6) | async-done | bytes 1966112 | tf_op jit(solution)/shard_map/all_to_all | solution.py:1088
  1142.3 7.1 norm_back.1
  1149.3 14.4 %backward_product.7 = bf16[1280,1536]{1,0:T(8,128)(2,1)} custom-call(s32[9]{0:T(128)S(1)} %pad_add_fusion.1.spots, bf16[1280,1152]{1,0:T(8,128)(2,1)S(1)} %get-tuple-element.98.dy_ref, bf16[8,2,192,1152]{3,2,1,0:T(8,128)(2,1)} %bitcast.82, bf16[8,2,192,1152]{3,2,1,0:T(8,128)(2,1)} %bitcast.83, s32[1280,1]{1,0:T(8,128)S(1)} %convert_element_type.212.image_ref), custom_call_target="tpu_custom_call" | custom-call | flops 566231040 | bytes 4194304 | tf_op jit(solution)/shard_map/backward_product/pallas_call | solution.py:651
  1166.5 4.9 collective-permute-start.34
  1186.5 16.6 %gradient.7.terms = bf16[8,2,192,1152]{3,2,1,0:T(8,128)(2,1)} custom-call(s32[9]{0:T(128)S(1)} %pad_add_fusion.1.spots, bf16[1280,1536]{1,0:T(8,128)(2,1)} %pad_maximum_fusion.x_ref, bf16[1280,1152]{1,0:T(8,128)(2,1)S(1)} %copy-done.16, s32[1280,1]{1,0:T(8,128)S(1)} %convert_element_type.212.image_ref), custom_call_target="tpu_custom_call" | custom-call | flops 566231040 | bytes 4194304 | tf_op jit(solution)/shard_map/gradient/pallas_call | solution.py:732
  1210.8 4.1 multiply_dynamic-update-slice_fusion.1
  1218.9 9.3 collective-permute-done.32
  1228.2 3.7 fusion.21
  1231.9 7.1 fusion.51
  1240.4 3.2 all-to-all-start.8
  1244.8 3.7 collective-permute-start.40
  1251.2 3.0 copy-done.8
  1254.2 132.1 %ring_scatter.1 = bf16[2,192,1152]{2,1,0:T(8,128)(2,1)S(1)} custom-call(bf16[8,2,192,1152]{3,2,1,0:T(8,128)(2,1)S(1)} %copy-done.8), custom_call_target="tpu_custom_call" | custom-call | flops 1048576 | bytes 268435456 | tf_op jit(solution)/shard_map/ring_scatter/pallas_call | solution.py:930
  1386.4 5.0 fusion.70
  1392.1 4.6 fusion.67
  1403.2 3.1 reshape.447
  1412.3 7.5 fusion.79
  1420.6 3.6 fusion.76
  (421 shorter events, 149.0 us)
Async XLA Ops:
  7.2 225.2 %all-gather.7.cloned.1.call-start = ((), (), s32[]{:S(2)}) async-start(), calls=%async_computation.13 | async-start | bytes 7962624 | tf_op jit(solution)/shard_map/all_gather | solution.py:793
  8.9 8.1 collective-permute-start.6
  12.9 4.1 collective-permute-start.7
  13.0 4.0 collective-permute-start.8
  25.5 43.0 %all-to-all-start = ((bf16[32,4,2304]{2,1,0:T(4,128)(2,1)}), bf16[32,4,2304]{2,1,0:T(4,128)(2,1)S(1)}, u32[]{:S(2)}, u32[]{:S(2)}) async-start(bf16[32,4,2304]{2,1,0:T(4,128)(2,1)} %reshape.434), calls=%async_computation | async-start | bytes 1179648 | tf_op jit(solution)/shard_map/all_to_all | solution.py:1025
  38.3 62.0 %copy-start.83 = (pred[320]{0:T(512)(128)(4,1)}, pred[320]{0:T(512)(128)(4,1)S(1)}, u32[]{:S(2)}) copy-start(pred[320]{0:T(512)(128)(4,1)S(1)} %get-tuple-element.158) | copy-start | bytes 964
  73.1 30.6 %collective-permute-start.4 = (bf16[320,1536]{1,0:T(8,128)(2,1)S(1)}, bf16[320,1536]{1,0:T(8,128)(2,1)S(1)}, u32[]{:S(2)}, u32[]{:S(2)}) collective-permute-start(bf16[320,1536]{1,0:T(8,128)(2,1)S(1)} %fusion.16), channel_id=1, source_target_pairs={{0,16},{8,24},{16,0},{24,8},{1,17},{9,25},{17,1},{25,9},{2,18},{10... | collective-permute-start | bytes 2949128 | tf_op jit(solution)/shard_map/ppermute | solution.py:760
  74.2 21.5 %collective-permute-start.1 = (s32[320]{0:T(512)S(1)}, s32[320]{0:T(512)S(1)}, u32[]{:S(2)}, u32[]{:S(2)}) collective-permute-start(s32[320]{0:T(512)S(1)} %copy-done.91), channel_id=1, source_target_pairs={{0,16},{8,24},{16,0},{24,8},{1,17},{9,25},{17,1},{25,9},{2,18},{10... | collective-permute-start | bytes 3848 | tf_op jit(solution)/shard_map/ppermute | solution.py:760
  74.7 28.5 %collective-permute-start = (s32[320]{0:T(512)S(1)}, s32[320]{0:T(512)S(1)}, u32[]{:S(2)}, u32[]{:S(2)}) collective-permute-start(s32[320]{0:T(512)S(1)} %copy-done.91), channel_id=1, source_target_pairs={{0,8},{8,0},{16,24},{24,16},{1,9},{9,1},{17,25},{25,17},{2,10},{10... | collective-permute-start | bytes 3848 | tf_op jit(solution)/shard_map/ppermute | solution.py:760
  95.7 7.5 collective-permute-start.2
  103.7 2.8 collective-permute-start.3
  103.7 4.1 collective-permute-start.5
  303.9 147.6 %copy-start.9 = (bf16[8,320,384]{2,1,0:T(8,128)(2,1)}, bf16[8,320,384]{2,1,0:T(8,128)(2,1)S(1)}, u32[]{:S(2)}) copy-start(bf16[8,320,384]{2,1,0:T(8,128)(2,1)S(1)} %all_to_all.45) | copy-start | bytes 5898244
  307.0 62.5 %all-to-all-start.2 = ((bf16[8,320,192]{1,2,0:T(8,128)(2,1)}), bf16[8,320,192]{1,2,0:T(8,128)(2,1)}, u32[]{:S(2)}, u32[]{:S(2)}) async-start(bf16[8,320,192]{1,2,0:T(8,128)(2,1)} %copy.104), calls=%async_computation.2 | async-start | bytes 2359296 | tf_op jit(solution)/shard_map/all_to_all | solution.py:1088
  311.3 254.8 %all-gather.9.cloned.1.call-start = ((), (), s32[]{:S(2)}) async-start(), calls=%async_computation.14 | async-start | bytes 2654208 | tf_op jit(solution)/shard_map/all_gather | solution.py:793
  311.3 60.6 %collective-permute-start.10 = (bf16[2,768,384]{2,1,0:T(8,128)(2,1)}, bf16[2,768,384]{2,1,0:T(8,128)(2,1)}, u32[]{:S(2)}, u32[]{:S(2)}) collective-permute-start(bf16[2,768,384]{2,1,0:T(8,128)(2,1)} %convert_element_type.206), channel_id=1, source_target_pairs={{0,0},{1,1},{2,8},{3,9},{4,16},{5,17},{6,24},{7,25},{8,2},{9,3},{1... | collective-permute-start | bytes 3538952 | tf_op jit(solution)/shard_map/ppermute | solution.py:789
  317.8 54.1 %collective-permute-start.9 = (bf16[2,192,384]{2,1,0:T(8,128)(2,1)S(1)}, bf16[2,192,384]{2,1,0:T(8,128)(2,1)S(1)}, u32[]{:S(2)}, u32[]{:S(2)}) collective-permute-start(bf16[2,192,384]{2,1,0:T(8,128)(2,1)S(1)} %convert_element_type.205), channel_id=1, source_target_pairs={{0,0},{1,1},{2,8},{3,9},{4,16},{5,17},{6,24},{7,25},{8,2},{9,3},{1... | collective-permute-start | bytes 884744 | tf_op jit(solution)/shard_map/ppermute | solution.py:789
  372.6 329.8 %all-gather.11.cloned.1.call-start = ((), (), s32[]{:S(2)}) async-start(), calls=%async_computation.15 | async-start | bytes 10616832 | tf_op jit(solution)/shard_map/all_gather | solution.py:793
  373.4 865.8 %reduce-scatter.5.cloned.1.call-start = ((), (), s32[]{:S(2)}) async-start(), calls=%async_computation.12 | async-start | bytes 10616832 | tf_op jit(solution)/shard_map/reduce_scatter | solution.py:950
  375.3 76.1 %copy-start.18 = (bf16[8,320,192]{2,1,0:T(8,128)(2,1)S(1)}, bf16[8,320,192]{2,1,0:T(8,128)(2,1)}, u32[]{:S(2)}) copy-start(bf16[8,320,192]{2,1,0:T(8,128)(2,1)} %copy.105) | copy-start | bytes 2949124
  375.6 16.9 %collective-permute-start.11 = (bf16[1280,384]{1,0:T(8,128)(2,1)S(1)}, bf16[1280,384]{1,0:T(8,128)(2,1)S(1)}, u32[]{:S(2)}, u32[]{:S(2)}) collective-permute-start(bf16[1280,384]{1,0:T(8,128)(2,1)S(1)} %get-tuple-element.181), channel_id=1, source_target_pairs={{0,2},{1,3},{2,4},{3,5},{4,6},{5,7},{8,10},{9,11},{10,12},{11,13},... | collective-permute-start | bytes 2949128 | tf_op jit(solution)/shard_map/ppermute | solution.py:1106
  377.0 74.4 %collective-permute-start.12 = (bf16[1280,384]{1,0:T(8,128)(2,1)S(1)}, bf16[1280,384]{1,0:T(8,128)(2,1)S(1)}, u32[]{:S(2)}, u32[]{:S(2)}) collective-permute-start(bf16[1280,384]{1,0:T(8,128)(2,1)S(1)} %get-tuple-element.180), channel_id=1, source_target_pairs={{2,0},{3,1},{4,2},{5,3},{6,4},{7,5},{10,8},{11,9},{12,10},{13,11},... | collective-permute-start | bytes 2949128 | tf_op jit(solution)/shard_map/ppermute | solution.py:1106
  378.4 115.8 %copy-start.25 = (s32[10]{0:T(128)}, s32[10]{0:T(128)S(1)}, u32[]{:S(2)}) copy-start(s32[10]{0:T(128)S(1)} %fusion.62.hi_ref) | copy-start | bytes 124
  378.4 115.8 %copy-start.26 = (s32[10]{0:T(128)}, s32[10]{0:T(128)S(1)}, u32[]{:S(2)}) copy-start(s32[10]{0:T(128)S(1)} %fusion.63.lo_ref) | copy-start | bytes 124
  392.5 101.7 %copy-start.23 = (bf16[1280,384]{1,0:T(8,128)(2,1)}, bf16[1280,384]{1,0:T(8,128)(2,1)S(1)}, u32[]{:S(2)}) copy-start(bf16[1280,384]{1,0:T(8,128)(2,1)S(1)} %collective-permute-done.11.before_ref) | copy-start | bytes 2949124
  495.3 69.2 %copy-start.29 = (f32[10,8,256]{2,1,0:T(8,128)}, f32[10,8,256]{2,1,0:T(8,128)S(1)}, u32[]{:S(2)}) copy-start(f32[10,8,256]{2,1,0:T(8,128)S(1)} %get-tuple-element.88.l_ref) | copy-start | bytes 245764
  576.2 2.6 collective-permute-start.14
  576.3 4.4 collective-permute-start.13
  579.1 23.4 %collective-permute-start.15 = (bf16[320,1536]{1,0:T(8,128)(2,1)S(1)}, bf16[320,1536]{1,0:T(8,128)(2,1)S(1)}, u32[]{:S(2)}, u32[]{:S(2)}) collective-permute-start(bf16[320,1536]{1,0:T(8,128)(2,1)S(1)} %add_convert_fusion.5), channel_id=1, source_target_pairs={{0,16},{8,24},{16,0},{24,8},{1,17},{9,25},{17,1},{25,9},{2,18},{10... | collective-permute-start | bytes 2949128 | tf_op jit(solution)/shard_map/ppermute | solution.py:760
  607.9 22.5 %collective-permute-start.17 = (bf16[320,1536]{1,0:T(8,128)(2,1)S(1)}, bf16[320,1536]{1,0:T(8,128)(2,1)S(1)}, u32[]{:S(2)}, u32[]{:S(2)}) collective-permute-start(bf16[320,1536]{1,0:T(8,128)(2,1)S(1)} %add_convert_fusion.4), channel_id=1, source_target_pairs={{0,16},{8,24},{16,0},{24,8},{1,17},{9,25},{17,1},{25,9},{2,18},{10... | collective-permute-start | bytes 2949128 | tf_op jit(solution)/shard_map/ppermute | solution.py:760
  608.9 42.5 %collective-permute-start.20 = (bf16[320,1536]{1,0:T(8,128)(2,1)S(1)}, bf16[320,1536]{1,0:T(8,128)(2,1)S(1)}, u32[]{:S(2)}, u32[]{:S(2)}) collective-permute-start(bf16[320,1536]{1,0:T(8,128)(2,1)S(1)} %get-tuple-element.218), channel_id=1, source_target_pairs={{0,16},{8,24},{16,0},{24,8},{1,17},{9,25},{17,1},{25,9},{2,18},{10... | collective-permute-start | bytes 2949128 | tf_op jit(solution)/shard_map/ppermute | solution.py:760
  609.4 43.8 %collective-permute-start.16 = (bf16[320,1536]{1,0:T(8,128)(2,1)S(1)}, bf16[320,1536]{1,0:T(8,128)(2,1)S(1)}, u32[]{:S(2)}, u32[]{:S(2)}) collective-permute-start(bf16[320,1536]{1,0:T(8,128)(2,1)S(1)} %add_convert_fusion.4), channel_id=1, source_target_pairs={{0,8},{8,0},{16,24},{24,16},{1,9},{9,1},{17,25},{25,17},{2,10},{10... | collective-permute-start | bytes 2949128 | tf_op jit(solution)/shard_map/ppermute | solution.py:760
  630.4 22.8 %collective-permute-start.18 = (bf16[320,1536]{1,0:T(8,128)(2,1)S(1)}, bf16[320,1536]{1,0:T(8,128)(2,1)S(1)}, u32[]{:S(2)}, u32[]{:S(2)}) collective-permute-start(bf16[320,1536]{1,0:T(8,128)(2,1)S(1)} %collective-permute-done.17), channel_id=1, source_target_pairs={{0,8},{8,0},{16,24},{24,16},{1,9},{9,1},{17,25},{25,17},{2,10},{10... | collective-permute-start | bytes 2949128 | tf_op jit(solution)/shard_map/ppermute | solution.py:760
  633.4 41.1 %collective-permute-start.19 = (bf16[320,1536]{1,0:T(8,128)(2,1)S(1)}, bf16[320,1536]{1,0:T(8,128)(2,1)S(1)}, u32[]{:S(2)}, u32[]{:S(2)}) collective-permute-start(bf16[320,1536]{1,0:T(8,128)(2,1)S(1)} %get-tuple-element.218), channel_id=1, source_target_pairs={{0,8},{8,0},{16,24},{24,16},{1,9},{9,1},{17,25},{25,17},{2,10},{10... | collective-permute-start | bytes 2949128 | tf_op jit(solution)/shard_map/ppermute | solution.py:760
  651.4 23.1 %collective-permute-start.21 = (bf16[320,1536]{1,0:T(8,128)(2,1)S(1)}, bf16[320,1536]{1,0:T(8,128)(2,1)S(1)}, u32[]{:S(2)}, u32[]{:S(2)}) collective-permute-start(bf16[320,1536]{1,0:T(8,128)(2,1)S(1)} %collective-permute-done.20), channel_id=1, source_target_pairs={{0,8},{8,0},{16,24},{24,16},{1,9},{9,1},{17,25},{25,17},{2,10},{10... | collective-permute-start | bytes 2949128 | tf_op jit(solution)/shard_map/ppermute | solution.py:760
  742.7 3.9 collective-permute-start.23
  742.7 28.6 %collective-permute-start.22 = (bf16[320,1536]{1,0:T(8,128)(2,1)}, bf16[320,1536]{1,0:T(8,128)(2,1)S(1)}, u32[]{:S(2)}, u32[]{:S(2)}) collective-permute-start(bf16[320,1536]{1,0:T(8,128)(2,1)} %get-tuple-element.174), channel_id=1, source_target_pairs={{0,8},{8,0},{16,24},{24,16},{1,9},{9,1},{17,25},{25,17},{2,10},{10... | collective-permute-start | bytes 2949128 | tf_op jit(solution)/shard_map/ppermute | solution.py:760
  746.9 24.4 %collective-permute-start.24 = (bf16[320,1536]{1,0:T(8,128)(2,1)S(1)}, bf16[320,1536]{1,0:T(8,128)(2,1)S(1)}, u32[]{:S(2)}, u32[]{:S(2)}) collective-permute-start(bf16[320,1536]{1,0:T(8,128)(2,1)S(1)} %add_convert_fusion.3), channel_id=1, source_target_pairs={{0,16},{8,24},{16,0},{24,8},{1,17},{9,25},{17,1},{25,9},{2,18},{10... | collective-permute-start | bytes 2949128 | tf_op jit(solution)/shard_map/ppermute | solution.py:760
  775.1 22.9 %collective-permute-start.26 = (bf16[320,1536]{1,0:T(8,128)(2,1)S(1)}, bf16[320,1536]{1,0:T(8,128)(2,1)S(1)}, u32[]{:S(2)}, u32[]{:S(2)}) collective-permute-start(bf16[320,1536]{1,0:T(8,128)(2,1)S(1)} %multiply_convert_fusion), channel_id=1, source_target_pairs={{0,16},{8,24},{16,0},{24,8},{1,17},{9,25},{17,1},{25,9},{2,18},{10... | collective-permute-start | bytes 2949128 | tf_op jit(solution)/shard_map/ppermute | solution.py:760
  776.1 23.2 %collective-permute-start.25 = (bf16[320,1536]{1,0:T(8,128)(2,1)S(1)}, bf16[320,1536]{1,0:T(8,128)(2,1)S(1)}, u32[]{:S(2)}, u32[]{:S(2)}) collective-permute-start(bf16[320,1536]{1,0:T(8,128)(2,1)S(1)} %multiply_convert_fusion), channel_id=1, source_target_pairs={{0,8},{8,0},{16,24},{24,16},{1,9},{9,1},{17,25},{25,17},{2,10},{10... | collective-permute-start | bytes 2949128 | tf_op jit(solution)/shard_map/ppermute | solution.py:760
  798.0 3.4 collective-permute-start.27
  814.1 58.2 %all-to-all-start.4 = ((bf16[8,320,192]{1,2,0:T(8,128)(2,1)}), bf16[8,320,192]{1,2,0:T(8,128)(2,1)S(1)}, u32[]{:S(2)}, u32[]{:S(2)}) async-start(bf16[8,320,192]{1,2,0:T(8,128)(2,1)} %copy.109), calls=%async_computation.4 | async-start | bytes 2359296 | tf_op jit(solution)/shard_map/all_to_all | solution.py:1088
  872.3 114.5 %all-to-all-start.5 = ((bf16[8,384,384]{2,1,0:T(8,128)(2,1)}), bf16[8,384,384]{2,1,0:T(8,128)(2,1)}, u32[]{:S(2)}, u32[]{:S(2)}) async-start(bf16[8,384,384]{2,1,0:T(8,128)(2,1)} %bitcast.20), calls=%async_computation.5 | async-start | bytes 4718592 | tf_op jit(solution)/shard_map/all_to_all | solution.py:1167
  878.4 360.8 %reduce-scatter.3.cloned.1.call-start = ((), (), s32[]{:S(2)}) async-start(), calls=%async_computation.11 | async-start | bytes 10616832 | tf_op jit(solution)/shard_map/reduce_scatter | solution.py:950
  971.2 61.0 %collective-permute-start.28 = (bf16[1280,384]{1,0:T(8,128)(2,1)}, bf16[1280,384]{1,0:T(8,128)(2,1)S(1)}, u32[]{:S(2)}, u32[]{:S(2)}) collective-permute-start(bf16[1280,384]{1,0:T(8,128)(2,1)} %get-tuple-element.90), channel_id=1, source_target_pairs={{2,0},{3,1},{4,2},{5,3},{6,4},{7,5},{10,8},{11,9},{12,10},{13,11},... | collective-permute-start | bytes 2949128 | tf_op jit(solution)/shard_map/ppermute | solution.py:1106
  972.5 59.7 %collective-permute-start.29 = (bf16[1280,384]{1,0:T(8,128)(2,1)}, bf16[1280,384]{1,0:T(8,128)(2,1)}, u32[]{:S(2)}, u32[]{:S(2)}) collective-permute-start(bf16[1280,384]{1,0:T(8,128)(2,1)} %get-tuple-element.91), channel_id=1, source_target_pairs={{0,2},{1,3},{2,4},{3,5},{4,6},{5,7},{8,10},{9,11},{10,12},{11,13},... | collective-permute-start | bytes 2949128 | tf_op jit(solution)/shard_map/ppermute | solution.py:1106
  986.9 70.4 %all-to-all-start.7 = ((bf16[8,320,192]{1,2,0:T(8,128)(2,1)}), bf16[8,320,192]{1,2,0:T(8,128)(2,1)S(1)}, u32[]{:S(2)}, u32[]{:S(2)}) async-start(bf16[8,320,192]{1,2,0:T(8,128)(2,1)} %copy.112), calls=%async_computation.7 | async-start | bytes 2359296 | tf_op jit(solution)/shard_map/all_to_all | solution.py:1088
  1058.3 80.5 %all-to-all-start.6 = ((bf16[8,320,384]{2,1,0:T(8,128)(2,1)}), bf16[8,320,384]{2,1,0:T(8,128)(2,1)S(1)}, u32[]{:S(2)}, u32[]{:S(2)}) async-start(bf16[8,320,384]{2,1,0:T(8,128)(2,1)} %bitcast.86), calls=%async_computation.6 | async-start | bytes 3932160 | tf_op jit(solution)/shard_map/all_to_all | solution.py:1088
  1166.5 7.1 collective-permute-start.34
  1172.8 30.5 %collective-permute-start.31 = (bf16[320,1536]{1,0:T(8,128)(2,1)}, bf16[320,1536]{1,0:T(8,128)(2,1)}, u32[]{:S(2)}, u32[]{:S(2)}) collective-permute-start(bf16[320,1536]{1,0:T(8,128)(2,1)} %get-tuple-element.173), channel_id=1, source_target_pairs={{0,8},{8,0},{16,24},{24,16},{1,9},{9,1},{17,25},{25,17},{2,10},{10... | collective-permute-start | bytes 2949128 | tf_op jit(solution)/shard_map/ppermute | solution.py:760
  1172.8 33.0 %collective-permute-start.33 = (bf16[320,1536]{1,0:T(8,128)(2,1)}, bf16[320,1536]{1,0:T(8,128)(2,1)S(1)}, u32[]{:S(2)}, u32[]{:S(2)}) collective-permute-start(bf16[320,1536]{1,0:T(8,128)(2,1)} %get-tuple-element.170), channel_id=1, source_target_pairs={{0,8},{8,0},{16,24},{24,16},{1,9},{9,1},{17,25},{25,17},{2,10},{10... | collective-permute-start | bytes 2949128 | tf_op jit(solution)/shard_map/ppermute | solution.py:760
  1175.9 29.8 %collective-permute-start.35 = (bf16[320,1536]{1,0:T(8,128)(2,1)}, bf16[320,1536]{1,0:T(8,128)(2,1)S(1)}, u32[]{:S(2)}, u32[]{:S(2)}) collective-permute-start(bf16[320,1536]{1,0:T(8,128)(2,1)} %add_convert_fusion), channel_id=1, source_target_pairs={{0,16},{8,24},{16,0},{24,8},{1,17},{9,25},{17,1},{25,9},{2,18},{10... | collective-permute-start | bytes 2949128 | tf_op jit(solution)/shard_map/ppermute | solution.py:760
  1179.8 68.7 %collective-permute-start.39 = (bf16[2,192,384]{2,1,0:T(8,128)(2,1)}, bf16[2,192,384]{2,1,0:T(8,128)(2,1)}, u32[]{:S(2)}, u32[]{:S(2)}) collective-permute-start(bf16[2,192,384]{2,1,0:T(8,128)(2,1)} %bitcast.34), channel_id=1, source_target_pairs={{0,0},{1,1},{2,8},{3,9},{4,16},{5,17},{6,24},{7,25},{8,2},{9,3},{1... | collective-permute-start | bytes 884744 | tf_op jit(solution)/shard_map/ppermute | solution.py:789
  1182.2 36.7 %collective-permute-start.30 = (bf16[320,1536]{1,0:T(8,128)(2,1)}, bf16[320,1536]{1,0:T(8,128)(2,1)}, u32[]{:S(2)}, u32[]{:S(2)}) collective-permute-start(bf16[320,1536]{1,0:T(8,128)(2,1)} %get-tuple-element.172), channel_id=1, source_target_pairs={{0,8},{8,0},{16,24},{24,16},{1,9},{9,1},{17,25},{25,17},{2,10},{10... | collective-permute-start | bytes 2949128 | tf_op jit(solution)/shard_map/ppermute | solution.py:760
  1204.8 23.4 %collective-permute-start.32 = (bf16[320,1536]{1,0:T(8,128)(2,1)S(1)}, bf16[320,1536]{1,0:T(8,128)(2,1)S(1)}, u32[]{:S(2)}, u32[]{:S(2)}) collective-permute-start(bf16[320,1536]{1,0:T(8,128)(2,1)S(1)} %add_convert_fusion.2), channel_id=1, source_target_pairs={{0,16},{8,24},{16,0},{24,8},{1,17},{9,25},{17,1},{25,9},{2,18},{10... | collective-permute-start | bytes 2949128 | tf_op jit(solution)/shard_map/ppermute | solution.py:760
  1240.4 156.3 %all-to-all-start.8 = ((f32[32,4,2432]{2,1,0:T(4,128)}), f32[32,4,2432]{2,1,0:T(4,128)S(1)}, u32[]{:S(2)}, u32[]{:S(2)}) async-start(f32[32,4,2432]{2,1,0:T(4,128)} %bitcast.31), calls=%async_computation.10 | async-start | bytes 2490368 | tf_op jit(solution)/shard_map/all_to_all | solution.py:1235
  1244.8 146.6 %collective-permute-start.40 = (bf16[2,768,384]{2,1,0:T(8,128)(2,1)}, bf16[2,768,384]{2,1,0:T(8,128)(2,1)S(1)}, u32[]{:S(2)}, u32[]{:S(2)}) collective-permute-start(bf16[2,768,384]{2,1,0:T(8,128)(2,1)} %reduce-scatter.5.cloned.1.call-done), channel_id=1, source_target_pairs={{0,0},{1,1},{2,8},{3,9},{4,16},{5,17},{6,24},{7,25},{8,2},{9,3},{1... | collective-permute-start | bytes 3538952 | tf_op jit(solution)/shard_map/ppermute | solution.py:789
  1248.5 137.8 %copy-start.65 = (bf16[2,192,1536]{2,1,0:T(8,128)(2,1)S(1)}, bf16[2,192,1536]{2,1,0:T(8,128)(2,1)}, u32[]{:S(2)}) copy-start(bf16[2,192,1536]{2,1,0:T(8,128)(2,1)} %reduce-scatter.3.cloned.1.call-done) | copy-start | bytes 3538948
  1254.2 132.1 %copy-start.47 = (f32[2,192,1536]{2,1,0:T(8,128)S(1)}, f32[2,192,1536]{2,1,0:T(8,128)}, u32[]{:S(2)}) copy-start(f32[2,192,1536]{2,1,0:T(8,128)} %param.37) | copy-start | bytes 7077892
  1254.2 132.1 %copy-start.59 = (f32[2,192,1536]{2,1,0:T(8,128)S(1)}, f32[2,192,1536]{2,1,0:T(8,128)}, u32[]{:S(2)}) copy-start(f32[2,192,1536]{2,1,0:T(8,128)} %param.38) | copy-start | bytes 7077892
  1254.2 132.1 %copy-start.60 = (f32[2,192,1536]{2,1,0:T(8,128)S(1)}, f32[2,192,1536]{2,1,0:T(8,128)}, u32[]{:S(2)}) copy-start(f32[2,192,1536]{2,1,0:T(8,128)} %param.39) | copy-start | bytes 7077892
  1397.6 22.9 %collective-permute-start.36 = (bf16[2,192,384]{2,1,0:T(8,128)(2,1)}, bf16[2,192,384]{2,1,0:T(8,128)(2,1)S(1)}, u32[]{:S(2)}, u32[]{:S(2)}) collective-permute-start(bf16[2,192,384]{2,1,0:T(8,128)(2,1)} %get-tuple-element.184), channel_id=1, source_target_pairs={{0,0},{8,24},{16,16},{24,8},{1,1},{9,25},{17,17},{25,9},{2,2},{10,... | collective-permute-start | bytes 884744 | tf_op jit(solution)/shard_map/ppermute | solution.py:760
  1399.5 21.0 %collective-permute-start.37 = (bf16[2,192,384]{2,1,0:T(8,128)(2,1)S(1)}, bf16[2,192,384]{2,1,0:T(8,128)(2,1)S(1)}, u32[]{:S(2)}, u32[]{:S(2)}) collective-permute-start(bf16[2,192,384]{2,1,0:T(8,128)(2,1)S(1)} %get-tuple-element.185), channel_id=1, source_target_pairs={{0,8},{8,0},{16,24},{24,16},{1,9},{9,1},{17,25},{25,17},{2,10},{10... | collective-permute-start | bytes 884744 | tf_op jit(solution)/shard_map/ppermute | solution.py:760
  1401.2 19.3 %collective-permute-start.38 = (bf16[2,192,384]{2,1,0:T(8,128)(2,1)S(1)}, bf16[2,192,384]{2,1,0:T(8,128)(2,1)S(1)}, u32[]{:S(2)}, u32[]{:S(2)}) collective-permute-start(bf16[2,192,384]{2,1,0:T(8,128)(2,1)S(1)} %get-tuple-element.186), channel_id=1, source_target_pairs={{0,16},{8,8},{16,0},{24,24},{1,17},{9,9},{17,1},{25,25},{2,18},{10... | collective-permute-start | bytes 884744 | tf_op jit(solution)/shard_map/ppermute | solution.py:760
  (87 other events, 838.5 us)
Sparse Core Ops, SparseCore 0:
  18.3 145.3 all-gather.6
  372.8 91.2 all-gather.8
  466.2 151.2 all-gather.10
  702.6 184.8 reduce-scatter.4
  890.9 256.4 reduce-scatter.2

commit v3 on v2

--- a/solution.py
+++ b/solution.py
@@ -665,7 +665,8 @@
     )(*operands)
 
 
-def gradient_kernel(blocks, spots, x_ref, dy_ref, image_ref, out, turned_x, masked, acc):
+def gradient_kernel(blocks, spots, x_ref, dy_ref, image_ref, *rest):
+    *outs, turned_x, masked, acc = rest
     count, width = dy_ref.shape
     size = count // blocks
     cols_at_once = acc.shape[1]
@@ -682,6 +683,8 @@
 
     def store(stream, n, values):
         values = values.astype(bf16)
+        out = outs[min(stream, len(outs) - 1)]
+        stream = stream if len(outs) == 1 else 0
         if len(out.shape) == 5:
             tile, per = out.shape[4], out.shape[3]
             for t in range(cols_at_once // tile):
@@ -710,7 +713,7 @@
         store(1, n, acc[...])
 
 
-def gradient(spots, x, dy, image, shape):
+def gradient(spots, x, dy, image, shape, split=False):
     blocks = (spots.shape[0] - 1) // 2
     count, depth = x.shape
     width = dy.shape[1]
@@ -718,7 +721,8 @@
     cols = 1152 if width % 768 else 768
     if len(shape) == 4:
         per = step // shape[2]
-        out_spec = pl.BlockSpec((per, 2, shape[2], width), lambda j, s: (j, 0, 0, 0))
+        streams = 1 if split else 2
+        out_spec = pl.BlockSpec((per, streams, shape[2], width), lambda j, s: (j, 0, 0, 0))
     else:
         tiles, q, _, rows, tile = shape
         if rows < step:
@@ -729,6 +733,7 @@
             out_spec = pl.BlockSpec(
                 (tiles, 1, 2, step, tile), lambda j, s: (0, j // per, 0, j % per, 0)
             )
+    half = jax.ShapeDtypeStruct((shape[0], 1, *shape[2:]), bf16)
     return pl.pallas_call(
         functools.partial(gradient_kernel, blocks),
         grid_spec=pltpu.PrefetchScalarGridSpec(
@@ -739,14 +744,14 @@
                 resident(dy.shape),
                 resident(image.shape),
             ],
-            out_specs=out_spec,
+            out_specs=[out_spec, out_spec] if split else out_spec,
             scratch_shapes=[
                 pltpu.VMEM((step, count), bf16),
                 pltpu.VMEM((count, width), bf16),
                 pltpu.VMEM((step, cols), f32),
             ],
         ),
-        out_shape=jax.ShapeDtypeStruct(shape, bf16),
+        out_shape=[half, half] if split else jax.ShapeDtypeStruct(shape, bf16),
         compiler_params=pltpu.CompilerParams(vmem_limit_bytes=48 << 20),
         cost_estimate=pl.CostEstimate(
             flops=count * depth // 4 * width, bytes_accessed=4 << 20, transcendentals=0
@@ -871,15 +876,21 @@
             pltpu.SemaphoreType.DMA((count,)),
         ],
         compiler_params=pltpu.CompilerParams(collective_id=0, has_side_effects=True),
-        cost_estimate=pl.CostEstimate(flops=1 << 20, bytes_accessed=8 << 20, transcendentals=0),
+        cost_estimate=pl.CostEstimate(flops=1 << 20, bytes_accessed=256 << 20, transcendentals=0),
         name="ring_gather",
     )(*blocks)
 
 
-def ring_scatter_kernel(terms, out, held, send_sem, recv_sem):
-    shards, _, rows, _ = terms.shape
-    pieces = held.shape[1]
-    part = rows // pieces
+def as_turned(full):
+    reps = lax.axis_size("rep")
+    return full.reshape(reps, full.shape[0] // reps, *full.shape[1:])
+
+
+def ring_scatter_kernel(count, *refs):
+    sources, outs, helds = refs[:count], refs[count : 2 * count], refs[2 * count : 3 * count]
+    send_sem, recv_sem = refs[3 * count :]
+    shards = sources[0].shape[0]
+    pieces = helds[0].shape[1]
     place = ring_place(shards)
     mine = ring_owner(place, shards)
     peers = [ring_owner(place + 1, shards), ring_owner(place - 1, shards)]
@@ -891,64 +902,69 @@
         )
     pl.semaphore_wait(barrier, 2)
 
-    chains = [(way, piece) for piece in range(pieces) for way in range(2)]
+    chains = [
+        (w, way, piece) for piece in range(pieces) for w in range(count) for way in range(2)
+    ]
     copies = {}
     for step in range(shards):
-        for way, piece in chains:
+        for chain in chains:
+            w, way, piece = chain
+            part = sources[w].shape[2] // pieces
             span = slice(piece * part, (piece + 1) * part)
             if step < shards - 1:
                 owner = ring_owner(place - 1 - step if way == 0 else place + 1 + step, shards)
             else:
                 owner = mine
-            source = terms.at[owner, way, span]
+            source = sources[w].at[owner, way, span]
             if step:
-                copies[way, piece, step - 1].wait_recv()
-                arrived = held.at[way, piece, step - 1]
+                copies[chain, step - 1].wait_recv()
+                arrived = helds[w].at[way, piece, step - 1]
                 total = arrived[...].astype(f32) + source[...].astype(f32)
                 if step == shards - 1:
-                    out[way, span] = total.astype(bf16)
+                    outs[w][way, span] = total.astype(bf16)
                     continue
                 arrived[...] = total.astype(bf16)
                 source = arrived
-            copies[way, piece, step] = pltpu.make_async_remote_copy(
+            copies[chain, step] = pltpu.make_async_remote_copy(
                 src_ref=source,
-                dst_ref=held.at[way, piece, step],
-                send_sem=send_sem.at[way, piece, step],
-                recv_sem=recv_sem.at[way, piece, step],
+                dst_ref=helds[w].at[way, piece, step],
+                send_sem=send_sem.at[w, way, piece, step],
+                recv_sem=recv_sem.at[w, way, piece, step],
                 device_id={"shard": peers[way]},
                 device_id_type=pl.DeviceIdType.MESH,
             )
-            copies[way, piece, step].start()
+            copies[chain, step].start()
     for copy in copies.values():
         copy.wait_send()
 
 
-def ring_scatter(terms):
-    shards, _, rows, width = terms.shape
+def ring_scatter(*terms):
+    shards, _, rows, _ = terms[0].shape
+    count = len(terms)
     pieces = 2 if rows % 32 == 0 else 1
-    sems = pltpu.SemaphoreType.DMA((2, pieces, shards - 1))
+    sems = pltpu.SemaphoreType.DMA((count, 2, pieces, shards - 1))
+    whole = pl.BlockSpec(memory_space=pltpu.VMEM)
     return pl.pallas_call(
-        ring_scatter_kernel,
-        in_specs=[pl.BlockSpec(memory_space=pltpu.VMEM)],
-        out_specs=pl.BlockSpec(memory_space=pltpu.VMEM),
-        out_shape=jax.ShapeDtypeStruct((2, rows, width), bf16),
+        functools.partial(ring_scatter_kernel, count),
+        in_specs=[whole] * count,
+        out_specs=[whole] * count,
+        out_shape=[jax.ShapeDtypeStruct(t.shape[1:], bf16) for t in terms],
         scratch_shapes=[
-            pltpu.VMEM((2, pieces, shards - 1, rows // pieces, width), bf16),
-            sems,
-            sems,
-        ],
+            pltpu.VMEM((2, pieces, shards - 1, t.shape[2] // pieces, t.shape[3]), bf16)
+            for t in terms
+        ]
+        + [sems, sems],
         compiler_params=pltpu.CompilerParams(
-            collective_id=1, has_side_effects=True, vmem_limit_bytes=32 << 20
+            collective_id=1, has_side_effects=True, vmem_limit_bytes=36 << 20
         ),
         cost_estimate=pl.CostEstimate(flops=1 << 20, bytes_accessed=256 << 20, transcendentals=0),
         name="ring_scatter",
-    )(terms)
+    )(*terms)
 
 
 def scatter_weight(terms):
-    blocks = terms.reshape(lax.axis_size("shard"), -1, *terms.shape[-3:])
     return lax.psum_scatter(
-        blocks.reshape(-1, *terms.shape[-2:]), "shard", scatter_dimension=0, tiled=True
+        terms.reshape(-1, *terms.shape[-2:]), "shard", scatter_dimension=0, tiled=True
     ).reshape(terms.shape[-3:])
 
 
@@ -1069,15 +1085,18 @@
     d_down = (gate_two * back_out).astype(bf16)
     d_down_group = jnp.concatenate(gather_rep(d_down))
 
-    fc1_low, act_one_group = lax.optimization_barrier((w_fc1.astype(bf16), act_one_group))
-    (fc1_weights,) = ring_gather(fc1_low)
-    act_one_group, fc1_weights = lax.optimization_barrier((act_one_group, fc1_weights))
+    out_turned, fc1_low, act_one_group = lax.optimization_barrier(
+        (turn(w_out.astype(bf16)), w_fc1.astype(bf16), act_one_group)
+    )
+    out_full, fc1_weights = ring_gather(out_turned, fc1_low)
+    out_weights = as_turned(out_full)
+    fc2_low, act_one = lax.optimization_barrier((w_fc2.astype(bf16), act_one))
+    fc2_turned = turn(fc2_low)
+    act_one_group, fc1_weights, d_down_group, fc2_turned = lax.optimization_barrier(
+        (act_one_group, fc1_weights, d_down_group, fc2_turned)
+    )
 
     query_sent, pair_sent, qk_pre = qkv_product(spots, act_one_group, qkv_weights, image, gains)
-    out_low, fc2_low, pair_sent = lax.optimization_barrier(
-        (w_out.astype(bf16), w_fc2.astype(bf16), pair_sent)
-    )
-    out_turned, fc2_turned = turn(out_low), turn(fc2_low)
 
     bunch = 2 * reps
     bunches = shards // bunch
@@ -1106,15 +1125,14 @@
         return lax.ppermute(value, "shard", pairs)
 
     pair_own = exchange(pair_sent).reshape(stretch_rows, 2 * half_width)
-    query_sent, pair_own = lax.optimization_barrier((query_sent, pair_own))
-    query_own = exchange(query_sent).reshape(stretch_rows, half_width)
-    out_turned, fc2_turned, query_own = lax.optimization_barrier(
-        (out_turned, fc2_turned, query_own)
-    )
-    out_weights = gather_turned(out_turned)
-    fc2_weights = gather_turned(fc2_turned)
     pair_before = stretch_shift(pair_own[-halo:], 1)
     pair_after = stretch_shift(pair_own[:halo], -1)
+    query_sent, pair_before, pair_after = lax.optimization_barrier(
+        (query_sent, pair_before, pair_after)
+    )
+    query_own = exchange(query_sent).reshape(stretch_rows, half_width)
+    fc2_turned, query_own = lax.optimization_barrier((fc2_turned, query_own))
+    fc2_weights = as_turned(gather_weight(fc2_turned))
     window_rows = stretch_rows + 2 * halo
     stretch = ((shard_index % bunch) // 2) * bunches + shard_index // bunch
     stretch_first = stretch * stretch_rows
@@ -1157,17 +1175,17 @@
     )
     d_mid = back_out + d_mid_norm
     d_branch = (gate_one * d_mid).astype(bf16)
-    fc1_terms = gradient(spots, act_two_group, d_up, image, fc1_weights.shape)
-    fc1_terms, d_branch = lax.optimization_barrier((fc1_terms, d_branch))
-    g_fc1 = scatter_weight(fc1_terms)
+    fc1_image, fc1_text = gradient(
+        spots, act_two_group, d_up, image, fc1_weights.shape, split=True
+    )
+    fc1_image, fc1_text, d_branch = lax.optimization_barrier((fc1_image, fc1_text, d_branch))
+    fc1_image = scatter_weight(fc1_image)
     d_gate_one = d_mid * branch
     d_branch_group = jnp.concatenate(gather_rep(d_branch))
     d_attended = backward_product(spots, d_branch_group, out_weights, image, packs=True)
     out_terms = gradient(spots, attended_low, d_branch_group, image, out_weights.shape)
-    out_came = lax.all_to_all(
-        out_terms.reshape(shards, -1, out_terms.shape[-1]), "shard", 0, 0, tiled=True
-    )
     d_attended_own = exchange(d_attended).reshape(stretch_rows, half_width)
+    d_attended_own, out_terms = lax.optimization_barrier((d_attended_own, out_terms))
     d_query_own, d_before, d_after, d_pair_own = attention_back(
         query_own,
         pair_own,
@@ -1190,10 +1208,12 @@
         + jnp.concatenate([rest, from_later], axis=0)
         + jnp.concatenate([from_earlier, rest], axis=0)
     )
-    d_pair_own, out_came = lax.optimization_barrier((d_pair_own, out_came))
-    g_out = turn(jnp.sum(out_came.astype(f32), axis=0).astype(bf16).reshape(w_out.shape))
     d_pair_came = exchange(d_pair_own.astype(bf16).reshape(bunch, tok_rows, 2 * half_width))
-    d_pair_came, down_terms = lax.optimization_barrier((d_pair_came, down_terms))
+    up_fc2 = adam_step(w_fc2, m_fc2, v_fc2, turn(fc2_own).astype(f32), rate_fc2)
+    d_pair_came, down_terms, fc1_text, up_fc2 = lax.optimization_barrier(
+        (d_pair_came, down_terms, fc1_text, up_fc2)
+    )
+    fc1_text = scatter_weight(fc1_text)
     down_proj = reduce_rep(split_group(down_terms))
     output = mid + gate_two * down_proj
     d_gate_two = back_out * down_proj
@@ -1228,16 +1248,18 @@
             for r in range(reps)
         ]
     )
-    qkv_terms, g_fc1, fc2_own, leaving = lax.optimization_barrier(
-        (qkv_terms, g_fc1, fc2_own, leaving)
+    qkv_terms, out_terms, fc1_image, leaving = lax.optimization_barrier(
+        (qkv_terms, out_terms, fc1_image, leaving)
     )
     leaving = jnp.broadcast_to(leaving[:, None], (reps, shards, *leaving.shape[1:]))
     came = lax.all_to_all(
         leaving.reshape(device_count, *leaving.shape[2:]), ("rep", "shard"), 0, 0, tiled=True
     )
-    g_fc2 = turn(fc2_own)
-    g_qkv_group = ring_scatter(qkv_terms)
-    g_qkv_group, came = lax.optimization_barrier((g_qkv_group, came))
+    out_terms = out_terms.reshape(shards, 2, -1, out_terms.shape[-1])
+    g_qkv_group, g_out = ring_scatter(qkv_terms, out_terms)
+    g_qkv_group, g_out, came = lax.optimization_barrier((g_qkv_group, g_out, came))
+    g_out = turn(g_out)
+    g_fc1 = jnp.concatenate([fc1_image, fc1_text], axis=0)
     g_parts = [
         g_qkv_group[:, :, t * part_width : (t + 1) * part_width] for t in range(3)
     ]
@@ -1267,7 +1289,6 @@
     up_qkv = adam_step(w_qkv, m_qkv, v_qkv, g_qkv.astype(f32), rate_qkv)
     up_out = adam_step(w_out, m_out, v_out, g_out.astype(f32), rate_out)
     up_fc1 = adam_step(w_fc1, m_fc1, v_fc1, g_fc1.astype(f32), rate_fc1)
-    up_fc2 = adam_step(w_fc2, m_fc2, v_fc2, g_fc2.astype(f32), rate_fc2)
     up_gains = adam_step(gains, m_gains, v_gains, g_gains, rate_gains)
     return (
         output.astype(bf16),

time: 1420 us -> 1420 us (level); the launches traced: 1430 us -> 1410 us
  waiting for transfers between devices: 437 us -> 294 us
  starting transfers between devices: 103 us -> 149 us
  Pallas kernels: 590 us -> 626 us
  blocking collectives: 113 us -> 144 us
    all_to_all x4 -> x3, waiting for transfers between devices: 168 us -> 78.8 us  [exchange(): lax.all_to_all(value, 'shard', 0, 0, axis_index_groups=None if bunches ==...]
    ppermute x4, waiting for transfers between devices: 114 us -> 43.7 us  [stretch_shift(): return lax.ppermute(value, 'shard', pairs)]
    pallas_call x1, Pallas kernels: 121 us -> 176 us  [ring_gather(): pl.pallas_call(functools.partial(ring_kernel, shards, count), in_specs=[a...]
    ppermute x33, starting transfers between devices: 37.9 us -> 79.4 us  [over_rep(): return lax.ppermute(value, 'rep', [(r, target(r)) for r in range(count)])]
    all_to_all x2 -> x3, blocking collectives: 113 us -> 144 us  [exchange(): lax.all_to_all(value, 'shard', 0, 0, axis_index_groups=None if bunches ==...]
    ppermute x4, waiting for transfers between devices: 0.01 us -> 16.9 us  [turn(): return lax.ppermute(value, ('rep', 'shard'), pairs)]
    unnamed x200 -> x184, local copies, waits for them, and re-layouts: 30.1 us -> 38.1 us
  transfers between devices with their start and end apart: 53 -> 51, of which waited for: 21 -> 22; matrix products, arithmetic and copies ran while one was open for 9% -> 9% of each run, Pallas kernels for 40% -> 43%
where the time goes in v3:
time: 1420 us; the launch traced here: 1410 us
  Pallas kernels  626 us (44%)
  waiting for transfers between devices  294 us (21%)
  starting transfers between devices  149 us (10%)
  blocking collectives  144 us (10%)
  other arithmetic  90.4 us (6%)
  local copies, waits for them, and re-layouts  74.1 us (5%)
  between operations  16 us (1%)
    pallas_call x1, Pallas kernels, ring_gather(): pl.pallas_call(functools.partial(ring_kernel, shards, count), in_specs=[a...  176 us
    all_to_all x3, blocking collectives, exchange(): lax.all_to_all(value, 'shard', 0, 0, axis_index_groups=None if bunches ==...  144 us
    pallas_call x1, Pallas kernels, ring_scatter(): pl.pallas_call(functools.partial(ring_scatter_kernel, count), in_specs=[w...  125 us
    ppermute x33, waiting for transfers between devices, over_rep(): return lax.ppermute(value, 'rep', [(r, target(r)) for r in range(count)])  124 us
    pallas_call x1, Pallas kernels, attention_back(): pl.pallas_call(attend_back_kernel, grid_spec=pltpu.PrefetchScalarGridSpec...  91 us
    ppermute x33, starting transfers between devices, over_rep(): return lax.ppermute(value, 'rep', [(r, target(r)) for r in range(count)])  79.4 us
    all_to_all x3, waiting for transfers between devices, exchange(): lax.all_to_all(value, 'shard', 0, 0, axis_index_groups=None if bunches ==...  78.8 us
    pallas_call x4, Pallas kernels, gradient(): pl.pallas_call(functools.partial(gradient_kernel, blocks), grid_spec=pltp...  63.2 us
  transfers between devices with their start and end apart: 51, of which 22 were waited for; matrix products, arithmetic and copies ran while one was open for 9% of the time, Pallas kernels for 43%

profile of v3, /device:TPU:1, one launch (start us, length us, event | category | flops | bytes accessed | tf_op | source)
XLA Modules:
  0.0 1406.8 jit_solution(17862737935116516040)
XLA Ops:
  9.8 4.0 collective-permute-start.11
  13.8 3.8 collective-permute-start.13
  27.2 11.1 all-to-all-start
  40.3 31.0 %all-to-all-done = bf16[32,4,2304]{2,1,0:T(4,128)(2,1)S(1)} async-done(((bf16[32,4,2304]{2,1,0:T(4,128)(2,1)}), bf16[32,4,2304]{2,1,0:T(4,128)(2,1)S(1)}, u32[]{:S(2)}, u32[]{:S(2)}) %all-to-all-start) | async-done | bytes 589856 | tf_op jit(solution)/shard_map/all_to_all | solution.py:1041
  72.0 2.8 fusion.20
  79.4 24.5 %collective-permute-done.1 = s32[320]{0:T(512)S(1)} collective-permute-done((s32[320]{0:T(512)S(1)}, s32[320]{0:T(512)S(1)}, u32[]{:S(2)}, u32[]{:S(2)}) %collective-permute-start.1) | collective-permute-done | bytes 1312 | tf_op jit(solution)/shard_map/ppermute | solution.py:765
  113.0 15.2 %collective-permute-done.8 = bf16[320,1536]{1,0:T(8,128)(2,1)} collective-permute-done((bf16[320,1536]{1,0:T(8,128)(2,1)}, bf16[320,1536]{1,0:T(8,128)(2,1)}, u32[]{:S(2)}, u32[]{:S(2)}) %collective-permute-start.8) | collective-permute-done | bytes 983072 | tf_op jit(solution)/shard_map/ppermute | solution.py:765
  131.4 3.5 pad_maximum_fusion.x_ref
  134.9 176.5 %ring_gather.1 = (bf16[8,2,192,384]{3,2,1,0:T(8,128)(2,1)}, bf16[8,2,192,1536]{3,2,1,0:T(8,128)(2,1)}) custom-call(bf16[2,192,384]{2,1,0:T(8,128)(2,1)} %collective-permute-done.3.refs_0_, bf16[2,192,1536]{2,1,0:T(8,128)(2,1)} %convert_element_type.204.refs_1_), custom_call_target="tpu_custom_call" | custom-call | flops 1048576 | bytes 268435456 | tf_op jit(solution)/shard_map/ring_gather/pallas_call | solution.py:868
  311.4 3.4 pad_maximum_fusion.1.dy_ref
  317.4 18.9 %qkv_product.1 = (bf16[8,320,192]{2,1,0:T(8,128)(2,1)S(1)}, bf16[8,320,384]{2,1,0:T(8,128)(2,1)S(1)}, f32[1280,768]{1,0:T(8,128)S(1)}) custom-call(s32[9]{0:T(128)S(1)} %pad_add_fusion.1.spots, bf16[1280,1536]{1,0:T(8,128)(2,1)S(1)} %copy-done.1, bf16[8,2,192,1152]{3,2,1,0:T(8,128)(2,1)} %bitcast.82, bf16[8,2,192,1152]{3,2,1,0:T(8,128)(2,1)} %bitcast.83, ...), custom_call_target="tpu_custom_call" | custom-call | flops 1073741824 | bytes 4194304 | tf_op jit(solution)/shard_map/qkv_product/pallas_call | solution.py:380
  338.2 51.5 %all_to_all.40 = bf16[8,320,384]{2,1,0:T(8,128)(2,1)S(1)} all-to-all(bf16[8,320,384]{2,1,0:T(8,128)(2,1)S(1)} %get-tuple-element.90), channel_id=1, replica_groups=mesh['rep'=4,'shard'=8] {'shard'}, dimensions={0} | all-to-all | bytes 3932160 | tf_op jit(solution)/shard_map/all_to_all | solution.py:1107
  389.9 3.2 collective-permute-start.14
  394.9 17.6 %collective-permute-done.14.before_ref = bf16[1280,384]{1,0:T(8,128)(2,1)S(1)} collective-permute-done((bf16[1280,384]{1,0:T(8,128)(2,1)S(1)}, bf16[1280,384]{1,0:T(8,128)(2,1)S(1)}, u32[]{:S(2)}, u32[]{:S(2)}) %collective-permute-start.14) | collective-permute-done | bytes 983072 | tf_op jit(solution)/shard_map/ppermute | solution.py:1125
  413.5 3.0 collective-permute-done.15.after_ref
  419.8 31.3 %all_to_all.41 = bf16[8,320,192]{1,2,0:T(8,128)(2,1)} all-to-all(bf16[8,320,192]{1,2,0:T(8,128)(2,1)} %copy.104), channel_id=1, replica_groups=mesh['rep'=4,'shard'=8] {'shard'}, dimensions={0} | all-to-all | bytes 1966080 | tf_op jit(solution)/shard_map/all_to_all | solution.py:1107
  459.3 46.3 %attend.1 = (bf16[2560,192]{1,0:T(8,128)(2,1)S(1)}, f32[10,8,256]{2,1,0:T(8,128)S(1)}) custom-call(s32[10]{0:T(128)S(1)} %fusion.63.lo_ref, s32[10]{0:T(128)S(1)} %fusion.62.hi_ref, bf16[2560,192]{1,0:T(8,128)(2,1)S(1)} %bitcast.75, bf16[2560,384]{1,0:T(8,128)(2,1)S(1)} %bitcast.71, bf16[1280,384]{1,0:T(8,128)(2,1)S(1)} %copy-done.25, ...), custom_call_target="tpu_custom_call" | custom-call | flops 1073741824 | bytes 4194304 | tf_op jit(solution)/shard_map/attend/pallas_call | solution.py:197
  509.8 61.0 %all_to_all.42 = bf16[8,320,192]{1,2,0:T(8,128)(2,1)} all-to-all(bf16[8,320,192]{1,2,0:T(8,128)(2,1)} %copy.107), channel_id=1, replica_groups=mesh['rep'=4,'shard'=8] {'shard'}, dimensions={0} | all-to-all | bytes 1966080 | tf_op jit(solution)/shard_map/all_to_all | solution.py:1107
  574.6 7.2 forward_product.3
  582.9 6.8 collective-permute-start.17
  593.3 21.9 %collective-permute-done.18 = bf16[320,1536]{1,0:T(8,128)(2,1)S(1)} collective-permute-done((bf16[320,1536]{1,0:T(8,128)(2,1)S(1)}, bf16[320,1536]{1,0:T(8,128)(2,1)S(1)}, u32[]{:S(2)}, u32[]{:S(2)}) %collective-permute-start.18) | collective-permute-done | bytes 983072 | tf_op jit(solution)/shard_map/ppermute | solution.py:765
  616.5 3.4 add_convert_fusion.5
  622.4 19.7 %collective-permute-done.20 = bf16[320,1536]{1,0:T(8,128)(2,1)S(1)} collective-permute-done((bf16[320,1536]{1,0:T(8,128)(2,1)S(1)}, bf16[320,1536]{1,0:T(8,128)(2,1)S(1)}, u32[]{:S(2)}, u32[]{:S(2)}) %collective-permute-start.20) | collective-permute-done | bytes 983072 | tf_op jit(solution)/shard_map/ppermute | solution.py:765
  646.7 19.1 %forward_product.4 = (bf16[1280,1536]{1,0:T(8,128)(2,1)S(1)}, bf16[1280,1536]{1,0:T(8,128)(2,1)S(1)}) custom-call(s32[9]{0:T(128)S(1)} %pad_add_fusion.1.spots, bf16[1280,1536]{1,0:T(8,128)(2,1)S(1)} %pad_maximum_fusion.2.x_ref, bf16[8,2,192,1536]{3,2,1,0:T(8,128)(2,1)} %get-tuple-element.100.w0.w1, bf16[8,2,192,1536]{3,2,1,0:T(8,128)(2,1)} %get-tuple-element.100.w0.w1, ...), custom_call_target="tpu_custom_call" | custom-call | flops 754974720 | bytes 4194304 | tf_op jit(solution)/shard_map/forward_product/pallas_call | solution.py:540
  667.8 20.9 %gradient.4 = bf16[4,2,2,768,384]{4,3,2,1,0:T(8,128)(2,1)} custom-call(s32[9]{0:T(128)S(1)} %pad_add_fusion.1.spots, bf16[1280,1536]{1,0:T(8,128)(2,1)S(1)} %get-tuple-element.101.x_ref, bf16[1280,1536]{1,0:T(8,128)(2,1)} %pad_maximum_fusion.1.dy_ref, s32[1280,1]{1,0:T(8,128)S(1)} %convert_element_type.213.image_ref), custom_call_target="tpu_custom_call" | custom-call | flops 754974720 | bytes 4194304 | tf_op jit(solution)/shard_map/gradient/pallas_call | solution.py:737
  688.8 18.1 %backward_product.4.dy_ref = bf16[1280,1536]{1,0:T(8,128)(2,1)S(1)} custom-call(s32[9]{0:T(128)S(1)} %pad_add_fusion.1.spots, bf16[1280,1536]{1,0:T(8,128)(2,1)} %pad_maximum_fusion.1.dy_ref, bf16[4,2,2,768,384]{4,3,2,1,0:T(8,128)(2,1)} %bitcast.78, bf16[4,2,2,768,384]{4,3,2,1,0:T(8,128)(2,1)} %bitcast.79, s32[1280,1]{1,0:T(8,128)S(1)} %convert_element_type.213.image_ref, ...), custom_call_target="tpu_custom_call" | custom-call | flops 754974720 | bytes 4194304 | tf_op jit(solution)/shard_map/backward_product/pallas_call | solution.py:651
  708.9 15.0 %backward_product.5 = bf16[1280,1536]{1,0:T(8,128)(2,1)S(1)} custom-call(s32[9]{0:T(128)S(1)} %pad_add_fusion.1.spots, bf16[1280,1536]{1,0:T(8,128)(2,1)} %copy-done.4, bf16[8,2,192,1536]{3,2,1,0:T(8,128)(2,1)} %get-tuple-element.100.w0.w1, bf16[8,2,192,1536]{3,2,1,0:T(8,128)(2,1)} %get-tuple-element.100.w0.w1, s32[1280,1]{1,0:T(8,128)S(1)} %convert_element_type.213.image_ref), custom_call_target="tpu_custom_call" | custom-call | flops 754974720 | bytes 4194304 | tf_op jit(solution)/shard_map/backward_product/pallas_call | solution.py:651
  729.0 20.2 %gradient.5 = (bf16[8,1,192,1536]{3,2,1,0:T(8,128)(2,1)}, bf16[8,1,192,1536]{3,2,1,0:T(8,128)(2,1)}) custom-call(s32[9]{0:T(128)S(1)} %pad_add_fusion.1.spots, bf16[1280,1536]{1,0:T(8,128)(2,1)S(1)} %copy-done.3, bf16[1280,1536]{1,0:T(8,128)(2,1)} %copy-done.4, s32[1280,1]{1,0:T(8,128)S(1)} %convert_element_type.213.image_ref), custom_call_target="tpu_custom_call" | custom-call | flops 754974720 | bytes 4194304 | tf_op jit(solution)/shard_map/gradient/pallas_call | solution.py:737
  758.3 19.8 %collective-permute-done.26 = bf16[320,1536]{1,0:T(8,128)(2,1)S(1)} collective-permute-done((bf16[320,1536]{1,0:T(8,128)(2,1)S(1)}, bf16[320,1536]{1,0:T(8,128)(2,1)S(1)}, u32[]{:S(2)}, u32[]{:S(2)}) %collective-permute-start.26) | collective-permute-done | bytes 983072 | tf_op jit(solution)/shard_map/ppermute | solution.py:765
  784.2 8.6 backward_product.6
  796.3 14.0 all-to-all-start.4
  815.0 7.4 gradient.6
  822.5 42.3 %all-to-all-done.4 = bf16[8,320,192]{1,2,0:T(8,128)(2,1)} async-done(((bf16[8,320,192]{1,2,0:T(8,128)(2,1)}), bf16[8,320,192]{1,2,0:T(8,128)(2,1)}, u32[]{:S(2)}, u32[]{:S(2)}) %all-to-all-start.4) | async-done | bytes 983072 | tf_op jit(solution)/shard_map/all_to_all | solution.py:1107
  867.2 91.0 %attend_back.1 = (bf16[2560,192]{1,0:T(8,128)(2,1)}, bf16[1280,384]{1,0:T(8,128)(2,1)}, bf16[1280,384]{1,0:T(8,128)(2,1)}, f32[2560,384]{1,0:T(8,128)}) custom-call(s32[10]{0:T(128)} %copy-done.32, s32[10]{0:T(128)} %copy-done.31, bf16[2560,192]{1,0:T(8,128)(2,1)} %bitcast.74, bf16[2560,384]{1,0:T(8,128)(2,1)} %bitcast.72, bf16[1280,384]{1,0:T(8,128)(2,1)} %copy-done.24, ...), custom_call_target="tpu_custom_call" | custom-call | flops 25769803776 | bytes 8388608 | tf_op jit(solution)/shard_map/attend_back/pallas_call | solution.py:237
  959.6 4.9 collective-permute-start.29
  967.0 4.3 all-to-all-start.6
  971.2 23.1 %collective-permute-done.28 = bf16[1280,384]{1,0:T(8,128)(2,1)} collective-permute-done((bf16[1280,384]{1,0:T(8,128)(2,1)}, bf16[1280,384]{1,0:T(8,128)(2,1)}, u32[]{:S(2)}, u32[]{:S(2)}) %collective-permute-start.28) | collective-permute-done | bytes 983072 | tf_op jit(solution)/shard_map/ppermute | solution.py:1125
  994.4 4.4 add_convert_fusion
  998.8 21.2 %all-to-all-done.6 = bf16[8,320,192]{1,2,0:T(8,128)(2,1)} async-done(((bf16[8,320,192]{1,2,0:T(8,128)(2,1)}), bf16[8,320,192]{1,2,0:T(8,128)(2,1)}, u32[]{:S(2)}, u32[]{:S(2)}) %all-to-all-start.6) | async-done | bytes 983072 | tf_op jit(solution)/shard_map/all_to_all | solution.py:1107
  1020.0 4.3 all-to-all-start.5
  1024.4 5.8 collective-permute-start.30
  1032.3 15.7 %forward_product.5 = bf16[1280,1536]{1,0:T(8,128)(2,1)S(1)} custom-call(s32[9]{0:T(128)S(1)} %pad_add_fusion.1.spots, bf16[1280,1536]{1,0:T(8,128)(2,1)S(1)} %copy-done.10, bf16[4,2,2,768,384]{4,3,2,1,0:T(8,128)(2,1)} %bitcast.80, bf16[4,2,2,768,384]{4,3,2,1,0:T(8,128)(2,1)} %bitcast.81, s32[1280,1]{1,0:T(8,128)S(1)} %convert_element_type.213.image_ref), custom_call_target="tpu_custom_call" | custom-call | flops 754974720 | bytes 4194304 | tf_op jit(solution)/shard_map/forward_product/pallas_call | solution.py:540
  1052.4 16.9 %collective-permute-done.30 = bf16[2,768,384]{2,1,0:T(8,128)(2,1)} collective-permute-done((bf16[2,768,384]{2,1,0:T(8,128)(2,1)}, bf16[2,768,384]{2,1,0:T(8,128)(2,1)}, u32[]{:S(2)}, u32[]{:S(2)}) %collective-permute-start.30) | collective-permute-done | bytes 1179680 | tf_op jit(solution)/shard_map/ppermute | solution.py:794
  1069.3 8.0 fusion.79
  1077.3 15.2 %all-to-all-done.5.kv_ref = bf16[8,320,384]{2,1,0:T(8,128)(2,1)} async-done(((bf16[8,320,384]{2,1,0:T(8,128)(2,1)}), bf16[8,320,384]{2,1,0:T(8,128)(2,1)}, u32[]{:S(2)}, u32[]{:S(2)}) %all-to-all-start.5) | async-done | bytes 1966112 | tf_op jit(solution)/shard_map/all_to_all | solution.py:1107
  1096.0 8.1 norm_back.1
  1104.1 13.1 backward_product.7
  1119.9 6.2 collective-permute-start.35
  1130.7 31.7 %collective-permute-start.36 = (bf16[320,1536]{1,0:T(8,128)(2,1)}, bf16[320,1536]{1,0:T(8,128)(2,1)}, u32[]{:S(2)}, u32[]{:S(2)}) collective-permute-start(bf16[320,1536]{1,0:T(8,128)(2,1)} %add_convert_fusion.1), channel_id=1, source_target_pairs={{0,16},{8,24},{16,0},{24,8},{1,17},{9,25},{17,1},{25,9},{2,18},{10... | collective-permute-start | bytes 2949128 | tf_op jit(solution)/shard_map/ppermute | solution.py:765
  1165.1 14.7 %gradient.7.refs_0_ = bf16[8,2,192,1152]{3,2,1,0:T(8,128)(2,1)} custom-call(s32[9]{0:T(128)S(1)} %pad_add_fusion.1.spots, bf16[1280,1536]{1,0:T(8,128)(2,1)} %pad_maximum_fusion.x_ref, bf16[1280,1152]{1,0:T(8,128)(2,1)S(1)} %copy-done.15, s32[1280,1]{1,0:T(8,128)S(1)} %convert_element_type.213.image_ref), custom_call_target="tpu_custom_call" | custom-call | flops 566231040 | bytes 4194304 | tf_op jit(solution)/shard_map/gradient/pallas_call | solution.py:737
  1187.2 3.2 fusion.78
  1190.5 3.8 multiply_dynamic-update-slice_fusion.1
  1196.5 9.6 collective-permute-done.33
  1206.1 3.4 fusion.21
  1209.5 4.0 fusion.51
  1214.9 6.2 all-to-all-start.7
  1222.8 3.0 copy-done.7
  1225.9 125.5 %ring_scatter.1 = (bf16[2,192,1152]{2,1,0:T(8,128)(2,1)S(1)}, bf16[2,192,384]{2,1,0:T(8,128)(2,1)S(1)}) custom-call(bf16[8,2,192,1152]{3,2,1,0:T(8,128)(2,1)S(1)} %copy-done.7, bf16[8,2,192,384]{3,2,1,0:T(8,128)(2,1)S(1)} %bitcast.73), custom_call_target="tpu_custom_call" | custom-call | flops 1048576 | bytes 268435456 | tf_op jit(solution)/shard_map/ring_scatter/pallas_call | solution.py:947
  1354.4 3.1 collective-permute-start.37
  1358.0 3.7 collective-permute-start.39
  1364.0 8.8 collective-permute-start.40
  1377.1 7.9 fusion.76
  1389.2 4.6 fusion.73
  1393.8 6.0 fusion.67
  (401 shorter events, 156.2 us)
Async XLA Ops:
  7.2 307.7 %all-gather.5.cloned.1.call-start = ((), (), s32[]{:S(2)}) async-start(), calls=%async_computation.14 | async-start | bytes 7962624 | tf_op jit(solution)/shard_map/all_gather | solution.py:798
  9.8 8.4 collective-permute-start.11
  13.7 4.4 collective-permute-start.12
  13.8 4.3 collective-permute-start.13
  27.2 44.7 %copy-start.50 = (bf16[320,1536]{1,0:T(8,128)(2,1)S(1)}, bf16[320,1536]{1,0:T(8,128)(2,1)}, u32[]{:S(2)}) copy-start(bf16[320,1536]{1,0:T(8,128)(2,1)} %param.24) | copy-start | bytes 2949124
  27.2 44.1 %all-to-all-start = ((bf16[32,4,2304]{2,1,0:T(4,128)(2,1)}), bf16[32,4,2304]{2,1,0:T(4,128)(2,1)S(1)}, u32[]{:S(2)}, u32[]{:S(2)}) async-start(bf16[32,4,2304]{2,1,0:T(4,128)(2,1)} %reshape.442), calls=%async_computation | async-start | bytes 1179648 | tf_op jit(solution)/shard_map/all_to_all | solution.py:1041
  38.3 650.5 %all-gather.7.cloned.1.call-start = ((), (), s32[]{:S(2)}) async-start(), calls=%async_computation.15 | async-start | bytes 10616832 | tf_op jit(solution)/shard_map/all_gather | solution.py:798
  74.8 36.6 %collective-permute-start.5 = (bf16[320,1536]{1,0:T(8,128)(2,1)}, bf16[320,1536]{1,0:T(8,128)(2,1)}, u32[]{:S(2)}, u32[]{:S(2)}) collective-permute-start(bf16[320,1536]{1,0:T(8,128)(2,1)} %get-tuple-element.249), channel_id=1, source_target_pairs={{0,16},{8,24},{16,0},{24,8},{1,17},{9,25},{17,1},{25,9},{2,18},{10... | collective-permute-start | bytes 2949128 | tf_op jit(solution)/shard_map/ppermute | solution.py:765
  76.1 27.8 %collective-permute-start.1 = (s32[320]{0:T(512)S(1)}, s32[320]{0:T(512)S(1)}, u32[]{:S(2)}, u32[]{:S(2)}) collective-permute-start(s32[320]{0:T(512)S(1)} %copy-done.84), channel_id=1, source_target_pairs={{0,16},{8,24},{16,0},{24,8},{1,17},{9,25},{17,1},{25,9},{2,18},{10... | collective-permute-start | bytes 3848 | tf_op jit(solution)/shard_map/ppermute | solution.py:765
  76.4 33.8 %collective-permute-start = (s32[320]{0:T(512)S(1)}, s32[320]{0:T(512)S(1)}, u32[]{:S(2)}, u32[]{:S(2)}) collective-permute-start(s32[320]{0:T(512)S(1)} %copy-done.84), channel_id=1, source_target_pairs={{0,8},{8,0},{16,24},{24,16},{1,9},{9,1},{17,25},{25,17},{2,10},{10... | collective-permute-start | bytes 3848 | tf_op jit(solution)/shard_map/ppermute | solution.py:765
  77.0 31.9 %copy-start.55 = (f32[2,768,384]{2,1,0:T(8,128)S(1)}, f32[2,768,384]{2,1,0:T(8,128)}, u32[]{:S(2)}) copy-start(f32[2,768,384]{2,1,0:T(8,128)} %param.40) | copy-start | bytes 7077892
  77.1 57.9 %collective-permute-start.3 = (bf16[2,192,384]{2,1,0:T(8,128)(2,1)S(1)}, bf16[2,192,384]{2,1,0:T(8,128)(2,1)}, u32[]{:S(2)}, u32[]{:S(2)}) collective-permute-start(bf16[2,192,384]{2,1,0:T(8,128)(2,1)S(1)} %convert_element_type.203), channel_id=1, source_target_pairs={{0,0},{1,1},{2,8},{3,9},{4,16},{5,17},{6,24},{7,25},{8,2},{9,3},{1... | collective-permute-start | bytes 884744 | tf_op jit(solution)/shard_map/ppermute | solution.py:794
  103.9 6.2 collective-permute-start.2
  104.0 24.2 %collective-permute-start.8 = (bf16[320,1536]{1,0:T(8,128)(2,1)}, bf16[320,1536]{1,0:T(8,128)(2,1)}, u32[]{:S(2)}, u32[]{:S(2)}) collective-permute-start(bf16[320,1536]{1,0:T(8,128)(2,1)} %get-tuple-element.248), channel_id=1, source_target_pairs={{0,16},{8,24},{16,0},{24,8},{1,17},{9,25},{17,1},{25,9},{2,18},{10... | collective-permute-start | bytes 2949128 | tf_op jit(solution)/shard_map/ppermute | solution.py:765
  110.6 18.7 %collective-permute-start.4 = (bf16[320,1536]{1,0:T(8,128)(2,1)}, bf16[320,1536]{1,0:T(8,128)(2,1)S(1)}, u32[]{:S(2)}, u32[]{:S(2)}) collective-permute-start(bf16[320,1536]{1,0:T(8,128)(2,1)} %get-tuple-element.249), channel_id=1, source_target_pairs={{0,8},{8,0},{16,24},{24,16},{1,9},{9,1},{17,25},{25,17},{2,10},{10... | collective-permute-start | bytes 2949128 | tf_op jit(solution)/shard_map/ppermute | solution.py:765
  111.4 20.0 %collective-permute-start.6 = (bf16[320,1536]{1,0:T(8,128)(2,1)}, bf16[320,1536]{1,0:T(8,128)(2,1)}, u32[]{:S(2)}, u32[]{:S(2)}) collective-permute-start(bf16[320,1536]{1,0:T(8,128)(2,1)} %collective-permute-done.5), channel_id=1, source_target_pairs={{0,8},{8,0},{16,24},{24,16},{1,9},{9,1},{17,25},{25,17},{2,10},{10... | collective-permute-start | bytes 2949128 | tf_op jit(solution)/shard_map/ppermute | solution.py:765
  112.5 198.9 %collective-permute-start.7 = (bf16[320,1536]{1,0:T(8,128)(2,1)}, bf16[320,1536]{1,0:T(8,128)(2,1)}, u32[]{:S(2)}, u32[]{:S(2)}) collective-permute-start(bf16[320,1536]{1,0:T(8,128)(2,1)} %get-tuple-element.248), channel_id=1, source_target_pairs={{0,8},{8,0},{16,24},{24,16},{1,9},{9,1},{17,25},{25,17},{2,10},{10... | collective-permute-start | bytes 2949128 | tf_op jit(solution)/shard_map/ppermute | solution.py:765
  128.2 183.2 %collective-permute-start.9 = (bf16[320,1536]{1,0:T(8,128)(2,1)}, bf16[320,1536]{1,0:T(8,128)(2,1)}, u32[]{:S(2)}, u32[]{:S(2)}) collective-permute-start(bf16[320,1536]{1,0:T(8,128)(2,1)} %collective-permute-done.8), channel_id=1, source_target_pairs={{0,8},{8,0},{16,24},{24,16},{1,9},{9,1},{17,25},{25,17},{2,10},{10... | collective-permute-start | bytes 2949128 | tf_op jit(solution)/shard_map/ppermute | solution.py:765
  129.3 185.6 %collective-permute-start.10 = (bf16[2,768,384]{2,1,0:T(8,128)(2,1)}, bf16[2,768,384]{2,1,0:T(8,128)(2,1)S(1)}, u32[]{:S(2)}, u32[]{:S(2)}) collective-permute-start(bf16[2,768,384]{2,1,0:T(8,128)(2,1)} %convert_element_type.211), channel_id=1, source_target_pairs={{0,0},{1,1},{2,8},{3,9},{4,16},{5,17},{6,24},{7,25},{8,2},{9,3},{1... | collective-permute-start | bytes 3538952 | tf_op jit(solution)/shard_map/ppermute | solution.py:794
  134.9 176.5 %copy-start.58 = (bf16[320,1536]{1,0:T(8,128)(2,1)S(1)}, bf16[320,1536]{1,0:T(8,128)(2,1)}, u32[]{:S(2)}) copy-start(bf16[320,1536]{1,0:T(8,128)(2,1)} %get-tuple-element.248) | copy-start | bytes 2949124
  338.2 51.5 %copy-start.22 = (bf16[8,320,192]{2,1,0:T(8,128)(2,1)}, bf16[8,320,192]{2,1,0:T(8,128)(2,1)S(1)}, u32[]{:S(2)}) copy-start(bf16[8,320,192]{2,1,0:T(8,128)(2,1)S(1)} %get-tuple-element.91) | copy-start | bytes 2949124
  389.7 66.3 %copy-start.8 = (bf16[8,320,384]{2,1,0:T(8,128)(2,1)}, bf16[8,320,384]{2,1,0:T(8,128)(2,1)S(1)}, u32[]{:S(2)}) copy-start(bf16[8,320,384]{2,1,0:T(8,128)(2,1)S(1)} %all_to_all.40) | copy-start | bytes 5898244
  389.9 22.6 %collective-permute-start.14 = (bf16[1280,384]{1,0:T(8,128)(2,1)S(1)}, bf16[1280,384]{1,0:T(8,128)(2,1)S(1)}, u32[]{:S(2)}, u32[]{:S(2)}) collective-permute-start(bf16[1280,384]{1,0:T(8,128)(2,1)S(1)} %bitcast.94), channel_id=1, source_target_pairs={{0,2},{1,3},{2,4},{3,5},{4,6},{5,7},{8,10},{9,11},{10,12},{11,13},... | collective-permute-start | bytes 2949128 | tf_op jit(solution)/shard_map/ppermute | solution.py:1125
  393.2 23.2 %collective-permute-start.15 = (bf16[1280,384]{1,0:T(8,128)(2,1)S(1)}, bf16[1280,384]{1,0:T(8,128)(2,1)S(1)}, u32[]{:S(2)}, u32[]{:S(2)}) collective-permute-start(bf16[1280,384]{1,0:T(8,128)(2,1)S(1)} %bitcast.93), channel_id=1, source_target_pairs={{2,0},{3,1},{4,2},{5,3},{6,4},{7,5},{10,8},{11,9},{12,10},{13,11},... | collective-permute-start | bytes 2949128 | tf_op jit(solution)/shard_map/ppermute | solution.py:1125
  453.6 570.8 %reduce-scatter.4.cloned.1.call-start = ((), (), s32[]{:S(2)}) async-start(), calls=%async_computation.11 | async-start | bytes 10616832 | tf_op jit(solution)/shard_map/reduce_scatter | solution.py:966
  455.5 50.0 %copy-start.31 = (s32[10]{0:T(128)}, s32[10]{0:T(128)S(1)}, u32[]{:S(2)}) copy-start(s32[10]{0:T(128)S(1)} %fusion.62.hi_ref) | copy-start | bytes 124
  455.6 50.0 %copy-start.32 = (s32[10]{0:T(128)}, s32[10]{0:T(128)S(1)}, u32[]{:S(2)}) copy-start(s32[10]{0:T(128)S(1)} %fusion.63.lo_ref) | copy-start | bytes 124
  509.8 63.5 %copy-start = (bf16[8,2,192,384]{3,2,1,0:T(8,128)(2,1)S(1)}, bf16[8,2,192,384]{3,2,1,0:T(8,128)(2,1)}, u32[]{:S(2)}) copy-start(bf16[8,2,192,384]{3,2,1,0:T(8,128)(2,1)} %get-tuple-element.96) | copy-start | bytes 7077892
  582.7 32.4 %copy-start.16 = (bf16[1280,1536]{1,0:T(8,128)(2,1)}, bf16[1280,1536]{1,0:T(8,128)(2,1)S(1)}, u32[]{:S(2)}) copy-start(bf16[1280,1536]{1,0:T(8,128)(2,1)S(1)} %get-tuple-element.97) | copy-start | bytes 11796484
  582.9 32.3 %copy-start.40 = (bf16[320,1536]{1,0:T(8,128)(2,1)S(1)}, bf16[320,1536]{1,0:T(8,128)(2,1)}, u32[]{:S(2)}) copy-start(bf16[320,1536]{1,0:T(8,128)(2,1)} %param.23) | copy-start | bytes 2949124
  582.9 9.0 collective-permute-start.17
  589.7 3.6 collective-permute-start.16
  592.1 23.0 %collective-permute-start.18 = (bf16[320,1536]{1,0:T(8,128)(2,1)S(1)}, bf16[320,1536]{1,0:T(8,128)(2,1)S(1)}, u32[]{:S(2)}, u32[]{:S(2)}) collective-permute-start(bf16[320,1536]{1,0:T(8,128)(2,1)S(1)} %add_convert_fusion.6), channel_id=1, source_target_pairs={{0,16},{8,24},{16,0},{24,8},{1,17},{9,25},{17,1},{25,9},{2,18},{10... | collective-permute-start | bytes 2949128 | tf_op jit(solution)/shard_map/ppermute | solution.py:765
  593.3 22.8 %copy-start.59 = (bf16[320,1536]{1,0:T(8,128)(2,1)}, bf16[320,1536]{1,0:T(8,128)(2,1)S(1)}, u32[]{:S(2)}) copy-start(bf16[320,1536]{1,0:T(8,128)(2,1)S(1)} %collective-permute-done.16) | copy-start | bytes 2949124
  620.0 22.1 %collective-permute-start.20 = (bf16[320,1536]{1,0:T(8,128)(2,1)S(1)}, bf16[320,1536]{1,0:T(8,128)(2,1)S(1)}, u32[]{:S(2)}, u32[]{:S(2)}) collective-permute-start(bf16[320,1536]{1,0:T(8,128)(2,1)S(1)} %add_convert_fusion.5), channel_id=1, source_target_pairs={{0,16},{8,24},{16,0},{24,8},{1,17},{9,25},{17,1},{25,9},{2,18},{10... | collective-permute-start | bytes 2949128 | tf_op jit(solution)/shard_map/ppermute | solution.py:765
  621.0 23.2 %collective-permute-start.19 = (bf16[320,1536]{1,0:T(8,128)(2,1)S(1)}, bf16[320,1536]{1,0:T(8,128)(2,1)S(1)}, u32[]{:S(2)}, u32[]{:S(2)}) collective-permute-start(bf16[320,1536]{1,0:T(8,128)(2,1)S(1)} %add_convert_fusion.5), channel_id=1, source_target_pairs={{0,8},{8,0},{16,24},{24,16},{1,9},{9,1},{17,25},{25,17},{2,10},{10... | collective-permute-start | bytes 2949128 | tf_op jit(solution)/shard_map/ppermute | solution.py:765
  642.1 4.3 collective-permute-start.21
  723.8 28.2 %copy-start.5 = (bf16[1280,1536]{1,0:T(8,128)(2,1)}, bf16[1280,1536]{1,0:T(8,128)(2,1)S(1)}, u32[]{:S(2)}) copy-start(bf16[1280,1536]{1,0:T(8,128)(2,1)S(1)} %backward_product.5) | copy-start | bytes 11796484
  724.9 2.6 collective-permute-start.23
  725.3 23.9 %collective-permute-start.22 = (bf16[320,1536]{1,0:T(8,128)(2,1)}, bf16[320,1536]{1,0:T(8,128)(2,1)S(1)}, u32[]{:S(2)}, u32[]{:S(2)}) collective-permute-start(bf16[320,1536]{1,0:T(8,128)(2,1)} %get-tuple-element.202), channel_id=1, source_target_pairs={{0,8},{8,0},{16,24},{24,16},{1,9},{9,1},{17,25},{25,17},{2,10},{10... | collective-permute-start | bytes 2949128 | tf_op jit(solution)/shard_map/ppermute | solution.py:765
  727.7 23.2 %copy-start.37 = (f32[320,1536]{1,0:T(8,128)S(1)}, f32[320,1536]{1,0:T(8,128)}, u32[]{:S(2)}) copy-start(f32[320,1536]{1,0:T(8,128)} %copy-done.36) | copy-start | bytes 5898244
  727.7 23.2 %collective-permute-start.24 = (bf16[320,1536]{1,0:T(8,128)(2,1)S(1)}, bf16[320,1536]{1,0:T(8,128)(2,1)S(1)}, u32[]{:S(2)}, u32[]{:S(2)}) collective-permute-start(bf16[320,1536]{1,0:T(8,128)(2,1)S(1)} %add_convert_fusion.4), channel_id=1, source_target_pairs={{0,16},{8,24},{16,0},{24,8},{1,17},{9,25},{17,1},{25,9},{2,18},{10... | collective-permute-start | bytes 2949128 | tf_op jit(solution)/shard_map/ppermute | solution.py:765
  755.8 22.3 %collective-permute-start.26 = (bf16[320,1536]{1,0:T(8,128)(2,1)S(1)}, bf16[320,1536]{1,0:T(8,128)(2,1)S(1)}, u32[]{:S(2)}, u32[]{:S(2)}) collective-permute-start(bf16[320,1536]{1,0:T(8,128)(2,1)S(1)} %multiply_convert_fusion), channel_id=1, source_target_pairs={{0,16},{8,24},{16,0},{24,8},{1,17},{9,25},{17,1},{25,9},{2,18},{10... | collective-permute-start | bytes 2949128 | tf_op jit(solution)/shard_map/ppermute | solution.py:765
  756.9 23.1 %collective-permute-start.25 = (bf16[320,1536]{1,0:T(8,128)(2,1)S(1)}, bf16[320,1536]{1,0:T(8,128)(2,1)S(1)}, u32[]{:S(2)}, u32[]{:S(2)}) collective-permute-start(bf16[320,1536]{1,0:T(8,128)(2,1)S(1)} %multiply_convert_fusion), channel_id=1, source_target_pairs={{0,8},{8,0},{16,24},{24,16},{1,9},{9,1},{17,25},{25,17},{2,10},{10... | collective-permute-start | bytes 2949128 | tf_op jit(solution)/shard_map/ppermute | solution.py:765
  778.1 4.1 collective-permute-start.27
  796.3 68.5 %all-to-all-start.4 = ((bf16[8,320,192]{1,2,0:T(8,128)(2,1)}), bf16[8,320,192]{1,2,0:T(8,128)(2,1)}, u32[]{:S(2)}, u32[]{:S(2)}) async-start(bf16[8,320,192]{1,2,0:T(8,128)(2,1)} %copy.109), calls=%async_computation.4 | async-start | bytes 2359296 | tf_op jit(solution)/shard_map/all_to_all | solution.py:1107
  810.3 403.4 %reduce-scatter.6.cloned.1.call-start = ((), (), s32[]{:S(2)}) async-start(), calls=%async_computation.12 | async-start | bytes 5308416 | tf_op jit(solution)/shard_map/reduce_scatter | solution.py:966
  958.3 36.1 %collective-permute-start.28 = (bf16[1280,384]{1,0:T(8,128)(2,1)}, bf16[1280,384]{1,0:T(8,128)(2,1)}, u32[]{:S(2)}, u32[]{:S(2)}) collective-permute-start(bf16[1280,384]{1,0:T(8,128)(2,1)} %get-tuple-element.111), channel_id=1, source_target_pairs={{2,0},{3,1},{4,2},{5,3},{6,4},{7,5},{10,8},{11,9},{12,10},{13,11},... | collective-permute-start | bytes 2949128 | tf_op jit(solution)/shard_map/ppermute | solution.py:1125
  959.6 34.8 %collective-permute-start.29 = (bf16[1280,384]{1,0:T(8,128)(2,1)}, bf16[1280,384]{1,0:T(8,128)(2,1)}, u32[]{:S(2)}, u32[]{:S(2)}) collective-permute-start(bf16[1280,384]{1,0:T(8,128)(2,1)} %get-tuple-element.112), channel_id=1, source_target_pairs={{0,2},{1,3},{2,4},{3,5},{4,6},{5,7},{8,10},{9,11},{10,12},{11,13},... | collective-permute-start | bytes 2949128 | tf_op jit(solution)/shard_map/ppermute | solution.py:1125
  967.0 53.0 %all-to-all-start.6 = ((bf16[8,320,192]{1,2,0:T(8,128)(2,1)}), bf16[8,320,192]{1,2,0:T(8,128)(2,1)}, u32[]{:S(2)}, u32[]{:S(2)}) async-start(bf16[8,320,192]{1,2,0:T(8,128)(2,1)} %copy.112), calls=%async_computation.7 | async-start | bytes 2359296 | tf_op jit(solution)/shard_map/all_to_all | solution.py:1107
  1020.0 72.6 %all-to-all-start.5 = ((bf16[8,320,384]{2,1,0:T(8,128)(2,1)}), bf16[8,320,384]{2,1,0:T(8,128)(2,1)}, u32[]{:S(2)}, u32[]{:S(2)}) async-start(bf16[8,320,384]{2,1,0:T(8,128)(2,1)} %bitcast.87), calls=%async_computation.5 | async-start | bytes 3932160 | tf_op jit(solution)/shard_map/all_to_all | solution.py:1107
  1024.3 369.5 %reduce-scatter.8.cloned.1.call-start = ((), (), s32[]{:S(2)}) async-start(), calls=%async_computation.13 | async-start | bytes 5308416 | tf_op jit(solution)/shard_map/reduce_scatter | solution.py:966
  1024.4 45.0 %collective-permute-start.30 = (bf16[2,768,384]{2,1,0:T(8,128)(2,1)}, bf16[2,768,384]{2,1,0:T(8,128)(2,1)}, u32[]{:S(2)}, u32[]{:S(2)}) collective-permute-start(bf16[2,768,384]{2,1,0:T(8,128)(2,1)} %reduce-scatter.4.cloned.1.call-done), channel_id=1, source_target_pairs={{0,0},{1,1},{2,8},{3,9},{4,16},{5,17},{6,24},{7,25},{8,2},{9,3},{1... | collective-permute-start | bytes 3538952 | tf_op jit(solution)/shard_map/ppermute | solution.py:794
  1119.9 8.4 collective-permute-start.35
  1127.5 52.5 %collective-permute-start.32 = (bf16[320,1536]{1,0:T(8,128)(2,1)}, bf16[320,1536]{1,0:T(8,128)(2,1)}, u32[]{:S(2)}, u32[]{:S(2)}) collective-permute-start(bf16[320,1536]{1,0:T(8,128)(2,1)} %get-tuple-element.201), channel_id=1, source_target_pairs={{0,8},{8,0},{16,24},{24,16},{1,9},{9,1},{17,25},{25,17},{2,10},{10... | collective-permute-start | bytes 2949128 | tf_op jit(solution)/shard_map/ppermute | solution.py:765
  1127.5 54.9 %collective-permute-start.34 = (bf16[320,1536]{1,0:T(8,128)(2,1)}, bf16[320,1536]{1,0:T(8,128)(2,1)}, u32[]{:S(2)}, u32[]{:S(2)}) collective-permute-start(bf16[320,1536]{1,0:T(8,128)(2,1)} %get-tuple-element.198), channel_id=1, source_target_pairs={{0,8},{8,0},{16,24},{24,16},{1,9},{9,1},{17,25},{25,17},{2,10},{10... | collective-permute-start | bytes 2949128 | tf_op jit(solution)/shard_map/ppermute | solution.py:765
  1130.7 53.8 %collective-permute-start.36 = (bf16[320,1536]{1,0:T(8,128)(2,1)}, bf16[320,1536]{1,0:T(8,128)(2,1)}, u32[]{:S(2)}, u32[]{:S(2)}) collective-permute-start(bf16[320,1536]{1,0:T(8,128)(2,1)} %add_convert_fusion.1), channel_id=1, source_target_pairs={{0,16},{8,24},{16,0},{24,8},{1,17},{9,25},{17,1},{25,9},{2,18},{10... | collective-permute-start | bytes 2949128 | tf_op jit(solution)/shard_map/ppermute | solution.py:765
  1162.6 33.9 %collective-permute-start.31 = (bf16[320,1536]{1,0:T(8,128)(2,1)}, bf16[320,1536]{1,0:T(8,128)(2,1)}, u32[]{:S(2)}, u32[]{:S(2)}) collective-permute-start(bf16[320,1536]{1,0:T(8,128)(2,1)} %get-tuple-element.200), channel_id=1, source_target_pairs={{0,8},{8,0},{16,24},{24,16},{1,9},{9,1},{17,25},{25,17},{2,10},{10... | collective-permute-start | bytes 2949128 | tf_op jit(solution)/shard_map/ppermute | solution.py:765
  1182.4 23.7 %collective-permute-start.33 = (bf16[320,1536]{1,0:T(8,128)(2,1)}, bf16[320,1536]{1,0:T(8,128)(2,1)}, u32[]{:S(2)}, u32[]{:S(2)}) collective-permute-start(bf16[320,1536]{1,0:T(8,128)(2,1)} %add_convert_fusion.3), channel_id=1, source_target_pairs={{0,16},{8,24},{16,0},{24,8},{1,17},{9,25},{17,1},{25,9},{2,18},{10... | collective-permute-start | bytes 2949128 | tf_op jit(solution)/shard_map/ppermute | solution.py:765
  1214.9 137.4 %all-to-all-start.7 = ((f32[32,4,2432]{2,1,0:T(4,128)}), f32[32,4,2432]{2,1,0:T(4,128)}, u32[]{:S(2)}, u32[]{:S(2)}) async-start(f32[32,4,2432]{2,1,0:T(4,128)} %bitcast.88), calls=%async_computation.9 | async-start | bytes 2490368 | tf_op jit(solution)/shard_map/all_to_all | solution.py:1255
  1354.4 33.7 %collective-permute-start.37 = (bf16[2,192,384]{2,1,0:T(8,128)(2,1)}, bf16[2,192,384]{2,1,0:T(8,128)(2,1)S(1)}, u32[]{:S(2)}, u32[]{:S(2)}) collective-permute-start(bf16[2,192,384]{2,1,0:T(8,128)(2,1)} %get-tuple-element.212), channel_id=1, source_target_pairs={{0,0},{8,24},{16,16},{24,8},{1,1},{9,25},{17,17},{25,9},{2,2},{10,... | collective-permute-start | bytes 884744 | tf_op jit(solution)/shard_map/ppermute | solution.py:765
  1357.5 30.6 %collective-permute-start.38 = (bf16[2,192,384]{2,1,0:T(8,128)(2,1)}, bf16[2,192,384]{2,1,0:T(8,128)(2,1)S(1)}, u32[]{:S(2)}, u32[]{:S(2)}) collective-permute-start(bf16[2,192,384]{2,1,0:T(8,128)(2,1)} %get-tuple-element.213), channel_id=1, source_target_pairs={{0,8},{8,0},{16,24},{24,16},{1,9},{9,1},{17,25},{25,17},{2,10},{10... | collective-permute-start | bytes 884744 | tf_op jit(solution)/shard_map/ppermute | solution.py:765
  1358.0 30.1 %collective-permute-start.39 = (bf16[2,192,384]{2,1,0:T(8,128)(2,1)}, bf16[2,192,384]{2,1,0:T(8,128)(2,1)}, u32[]{:S(2)}, u32[]{:S(2)}) collective-permute-start(bf16[2,192,384]{2,1,0:T(8,128)(2,1)} %get-tuple-element.214), channel_id=1, source_target_pairs={{0,16},{8,8},{16,0},{24,24},{1,17},{9,9},{17,1},{25,25},{2,18},{10... | collective-permute-start | bytes 884744 | tf_op jit(solution)/shard_map/ppermute | solution.py:765
  1364.0 22.4 %collective-permute-start.40 = (bf16[2,192,384]{2,1,0:T(8,128)(2,1)S(1)}, bf16[2,192,384]{2,1,0:T(8,128)(2,1)S(1)}, u32[]{:S(2)}, u32[]{:S(2)}) collective-permute-start(bf16[2,192,384]{2,1,0:T(8,128)(2,1)S(1)} %get-tuple-element.130), channel_id=1, source_target_pairs={{0,0},{1,1},{2,8},{3,9},{4,16},{5,17},{6,24},{7,25},{8,2},{9,3},{1... | collective-permute-start | bytes 884744 | tf_op jit(solution)/shard_map/ppermute | solution.py:794
  (77 other events, 410.8 us)
Sparse Core Ops, SparseCore 0:
  20.8 167.0 all-gather.4
  453.7 161.2 all-gather.6
  688.9 189.9 reduce-scatter.3
  882.3 98.5 reduce-scatter.5
  1163.4 118.0 reduce-scatter.7

commit v4 on v3

--- a/solution.py
+++ b/solution.py
@@ -1064,7 +1064,14 @@
             for t in range(3)
         ]
 
-    qkv_weights = gather_weight(jnp.concatenate(rolled(chunks, turns), axis=2))
+    qkv_weights, out_full = ring_gather(
+        jnp.concatenate(rolled(chunks, turns), axis=2), turn(w_out.astype(bf16))
+    )
+    out_weights = as_turned(out_full)
+    qkv_weights, mod_rows, fc1_low = lax.optimization_barrier(
+        (qkv_weights, mod_rows, w_fc1.astype(bf16))
+    )
+    fc1_weights = gather_weight(fc1_low)
     first_seq = seq_ids[0]
     second_seq = jnp.minimum(first_seq + 1, slot_count - 1)
     is_second = (seq_ids != first_seq)[:, None]
@@ -1085,18 +1092,11 @@
     d_down = (gate_two * back_out).astype(bf16)
     d_down_group = jnp.concatenate(gather_rep(d_down))
 
-    out_turned, fc1_low, act_one_group = lax.optimization_barrier(
-        (turn(w_out.astype(bf16)), w_fc1.astype(bf16), act_one_group)
-    )
-    out_full, fc1_weights = ring_gather(out_turned, fc1_low)
-    out_weights = as_turned(out_full)
     fc2_low, act_one = lax.optimization_barrier((w_fc2.astype(bf16), act_one))
     fc2_turned = turn(fc2_low)
-    act_one_group, fc1_weights, d_down_group, fc2_turned = lax.optimization_barrier(
-        (act_one_group, fc1_weights, d_down_group, fc2_turned)
-    )
 
     query_sent, pair_sent, qk_pre = qkv_product(spots, act_one_group, qkv_weights, image, gains)
+    pair_sent, fc2_turned = lax.optimization_barrier((pair_sent, fc2_turned))
 
     bunch = 2 * reps
     bunches = shards // bunch
@@ -1131,7 +1131,9 @@
         (query_sent, pair_before, pair_after)
     )
     query_own = exchange(query_sent).reshape(stretch_rows, half_width)
-    fc2_turned, query_own = lax.optimization_barrier((fc2_turned, query_own))
+    fc2_turned, query_own, fc1_weights, d_down_group = lax.optimization_barrier(
+        (fc2_turned, query_own, fc1_weights, d_down_group)
+    )
     fc2_weights = as_turned(gather_weight(fc2_turned))
     window_rows = stretch_rows + 2 * halo
     stretch = ((shard_index % bunch) // 2) * bunches + shard_index // bunch
@@ -1248,8 +1250,8 @@
             for r in range(reps)
         ]
     )
-    qkv_terms, out_terms, fc1_image, leaving = lax.optimization_barrier(
-        (qkv_terms, out_terms, fc1_image, leaving)
+    qkv_terms, out_terms, fc1_image, fc1_text, leaving = lax.optimization_barrier(
+        (qkv_terms, out_terms, fc1_image, fc1_text, leaving)
     )
     leaving = jnp.broadcast_to(leaving[:, None], (reps, shards, *leaving.shape[1:]))
     came = lax.all_to_all(

time: 1420 us -> 1400 us (0.986)
  waiting for transfers between devices: 294 us -> 397 us
  Pallas kernels: 626 us -> 527 us
  blocking collectives: 144 us -> 68.3 us
  starting transfers between devices: 149 us -> 211 us
    all_to_all x3 -> x5, waiting for transfers between devices: 78.8 us -> 182 us  [exchange(): lax.all_to_all(value, 'shard', 0, 0, axis_index_groups=None if bunches ==...]
    all_to_all x3 -> x5, starting transfers between devices: 22.6 us -> 102 us  [exchange(): lax.all_to_all(value, 'shard', 0, 0, axis_index_groups=None if bunches ==...]
    pallas_call x1, Pallas kernels: 176 us -> 99.5 us  [ring_gather(): pl.pallas_call(functools.partial(ring_kernel, shards, count), in_specs=[a...]
    all_to_all x3 -> x1, blocking collectives: 144 us -> 68.3 us  [exchange(): lax.all_to_all(value, 'shard', 0, 0, axis_index_groups=None if bunches ==...]
    reduce_scatter x3, waiting for transfers between devices: 0.04 us -> 33 us  [scatter_weight(): lax.psum_scatter(terms.reshape(-1, *terms.shape[-2:]), 'shard', scatter_d...]
    all_to_all x1, waiting for transfers between devices: 31 us -> 0.01 us  [body(): lax.all_to_all(mod_sent.reshape(device_count, 4, mod_cols), ('rep', 'shar...]
    pallas_call x1, Pallas kernels: 125 us -> 107 us  [ring_scatter(): pl.pallas_call(functools.partial(ring_scatter_kernel, count), in_specs=[w...]
    ppermute x33, waiting for transfers between devices: 124 us -> 107 us  [over_rep(): return lax.ppermute(value, 'rep', [(r, target(r)) for r in range(count)])]
  transfers between devices with their start and end apart: 51 -> 53, of which waited for: 22 -> 27; matrix products, arithmetic and copies ran while one was open for 9% -> 9% of each run, Pallas kernels for 43% -> 38%
where the time goes in v4:
time: 1400 us; the launch traced here: 1390 us
  Pallas kernels  527 us (38%)
  waiting for transfers between devices  397 us (28%)
  starting transfers between devices  211 us (15%)
  other arithmetic  86.7 us (6%)
  local copies, waits for them, and re-layouts  74.6 us (5%)
  blocking collectives  68.3 us (5%)
  between operations  16 us (1%)
    all_to_all x5, waiting for transfers between devices, exchange(): lax.all_to_all(value, 'shard', 0, 0, axis_index_groups=None if bunches ==...  182 us
    ppermute x33, waiting for transfers between devices, over_rep(): return lax.ppermute(value, 'rep', [(r, target(r)) for r in range(count)])  107 us
    pallas_call x1, Pallas kernels, ring_scatter(): pl.pallas_call(functools.partial(ring_scatter_kernel, count), in_specs=[w...  107 us
    all_to_all x5, starting transfers between devices, exchange(): lax.all_to_all(value, 'shard', 0, 0, axis_index_groups=None if bunches ==...  102 us
    pallas_call x1, Pallas kernels, ring_gather(): pl.pallas_call(functools.partial(ring_kernel, shards, count), in_specs=[a...  99.5 us
    pallas_call x1, Pallas kernels, attention_back(): pl.pallas_call(attend_back_kernel, grid_spec=pltpu.PrefetchScalarGridSpec...  86.4 us
    all_to_all x1, blocking collectives, exchange(): lax.all_to_all(value, 'shard', 0, 0, axis_index_groups=None if bunches ==...  68.3 us
    ppermute x33, starting transfers between devices, over_rep(): return lax.ppermute(value, 'rep', [(r, target(r)) for r in range(count)])  67.9 us
  transfers between devices with their start and end apart: 53, of which 27 were waited for; matrix products, arithmetic and copies ran while one was open for 9% of the time, Pallas kernels for 38%

profile of v4, /device:TPU:1, one launch (start us, length us, event | category | flops | bytes accessed | tf_op | source)
XLA Modules:
  0.0 1391.3 jit_solution(962457815418659199)
XLA Ops:
  15.8 7.1 all-to-all-start
  24.0 3.4 collective-permute-start
  28.1 3.7 collective-permute-start.2
  31.9 2.9 collective-permute-start.3
  39.1 3.8 collective-permute-done.3.refs_1_
  42.9 99.5 %ring_gather.1 = (bf16[8,2,192,1152]{3,2,1,0:T(8,128)(2,1)}, bf16[8,2,192,384]{3,2,1,0:T(8,128)(2,1)}) custom-call(bf16[2,192,1152]{2,1,0:T(8,128)(2,1)} %pad_maximum_fusion.5.refs_0_, bf16[2,192,384]{2,1,0:T(8,128)(2,1)} %collective-permute-done.3.refs_1_), custom_call_target="tpu_custom_call" | custom-call | flops 1048576 | bytes 268435456 | tf_op jit(solution)/shard_map/ring_gather/pallas_call | solution.py:868
  150.4 21.3 %collective-permute-done.5 = s32[320]{0:T(512)S(1)} collective-permute-done((s32[320]{0:T(512)S(1)}, s32[320]{0:T(512)S(1)}, u32[]{:S(2)}, u32[]{:S(2)}) %collective-permute-start.5) | collective-permute-done | bytes 1312 | tf_op jit(solution)/shard_map/ppermute | solution.py:765
  180.9 19.9 %qkv_product.1 = (bf16[8,320,192]{2,1,0:T(8,128)(2,1)S(1)}, bf16[8,320,384]{2,1,0:T(8,128)(2,1)S(1)}, f32[1280,768]{1,0:T(8,128)S(1)}) custom-call(s32[9]{0:T(128)S(1)} %pad_add_fusion.1.spots, bf16[1280,1536]{1,0:T(8,128)(2,1)S(1)} %pad_maximum_fusion.x_ref, bf16[8,2,192,1152]{3,2,1,0:T(8,128)(2,1)} %get-tuple-element.85.w0.w1, ...), custom_call_target="tpu_custom_call" | custom-call | flops 1073741824 | bytes 4194304 | tf_op jit(solution)/shard_map/qkv_product/pallas_call | solution.py:380
  205.2 6.6 collective-permute-done.10
  211.8 71.4 %all-to-all-start.1 = ((bf16[8,320,384]{2,1,0:T(8,128)(2,1)}), bf16[8,320,384]{2,1,0:T(8,128)(2,1)S(1)}, u32[]{:S(2)}, u32[]{:S(2)}) async-start(bf16[8,320,384]{2,1,0:T(8,128)(2,1)} %copy-done.21), calls=%async_computation.1 | async-start | bytes 3932160 | tf_op jit(solution)/shard_map/all_to_all | solution.py:1107
  283.3 78.2 %all-to-all-done.1 = bf16[8,320,384]{2,1,0:T(8,128)(2,1)S(1)} async-done(((bf16[8,320,384]{2,1,0:T(8,128)(2,1)}), bf16[8,320,384]{2,1,0:T(8,128)(2,1)S(1)}, u32[]{:S(2)}, u32[]{:S(2)}) %all-to-all-start.1) | async-done | bytes 1966112 | tf_op jit(solution)/shard_map/all_to_all | solution.py:1107
  365.0 19.2 %collective-permute-done.11.before_ref = bf16[1280,384]{1,0:T(8,128)(2,1)S(1)} collective-permute-done((bf16[1280,384]{1,0:T(8,128)(2,1)S(1)}, bf16[1280,384]{1,0:T(8,128)(2,1)S(1)}, u32[]{:S(2)}, u32[]{:S(2)}) %collective-permute-start.11) | collective-permute-done | bytes 983072 | tf_op jit(solution)/shard_map/ppermute | solution.py:1125
  385.1 2.9 collective-permute-done.12.after_ref
  391.4 4.3 all-to-all-start.2
  396.2 3.5 pad_maximum_fusion.1.dy_ref
  399.8 23.2 %all-to-all-done.2 = bf16[8,320,192]{1,2,0:T(8,128)(2,1)} async-done(((bf16[8,320,192]{1,2,0:T(8,128)(2,1)}), bf16[8,320,192]{1,2,0:T(8,128)(2,1)}, u32[]{:S(2)}, u32[]{:S(2)}) %all-to-all-start.2) | async-done | bytes 983072 | tf_op jit(solution)/shard_map/all_to_all | solution.py:1107
  431.1 44.2 %attend.1 = (bf16[2560,192]{1,0:T(8,128)(2,1)S(1)}, f32[10,8,256]{2,1,0:T(8,128)S(1)}) custom-call(s32[10]{0:T(128)S(1)} %fusion.61.lo_ref, s32[10]{0:T(128)S(1)} %fusion.60.hi_ref, bf16[2560,192]{1,0:T(8,128)(2,1)S(1)} %bitcast.75, bf16[2560,384]{1,0:T(8,128)(2,1)S(1)} %bitcast.71, bf16[1280,384]{1,0:T(8,128)(2,1)S(1)} %copy-done.26, ...), custom_call_target="tpu_custom_call" | custom-call | flops 1073741824 | bytes 4194304 | tf_op jit(solution)/shard_map/attend/pallas_call | solution.py:197
  479.5 68.3 %all_to_all.40 = bf16[8,320,192]{1,2,0:T(8,128)(2,1)} all-to-all(bf16[8,320,192]{1,2,0:T(8,128)(2,1)} %copy.107), channel_id=1, replica_groups=mesh['rep'=4,'shard'=8] {'shard'}, dimensions={0} | all-to-all | bytes 1966080 | tf_op jit(solution)/shard_map/all_to_all | solution.py:1107
  551.6 7.3 forward_product.3
  564.9 21.9 %collective-permute-done.18 = bf16[320,1536]{1,0:T(8,128)(2,1)S(1)} collective-permute-done((bf16[320,1536]{1,0:T(8,128)(2,1)S(1)}, bf16[320,1536]{1,0:T(8,128)(2,1)S(1)}, u32[]{:S(2)}, u32[]{:S(2)}) %collective-permute-start.18) | collective-permute-done | bytes 983072 | tf_op jit(solution)/shard_map/ppermute | solution.py:765
  588.1 3.4 add_convert_fusion.5
  593.1 20.6 %collective-permute-done.20 = bf16[320,1536]{1,0:T(8,128)(2,1)S(1)} collective-permute-done((bf16[320,1536]{1,0:T(8,128)(2,1)S(1)}, bf16[320,1536]{1,0:T(8,128)(2,1)S(1)}, u32[]{:S(2)}, u32[]{:S(2)}) %collective-permute-start.20) | collective-permute-done | bytes 983072 | tf_op jit(solution)/shard_map/ppermute | solution.py:765
  618.3 19.2 %forward_product.4 = (bf16[1280,1536]{1,0:T(8,128)(2,1)S(1)}, bf16[1280,1536]{1,0:T(8,128)(2,1)S(1)}) custom-call(s32[9]{0:T(128)S(1)} %pad_add_fusion.1.spots, bf16[1280,1536]{1,0:T(8,128)(2,1)S(1)} %pad_maximum_fusion.2.x_ref, bf16[8,2,192,1536]{3,2,1,0:T(8,128)(2,1)} %bitcast.78, bf16[8,2,192,1536]{3,2,1,0:T(8,128)(2,1)} %bitcast.79, ...), custom_call_target="tpu_custom_call" | custom-call | flops 754974720 | bytes 4194304 | tf_op jit(solution)/shard_map/forward_product/pallas_call | solution.py:540
  639.5 20.9 %gradient.4 = bf16[4,2,2,768,384]{4,3,2,1,0:T(8,128)(2,1)} custom-call(s32[9]{0:T(128)S(1)} %pad_add_fusion.1.spots, bf16[1280,1536]{1,0:T(8,128)(2,1)S(1)} %get-tuple-element.102.x_ref, bf16[1280,1536]{1,0:T(8,128)(2,1)} %pad_maximum_fusion.1.dy_ref, s32[1280,1]{1,0:T(8,128)S(1)} %convert_element_type.209.image_ref), custom_call_target="tpu_custom_call" | custom-call | flops 754974720 | bytes 4194304 | tf_op jit(solution)/shard_map/gradient/pallas_call | solution.py:737
  660.4 18.3 %backward_product.4.dy_ref = bf16[1280,1536]{1,0:T(8,128)(2,1)S(1)} custom-call(s32[9]{0:T(128)S(1)} %pad_add_fusion.1.spots, bf16[1280,1536]{1,0:T(8,128)(2,1)} %pad_maximum_fusion.1.dy_ref, bf16[4,2,2,768,384]{4,3,2,1,0:T(8,128)(2,1)} %bitcast.82, bf16[4,2,2,768,384]{4,3,2,1,0:T(8,128)(2,1)} %bitcast.83, s32[1280,1]{1,0:T(8,128)S(1)} %convert_element_type.209.image_ref, ...), custom_call_target="tpu_custom_call" | custom-call | flops 754974720 | bytes 4194304 | tf_op jit(solution)/shard_map/backward_product/pallas_call | solution.py:651
  680.7 15.0 %backward_product.5 = bf16[1280,1536]{1,0:T(8,128)(2,1)S(1)} custom-call(s32[9]{0:T(128)S(1)} %pad_add_fusion.1.spots, bf16[1280,1536]{1,0:T(8,128)(2,1)} %copy-done.4, bf16[8,2,192,1536]{3,2,1,0:T(8,128)(2,1)} %bitcast.80, bf16[8,2,192,1536]{3,2,1,0:T(8,128)(2,1)} %bitcast.81, s32[1280,1]{1,0:T(8,128)S(1)} %convert_element_type.209.image_ref), custom_call_target="tpu_custom_call" | custom-call | flops 754974720 | bytes 4194304 | tf_op jit(solution)/shard_map/backward_product/pallas_call | solution.py:651
  700.4 20.3 %gradient.5 = (bf16[8,1,192,1536]{3,2,1,0:T(8,128)(2,1)}, bf16[8,1,192,1536]{3,2,1,0:T(8,128)(2,1)}) custom-call(s32[9]{0:T(128)S(1)} %pad_add_fusion.1.spots, bf16[1280,1536]{1,0:T(8,128)(2,1)S(1)} %copy-done.3, bf16[1280,1536]{1,0:T(8,128)(2,1)} %copy-done.4, s32[1280,1]{1,0:T(8,128)S(1)} %convert_element_type.209.image_ref), custom_call_target="tpu_custom_call" | custom-call | flops 754974720 | bytes 4194304 | tf_op jit(solution)/shard_map/gradient/pallas_call | solution.py:737
  729.8 20.2 %collective-permute-done.26 = bf16[320,1536]{1,0:T(8,128)(2,1)S(1)} collective-permute-done((bf16[320,1536]{1,0:T(8,128)(2,1)S(1)}, bf16[320,1536]{1,0:T(8,128)(2,1)S(1)}, u32[]{:S(2)}, u32[]{:S(2)}) %collective-permute-start.26) | collective-permute-done | bytes 983072 | tf_op jit(solution)/shard_map/ppermute | solution.py:765
  756.1 8.7 backward_product.6
  768.4 12.5 all-to-all-start.4
  784.9 7.4 gradient.6
  792.4 43.0 %all-to-all-done.4 = bf16[8,320,192]{1,2,0:T(8,128)(2,1)} async-done(((bf16[8,320,192]{1,2,0:T(8,128)(2,1)}), bf16[8,320,192]{1,2,0:T(8,128)(2,1)}, u32[]{:S(2)}, u32[]{:S(2)}) %all-to-all-start.4) | async-done | bytes 983072 | tf_op jit(solution)/shard_map/all_to_all | solution.py:1107
  837.8 86.4 %attend_back.1 = (bf16[2560,192]{1,0:T(8,128)(2,1)}, bf16[1280,384]{1,0:T(8,128)(2,1)}, bf16[1280,384]{1,0:T(8,128)(2,1)}, f32[2560,384]{1,0:T(8,128)}) custom-call(s32[10]{0:T(128)} %copy-done.33, s32[10]{0:T(128)} %copy-done.32, bf16[2560,192]{1,0:T(8,128)(2,1)} %bitcast.74, bf16[2560,384]{1,0:T(8,128)(2,1)} %bitcast.72, bf16[1280,384]{1,0:T(8,128)(2,1)} %copy-done.25, ...), custom_call_target="tpu_custom_call" | custom-call | flops 25769803776 | bytes 8388608 | tf_op jit(solution)/shard_map/attend_back/pallas_call | solution.py:237
  925.5 5.1 collective-permute-start.29
  933.0 9.1 all-to-all-start.6
  942.2 23.7 %collective-permute-done.28 = bf16[1280,384]{1,0:T(8,128)(2,1)} collective-permute-done((bf16[1280,384]{1,0:T(8,128)(2,1)}, bf16[1280,384]{1,0:T(8,128)(2,1)}, u32[]{:S(2)}, u32[]{:S(2)}) %collective-permute-start.28) | collective-permute-done | bytes 983072 | tf_op jit(solution)/shard_map/ppermute | solution.py:1125
  965.9 4.4 add_convert_fusion
  970.2 22.0 %all-to-all-done.6 = bf16[8,320,192]{1,2,0:T(8,128)(2,1)} async-done(((bf16[8,320,192]{1,2,0:T(8,128)(2,1)}), bf16[8,320,192]{1,2,0:T(8,128)(2,1)}, u32[]{:S(2)}, u32[]{:S(2)}) %all-to-all-start.6) | async-done | bytes 983072 | tf_op jit(solution)/shard_map/all_to_all | solution.py:1107
  992.2 4.3 all-to-all-start.5
  996.6 5.0 collective-permute-start.30
  1003.7 15.8 %forward_product.5 = bf16[1280,1536]{1,0:T(8,128)(2,1)S(1)} custom-call(s32[9]{0:T(128)S(1)} %pad_add_fusion.1.spots, bf16[1280,1536]{1,0:T(8,128)(2,1)S(1)} %copy-done.10, bf16[4,2,2,768,384]{4,3,2,1,0:T(8,128)(2,1)} %bitcast.84, bf16[4,2,2,768,384]{4,3,2,1,0:T(8,128)(2,1)} %bitcast.85, s32[1280,1]{1,0:T(8,128)S(1)} %convert_element_type.209.image_ref), custom_call_target="tpu_custom_call" | custom-call | flops 754974720 | bytes 4194304 | tf_op jit(solution)/shard_map/forward_product/pallas_call | solution.py:540
  1024.0 17.9 %collective-permute-done.30 = bf16[2,768,384]{2,1,0:T(8,128)(2,1)} collective-permute-done((bf16[2,768,384]{2,1,0:T(8,128)(2,1)}, bf16[2,768,384]{2,1,0:T(8,128)(2,1)}, u32[]{:S(2)}, u32[]{:S(2)}) %collective-permute-start.30) | collective-permute-done | bytes 1179680 | tf_op jit(solution)/shard_map/ppermute | solution.py:794
  1041.9 8.0 fusion.77
  1049.9 15.9 %all-to-all-done.5.kv_ref = bf16[8,320,384]{2,1,0:T(8,128)(2,1)} async-done(((bf16[8,320,384]{2,1,0:T(8,128)(2,1)}), bf16[8,320,384]{2,1,0:T(8,128)(2,1)}, u32[]{:S(2)}, u32[]{:S(2)}) %all-to-all-start.5) | async-done | bytes 1966112 | tf_op jit(solution)/shard_map/all_to_all | solution.py:1107
  1069.2 8.6 norm_back.1
  1077.8 13.2 backward_product.7
  1093.8 4.4 collective-permute-start.35
  1102.8 32.7 %collective-permute-start.36 = (bf16[320,1536]{1,0:T(8,128)(2,1)}, bf16[320,1536]{1,0:T(8,128)(2,1)}, u32[]{:S(2)}, u32[]{:S(2)}) collective-permute-start(bf16[320,1536]{1,0:T(8,128)(2,1)} %add_convert_fusion.1), channel_id=1, source_target_pairs={{0,16},{8,24},{16,0},{24,8},{1,17},{9,25},{17,1},{25,9},{2,18},{10... | collective-permute-start | bytes 2949128 | tf_op jit(solution)/shard_map/ppermute | solution.py:765
  1138.2 14.8 %gradient.7.refs_0_ = bf16[8,2,192,1152]{3,2,1,0:T(8,128)(2,1)} custom-call(s32[9]{0:T(128)S(1)} %pad_add_fusion.1.spots, bf16[1280,1536]{1,0:T(8,128)(2,1)} %copy-done.1, bf16[1280,1152]{1,0:T(8,128)(2,1)S(1)} %copy-done.15, s32[1280,1]{1,0:T(8,128)S(1)} %convert_element_type.209.image_ref), custom_call_target="tpu_custom_call" | custom-call | flops 566231040 | bytes 4194304 | tf_op jit(solution)/shard_map/gradient/pallas_call | solution.py:737
  1160.3 4.3 fusion.76
  1164.6 4.1 multiply_dynamic-update-slice_fusion.1
  1170.9 8.3 collective-permute-done.33
  1179.3 3.4 fusion.21
  1182.7 4.0 fusion.49
  1186.9 32.9 %reduce-scatter.8.cloned.1.call-done = bf16[1,192,1536]{2,1,0:T(8,128)(2,1)} async-done(((bf16[8,192,1536]{2,1,0:T(8,128)(2,1)}), bf16[1,192,1536]{2,1,0:T(8,128)(2,1)}) %reduce-scatter.8.cloned.1.call-update) | async-done | bytes 589840 | tf_op jit(solution)/shard_map/reduce_scatter | solution.py:966
  1221.0 5.3 all-to-all-start.7
  1227.4 3.0 copy-done.7
  1230.4 107.2 %ring_scatter.1 = (bf16[2,192,1152]{2,1,0:T(8,128)(2,1)S(1)}, bf16[2,192,384]{2,1,0:T(8,128)(2,1)S(1)}) custom-call(bf16[8,2,192,1152]{3,2,1,0:T(8,128)(2,1)S(1)} %copy-done.7, bf16[8,2,192,384]{3,2,1,0:T(8,128)(2,1)S(1)} %bitcast.73), custom_call_target="tpu_custom_call" | custom-call | flops 1048576 | bytes 268435456 | tf_op jit(solution)/shard_map/ring_scatter/pallas_call | solution.py:947
  1338.6 4.3 fusion.65
  1345.0 3.1 collective-permute-start.37
  1348.5 3.7 collective-permute-start.39
  1358.8 8.9 collective-permute-start.40
  1367.7 7.8 fusion.74
  1379.8 4.5 fusion.71
  (405 shorter events, 156.7 us)
Async XLA Ops:
  15.8 126.7 %all-to-all-start = ((bf16[32,4,2304]{2,1,0:T(4,128)(2,1)}), bf16[32,4,2304]{2,1,0:T(4,128)(2,1)S(1)}, u32[]{:S(2)}, u32[]{:S(2)}) async-start(bf16[32,4,2304]{2,1,0:T(4,128)(2,1)} %reshape.442), calls=%async_computation | async-start | bytes 1179648 | tf_op jit(solution)/shard_map/all_to_all | solution.py:1041
  22.8 402.6 %all-gather.5.cloned.1.call-start = ((), (), s32[]{:S(2)}) async-start(), calls=%async_computation.14 | async-start | bytes 10616832 | tf_op jit(solution)/shard_map/all_gather | solution.py:798
  24.0 12.9 collective-permute-start
  27.4 9.5 collective-permute-start.1
  28.1 8.8 collective-permute-start.2
  31.9 11.0 collective-permute-start.3
  39.1 104.4 %copy-start.40 = (bf16[320,1536]{1,0:T(8,128)(2,1)S(1)}, bf16[320,1536]{1,0:T(8,128)(2,1)}, u32[]{:S(2)}) copy-start(bf16[320,1536]{1,0:T(8,128)(2,1)} %param.23) | copy-start | bytes 2949124
  148.0 26.9 %collective-permute-start.8 = (bf16[320,1536]{1,0:T(8,128)(2,1)}, bf16[320,1536]{1,0:T(8,128)(2,1)S(1)}, u32[]{:S(2)}, u32[]{:S(2)}) collective-permute-start(bf16[320,1536]{1,0:T(8,128)(2,1)} %get-tuple-element.249), channel_id=1, source_target_pairs={{0,16},{8,24},{16,0},{24,8},{1,17},{9,25},{17,1},{25,9},{2,18},{10... | collective-permute-start | bytes 2949128 | tf_op jit(solution)/shard_map/ppermute | solution.py:765
  148.0 23.7 %collective-permute-start.5 = (s32[320]{0:T(512)S(1)}, s32[320]{0:T(512)S(1)}, u32[]{:S(2)}, u32[]{:S(2)}) collective-permute-start(s32[320]{0:T(512)S(1)} %copy-done.85), channel_id=1, source_target_pairs={{0,16},{8,24},{16,0},{24,8},{1,17},{9,25},{17,1},{25,9},{2,18},{10... | collective-permute-start | bytes 3848 | tf_op jit(solution)/shard_map/ppermute | solution.py:765
  149.5 24.8 %collective-permute-start.4 = (s32[320]{0:T(512)S(1)}, s32[320]{0:T(512)S(1)}, u32[]{:S(2)}, u32[]{:S(2)}) collective-permute-start(s32[320]{0:T(512)S(1)} %copy-done.85), channel_id=1, source_target_pairs={{0,8},{8,0},{16,24},{24,16},{1,9},{9,1},{17,25},{25,17},{2,10},{10... | collective-permute-start | bytes 3848 | tf_op jit(solution)/shard_map/ppermute | solution.py:765
  171.7 2.6 collective-permute-start.6
  174.7 3.9 collective-permute-start.7
  174.8 4.1 collective-permute-start.9
  176.4 35.4 %collective-permute-start.10 = (bf16[2,768,384]{2,1,0:T(8,128)(2,1)S(1)}, bf16[2,768,384]{2,1,0:T(8,128)(2,1)}, u32[]{:S(2)}, u32[]{:S(2)}) collective-permute-start(bf16[2,768,384]{2,1,0:T(8,128)(2,1)S(1)} %convert_element_type.210), channel_id=1, source_target_pairs={{0,0},{1,1},{2,8},{3,9},{4,16},{5,17},{6,24},{7,25},{8,2},{9,3},{1... | collective-permute-start | bytes 3538952 | tf_op jit(solution)/shard_map/ppermute | solution.py:794
  211.8 149.7 %all-to-all-start.1 = ((bf16[8,320,384]{2,1,0:T(8,128)(2,1)}), bf16[8,320,384]{2,1,0:T(8,128)(2,1)S(1)}, u32[]{:S(2)}, u32[]{:S(2)}) async-start(bf16[8,320,384]{2,1,0:T(8,128)(2,1)} %copy-done.21), calls=%async_computation.1 | async-start | bytes 3932160 | tf_op jit(solution)/shard_map/all_to_all | solution.py:1107
  283.3 81.5 %collective-permute-start.14 = (bf16[320,1536]{1,0:T(8,128)(2,1)}, bf16[320,1536]{1,0:T(8,128)(2,1)}, u32[]{:S(2)}, u32[]{:S(2)}) collective-permute-start(bf16[320,1536]{1,0:T(8,128)(2,1)} %get-tuple-element.248), channel_id=1, source_target_pairs={{0,16},{8,24},{16,0},{24,8},{1,17},{9,25},{17,1},{25,9},{2,18},{10... | collective-permute-start | bytes 2949128 | tf_op jit(solution)/shard_map/ppermute | solution.py:765
  361.5 66.4 %copy-start.8 = (bf16[8,320,384]{2,1,0:T(8,128)(2,1)}, bf16[8,320,384]{2,1,0:T(8,128)(2,1)S(1)}, u32[]{:S(2)}) copy-start(bf16[8,320,384]{2,1,0:T(8,128)(2,1)S(1)} %all-to-all-done.1) | copy-start | bytes 5898244
  361.7 22.5 %collective-permute-start.11 = (bf16[1280,384]{1,0:T(8,128)(2,1)S(1)}, bf16[1280,384]{1,0:T(8,128)(2,1)S(1)}, u32[]{:S(2)}, u32[]{:S(2)}) collective-permute-start(bf16[1280,384]{1,0:T(8,128)(2,1)S(1)} %bitcast.94), channel_id=1, source_target_pairs={{0,2},{1,3},{2,4},{3,5},{4,6},{5,7},{8,10},{9,11},{10,12},{11,13},... | collective-permute-start | bytes 2949128 | tf_op jit(solution)/shard_map/ppermute | solution.py:1125
  363.1 24.9 %collective-permute-start.12 = (bf16[1280,384]{1,0:T(8,128)(2,1)S(1)}, bf16[1280,384]{1,0:T(8,128)(2,1)S(1)}, u32[]{:S(2)}, u32[]{:S(2)}) collective-permute-start(bf16[1280,384]{1,0:T(8,128)(2,1)S(1)} %bitcast.93), channel_id=1, source_target_pairs={{2,0},{3,1},{4,2},{5,3},{6,4},{7,5},{10,8},{11,9},{12,10},{13,11},... | collective-permute-start | bytes 2949128 | tf_op jit(solution)/shard_map/ppermute | solution.py:1125
  364.4 31.8 %collective-permute-start.13 = (bf16[320,1536]{1,0:T(8,128)(2,1)}, bf16[320,1536]{1,0:T(8,128)(2,1)}, u32[]{:S(2)}, u32[]{:S(2)}) collective-permute-start(bf16[320,1536]{1,0:T(8,128)(2,1)} %get-tuple-element.248), channel_id=1, source_target_pairs={{0,8},{8,0},{16,24},{24,16},{1,9},{9,1},{17,25},{25,17},{2,10},{10... | collective-permute-start | bytes 2949128 | tf_op jit(solution)/shard_map/ppermute | solution.py:765
  364.7 31.5 %collective-permute-start.15 = (bf16[320,1536]{1,0:T(8,128)(2,1)}, bf16[320,1536]{1,0:T(8,128)(2,1)}, u32[]{:S(2)}, u32[]{:S(2)}) collective-permute-start(bf16[320,1536]{1,0:T(8,128)(2,1)} %collective-permute-done.14), channel_id=1, source_target_pairs={{0,8},{8,0},{16,24},{24,16},{1,9},{9,1},{17,25},{25,17},{2,10},{10... | collective-permute-start | bytes 2949128 | tf_op jit(solution)/shard_map/ppermute | solution.py:765
  391.4 31.5 %all-to-all-start.2 = ((bf16[8,320,192]{1,2,0:T(8,128)(2,1)}), bf16[8,320,192]{1,2,0:T(8,128)(2,1)}, u32[]{:S(2)}, u32[]{:S(2)}) async-start(bf16[8,320,192]{1,2,0:T(8,128)(2,1)} %copy.104), calls=%async_computation.2 | async-start | bytes 2359296 | tf_op jit(solution)/shard_map/all_to_all | solution.py:1107
  395.7 264.7 %all-gather.7.cloned.1.call-start = ((), (), s32[]{:S(2)}) async-start(), calls=%async_computation.15 | async-start | bytes 10616832 | tf_op jit(solution)/shard_map/all_gather | solution.py:798
  425.4 571.1 %reduce-scatter.4.cloned.1.call-start = ((), (), s32[]{:S(2)}) async-start(), calls=%async_computation.11 | async-start | bytes 10616832 | tf_op jit(solution)/shard_map/reduce_scatter | solution.py:966
  427.4 47.9 %copy-start.32 = (s32[10]{0:T(128)}, s32[10]{0:T(128)S(1)}, u32[]{:S(2)}) copy-start(s32[10]{0:T(128)S(1)} %fusion.60.hi_ref) | copy-start | bytes 124
  427.4 47.9 %copy-start.33 = (s32[10]{0:T(128)}, s32[10]{0:T(128)S(1)}, u32[]{:S(2)}) copy-start(s32[10]{0:T(128)S(1)} %fusion.61.lo_ref) | copy-start | bytes 124
  479.5 70.8 %copy-start = (bf16[8,2,192,384]{3,2,1,0:T(8,128)(2,1)S(1)}, bf16[8,2,192,384]{3,2,1,0:T(8,128)(2,1)}, u32[]{:S(2)}) copy-start(bf16[8,2,192,384]{3,2,1,0:T(8,128)(2,1)} %get-tuple-element.97) | copy-start | bytes 7077892
  560.0 3.5 collective-permute-start.17
  561.3 3.6 collective-permute-start.16
  563.7 23.0 %collective-permute-start.18 = (bf16[320,1536]{1,0:T(8,128)(2,1)S(1)}, bf16[320,1536]{1,0:T(8,128)(2,1)S(1)}, u32[]{:S(2)}, u32[]{:S(2)}) collective-permute-start(bf16[320,1536]{1,0:T(8,128)(2,1)S(1)} %add_convert_fusion.6), channel_id=1, source_target_pairs={{0,16},{8,24},{16,0},{24,8},{1,17},{9,25},{17,1},{25,9},{2,18},{10... | collective-permute-start | bytes 2949128 | tf_op jit(solution)/shard_map/ppermute | solution.py:765
  591.6 22.1 %collective-permute-start.20 = (bf16[320,1536]{1,0:T(8,128)(2,1)S(1)}, bf16[320,1536]{1,0:T(8,128)(2,1)S(1)}, u32[]{:S(2)}, u32[]{:S(2)}) collective-permute-start(bf16[320,1536]{1,0:T(8,128)(2,1)S(1)} %add_convert_fusion.5), channel_id=1, source_target_pairs={{0,16},{8,24},{16,0},{24,8},{1,17},{9,25},{17,1},{25,9},{2,18},{10... | collective-permute-start | bytes 2949128 | tf_op jit(solution)/shard_map/ppermute | solution.py:765
  592.0 23.8 %collective-permute-start.19 = (bf16[320,1536]{1,0:T(8,128)(2,1)S(1)}, bf16[320,1536]{1,0:T(8,128)(2,1)S(1)}, u32[]{:S(2)}, u32[]{:S(2)}) collective-permute-start(bf16[320,1536]{1,0:T(8,128)(2,1)S(1)} %add_convert_fusion.5), channel_id=1, source_target_pairs={{0,8},{8,0},{16,24},{24,16},{1,9},{9,1},{17,25},{25,17},{2,10},{10... | collective-permute-start | bytes 2949128 | tf_op jit(solution)/shard_map/ppermute | solution.py:765
  613.7 4.3 collective-permute-start.21
  696.8 2.6 collective-permute-start.23
  697.1 23.6 %collective-permute-start.22 = (bf16[320,1536]{1,0:T(8,128)(2,1)}, bf16[320,1536]{1,0:T(8,128)(2,1)S(1)}, u32[]{:S(2)}, u32[]{:S(2)}) collective-permute-start(bf16[320,1536]{1,0:T(8,128)(2,1)} %get-tuple-element.204), channel_id=1, source_target_pairs={{0,8},{8,0},{16,24},{24,16},{1,9},{9,1},{17,25},{25,17},{2,10},{10... | collective-permute-start | bytes 2949128 | tf_op jit(solution)/shard_map/ppermute | solution.py:765
  699.6 23.2 %collective-permute-start.24 = (bf16[320,1536]{1,0:T(8,128)(2,1)S(1)}, bf16[320,1536]{1,0:T(8,128)(2,1)S(1)}, u32[]{:S(2)}, u32[]{:S(2)}) collective-permute-start(bf16[320,1536]{1,0:T(8,128)(2,1)S(1)} %add_convert_fusion.4), channel_id=1, source_target_pairs={{0,16},{8,24},{16,0},{24,8},{1,17},{9,25},{17,1},{25,9},{2,18},{10... | collective-permute-start | bytes 2949128 | tf_op jit(solution)/shard_map/ppermute | solution.py:765
  727.8 22.2 %collective-permute-start.26 = (bf16[320,1536]{1,0:T(8,128)(2,1)S(1)}, bf16[320,1536]{1,0:T(8,128)(2,1)S(1)}, u32[]{:S(2)}, u32[]{:S(2)}) collective-permute-start(bf16[320,1536]{1,0:T(8,128)(2,1)S(1)} %multiply_convert_fusion), channel_id=1, source_target_pairs={{0,16},{8,24},{16,0},{24,8},{1,17},{9,25},{17,1},{25,9},{2,18},{10... | collective-permute-start | bytes 2949128 | tf_op jit(solution)/shard_map/ppermute | solution.py:765
  728.4 23.6 %collective-permute-start.25 = (bf16[320,1536]{1,0:T(8,128)(2,1)S(1)}, bf16[320,1536]{1,0:T(8,128)(2,1)S(1)}, u32[]{:S(2)}, u32[]{:S(2)}) collective-permute-start(bf16[320,1536]{1,0:T(8,128)(2,1)S(1)} %multiply_convert_fusion), channel_id=1, source_target_pairs={{0,8},{8,0},{16,24},{24,16},{1,9},{9,1},{17,25},{25,17},{2,10},{10... | collective-permute-start | bytes 2949128 | tf_op jit(solution)/shard_map/ppermute | solution.py:765
  750.0 4.1 collective-permute-start.27
  768.4 67.0 %all-to-all-start.4 = ((bf16[8,320,192]{1,2,0:T(8,128)(2,1)}), bf16[8,320,192]{1,2,0:T(8,128)(2,1)}, u32[]{:S(2)}, u32[]{:S(2)}) async-start(bf16[8,320,192]{1,2,0:T(8,128)(2,1)} %copy.109), calls=%async_computation.4 | async-start | bytes 2359296 | tf_op jit(solution)/shard_map/all_to_all | solution.py:1107
  780.9 405.9 %reduce-scatter.6.cloned.1.call-start = ((), (), s32[]{:S(2)}) async-start(), calls=%async_computation.12 | async-start | bytes 5308416 | tf_op jit(solution)/shard_map/reduce_scatter | solution.py:966
  924.2 41.7 %collective-permute-start.28 = (bf16[1280,384]{1,0:T(8,128)(2,1)}, bf16[1280,384]{1,0:T(8,128)(2,1)}, u32[]{:S(2)}, u32[]{:S(2)}) collective-permute-start(bf16[1280,384]{1,0:T(8,128)(2,1)} %get-tuple-element.112), channel_id=1, source_target_pairs={{2,0},{3,1},{4,2},{5,3},{6,4},{7,5},{10,8},{11,9},{12,10},{13,11},... | collective-permute-start | bytes 2949128 | tf_op jit(solution)/shard_map/ppermute | solution.py:1125
  925.5 40.4 %collective-permute-start.29 = (bf16[1280,384]{1,0:T(8,128)(2,1)}, bf16[1280,384]{1,0:T(8,128)(2,1)}, u32[]{:S(2)}, u32[]{:S(2)}) collective-permute-start(bf16[1280,384]{1,0:T(8,128)(2,1)} %get-tuple-element.113), channel_id=1, source_target_pairs={{0,2},{1,3},{2,4},{3,5},{4,6},{5,7},{8,10},{9,11},{10,12},{11,13},... | collective-permute-start | bytes 2949128 | tf_op jit(solution)/shard_map/ppermute | solution.py:1125
  933.0 59.1 %all-to-all-start.6 = ((bf16[8,320,192]{1,2,0:T(8,128)(2,1)}), bf16[8,320,192]{1,2,0:T(8,128)(2,1)}, u32[]{:S(2)}, u32[]{:S(2)}) async-start(bf16[8,320,192]{1,2,0:T(8,128)(2,1)} %copy.112), calls=%async_computation.7 | async-start | bytes 2359296 | tf_op jit(solution)/shard_map/all_to_all | solution.py:1107
  992.2 73.6 %all-to-all-start.5 = ((bf16[8,320,384]{2,1,0:T(8,128)(2,1)}), bf16[8,320,384]{2,1,0:T(8,128)(2,1)}, u32[]{:S(2)}, u32[]{:S(2)}) async-start(bf16[8,320,384]{2,1,0:T(8,128)(2,1)} %bitcast.87), calls=%async_computation.5 | async-start | bytes 3932160 | tf_op jit(solution)/shard_map/all_to_all | solution.py:1107
  996.5 223.3 %reduce-scatter.8.cloned.1.call-start = ((), (), s32[]{:S(2)}) async-start(), calls=%async_computation.13 | async-start | bytes 5308416 | tf_op jit(solution)/shard_map/reduce_scatter | solution.py:966
  996.6 45.3 %collective-permute-start.30 = (bf16[2,768,384]{2,1,0:T(8,128)(2,1)}, bf16[2,768,384]{2,1,0:T(8,128)(2,1)}, u32[]{:S(2)}, u32[]{:S(2)}) collective-permute-start(bf16[2,768,384]{2,1,0:T(8,128)(2,1)} %reduce-scatter.4.cloned.1.call-done), channel_id=1, source_target_pairs={{0,0},{1,1},{2,8},{3,9},{4,16},{5,17},{6,24},{7,25},{8,2},{9,3},{1... | collective-permute-start | bytes 3538952 | tf_op jit(solution)/shard_map/ppermute | solution.py:794
  1093.8 6.6 collective-permute-start.35
  1099.5 53.5 %collective-permute-start.32 = (bf16[320,1536]{1,0:T(8,128)(2,1)}, bf16[320,1536]{1,0:T(8,128)(2,1)}, u32[]{:S(2)}, u32[]{:S(2)}) collective-permute-start(bf16[320,1536]{1,0:T(8,128)(2,1)} %get-tuple-element.203), channel_id=1, source_target_pairs={{0,8},{8,0},{16,24},{24,16},{1,9},{9,1},{17,25},{25,17},{2,10},{10... | collective-permute-start | bytes 2949128 | tf_op jit(solution)/shard_map/ppermute | solution.py:765
  1099.5 56.0 %collective-permute-start.34 = (bf16[320,1536]{1,0:T(8,128)(2,1)}, bf16[320,1536]{1,0:T(8,128)(2,1)}, u32[]{:S(2)}, u32[]{:S(2)}) collective-permute-start(bf16[320,1536]{1,0:T(8,128)(2,1)} %get-tuple-element.200), channel_id=1, source_target_pairs={{0,8},{8,0},{16,24},{24,16},{1,9},{9,1},{17,25},{25,17},{2,10},{10... | collective-permute-start | bytes 2949128 | tf_op jit(solution)/shard_map/ppermute | solution.py:765
  1102.8 54.9 %collective-permute-start.36 = (bf16[320,1536]{1,0:T(8,128)(2,1)}, bf16[320,1536]{1,0:T(8,128)(2,1)}, u32[]{:S(2)}, u32[]{:S(2)}) collective-permute-start(bf16[320,1536]{1,0:T(8,128)(2,1)} %add_convert_fusion.1), channel_id=1, source_target_pairs={{0,16},{8,24},{16,0},{24,8},{1,17},{9,25},{17,1},{25,9},{2,18},{10... | collective-permute-start | bytes 2949128 | tf_op jit(solution)/shard_map/ppermute | solution.py:765
  1135.6 35.3 %collective-permute-start.31 = (bf16[320,1536]{1,0:T(8,128)(2,1)}, bf16[320,1536]{1,0:T(8,128)(2,1)}, u32[]{:S(2)}, u32[]{:S(2)}) collective-permute-start(bf16[320,1536]{1,0:T(8,128)(2,1)} %get-tuple-element.202), channel_id=1, source_target_pairs={{0,8},{8,0},{16,24},{24,16},{1,9},{9,1},{17,25},{25,17},{2,10},{10... | collective-permute-start | bytes 2949128 | tf_op jit(solution)/shard_map/ppermute | solution.py:765
  1155.6 23.7 %collective-permute-start.33 = (bf16[320,1536]{1,0:T(8,128)(2,1)}, bf16[320,1536]{1,0:T(8,128)(2,1)}, u32[]{:S(2)}, u32[]{:S(2)}) collective-permute-start(bf16[320,1536]{1,0:T(8,128)(2,1)} %add_convert_fusion.3), channel_id=1, source_target_pairs={{0,16},{8,24},{16,0},{24,8},{1,17},{9,25},{17,1},{25,9},{2,18},{10... | collective-permute-start | bytes 2949128 | tf_op jit(solution)/shard_map/ppermute | solution.py:765
  1186.8 39.5 %copy-start.76 = (s32[32,2]{1,0:T(8,128)S(1)}, s32[32,2]{1,0:T(8,128)}, u32[]{:S(2)}) copy-start(s32[32,2]{1,0:T(8,128)} %copy-done.75) | copy-start | bytes 772
  1221.0 121.8 %all-to-all-start.7 = ((f32[32,4,2432]{2,1,0:T(4,128)}), f32[32,4,2432]{2,1,0:T(4,128)}, u32[]{:S(2)}, u32[]{:S(2)}) async-start(f32[32,4,2432]{2,1,0:T(4,128)} %bitcast.88), calls=%async_computation.10 | async-start | bytes 2490368 | tf_op jit(solution)/shard_map/all_to_all | solution.py:1257
  1230.4 108.1 %copy-start.56 = (f32[2,192,1536]{2,1,0:T(8,128)S(1)}, f32[2,192,1536]{2,1,0:T(8,128)}, u32[]{:S(2)}) copy-start(f32[2,192,1536]{2,1,0:T(8,128)} %param.37) | copy-start | bytes 7077892
  1230.4 108.1 %copy-start.67 = (f32[2,192,1536]{2,1,0:T(8,128)S(1)}, f32[2,192,1536]{2,1,0:T(8,128)}, u32[]{:S(2)}) copy-start(f32[2,192,1536]{2,1,0:T(8,128)} %param.38) | copy-start | bytes 7077892
  1230.4 108.1 %copy-start.68 = (f32[2,192,1536]{2,1,0:T(8,128)S(1)}, f32[2,192,1536]{2,1,0:T(8,128)}, u32[]{:S(2)}) copy-start(f32[2,192,1536]{2,1,0:T(8,128)} %param.39) | copy-start | bytes 7077892
  1230.4 108.1 %copy-start.71 = (bf16[1,192,1536]{2,1,0:T(8,128)(2,1)S(1)}, bf16[1,192,1536]{2,1,0:T(8,128)(2,1)}, u32[]{:S(2)}) copy-start(bf16[1,192,1536]{2,1,0:T(8,128)(2,1)} %reduce-scatter.6.cloned.1.call-done) | copy-start | bytes 1769476
  1230.4 108.1 %copy-start.72 = (bf16[1,192,1536]{2,1,0:T(8,128)(2,1)S(1)}, bf16[1,192,1536]{2,1,0:T(8,128)(2,1)}, u32[]{:S(2)}) copy-start(bf16[1,192,1536]{2,1,0:T(8,128)(2,1)} %reduce-scatter.8.cloned.1.call-done) | copy-start | bytes 1769476
  1345.0 33.7 %collective-permute-start.37 = (bf16[2,192,384]{2,1,0:T(8,128)(2,1)}, bf16[2,192,384]{2,1,0:T(8,128)(2,1)S(1)}, u32[]{:S(2)}, u32[]{:S(2)}) collective-permute-start(bf16[2,192,384]{2,1,0:T(8,128)(2,1)} %get-tuple-element.214), channel_id=1, source_target_pairs={{0,0},{8,24},{16,16},{24,8},{1,1},{9,25},{17,17},{25,9},{2,2},{10,... | collective-permute-start | bytes 884744 | tf_op jit(solution)/shard_map/ppermute | solution.py:765
  1348.1 30.6 %collective-permute-start.38 = (bf16[2,192,384]{2,1,0:T(8,128)(2,1)}, bf16[2,192,384]{2,1,0:T(8,128)(2,1)S(1)}, u32[]{:S(2)}, u32[]{:S(2)}) collective-permute-start(bf16[2,192,384]{2,1,0:T(8,128)(2,1)} %get-tuple-element.215), channel_id=1, source_target_pairs={{0,8},{8,0},{16,24},{24,16},{1,9},{9,1},{17,25},{25,17},{2,10},{10... | collective-permute-start | bytes 884744 | tf_op jit(solution)/shard_map/ppermute | solution.py:765
  1348.5 30.1 %collective-permute-start.39 = (bf16[2,192,384]{2,1,0:T(8,128)(2,1)}, bf16[2,192,384]{2,1,0:T(8,128)(2,1)}, u32[]{:S(2)}, u32[]{:S(2)}) collective-permute-start(bf16[2,192,384]{2,1,0:T(8,128)(2,1)} %get-tuple-element.216), channel_id=1, source_target_pairs={{0,16},{8,8},{16,0},{24,24},{1,17},{9,9},{17,1},{25,25},{2,18},{10... | collective-permute-start | bytes 884744 | tf_op jit(solution)/shard_map/ppermute | solution.py:765
  1358.8 18.3 %collective-permute-start.40 = (bf16[2,192,384]{2,1,0:T(8,128)(2,1)S(1)}, bf16[2,192,384]{2,1,0:T(8,128)(2,1)S(1)}, u32[]{:S(2)}, u32[]{:S(2)}) collective-permute-start(bf16[2,192,384]{2,1,0:T(8,128)(2,1)S(1)} %get-tuple-element.132), channel_id=1, source_target_pairs={{0,0},{1,1},{2,8},{3,9},{4,16},{5,17},{6,24},{7,25},{8,2},{9,3},{1... | collective-permute-start | bytes 884744 | tf_op jit(solution)/shard_map/ppermute | solution.py:794
  (80 other events, 578.0 us)
Sparse Core Ops, SparseCore 0:
  143.0 218.8 all-gather.4
  425.6 160.4 all-gather.6
  660.5 189.0 reduce-scatter.3
  853.1 103.2 reduce-scatter.5
  1091.1 128.6 reduce-scatter.7

commit v5 on v4

--- a/solution.py
+++ b/solution.py
@@ -1068,8 +1068,8 @@
         jnp.concatenate(rolled(chunks, turns), axis=2), turn(w_out.astype(bf16))
     )
     out_weights = as_turned(out_full)
-    qkv_weights, mod_rows, fc1_low = lax.optimization_barrier(
-        (qkv_weights, mod_rows, w_fc1.astype(bf16))
+    qkv_weights, mod_rows, fc1_low, fc2_turned = lax.optimization_barrier(
+        (qkv_weights, mod_rows, w_fc1.astype(bf16), turn(w_fc2.astype(bf16)))
     )
     fc1_weights = gather_weight(fc1_low)
     first_seq = seq_ids[0]
@@ -1092,11 +1092,7 @@
     d_down = (gate_two * back_out).astype(bf16)
     d_down_group = jnp.concatenate(gather_rep(d_down))
 
-    fc2_low, act_one = lax.optimization_barrier((w_fc2.astype(bf16), act_one))
-    fc2_turned = turn(fc2_low)
-
     query_sent, pair_sent, qk_pre = qkv_product(spots, act_one_group, qkv_weights, image, gains)
-    pair_sent, fc2_turned = lax.optimization_barrier((pair_sent, fc2_turned))
 
     bunch = 2 * reps
     bunches = shards // bunch
@@ -1211,10 +1207,10 @@
         + jnp.concatenate([from_earlier, rest], axis=0)
     )
     d_pair_came = exchange(d_pair_own.astype(bf16).reshape(bunch, tok_rows, 2 * half_width))
-    up_fc2 = adam_step(w_fc2, m_fc2, v_fc2, turn(fc2_own).astype(f32), rate_fc2)
-    d_pair_came, down_terms, fc1_text, up_fc2 = lax.optimization_barrier(
-        (d_pair_came, down_terms, fc1_text, up_fc2)
-    )
+    d_pair_came, down_terms, fc1_text, fc2_own = lax.optimization_barrier(
+        (d_pair_came, down_terms, fc1_text, fc2_own)
+    )
+    g_fc2 = turn(fc2_own)
     fc1_text = scatter_weight(fc1_text)
     down_proj = reduce_rep(split_group(down_terms))
     output = mid + gate_two * down_proj
@@ -1250,8 +1246,8 @@
             for r in range(reps)
         ]
     )
-    qkv_terms, out_terms, fc1_image, fc1_text, leaving = lax.optimization_barrier(
-        (qkv_terms, out_terms, fc1_image, fc1_text, leaving)
+    qkv_terms, out_terms, fc1_image, fc1_text, g_fc2, leaving = lax.optimization_barrier(
+        (qkv_terms, out_terms, fc1_image, fc1_text, g_fc2, leaving)
     )
     leaving = jnp.broadcast_to(leaving[:, None], (reps, shards, *leaving.shape[1:]))
     came = lax.all_to_all(
@@ -1291,6 +1287,7 @@
     up_qkv = adam_step(w_qkv, m_qkv, v_qkv, g_qkv.astype(f32), rate_qkv)
     up_out = adam_step(w_out, m_out, v_out, g_out.astype(f32), rate_out)
     up_fc1 = adam_step(w_fc1, m_fc1, v_fc1, g_fc1.astype(f32), rate_fc1)
+    up_fc2 = adam_step(w_fc2, m_fc2, v_fc2, g_fc2.astype(f32), rate_fc2)
     up_gains = adam_step(gains, m_gains, v_gains, g_gains, rate_gains)
     return (
         output.astype(bf16),

time: 1400 us -> 1390 us (level)
  starting transfers between devices: 211 us -> 121 us
  Pallas kernels: 527 us -> 572 us
  waiting for transfers between devices: 397 us -> 436 us
    all_to_all x5, starting transfers between devices: 102 us -> 39.1 us  [exchange(): lax.all_to_all(value, 'shard', 0, 0, axis_index_groups=None if bunches ==...]
    pallas_call x1, Pallas kernels: 99.5 us -> 145 us  [ring_gather(): pl.pallas_call(functools.partial(ring_kernel, shards, count), in_specs=[a...]
    reduce_scatter x3, waiting for transfers between devices: 33 us -> 62.5 us  [scatter_weight(): lax.psum_scatter(terms.reshape(-1, *terms.shape[-2:]), 'shard', scatter_d...]
    ppermute x4, waiting for transfers between devices: 28.3 us -> 0.87 us  [turn(): return lax.ppermute(value, ('rep', 'shard'), pairs)]
    all_to_all x5, waiting for transfers between devices: 182 us -> 208 us  [exchange(): lax.all_to_all(value, 'shard', 0, 0, axis_index_groups=None if bunches ==...]
    ppermute x33, starting transfers between devices: 67.9 us -> 44 us  [over_rep(): return lax.ppermute(value, 'rep', [(r, target(r)) for r in range(count)])]
    unnamed x186 -> x194, local copies, waits for them, and re-layouts: 38.5 us -> 37.6 us
  transfers between devices with their start and end apart: 53 -> 53, of which waited for: 27 -> 25; matrix products, arithmetic and copies ran while one was open for 9% -> 8% of each run, Pallas kernels for 38% -> 41%
where the time goes in v5:
time: 1390 us; the launch traced here: 1380 us
  Pallas kernels  572 us (41%)
  waiting for transfers between devices  436 us (31%)
  starting transfers between devices  121 us (9%)
  other arithmetic  84.5 us (6%)
  local copies, waits for them, and re-layouts  73.7 us (5%)
  blocking collectives  68.8 us (5%)
  between operations  15.8 us (1%)
    all_to_all x5, waiting for transfers between devices, exchange(): lax.all_to_all(value, 'shard', 0, 0, axis_index_groups=None if bunches ==...  208 us
    pallas_call x1, Pallas kernels, ring_gather(): pl.pallas_call(functools.partial(ring_kernel, shards, count), in_specs=[a...  145 us
    ppermute x33, waiting for transfers between devices, over_rep(): return lax.ppermute(value, 'rep', [(r, target(r)) for r in range(count)])  114 us
    pallas_call x1, Pallas kernels, ring_scatter(): pl.pallas_call(functools.partial(ring_scatter_kernel, count), in_specs=[w...  107 us
    pallas_call x1, Pallas kernels, attention_back(): pl.pallas_call(attend_back_kernel, grid_spec=pltpu.PrefetchScalarGridSpec...  86.3 us
    all_to_all x1, blocking collectives, exchange(): lax.all_to_all(value, 'shard', 0, 0, axis_index_groups=None if bunches ==...  68.8 us
    pallas_call x4, Pallas kernels, gradient(): pl.pallas_call(functools.partial(gradient_kernel, blocks), grid_spec=pltp...  63.4 us
    reduce_scatter x3, waiting for transfers between devices, scatter_weight(): lax.psum_scatter(terms.reshape(-1, *terms.shape[-2:]), 'shard', scatter_d...  62.5 us
  transfers between devices with their start and end apart: 53, of which 25 were waited for; matrix products, arithmetic and copies ran while one was open for 8% of the time, Pallas kernels for 41%

profile of v5, /device:TPU:1, one launch (start us, length us, event | category | flops | bytes accessed | tf_op | source)
XLA Modules:
  0.0 1383.3 jit_solution(7154694525288394655)
XLA Ops:
  15.8 7.1 all-to-all-start
  24.0 3.4 collective-permute-start
  28.1 3.8 collective-permute-start.2
  31.9 3.1 collective-permute-start.3
  36.1 2.6 collective-permute-start.4
  43.1 145.0 %ring_gather.1 = (bf16[8,2,192,1152]{3,2,1,0:T(8,128)(2,1)}, bf16[8,2,192,384]{3,2,1,0:T(8,128)(2,1)}) custom-call(bf16[2,192,1152]{2,1,0:T(8,128)(2,1)} %pad_maximum_fusion.5.refs_0_, bf16[2,192,384]{2,1,0:T(8,128)(2,1)} %collective-permute-done.3.refs_1_), custom_call_target="tpu_custom_call" | custom-call | flops 1048576 | bytes 268435456 | tf_op jit(solution)/shard_map/ring_gather/pallas_call | solution.py:868
  190.7 2.8 fusion.20
  197.9 18.2 %collective-permute-done.6 = s32[320]{0:T(512)S(1)} collective-permute-done((s32[320]{0:T(512)S(1)}, s32[320]{0:T(512)S(1)}, u32[]{:S(2)}, u32[]{:S(2)}) %collective-permute-start.6) | collective-permute-done | bytes 1312 | tf_op jit(solution)/shard_map/ppermute | solution.py:765
  225.6 19.9 %qkv_product.1 = (bf16[8,320,192]{2,1,0:T(8,128)(2,1)S(1)}, bf16[8,320,384]{2,1,0:T(8,128)(2,1)S(1)}, f32[1280,768]{1,0:T(8,128)S(1)}) custom-call(s32[9]{0:T(128)S(1)} %pad_add_fusion.1.spots, bf16[1280,1536]{1,0:T(8,128)(2,1)S(1)} %pad_maximum_fusion.x_ref, bf16[8,2,192,1152]{3,2,1,0:T(8,128)(2,1)} %get-tuple-element.82.w0.w1, ...), custom_call_target="tpu_custom_call" | custom-call | flops 1073741824 | bytes 4194304 | tf_op jit(solution)/shard_map/qkv_product/pallas_call | solution.py:380
  249.9 7.2 all-to-all-start.1
  257.8 97.7 %all-to-all-done.1 = bf16[8,320,384]{2,1,0:T(8,128)(2,1)S(1)} async-done(((bf16[8,320,384]{2,1,0:T(8,128)(2,1)}), bf16[8,320,384]{2,1,0:T(8,128)(2,1)S(1)}, u32[]{:S(2)}, u32[]{:S(2)}) %all-to-all-start.1) | async-done | bytes 1966112 | tf_op jit(solution)/shard_map/all_to_all | solution.py:1103
  359.9 17.1 %collective-permute-done.11.before_ref = bf16[1280,384]{1,0:T(8,128)(2,1)S(1)} collective-permute-done((bf16[1280,384]{1,0:T(8,128)(2,1)S(1)}, bf16[1280,384]{1,0:T(8,128)(2,1)S(1)}, u32[]{:S(2)}, u32[]{:S(2)}) %collective-permute-start.11) | collective-permute-done | bytes 983072 | tf_op jit(solution)/shard_map/ppermute | solution.py:1121
  377.9 10.0 collective-permute-done.12.after_ref
  391.3 4.7 all-to-all-start.2
  396.1 4.0 pad_maximum_fusion.1.dy_ref
  400.0 23.3 %all-to-all-done.2 = bf16[8,320,192]{1,2,0:T(8,128)(2,1)} async-done(((bf16[8,320,192]{1,2,0:T(8,128)(2,1)}), bf16[8,320,192]{1,2,0:T(8,128)(2,1)}, u32[]{:S(2)}, u32[]{:S(2)}) %all-to-all-start.2) | async-done | bytes 983072 | tf_op jit(solution)/shard_map/all_to_all | solution.py:1103
  431.5 44.2 %attend.1 = (bf16[2560,192]{1,0:T(8,128)(2,1)S(1)}, f32[10,8,256]{2,1,0:T(8,128)S(1)}) custom-call(s32[10]{0:T(128)S(1)} %fusion.61.lo_ref, s32[10]{0:T(128)S(1)} %fusion.60.hi_ref, bf16[2560,192]{1,0:T(8,128)(2,1)S(1)} %bitcast.75, bf16[2560,384]{1,0:T(8,128)(2,1)S(1)} %bitcast.71, bf16[1280,384]{1,0:T(8,128)(2,1)S(1)} %copy-done.26, ...), custom_call_target="tpu_custom_call" | custom-call | flops 1073741824 | bytes 4194304 | tf_op jit(solution)/shard_map/attend/pallas_call | solution.py:197
  479.9 68.8 %all_to_all.40 = bf16[8,320,192]{1,2,0:T(8,128)(2,1)} all-to-all(bf16[8,320,192]{1,2,0:T(8,128)(2,1)} %copy.107), channel_id=1, replica_groups=mesh['rep'=4,'shard'=8] {'shard'}, dimensions={0} | all-to-all | bytes 1966080 | tf_op jit(solution)/shard_map/all_to_all | solution.py:1103
  552.5 7.3 forward_product.3
  566.3 21.6 %collective-permute-done.18 = bf16[320,1536]{1,0:T(8,128)(2,1)S(1)} collective-permute-done((bf16[320,1536]{1,0:T(8,128)(2,1)S(1)}, bf16[320,1536]{1,0:T(8,128)(2,1)S(1)}, u32[]{:S(2)}, u32[]{:S(2)}) %collective-permute-start.18) | collective-permute-done | bytes 983072 | tf_op jit(solution)/shard_map/ppermute | solution.py:765
  589.3 3.4 add_convert_fusion.5
  595.4 19.4 %collective-permute-done.20 = bf16[320,1536]{1,0:T(8,128)(2,1)S(1)} collective-permute-done((bf16[320,1536]{1,0:T(8,128)(2,1)S(1)}, bf16[320,1536]{1,0:T(8,128)(2,1)S(1)}, u32[]{:S(2)}, u32[]{:S(2)}) %collective-permute-start.20) | collective-permute-done | bytes 983072 | tf_op jit(solution)/shard_map/ppermute | solution.py:765
  619.5 19.2 %forward_product.4 = (bf16[1280,1536]{1,0:T(8,128)(2,1)S(1)}, bf16[1280,1536]{1,0:T(8,128)(2,1)S(1)}) custom-call(s32[9]{0:T(128)S(1)} %pad_add_fusion.1.spots, bf16[1280,1536]{1,0:T(8,128)(2,1)S(1)} %pad_maximum_fusion.2.x_ref, bf16[8,2,192,1536]{3,2,1,0:T(8,128)(2,1)} %bitcast.78, bf16[8,2,192,1536]{3,2,1,0:T(8,128)(2,1)} %bitcast.79, ...), custom_call_target="tpu_custom_call" | custom-call | flops 754974720 | bytes 4194304 | tf_op jit(solution)/shard_map/forward_product/pallas_call | solution.py:540
  640.7 20.9 %gradient.4 = bf16[4,2,2,768,384]{4,3,2,1,0:T(8,128)(2,1)} custom-call(s32[9]{0:T(128)S(1)} %pad_add_fusion.1.spots, bf16[1280,1536]{1,0:T(8,128)(2,1)S(1)} %get-tuple-element.96.x_ref, bf16[1280,1536]{1,0:T(8,128)(2,1)} %pad_maximum_fusion.1.dy_ref, s32[1280,1]{1,0:T(8,128)S(1)} %convert_element_type.210.image_ref), custom_call_target="tpu_custom_call" | custom-call | flops 754974720 | bytes 4194304 | tf_op jit(solution)/shard_map/gradient/pallas_call | solution.py:737
  661.6 18.3 %backward_product.4.dy_ref = bf16[1280,1536]{1,0:T(8,128)(2,1)S(1)} custom-call(s32[9]{0:T(128)S(1)} %pad_add_fusion.1.spots, bf16[1280,1536]{1,0:T(8,128)(2,1)} %pad_maximum_fusion.1.dy_ref, bf16[4,2,2,768,384]{4,3,2,1,0:T(8,128)(2,1)} %bitcast.82, bf16[4,2,2,768,384]{4,3,2,1,0:T(8,128)(2,1)} %bitcast.83, s32[1280,1]{1,0:T(8,128)S(1)} %convert_element_type.210.image_ref, ...), custom_call_target="tpu_custom_call" | custom-call | flops 754974720 | bytes 4194304 | tf_op jit(solution)/shard_map/backward_product/pallas_call | solution.py:651
  681.8 15.0 %backward_product.5 = bf16[1280,1536]{1,0:T(8,128)(2,1)S(1)} custom-call(s32[9]{0:T(128)S(1)} %pad_add_fusion.1.spots, bf16[1280,1536]{1,0:T(8,128)(2,1)} %copy-done.4, bf16[8,2,192,1536]{3,2,1,0:T(8,128)(2,1)} %bitcast.80, bf16[8,2,192,1536]{3,2,1,0:T(8,128)(2,1)} %bitcast.81, s32[1280,1]{1,0:T(8,128)S(1)} %convert_element_type.210.image_ref), custom_call_target="tpu_custom_call" | custom-call | flops 754974720 | bytes 4194304 | tf_op jit(solution)/shard_map/backward_product/pallas_call | solution.py:651
  698.4 2.9 collective-permute-done.23
  702.4 20.4 %gradient.5 = (bf16[8,1,192,1536]{3,2,1,0:T(8,128)(2,1)}, bf16[8,1,192,1536]{3,2,1,0:T(8,128)(2,1)}) custom-call(s32[9]{0:T(128)S(1)} %pad_add_fusion.1.spots, bf16[1280,1536]{1,0:T(8,128)(2,1)S(1)} %copy-done.3, bf16[1280,1536]{1,0:T(8,128)(2,1)} %copy-done.4, s32[1280,1]{1,0:T(8,128)S(1)} %convert_element_type.210.image_ref), custom_call_target="tpu_custom_call" | custom-call | flops 754974720 | bytes 4194304 | tf_op jit(solution)/shard_map/gradient/pallas_call | solution.py:737
  731.8 20.0 %collective-permute-done.26 = bf16[320,1536]{1,0:T(8,128)(2,1)S(1)} collective-permute-done((bf16[320,1536]{1,0:T(8,128)(2,1)S(1)}, bf16[320,1536]{1,0:T(8,128)(2,1)S(1)}, u32[]{:S(2)}, u32[]{:S(2)}) %collective-permute-start.26) | collective-permute-done | bytes 983072 | tf_op jit(solution)/shard_map/ppermute | solution.py:765
  758.0 8.7 backward_product.6
  770.2 12.7 all-to-all-start.4
  786.9 7.4 gradient.6
  794.4 43.3 %all-to-all-done.4 = bf16[8,320,192]{1,2,0:T(8,128)(2,1)} async-done(((bf16[8,320,192]{1,2,0:T(8,128)(2,1)}), bf16[8,320,192]{1,2,0:T(8,128)(2,1)}, u32[]{:S(2)}, u32[]{:S(2)}) %all-to-all-start.4) | async-done | bytes 983072 | tf_op jit(solution)/shard_map/all_to_all | solution.py:1103
  840.1 86.3 %attend_back.1 = (bf16[2560,192]{1,0:T(8,128)(2,1)}, bf16[1280,384]{1,0:T(8,128)(2,1)}, bf16[1280,384]{1,0:T(8,128)(2,1)}, f32[2560,384]{1,0:T(8,128)}) custom-call(s32[10]{0:T(128)} %copy-done.33, s32[10]{0:T(128)} %copy-done.32, bf16[2560,192]{1,0:T(8,128)(2,1)} %bitcast.74, bf16[2560,384]{1,0:T(8,128)(2,1)} %bitcast.72, bf16[1280,384]{1,0:T(8,128)(2,1)} %copy-done.25, ...), custom_call_target="tpu_custom_call" | custom-call | flops 25769803776 | bytes 8388608 | tf_op jit(solution)/shard_map/attend_back/pallas_call | solution.py:237
  927.7 4.9 collective-permute-start.29
  935.1 10.2 all-to-all-start.6
  945.3 22.3 %collective-permute-done.28 = bf16[1280,384]{1,0:T(8,128)(2,1)} collective-permute-done((bf16[1280,384]{1,0:T(8,128)(2,1)}, bf16[1280,384]{1,0:T(8,128)(2,1)}, u32[]{:S(2)}, u32[]{:S(2)}) %collective-permute-start.28) | collective-permute-done | bytes 983072 | tf_op jit(solution)/shard_map/ppermute | solution.py:1121
  967.6 4.4 add_convert_fusion
  972.0 22.4 %all-to-all-done.6 = bf16[8,320,192]{1,2,0:T(8,128)(2,1)} async-done(((bf16[8,320,192]{1,2,0:T(8,128)(2,1)}), bf16[8,320,192]{1,2,0:T(8,128)(2,1)}, u32[]{:S(2)}, u32[]{:S(2)}) %all-to-all-start.6) | async-done | bytes 983072 | tf_op jit(solution)/shard_map/all_to_all | solution.py:1103
  994.3 4.3 all-to-all-start.5
  1001.0 15.8 %forward_product.5 = bf16[1280,1536]{1,0:T(8,128)(2,1)S(1)} custom-call(s32[9]{0:T(128)S(1)} %pad_add_fusion.1.spots, bf16[1280,1536]{1,0:T(8,128)(2,1)S(1)} %copy-done.10, bf16[4,2,2,768,384]{4,3,2,1,0:T(8,128)(2,1)} %bitcast.84, bf16[4,2,2,768,384]{4,3,2,1,0:T(8,128)(2,1)} %bitcast.85, s32[1280,1]{1,0:T(8,128)S(1)} %convert_element_type.210.image_ref), custom_call_target="tpu_custom_call" | custom-call | flops 754974720 | bytes 4194304 | tf_op jit(solution)/shard_map/forward_product/pallas_call | solution.py:540
  1021.2 21.7 %all-to-all-done.5.kv_ref = bf16[8,320,384]{2,1,0:T(8,128)(2,1)} async-done(((bf16[8,320,384]{2,1,0:T(8,128)(2,1)}), bf16[8,320,384]{2,1,0:T(8,128)(2,1)}, u32[]{:S(2)}, u32[]{:S(2)}) %all-to-all-start.5) | async-done | bytes 1966112 | tf_op jit(solution)/shard_map/all_to_all | solution.py:1103
  1046.4 8.6 norm_back.1
  1055.0 13.2 backward_product.7
  1068.2 2.7 fusion.82
  1083.8 14.8 %gradient.7.refs_0_ = bf16[8,2,192,1152]{3,2,1,0:T(8,128)(2,1)} custom-call(s32[9]{0:T(128)S(1)} %pad_add_fusion.1.spots, bf16[1280,1536]{1,0:T(8,128)(2,1)} %copy-done.1, bf16[1280,1152]{1,0:T(8,128)(2,1)S(1)} %copy-done.15, s32[1280,1]{1,0:T(8,128)S(1)} %convert_element_type.210.image_ref), custom_call_target="tpu_custom_call" | custom-call | flops 566231040 | bytes 4194304 | tf_op jit(solution)/shard_map/gradient/pallas_call | solution.py:737
  1103.0 3.7 collective-permute-done.35
  1106.7 2.6 constant_dynamic-update-slice_fusion.7
  1109.3 4.3 fusion.79
  1113.7 4.1 multiply_dynamic-update-slice_fusion.1
  1120.0 16.4 %collective-permute-done.32 = bf16[320,1536]{1,0:T(8,128)(2,1)} collective-permute-done((bf16[320,1536]{1,0:T(8,128)(2,1)}, bf16[320,1536]{1,0:T(8,128)(2,1)}, u32[]{:S(2)}, u32[]{:S(2)}) %collective-permute-start.32) | collective-permute-done | bytes 983072 | tf_op jit(solution)/shard_map/ppermute | solution.py:765
  1136.5 3.4 fusion.21
  1139.9 4.0 fusion.49
  1144.1 62.5 %reduce-scatter.8.cloned.1.call-done = bf16[1,192,1536]{2,1,0:T(8,128)(2,1)} async-done(((bf16[8,192,1536]{2,1,0:T(8,128)(2,1)}), bf16[1,192,1536]{2,1,0:T(8,128)(2,1)}) %reduce-scatter.8.cloned.1.call-update) | async-done | bytes 589840 | tf_op jit(solution)/shard_map/reduce_scatter | solution.py:966
  1207.8 5.5 all-to-all-start.7
  1214.3 3.0 copy-done.7
  1217.3 107.2 %ring_scatter.1 = (bf16[2,192,1152]{2,1,0:T(8,128)(2,1)S(1)}, bf16[2,192,384]{2,1,0:T(8,128)(2,1)S(1)}) custom-call(bf16[8,2,192,1152]{3,2,1,0:T(8,128)(2,1)S(1)} %copy-done.7, bf16[8,2,192,384]{3,2,1,0:T(8,128)(2,1)S(1)} %bitcast.73), custom_call_target="tpu_custom_call" | custom-call | flops 1048576 | bytes 268435456 | tf_op jit(solution)/shard_map/ring_scatter/pallas_call | solution.py:947
  1324.6 6.3 fusion.65
  1330.9 4.3 fusion.68
  1337.4 3.1 collective-permute-start.37
  1341.0 3.7 collective-permute-start.39
  1351.2 8.9 collective-permute-start.40
  1360.1 7.7 fusion.77
  1372.0 4.5 fusion.74
  (413 shorter events, 157.3 us)
Async XLA Ops:
  15.8 172.3 %all-to-all-start = ((bf16[32,4,2304]{2,1,0:T(4,128)(2,1)}), bf16[32,4,2304]{2,1,0:T(4,128)(2,1)S(1)}, u32[]{:S(2)}, u32[]{:S(2)}) async-start(bf16[32,4,2304]{2,1,0:T(4,128)(2,1)} %reshape.442), calls=%async_computation | async-start | bytes 1179648 | tf_op jit(solution)/shard_map/all_to_all | solution.py:1041
  22.9 403.0 %all-gather.5.cloned.1.call-start = ((), (), s32[]{:S(2)}) async-start(), calls=%async_computation.14 | async-start | bytes 10616832 | tf_op jit(solution)/shard_map/all_gather | solution.py:798
  24.0 16.0 %collective-permute-start = (bf16[2,192,384]{2,1,0:T(8,128)(2,1)}, bf16[2,192,384]{2,1,0:T(8,128)(2,1)}, u32[]{:S(2)}, u32[]{:S(2)}) collective-permute-start(bf16[2,192,384]{2,1,0:T(8,128)(2,1)} %get-tuple-element.214), channel_id=1, source_target_pairs={{0,0},{8,24},{16,16},{24,8},{1,1},{9,25},{17,17},{25,9},{2,2},{10,... | collective-permute-start | bytes 884744 | tf_op jit(solution)/shard_map/ppermute | solution.py:765
  27.4 12.5 collective-permute-start.1
  28.1 11.8 collective-permute-start.2
  31.9 11.2 collective-permute-start.3
  36.1 152.3 %collective-permute-start.4 = (bf16[2,768,384]{2,1,0:T(8,128)(2,1)}, bf16[2,768,384]{2,1,0:T(8,128)(2,1)}, u32[]{:S(2)}, u32[]{:S(2)}) collective-permute-start(bf16[2,768,384]{2,1,0:T(8,128)(2,1)} %convert_element_type.203), channel_id=1, source_target_pairs={{0,0},{1,1},{2,8},{3,9},{4,16},{5,17},{6,24},{7,25},{8,2},{9,3},{1... | collective-permute-start | bytes 3538952 | tf_op jit(solution)/shard_map/ppermute | solution.py:794
  42.2 146.9 %copy-start.40 = (bf16[320,1536]{1,0:T(8,128)(2,1)S(1)}, bf16[320,1536]{1,0:T(8,128)(2,1)}, u32[]{:S(2)}) copy-start(bf16[320,1536]{1,0:T(8,128)(2,1)} %param.23) | copy-start | bytes 2949124
  193.6 26.6 %collective-permute-start.9 = (bf16[320,1536]{1,0:T(8,128)(2,1)}, bf16[320,1536]{1,0:T(8,128)(2,1)S(1)}, u32[]{:S(2)}, u32[]{:S(2)}) collective-permute-start(bf16[320,1536]{1,0:T(8,128)(2,1)} %get-tuple-element.241), channel_id=1, source_target_pairs={{0,16},{8,24},{16,0},{24,8},{1,17},{9,25},{17,1},{25,9},{2,18},{10... | collective-permute-start | bytes 2949128 | tf_op jit(solution)/shard_map/ppermute | solution.py:765
  195.5 20.6 %collective-permute-start.6 = (s32[320]{0:T(512)S(1)}, s32[320]{0:T(512)S(1)}, u32[]{:S(2)}, u32[]{:S(2)}) collective-permute-start(s32[320]{0:T(512)S(1)} %copy-done.89), channel_id=1, source_target_pairs={{0,16},{8,24},{16,0},{24,8},{1,17},{9,25},{17,1},{25,9},{2,18},{10... | collective-permute-start | bytes 3848 | tf_op jit(solution)/shard_map/ppermute | solution.py:765
  195.6 22.9 %collective-permute-start.5 = (s32[320]{0:T(512)S(1)}, s32[320]{0:T(512)S(1)}, u32[]{:S(2)}, u32[]{:S(2)}) collective-permute-start(s32[320]{0:T(512)S(1)} %copy-done.89), channel_id=1, source_target_pairs={{0,8},{8,0},{16,24},{24,16},{1,9},{9,1},{17,25},{25,17},{2,10},{10... | collective-permute-start | bytes 3848 | tf_op jit(solution)/shard_map/ppermute | solution.py:765
  216.1 3.2 collective-permute-start.7
  219.7 2.8 collective-permute-start.8
  220.1 3.8 collective-permute-start.10
  249.9 105.6 %all-to-all-start.1 = ((bf16[8,320,384]{2,1,0:T(8,128)(2,1)}), bf16[8,320,384]{2,1,0:T(8,128)(2,1)S(1)}, u32[]{:S(2)}, u32[]{:S(2)}) async-start(bf16[8,320,384]{2,1,0:T(8,128)(2,1)} %copy-done.21), calls=%async_computation.1 | async-start | bytes 3932160 | tf_op jit(solution)/shard_map/all_to_all | solution.py:1103
  257.1 102.7 %collective-permute-start.14 = (bf16[320,1536]{1,0:T(8,128)(2,1)}, bf16[320,1536]{1,0:T(8,128)(2,1)}, u32[]{:S(2)}, u32[]{:S(2)}) collective-permute-start(bf16[320,1536]{1,0:T(8,128)(2,1)} %get-tuple-element.240), channel_id=1, source_target_pairs={{0,16},{8,24},{16,0},{24,8},{1,17},{9,25},{17,1},{25,9},{2,18},{10... | collective-permute-start | bytes 2949128 | tf_op jit(solution)/shard_map/ppermute | solution.py:765
  355.5 72.8 %copy-start.8 = (bf16[8,320,384]{2,1,0:T(8,128)(2,1)}, bf16[8,320,384]{2,1,0:T(8,128)(2,1)S(1)}, u32[]{:S(2)}) copy-start(bf16[8,320,384]{2,1,0:T(8,128)(2,1)S(1)} %all-to-all-done.1) | copy-start | bytes 5898244
  355.7 21.3 %collective-permute-start.11 = (bf16[1280,384]{1,0:T(8,128)(2,1)S(1)}, bf16[1280,384]{1,0:T(8,128)(2,1)S(1)}, u32[]{:S(2)}, u32[]{:S(2)}) collective-permute-start(bf16[1280,384]{1,0:T(8,128)(2,1)S(1)} %bitcast.94), channel_id=1, source_target_pairs={{0,2},{1,3},{2,4},{3,5},{4,6},{5,7},{8,10},{9,11},{10,12},{11,13},... | collective-permute-start | bytes 2949128 | tf_op jit(solution)/shard_map/ppermute | solution.py:1121
  357.1 30.8 %collective-permute-start.12 = (bf16[1280,384]{1,0:T(8,128)(2,1)S(1)}, bf16[1280,384]{1,0:T(8,128)(2,1)S(1)}, u32[]{:S(2)}, u32[]{:S(2)}) collective-permute-start(bf16[1280,384]{1,0:T(8,128)(2,1)S(1)} %bitcast.93), channel_id=1, source_target_pairs={{2,0},{3,1},{4,2},{5,3},{6,4},{7,5},{10,8},{11,9},{12,10},{13,11},... | collective-permute-start | bytes 2949128 | tf_op jit(solution)/shard_map/ppermute | solution.py:1121
  358.4 37.7 %collective-permute-start.13 = (bf16[320,1536]{1,0:T(8,128)(2,1)}, bf16[320,1536]{1,0:T(8,128)(2,1)}, u32[]{:S(2)}, u32[]{:S(2)}) collective-permute-start(bf16[320,1536]{1,0:T(8,128)(2,1)} %get-tuple-element.240), channel_id=1, source_target_pairs={{0,8},{8,0},{16,24},{24,16},{1,9},{9,1},{17,25},{25,17},{2,10},{10... | collective-permute-start | bytes 2949128 | tf_op jit(solution)/shard_map/ppermute | solution.py:765
  359.8 36.3 %collective-permute-start.15 = (bf16[320,1536]{1,0:T(8,128)(2,1)}, bf16[320,1536]{1,0:T(8,128)(2,1)}, u32[]{:S(2)}, u32[]{:S(2)}) collective-permute-start(bf16[320,1536]{1,0:T(8,128)(2,1)} %collective-permute-done.14), channel_id=1, source_target_pairs={{0,8},{8,0},{16,24},{24,16},{1,9},{9,1},{17,25},{25,17},{2,10},{10... | collective-permute-start | bytes 2949128 | tf_op jit(solution)/shard_map/ppermute | solution.py:765
  391.3 32.0 %all-to-all-start.2 = ((bf16[8,320,192]{1,2,0:T(8,128)(2,1)}), bf16[8,320,192]{1,2,0:T(8,128)(2,1)}, u32[]{:S(2)}, u32[]{:S(2)}) async-start(bf16[8,320,192]{1,2,0:T(8,128)(2,1)} %copy.104), calls=%async_computation.2 | async-start | bytes 2359296 | tf_op jit(solution)/shard_map/all_to_all | solution.py:1103
  396.0 265.6 %all-gather.7.cloned.1.call-start = ((), (), s32[]{:S(2)}) async-start(), calls=%async_computation.15 | async-start | bytes 10616832 | tf_op jit(solution)/shard_map/all_gather | solution.py:798
  425.8 595.3 %reduce-scatter.4.cloned.1.call-start = ((), (), s32[]{:S(2)}) async-start(), calls=%async_computation.11 | async-start | bytes 10616832 | tf_op jit(solution)/shard_map/reduce_scatter | solution.py:966
  427.8 47.9 %copy-start.32 = (s32[10]{0:T(128)}, s32[10]{0:T(128)S(1)}, u32[]{:S(2)}) copy-start(s32[10]{0:T(128)S(1)} %fusion.60.hi_ref) | copy-start | bytes 124
  427.9 47.9 %copy-start.33 = (s32[10]{0:T(128)}, s32[10]{0:T(128)S(1)}, u32[]{:S(2)}) copy-start(s32[10]{0:T(128)S(1)} %fusion.61.lo_ref) | copy-start | bytes 124
  479.9 71.3 %copy-start = (bf16[8,2,192,384]{3,2,1,0:T(8,128)(2,1)S(1)}, bf16[8,2,192,384]{3,2,1,0:T(8,128)(2,1)}, u32[]{:S(2)}) copy-start(bf16[8,2,192,384]{3,2,1,0:T(8,128)(2,1)} %get-tuple-element.91) | copy-start | bytes 7077892
  560.8 27.1 %copy-start.16 = (bf16[1280,1536]{1,0:T(8,128)(2,1)}, bf16[1280,1536]{1,0:T(8,128)(2,1)S(1)}, u32[]{:S(2)}) copy-start(bf16[1280,1536]{1,0:T(8,128)(2,1)S(1)} %get-tuple-element.92) | copy-start | bytes 11796484
  560.9 3.7 collective-permute-start.17
  562.4 3.8 collective-permute-start.16
  564.9 23.0 %collective-permute-start.18 = (bf16[320,1536]{1,0:T(8,128)(2,1)S(1)}, bf16[320,1536]{1,0:T(8,128)(2,1)S(1)}, u32[]{:S(2)}, u32[]{:S(2)}) collective-permute-start(bf16[320,1536]{1,0:T(8,128)(2,1)S(1)} %add_convert_fusion.6), channel_id=1, source_target_pairs={{0,16},{8,24},{16,0},{24,8},{1,17},{9,25},{17,1},{25,9},{2,18},{10... | collective-permute-start | bytes 2949128 | tf_op jit(solution)/shard_map/ppermute | solution.py:765
  592.7 22.1 %collective-permute-start.20 = (bf16[320,1536]{1,0:T(8,128)(2,1)S(1)}, bf16[320,1536]{1,0:T(8,128)(2,1)S(1)}, u32[]{:S(2)}, u32[]{:S(2)}) collective-permute-start(bf16[320,1536]{1,0:T(8,128)(2,1)S(1)} %add_convert_fusion.5), channel_id=1, source_target_pairs={{0,16},{8,24},{16,0},{24,8},{1,17},{9,25},{17,1},{25,9},{2,18},{10... | collective-permute-start | bytes 2949128 | tf_op jit(solution)/shard_map/ppermute | solution.py:765
  593.9 23.1 %collective-permute-start.19 = (bf16[320,1536]{1,0:T(8,128)(2,1)S(1)}, bf16[320,1536]{1,0:T(8,128)(2,1)S(1)}, u32[]{:S(2)}, u32[]{:S(2)}) collective-permute-start(bf16[320,1536]{1,0:T(8,128)(2,1)S(1)} %add_convert_fusion.5), channel_id=1, source_target_pairs={{0,8},{8,0},{16,24},{24,16},{1,9},{9,1},{17,25},{25,17},{2,10},{10... | collective-permute-start | bytes 2949128 | tf_op jit(solution)/shard_map/ppermute | solution.py:765
  614.9 4.3 collective-permute-start.21
  696.8 29.0 %copy-start.5 = (bf16[1280,1536]{1,0:T(8,128)(2,1)}, bf16[1280,1536]{1,0:T(8,128)(2,1)S(1)}, u32[]{:S(2)}) copy-start(bf16[1280,1536]{1,0:T(8,128)(2,1)S(1)} %backward_product.5) | copy-start | bytes 11796484
  697.9 3.4 collective-permute-start.23
  698.3 24.4 %collective-permute-start.22 = (bf16[320,1536]{1,0:T(8,128)(2,1)}, bf16[320,1536]{1,0:T(8,128)(2,1)S(1)}, u32[]{:S(2)}, u32[]{:S(2)}) collective-permute-start(bf16[320,1536]{1,0:T(8,128)(2,1)} %get-tuple-element.196), channel_id=1, source_target_pairs={{0,8},{8,0},{16,24},{24,16},{1,9},{9,1},{17,25},{25,17},{2,10},{10... | collective-permute-start | bytes 2949128 | tf_op jit(solution)/shard_map/ppermute | solution.py:765
  701.6 23.1 %collective-permute-start.24 = (bf16[320,1536]{1,0:T(8,128)(2,1)S(1)}, bf16[320,1536]{1,0:T(8,128)(2,1)S(1)}, u32[]{:S(2)}, u32[]{:S(2)}) collective-permute-start(bf16[320,1536]{1,0:T(8,128)(2,1)S(1)} %add_convert_fusion.4), channel_id=1, source_target_pairs={{0,16},{8,24},{16,0},{24,8},{1,17},{9,25},{17,1},{25,9},{2,18},{10... | collective-permute-start | bytes 2949128 | tf_op jit(solution)/shard_map/ppermute | solution.py:765
  729.7 22.2 %collective-permute-start.26 = (bf16[320,1536]{1,0:T(8,128)(2,1)S(1)}, bf16[320,1536]{1,0:T(8,128)(2,1)S(1)}, u32[]{:S(2)}, u32[]{:S(2)}) collective-permute-start(bf16[320,1536]{1,0:T(8,128)(2,1)S(1)} %multiply_convert_fusion), channel_id=1, source_target_pairs={{0,16},{8,24},{16,0},{24,8},{1,17},{9,25},{17,1},{25,9},{2,18},{10... | collective-permute-start | bytes 2949128 | tf_op jit(solution)/shard_map/ppermute | solution.py:765
  730.4 23.5 %collective-permute-start.25 = (bf16[320,1536]{1,0:T(8,128)(2,1)S(1)}, bf16[320,1536]{1,0:T(8,128)(2,1)S(1)}, u32[]{:S(2)}, u32[]{:S(2)}) collective-permute-start(bf16[320,1536]{1,0:T(8,128)(2,1)S(1)} %multiply_convert_fusion), channel_id=1, source_target_pairs={{0,8},{8,0},{16,24},{24,16},{1,9},{9,1},{17,25},{25,17},{2,10},{10... | collective-permute-start | bytes 2949128 | tf_op jit(solution)/shard_map/ppermute | solution.py:765
  751.8 4.2 collective-permute-start.27
  770.2 67.4 %all-to-all-start.4 = ((bf16[8,320,192]{1,2,0:T(8,128)(2,1)}), bf16[8,320,192]{1,2,0:T(8,128)(2,1)}, u32[]{:S(2)}, u32[]{:S(2)}) async-start(bf16[8,320,192]{1,2,0:T(8,128)(2,1)} %copy.109), calls=%async_computation.4 | async-start | bytes 2359296 | tf_op jit(solution)/shard_map/all_to_all | solution.py:1103
  783.0 361.1 %reduce-scatter.6.cloned.1.call-start = ((), (), s32[]{:S(2)}) async-start(), calls=%async_computation.12 | async-start | bytes 5308416 | tf_op jit(solution)/shard_map/reduce_scatter | solution.py:966
  926.4 41.2 %collective-permute-start.28 = (bf16[1280,384]{1,0:T(8,128)(2,1)}, bf16[1280,384]{1,0:T(8,128)(2,1)}, u32[]{:S(2)}, u32[]{:S(2)}) collective-permute-start(bf16[1280,384]{1,0:T(8,128)(2,1)} %get-tuple-element.106), channel_id=1, source_target_pairs={{2,0},{3,1},{4,2},{5,3},{6,4},{7,5},{10,8},{11,9},{12,10},{13,11},... | collective-permute-start | bytes 2949128 | tf_op jit(solution)/shard_map/ppermute | solution.py:1121
  927.7 39.9 %collective-permute-start.29 = (bf16[1280,384]{1,0:T(8,128)(2,1)}, bf16[1280,384]{1,0:T(8,128)(2,1)}, u32[]{:S(2)}, u32[]{:S(2)}) collective-permute-start(bf16[1280,384]{1,0:T(8,128)(2,1)} %get-tuple-element.107), channel_id=1, source_target_pairs={{0,2},{1,3},{2,4},{3,5},{4,6},{5,7},{8,10},{9,11},{10,12},{11,13},... | collective-permute-start | bytes 2949128 | tf_op jit(solution)/shard_map/ppermute | solution.py:1121
  935.1 59.2 %all-to-all-start.6 = ((bf16[8,320,192]{1,2,0:T(8,128)(2,1)}), bf16[8,320,192]{1,2,0:T(8,128)(2,1)}, u32[]{:S(2)}, u32[]{:S(2)}) async-start(bf16[8,320,192]{1,2,0:T(8,128)(2,1)} %copy.112), calls=%async_computation.7 | async-start | bytes 2359296 | tf_op jit(solution)/shard_map/all_to_all | solution.py:1103
  994.3 48.6 %all-to-all-start.5 = ((bf16[8,320,384]{2,1,0:T(8,128)(2,1)}), bf16[8,320,384]{2,1,0:T(8,128)(2,1)}, u32[]{:S(2)}, u32[]{:S(2)}) async-start(bf16[8,320,384]{2,1,0:T(8,128)(2,1)} %bitcast.87), calls=%async_computation.5 | async-start | bytes 3932160 | tf_op jit(solution)/shard_map/all_to_all | solution.py:1103
  998.7 207.9 %reduce-scatter.8.cloned.1.call-start = ((), (), s32[]{:S(2)}) async-start(), calls=%async_computation.13 | async-start | bytes 5308416 | tf_op jit(solution)/shard_map/reduce_scatter | solution.py:966
  1070.9 4.3 collective-permute-start.34
  1074.4 24.3 %collective-permute-start.31 = (bf16[320,1536]{1,0:T(8,128)(2,1)}, bf16[320,1536]{1,0:T(8,128)(2,1)}, u32[]{:S(2)}, u32[]{:S(2)}) collective-permute-start(bf16[320,1536]{1,0:T(8,128)(2,1)} %get-tuple-element.195), channel_id=1, source_target_pairs={{0,8},{8,0},{16,24},{24,16},{1,9},{9,1},{17,25},{25,17},{2,10},{10... | collective-permute-start | bytes 2949128 | tf_op jit(solution)/shard_map/ppermute | solution.py:765
  1074.4 28.5 %collective-permute-start.33 = (bf16[320,1536]{1,0:T(8,128)(2,1)}, bf16[320,1536]{1,0:T(8,128)(2,1)}, u32[]{:S(2)}, u32[]{:S(2)}) collective-permute-start(bf16[320,1536]{1,0:T(8,128)(2,1)} %get-tuple-element.192), channel_id=1, source_target_pairs={{0,8},{8,0},{16,24},{24,16},{1,9},{9,1},{17,25},{25,17},{2,10},{10... | collective-permute-start | bytes 2949128 | tf_op jit(solution)/shard_map/ppermute | solution.py:765
  1077.7 29.0 %collective-permute-start.35 = (bf16[320,1536]{1,0:T(8,128)(2,1)}, bf16[320,1536]{1,0:T(8,128)(2,1)}, u32[]{:S(2)}, u32[]{:S(2)}) collective-permute-start(bf16[320,1536]{1,0:T(8,128)(2,1)} %add_convert_fusion.1), channel_id=1, source_target_pairs={{0,16},{8,24},{16,0},{24,8},{1,17},{9,25},{17,1},{25,9},{2,18},{10... | collective-permute-start | bytes 2949128 | tf_op jit(solution)/shard_map/ppermute | solution.py:765
  1079.3 40.7 %collective-permute-start.30 = (bf16[320,1536]{1,0:T(8,128)(2,1)}, bf16[320,1536]{1,0:T(8,128)(2,1)}, u32[]{:S(2)}, u32[]{:S(2)}) collective-permute-start(bf16[320,1536]{1,0:T(8,128)(2,1)} %get-tuple-element.194), channel_id=1, source_target_pairs={{0,8},{8,0},{16,24},{24,16},{1,9},{9,1},{17,25},{25,17},{2,10},{10... | collective-permute-start | bytes 2949128 | tf_op jit(solution)/shard_map/ppermute | solution.py:765
  1080.0 64.0 %collective-permute-start.36 = (bf16[2,768,384]{2,1,0:T(8,128)(2,1)}, bf16[2,768,384]{2,1,0:T(8,128)(2,1)}, u32[]{:S(2)}, u32[]{:S(2)}) collective-permute-start(bf16[2,768,384]{2,1,0:T(8,128)(2,1)} %reduce-scatter.4.cloned.1.call-done), channel_id=1, source_target_pairs={{0,0},{1,1},{2,8},{3,9},{4,16},{5,17},{6,24},{7,25},{8,2},{9,3},{1... | collective-permute-start | bytes 3538952 | tf_op jit(solution)/shard_map/ppermute | solution.py:794
  1101.2 35.3 %collective-permute-start.32 = (bf16[320,1536]{1,0:T(8,128)(2,1)}, bf16[320,1536]{1,0:T(8,128)(2,1)}, u32[]{:S(2)}, u32[]{:S(2)}) collective-permute-start(bf16[320,1536]{1,0:T(8,128)(2,1)} %add_convert_fusion.3), channel_id=1, source_target_pairs={{0,16},{8,24},{16,0},{24,8},{1,17},{9,25},{17,1},{25,9},{2,18},{10... | collective-permute-start | bytes 2949128 | tf_op jit(solution)/shard_map/ppermute | solution.py:765
  1144.0 69.2 %copy-start.80 = (s32[32,2]{1,0:T(8,128)S(1)}, s32[32,2]{1,0:T(8,128)}, u32[]{:S(2)}) copy-start(s32[32,2]{1,0:T(8,128)} %copy-done.79) | copy-start | bytes 772
  1207.8 127.5 %all-to-all-start.7 = ((f32[32,4,2432]{2,1,0:T(4,128)}), f32[32,4,2432]{2,1,0:T(4,128)}, u32[]{:S(2)}, u32[]{:S(2)}) async-start(f32[32,4,2432]{2,1,0:T(4,128)} %bitcast.88), calls=%async_computation.10 | async-start | bytes 2490368 | tf_op jit(solution)/shard_map/all_to_all | solution.py:1253
  1217.3 107.2 %copy-start.56 = (f32[2,768,384]{2,1,0:T(8,128)S(1)}, f32[2,768,384]{2,1,0:T(8,128)}, u32[]{:S(2)}) copy-start(f32[2,768,384]{2,1,0:T(8,128)} %param.40) | copy-start | bytes 7077892
  1217.3 107.2 %copy-start.69 = (f32[2,768,384]{2,1,0:T(8,128)S(1)}, f32[2,768,384]{2,1,0:T(8,128)}, u32[]{:S(2)}) copy-start(f32[2,768,384]{2,1,0:T(8,128)} %param.41) | copy-start | bytes 7077892
  1217.3 107.2 %copy-start.70 = (f32[2,768,384]{2,1,0:T(8,128)S(1)}, f32[2,768,384]{2,1,0:T(8,128)}, u32[]{:S(2)}) copy-start(f32[2,768,384]{2,1,0:T(8,128)} %param.42) | copy-start | bytes 7077892
  1337.4 33.5 %collective-permute-start.37 = (bf16[2,192,384]{2,1,0:T(8,128)(2,1)}, bf16[2,192,384]{2,1,0:T(8,128)(2,1)S(1)}, u32[]{:S(2)}, u32[]{:S(2)}) collective-permute-start(bf16[2,192,384]{2,1,0:T(8,128)(2,1)} %get-tuple-element.206), channel_id=1, source_target_pairs={{0,0},{8,24},{16,16},{24,8},{1,1},{9,25},{17,17},{25,9},{2,2},{10,... | collective-permute-start | bytes 884744 | tf_op jit(solution)/shard_map/ppermute | solution.py:765
  1340.5 30.4 %collective-permute-start.38 = (bf16[2,192,384]{2,1,0:T(8,128)(2,1)}, bf16[2,192,384]{2,1,0:T(8,128)(2,1)S(1)}, u32[]{:S(2)}, u32[]{:S(2)}) collective-permute-start(bf16[2,192,384]{2,1,0:T(8,128)(2,1)} %get-tuple-element.207), channel_id=1, source_target_pairs={{0,8},{8,0},{16,24},{24,16},{1,9},{9,1},{17,25},{25,17},{2,10},{10... | collective-permute-start | bytes 884744 | tf_op jit(solution)/shard_map/ppermute | solution.py:765
  1341.0 29.9 %collective-permute-start.39 = (bf16[2,192,384]{2,1,0:T(8,128)(2,1)}, bf16[2,192,384]{2,1,0:T(8,128)(2,1)}, u32[]{:S(2)}, u32[]{:S(2)}) collective-permute-start(bf16[2,192,384]{2,1,0:T(8,128)(2,1)} %get-tuple-element.208), channel_id=1, source_target_pairs={{0,16},{8,8},{16,0},{24,24},{1,17},{9,9},{17,1},{25,25},{2,18},{10... | collective-permute-start | bytes 884744 | tf_op jit(solution)/shard_map/ppermute | solution.py:765
  1351.2 18.1 %collective-permute-start.40 = (bf16[2,192,384]{2,1,0:T(8,128)(2,1)S(1)}, bf16[2,192,384]{2,1,0:T(8,128)(2,1)S(1)}, u32[]{:S(2)}, u32[]{:S(2)}) collective-permute-start(bf16[2,192,384]{2,1,0:T(8,128)(2,1)S(1)} %get-tuple-element.127), channel_id=1, source_target_pairs={{0,0},{1,1},{2,8},{3,9},{4,16},{5,17},{6,24},{7,25},{8,2},{9,3},{1... | collective-permute-start | bytes 884744 | tf_op jit(solution)/shard_map/ppermute | solution.py:794
  (84 other events, 605.5 us)
Sparse Core Ops, SparseCore 0:
  188.6 183.1 all-gather.4
  426.0 161.3 all-gather.6
  661.7 189.8 reduce-scatter.3
  855.1 102.5 reduce-scatter.5
  1068.3 138.2 reduce-scatter.7

commit v6 on v5

--- a/solution.py
+++ b/solution.py
@@ -1064,12 +1064,16 @@
             for t in range(3)
         ]
 
+    out_turned, fc2_low = lax.optimization_barrier(
+        (turn(w_out.astype(bf16)), w_fc2.astype(bf16))
+    )
+    fc2_turned = turn(fc2_low)
     qkv_weights, out_full = ring_gather(
-        jnp.concatenate(rolled(chunks, turns), axis=2), turn(w_out.astype(bf16))
+        jnp.concatenate(rolled(chunks, turns), axis=2), out_turned
     )
     out_weights = as_turned(out_full)
     qkv_weights, mod_rows, fc1_low, fc2_turned = lax.optimization_barrier(
-        (qkv_weights, mod_rows, w_fc1.astype(bf16), turn(w_fc2.astype(bf16)))
+        (qkv_weights, mod_rows, w_fc1.astype(bf16), fc2_turned)
     )
     fc1_weights = gather_weight(fc1_low)
     first_seq = seq_ids[0]
@@ -1183,7 +1187,10 @@
     d_attended = backward_product(spots, d_branch_group, out_weights, image, packs=True)
     out_terms = gradient(spots, attended_low, d_branch_group, image, out_weights.shape)
     d_attended_own = exchange(d_attended).reshape(stretch_rows, half_width)
-    d_attended_own, out_terms = lax.optimization_barrier((d_attended_own, out_terms))
+    d_attended_own, out_terms, fc2_own = lax.optimization_barrier(
+        (d_attended_own, out_terms, fc2_own)
+    )
+    g_fc2 = turn(fc2_own)
     d_query_own, d_before, d_after, d_pair_own = attention_back(
         query_own,
         pair_own,
@@ -1197,6 +1204,7 @@
         kid,
         logsum,
     )
+    d_before, d_after, g_fc2 = lax.optimization_barrier((d_before, d_after, g_fc2))
     d_query_came = exchange(d_query_own.reshape(bunch, tok_rows, half_width))
     from_later = stretch_shift(d_before, -1).astype(f32)
     from_earlier = stretch_shift(d_after, 1).astype(f32)
@@ -1207,10 +1215,9 @@
         + jnp.concatenate([from_earlier, rest], axis=0)
     )
     d_pair_came = exchange(d_pair_own.astype(bf16).reshape(bunch, tok_rows, 2 * half_width))
-    d_pair_came, down_terms, fc1_text, fc2_own = lax.optimization_barrier(
-        (d_pair_came, down_terms, fc1_text, fc2_own)
-    )
-    g_fc2 = turn(fc2_own)
+    d_pair_came, down_terms, fc1_text = lax.optimization_barrier(
+        (d_pair_came, down_terms, fc1_text)
+    )
     fc1_text = scatter_weight(fc1_text)
     down_proj = reduce_rep(split_group(down_terms))
     output = mid + gate_two * down_proj
@@ -1246,8 +1253,9 @@
             for r in range(reps)
         ]
     )
-    qkv_terms, out_terms, fc1_image, fc1_text, g_fc2, leaving = lax.optimization_barrier(
-        (qkv_terms, out_terms, fc1_image, fc1_text, g_fc2, leaving)
+    up_fc2 = adam_step(w_fc2, m_fc2, v_fc2, g_fc2.astype(f32), rate_fc2)
+    qkv_terms, out_terms, fc1_image, fc1_text, up_fc2, leaving = lax.optimization_barrier(
+        (qkv_terms, out_terms, fc1_image, fc1_text, up_fc2, leaving)
     )
     leaving = jnp.broadcast_to(leaving[:, None], (reps, shards, *leaving.shape[1:]))
     came = lax.all_to_all(
@@ -1287,7 +1295,6 @@
     up_qkv = adam_step(w_qkv, m_qkv, v_qkv, g_qkv.astype(f32), rate_qkv)
     up_out = adam_step(w_out, m_out, v_out, g_out.astype(f32), rate_out)
     up_fc1 = adam_step(w_fc1, m_fc1, v_fc1, g_fc1.astype(f32), rate_fc1)
-    up_fc2 = adam_step(w_fc2, m_fc2, v_fc2, g_fc2.astype(f32), rate_fc2)
     up_gains = adam_step(gains, m_gains, v_gains, g_gains, rate_gains)
     return (
         output.astype(bf16),

time: 1390 us -> 1370 us (0.986)
  waiting for transfers between devices: 436 us -> 402 us
  Pallas kernels: 572 us -> 591 us
    reduce_scatter x3, waiting for transfers between devices: 62.5 us -> 34.4 us  [scatter_weight(): lax.psum_scatter(terms.reshape(-1, *terms.shape[-2:]), 'shard', scatter_d...]
    unnamed x194 -> x188, local copies, waits for them, and re-layouts: 37.6 us -> 38.4 us
  transfers between devices with their start and end apart: 53 -> 53, of which waited for: 25 -> 23; matrix products, arithmetic and copies ran while one was open for 8% -> 9% of each run, Pallas kernels for 41% -> 43%
where the time goes in v6:
time: 1370 us
  Pallas kernels  591 us (43%)
  waiting for transfers between devices  402 us (29%)
  starting transfers between devices  120 us (9%)
  other arithmetic  88 us (6%)
  local copies, waits for them, and re-layouts  74.5 us (5%)
  blocking collectives  64.6 us (5%)
  between operations  15.6 us (1%)
    all_to_all x5, waiting for transfers between devices, exchange(): lax.all_to_all(value, 'shard', 0, 0, axis_index_groups=None if bunches ==...  207 us
    pallas_call x1, Pallas kernels, ring_gather(): pl.pallas_call(functools.partial(ring_kernel, shards, count), in_specs=[a...  146 us
    pallas_call x1, Pallas kernels, ring_scatter(): pl.pallas_call(functools.partial(ring_scatter_kernel, count), in_specs=[w...  107 us
    ppermute x33, waiting for transfers between devices, over_rep(): return lax.ppermute(value, 'rep', [(r, target(r)) for r in range(count)])  101 us
    pallas_call x1, Pallas kernels, attention_back(): pl.pallas_call(attend_back_kernel, grid_spec=pltpu.PrefetchScalarGridSpec...  84 us
    pallas_call x4, Pallas kernels, gradient(): pl.pallas_call(functools.partial(gradient_kernel, blocks), grid_spec=pltp...  72.7 us
    all_to_all x1, blocking collectives, exchange(): lax.all_to_all(value, 'shard', 0, 0, axis_index_groups=None if bunches ==...  64.6 us
    pallas_call x4, Pallas kernels, backward_product(): pl.pallas_call(functools.partial(backward_kernel, blocks, turned, factor...  60.9 us
  transfers between devices with their start and end apart: 53, of which 23 were waited for; matrix products, arithmetic and copies ran while one was open for 9% of the time, Pallas kernels for 43%

profile of v6, /device:TPU:1, one launch (start us, length us, event | category | flops | bytes accessed | tf_op | source)
XLA Modules:
  0.0 1366.5 jit_solution(1140093965391524332)
XLA Ops:
  14.0 7.1 all-to-all-start
  21.9 3.7 collective-permute-start.3
  28.1 4.9 collective-permute-start
  37.7 3.9 collective-permute-start.4
  43.9 145.6 %ring_gather.1 = (bf16[8,2,192,1152]{3,2,1,0:T(8,128)(2,1)}, bf16[8,2,192,384]{3,2,1,0:T(8,128)(2,1)}) custom-call(bf16[2,192,1152]{2,1,0:T(8,128)(2,1)} %pad_maximum_fusion.5.refs_0_, bf16[2,192,384]{2,1,0:T(8,128)(2,1)} %collective-permute-done.3.refs_1_), custom_call_target="tpu_custom_call" | custom-call | flops 1048576 | bytes 268435456 | tf_op jit(solution)/shard_map/ring_gather/pallas_call | solution.py:868
  192.2 2.8 fusion.20
  195.0 3.4 collective-permute-start.9
  200.7 18.5 %collective-permute-done.6 = s32[320]{0:T(512)S(1)} collective-permute-done((s32[320]{0:T(512)S(1)}, s32[320]{0:T(512)S(1)}, u32[]{:S(2)}, u32[]{:S(2)}) %collective-permute-start.6) | collective-permute-done | bytes 1312 | tf_op jit(solution)/shard_map/ppermute | solution.py:765
  228.5 22.2 %qkv_product.1 = (bf16[8,320,192]{2,1,0:T(8,128)(2,1)S(1)}, bf16[8,320,384]{2,1,0:T(8,128)(2,1)S(1)}, f32[1280,768]{1,0:T(8,128)S(1)}) custom-call(s32[9]{0:T(128)S(1)} %pad_add_fusion.1.spots, bf16[1280,1536]{1,0:T(8,128)(2,1)S(1)} %pad_maximum_fusion.x_ref, bf16[8,2,192,1152]{3,2,1,0:T(8,128)(2,1)} %get-tuple-element.92.w0.w1, ...), custom_call_target="tpu_custom_call" | custom-call | flops 1073741824 | bytes 4194304 | tf_op jit(solution)/shard_map/qkv_product/pallas_call | solution.py:380
  255.0 6.2 all-to-all-start.1
  262.7 96.9 %all-to-all-done.1 = bf16[8,320,384]{2,1,0:T(8,128)(2,1)S(1)} async-done(((bf16[8,320,384]{2,1,0:T(8,128)(2,1)}), bf16[8,320,384]{2,1,0:T(8,128)(2,1)S(1)}, u32[]{:S(2)}, u32[]{:S(2)}) %all-to-all-start.1) | async-done | bytes 1966112 | tf_op jit(solution)/shard_map/all_to_all | solution.py:1107
  364.0 17.0 %collective-permute-done.11.before_ref = bf16[1280,384]{1,0:T(8,128)(2,1)S(1)} collective-permute-done((bf16[1280,384]{1,0:T(8,128)(2,1)S(1)}, bf16[1280,384]{1,0:T(8,128)(2,1)S(1)}, u32[]{:S(2)}, u32[]{:S(2)}) %collective-permute-start.11) | collective-permute-done | bytes 983072 | tf_op jit(solution)/shard_map/ppermute | solution.py:1125
  382.0 10.0 collective-permute-done.12.after_ref
  395.4 4.7 all-to-all-start.2
  400.2 4.1 pad_maximum_fusion.1.dy_ref
  404.3 23.2 %all-to-all-done.2 = bf16[8,320,192]{1,2,0:T(8,128)(2,1)} async-done(((bf16[8,320,192]{1,2,0:T(8,128)(2,1)}), bf16[8,320,192]{1,2,0:T(8,128)(2,1)}, u32[]{:S(2)}, u32[]{:S(2)}) %all-to-all-start.2) | async-done | bytes 983072 | tf_op jit(solution)/shard_map/all_to_all | solution.py:1107
  435.6 43.0 %attend.1 = (bf16[2560,192]{1,0:T(8,128)(2,1)S(1)}, f32[10,8,256]{2,1,0:T(8,128)S(1)}) custom-call(s32[10]{0:T(128)S(1)} %fusion.61.lo_ref, s32[10]{0:T(128)S(1)} %fusion.60.hi_ref, bf16[2560,192]{1,0:T(8,128)(2,1)S(1)} %bitcast.75, bf16[2560,384]{1,0:T(8,128)(2,1)S(1)} %bitcast.71, bf16[1280,384]{1,0:T(8,128)(2,1)S(1)} %copy-done.26, ...), custom_call_target="tpu_custom_call" | custom-call | flops 1073741824 | bytes 4194304 | tf_op jit(solution)/shard_map/attend/pallas_call | solution.py:197
  482.8 64.6 %all_to_all.40 = bf16[8,320,192]{1,2,0:T(8,128)(2,1)} all-to-all(bf16[8,320,192]{1,2,0:T(8,128)(2,1)} %copy.107), channel_id=1, replica_groups=mesh['rep'=4,'shard'=8] {'shard'}, dimensions={0} | all-to-all | bytes 1966080 | tf_op jit(solution)/shard_map/all_to_all | solution.py:1107
  551.1 8.3 forward_product.3
  560.5 5.1 collective-permute-start.17
  569.4 21.7 %collective-permute-done.18 = bf16[320,1536]{1,0:T(8,128)(2,1)S(1)} collective-permute-done((bf16[320,1536]{1,0:T(8,128)(2,1)S(1)}, bf16[320,1536]{1,0:T(8,128)(2,1)S(1)}, u32[]{:S(2)}, u32[]{:S(2)}) %collective-permute-start.18) | collective-permute-done | bytes 983072 | tf_op jit(solution)/shard_map/ppermute | solution.py:765
  592.5 3.4 add_convert_fusion.5
  598.5 19.7 %collective-permute-done.20 = bf16[320,1536]{1,0:T(8,128)(2,1)S(1)} collective-permute-done((bf16[320,1536]{1,0:T(8,128)(2,1)S(1)}, bf16[320,1536]{1,0:T(8,128)(2,1)S(1)}, u32[]{:S(2)}, u32[]{:S(2)}) %collective-permute-start.20) | collective-permute-done | bytes 983072 | tf_op jit(solution)/shard_map/ppermute | solution.py:765
  622.7 21.1 %forward_product.4 = (bf16[1280,1536]{1,0:T(8,128)(2,1)S(1)}, bf16[1280,1536]{1,0:T(8,128)(2,1)S(1)}) custom-call(s32[9]{0:T(128)S(1)} %pad_add_fusion.1.spots, bf16[1280,1536]{1,0:T(8,128)(2,1)S(1)} %pad_maximum_fusion.2.x_ref, bf16[8,2,192,1536]{3,2,1,0:T(8,128)(2,1)} %bitcast.78, bf16[8,2,192,1536]{3,2,1,0:T(8,128)(2,1)} %bitcast.79, ...), custom_call_target="tpu_custom_call" | custom-call | flops 754974720 | bytes 4194304 | tf_op jit(solution)/shard_map/forward_product/pallas_call | solution.py:540
  645.8 24.2 %gradient.4 = bf16[4,2,2,768,384]{4,3,2,1,0:T(8,128)(2,1)} custom-call(s32[9]{0:T(128)S(1)} %pad_add_fusion.1.spots, bf16[1280,1536]{1,0:T(8,128)(2,1)S(1)} %get-tuple-element.106.x_ref, bf16[1280,1536]{1,0:T(8,128)(2,1)} %pad_maximum_fusion.1.dy_ref, s32[1280,1]{1,0:T(8,128)S(1)} %convert_element_type.210.image_ref), custom_call_target="tpu_custom_call" | custom-call | flops 754974720 | bytes 4194304 | tf_op jit(solution)/shard_map/gradient/pallas_call | solution.py:737
  670.0 20.1 %backward_product.4.dy_ref = bf16[1280,1536]{1,0:T(8,128)(2,1)S(1)} custom-call(s32[9]{0:T(128)S(1)} %pad_add_fusion.1.spots, bf16[1280,1536]{1,0:T(8,128)(2,1)} %pad_maximum_fusion.1.dy_ref, bf16[4,2,2,768,384]{4,3,2,1,0:T(8,128)(2,1)} %bitcast.82, bf16[4,2,2,768,384]{4,3,2,1,0:T(8,128)(2,1)} %bitcast.83, s32[1280,1]{1,0:T(8,128)S(1)} %convert_element_type.210.image_ref, ...), custom_call_target="tpu_custom_call" | custom-call | flops 754974720 | bytes 4194304 | tf_op jit(solution)/shard_map/backward_product/pallas_call | solution.py:651
  692.1 16.9 %backward_product.5 = bf16[1280,1536]{1,0:T(8,128)(2,1)S(1)} custom-call(s32[9]{0:T(128)S(1)} %pad_add_fusion.1.spots, bf16[1280,1536]{1,0:T(8,128)(2,1)} %copy-done.4, bf16[8,2,192,1536]{3,2,1,0:T(8,128)(2,1)} %bitcast.80, bf16[8,2,192,1536]{3,2,1,0:T(8,128)(2,1)} %bitcast.81, s32[1280,1]{1,0:T(8,128)S(1)} %convert_element_type.210.image_ref), custom_call_target="tpu_custom_call" | custom-call | flops 754974720 | bytes 4194304 | tf_op jit(solution)/shard_map/backward_product/pallas_call | solution.py:651
  714.0 23.5 %gradient.5 = (bf16[8,1,192,1536]{3,2,1,0:T(8,128)(2,1)}, bf16[8,1,192,1536]{3,2,1,0:T(8,128)(2,1)}) custom-call(s32[9]{0:T(128)S(1)} %pad_add_fusion.1.spots, bf16[1280,1536]{1,0:T(8,128)(2,1)S(1)} %copy-done.3, bf16[1280,1536]{1,0:T(8,128)(2,1)} %copy-done.4, s32[1280,1]{1,0:T(8,128)S(1)} %convert_element_type.210.image_ref), custom_call_target="tpu_custom_call" | custom-call | flops 754974720 | bytes 4194304 | tf_op jit(solution)/shard_map/gradient/pallas_call | solution.py:737
  744.0 21.3 %collective-permute-done.26 = bf16[320,1536]{1,0:T(8,128)(2,1)S(1)} collective-permute-done((bf16[320,1536]{1,0:T(8,128)(2,1)S(1)}, bf16[320,1536]{1,0:T(8,128)(2,1)S(1)}, u32[]{:S(2)}, u32[]{:S(2)}) %collective-permute-start.26) | collective-permute-done | bytes 983072 | tf_op jit(solution)/shard_map/ppermute | solution.py:765
  770.9 9.4 backward_product.6
  783.8 4.3 all-to-all-start.4
  792.1 8.2 gradient.6
  800.3 44.4 %all-to-all-done.4 = bf16[8,320,192]{1,2,0:T(8,128)(2,1)} async-done(((bf16[8,320,192]{1,2,0:T(8,128)(2,1)}), bf16[8,320,192]{1,2,0:T(8,128)(2,1)}, u32[]{:S(2)}, u32[]{:S(2)}) %all-to-all-start.4) | async-done | bytes 983072 | tf_op jit(solution)/shard_map/all_to_all | solution.py:1107
  847.2 9.2 reduce-scatter.4.cloned.1.call-done
  858.3 84.0 %attend_back.1 = (bf16[2560,192]{1,0:T(8,128)(2,1)}, bf16[1280,384]{1,0:T(8,128)(2,1)}, bf16[1280,384]{1,0:T(8,128)(2,1)}, f32[2560,384]{1,0:T(8,128)}) custom-call(s32[10]{0:T(128)} %copy-done.33, s32[10]{0:T(128)} %copy-done.32, bf16[2560,192]{1,0:T(8,128)(2,1)} %bitcast.74, bf16[2560,384]{1,0:T(8,128)(2,1)} %bitcast.72, bf16[1280,384]{1,0:T(8,128)(2,1)} %copy-done.25, ...), custom_call_target="tpu_custom_call" | custom-call | flops 25769803776 | bytes 8388608 | tf_op jit(solution)/shard_map/attend_back/pallas_call | solution.py:237
  943.6 15.5 %collective-permute-start.30 = (bf16[1280,384]{1,0:T(8,128)(2,1)}, bf16[1280,384]{1,0:T(8,128)(2,1)}, u32[]{:S(2)}, u32[]{:S(2)}) collective-permute-start(bf16[1280,384]{1,0:T(8,128)(2,1)} %get-tuple-element.121), channel_id=1, source_target_pairs={{0,2},{1,3},{2,4},{3,5},{4,6},{5,7},{8,10},{9,11},{10,12},{11,13},... | collective-permute-start | bytes 2949128 | tf_op jit(solution)/shard_map/ppermute | solution.py:1125
  961.6 4.3 all-to-all-start.6
  965.8 32.4 %collective-permute-done.29 = bf16[1280,384]{1,0:T(8,128)(2,1)} collective-permute-done((bf16[1280,384]{1,0:T(8,128)(2,1)}, bf16[1280,384]{1,0:T(8,128)(2,1)}, u32[]{:S(2)}, u32[]{:S(2)}) %collective-permute-start.29) | collective-permute-done | bytes 983072 | tf_op jit(solution)/shard_map/ppermute | solution.py:1125
  998.3 4.4 add_convert_fusion
  1002.6 19.8 %all-to-all-done.6 = bf16[8,320,192]{1,2,0:T(8,128)(2,1)} async-done(((bf16[8,320,192]{1,2,0:T(8,128)(2,1)}), bf16[8,320,192]{1,2,0:T(8,128)(2,1)}, u32[]{:S(2)}, u32[]{:S(2)}) %all-to-all-start.6) | async-done | bytes 983072 | tf_op jit(solution)/shard_map/all_to_all | solution.py:1107
  1022.5 6.7 all-to-all-start.5
  1031.5 17.6 %forward_product.5 = bf16[1280,1536]{1,0:T(8,128)(2,1)S(1)} custom-call(s32[9]{0:T(128)S(1)} %pad_add_fusion.1.spots, bf16[1280,1536]{1,0:T(8,128)(2,1)S(1)} %copy-done.10, bf16[4,2,2,768,384]{4,3,2,1,0:T(8,128)(2,1)} %bitcast.84, bf16[4,2,2,768,384]{4,3,2,1,0:T(8,128)(2,1)} %bitcast.85, s32[1280,1]{1,0:T(8,128)S(1)} %convert_element_type.210.image_ref), custom_call_target="tpu_custom_call" | custom-call | flops 754974720 | bytes 4194304 | tf_op jit(solution)/shard_map/forward_product/pallas_call | solution.py:540
  1053.5 22.2 %all-to-all-done.5.kv_ref = bf16[8,320,384]{2,1,0:T(8,128)(2,1)} async-done(((bf16[8,320,384]{2,1,0:T(8,128)(2,1)}), bf16[8,320,384]{2,1,0:T(8,128)(2,1)}, u32[]{:S(2)}, u32[]{:S(2)}) %all-to-all-start.5) | async-done | bytes 1966112 | tf_op jit(solution)/shard_map/all_to_all | solution.py:1107
  1079.2 8.6 norm_back.1
  1087.8 14.6 %backward_product.7 = bf16[1280,1536]{1,0:T(8,128)(2,1)} custom-call(s32[9]{0:T(128)S(1)} %pad_add_fusion.1.spots, bf16[1280,1152]{1,0:T(8,128)(2,1)S(1)} %get-tuple-element.127.dy_ref, bf16[8,2,192,1152]{3,2,1,0:T(8,128)(2,1)} %get-tuple-element.92.w0.w1, bf16[8,2,192,1152]{3,2,1,0:T(8,128)(2,1)} %get-tuple-element.92.w0.w1, ...), custom_call_target="tpu_custom_call" | custom-call | flops 566231040 | bytes 4194304 | tf_op jit(solution)/shard_map/backward_product/pallas_call | solution.py:651
  1102.4 2.7 fusion.82
  1107.8 2.7 add_convert_fusion.1
  1110.5 6.7 fusion.76
  1119.3 16.8 %gradient.7.refs_0_ = bf16[8,2,192,1152]{3,2,1,0:T(8,128)(2,1)} custom-call(s32[9]{0:T(128)S(1)} %pad_add_fusion.1.spots, bf16[1280,1536]{1,0:T(8,128)(2,1)} %copy-done.1, bf16[1280,1152]{1,0:T(8,128)(2,1)S(1)} %copy-done.15, s32[1280,1]{1,0:T(8,128)S(1)} %convert_element_type.210.image_ref), custom_call_target="tpu_custom_call" | custom-call | flops 566231040 | bytes 4194304 | tf_op jit(solution)/shard_map/gradient/pallas_call | solution.py:737
  1143.2 4.3 fusion.79
  1147.5 4.2 multiply_dynamic-update-slice_fusion.1
  1153.9 8.7 collective-permute-done.33
  1162.6 3.4 fusion.21
  1166.1 4.0 fusion.49
  1170.2 25.1 %reduce-scatter.8.cloned.1.call-done = bf16[1,192,1536]{2,1,0:T(8,128)(2,1)} async-done(((bf16[8,192,1536]{2,1,0:T(8,128)(2,1)}), bf16[1,192,1536]{2,1,0:T(8,128)(2,1)}) %reduce-scatter.8.cloned.1.call-update) | async-done | bytes 589840 | tf_op jit(solution)/shard_map/reduce_scatter | solution.py:966
  1196.5 5.3 all-to-all-start.7
  1202.9 3.0 copy-done.7
  1205.9 107.2 %ring_scatter.1 = (bf16[2,192,1152]{2,1,0:T(8,128)(2,1)S(1)}, bf16[2,192,384]{2,1,0:T(8,128)(2,1)S(1)}) custom-call(bf16[8,2,192,1152]{3,2,1,0:T(8,128)(2,1)S(1)} %copy-done.7, bf16[8,2,192,384]{3,2,1,0:T(8,128)(2,1)S(1)} %bitcast.73), custom_call_target="tpu_custom_call" | custom-call | flops 1048576 | bytes 268435456 | tf_op jit(solution)/shard_map/ring_scatter/pallas_call | solution.py:947
  1314.1 4.3 fusion.65
  1320.5 3.1 collective-permute-start.37
  1324.0 3.8 collective-permute-start.39
  1334.3 8.9 collective-permute-start.40
  1343.2 7.9 fusion.74
  1355.3 4.5 fusion.71
  (407 shorter events, 151.9 us)
Async XLA Ops:
  14.0 175.5 %all-to-all-start = ((bf16[32,4,2304]{2,1,0:T(4,128)(2,1)}), bf16[32,4,2304]{2,1,0:T(4,128)(2,1)S(1)}, u32[]{:S(2)}, u32[]{:S(2)}) async-start(bf16[32,4,2304]{2,1,0:T(4,128)(2,1)} %reshape.442), calls=%async_computation | async-start | bytes 1179648 | tf_op jit(solution)/shard_map/all_to_all | solution.py:1041
  21.1 408.8 %all-gather.5.cloned.1.call-start = ((), (), s32[]{:S(2)}) async-start(), calls=%async_computation.14 | async-start | bytes 10616832 | tf_op jit(solution)/shard_map/all_gather | solution.py:798
  21.9 15.8 %collective-permute-start.3 = (bf16[2,192,384]{2,1,0:T(8,128)(2,1)}, bf16[2,192,384]{2,1,0:T(8,128)(2,1)}, u32[]{:S(2)}, u32[]{:S(2)}) collective-permute-start(bf16[2,192,384]{2,1,0:T(8,128)(2,1)} %convert_element_type.196), channel_id=1, source_target_pairs={{0,0},{1,1},{2,8},{3,9},{4,16},{5,17},{6,24},{7,25},{8,2},{9,3},{1... | collective-permute-start | bytes 884744 | tf_op jit(solution)/shard_map/ppermute | solution.py:794
  28.1 13.5 collective-permute-start
  33.0 8.6 collective-permute-start.1
  33.1 8.5 collective-permute-start.2
  37.7 152.2 %collective-permute-start.4 = (bf16[2,768,384]{2,1,0:T(8,128)(2,1)}, bf16[2,768,384]{2,1,0:T(8,128)(2,1)}, u32[]{:S(2)}, u32[]{:S(2)}) collective-permute-start(bf16[2,768,384]{2,1,0:T(8,128)(2,1)} %convert_element_type.197), channel_id=1, source_target_pairs={{0,0},{1,1},{2,8},{3,9},{4,16},{5,17},{6,24},{7,25},{8,2},{9,3},{1... | collective-permute-start | bytes 3538952 | tf_op jit(solution)/shard_map/ppermute | solution.py:794
  43.9 146.7 %copy-start.40 = (bf16[320,1536]{1,0:T(8,128)(2,1)S(1)}, bf16[320,1536]{1,0:T(8,128)(2,1)}, u32[]{:S(2)}) copy-start(bf16[320,1536]{1,0:T(8,128)(2,1)} %param.23) | copy-start | bytes 2949124
  195.0 28.0 %collective-permute-start.9 = (bf16[320,1536]{1,0:T(8,128)(2,1)}, bf16[320,1536]{1,0:T(8,128)(2,1)S(1)}, u32[]{:S(2)}, u32[]{:S(2)}) collective-permute-start(bf16[320,1536]{1,0:T(8,128)(2,1)} %get-tuple-element.257), channel_id=1, source_target_pairs={{0,16},{8,24},{16,0},{24,8},{1,17},{9,25},{17,1},{25,9},{2,18},{10... | collective-permute-start | bytes 2949128 | tf_op jit(solution)/shard_map/ppermute | solution.py:765
  198.4 20.7 %collective-permute-start.6 = (s32[320]{0:T(512)S(1)}, s32[320]{0:T(512)S(1)}, u32[]{:S(2)}, u32[]{:S(2)}) collective-permute-start(s32[320]{0:T(512)S(1)} %copy-done.86), channel_id=1, source_target_pairs={{0,16},{8,24},{16,0},{24,8},{1,17},{9,25},{17,1},{25,9},{2,18},{10... | collective-permute-start | bytes 3848 | tf_op jit(solution)/shard_map/ppermute | solution.py:765
  198.5 22.9 %collective-permute-start.5 = (s32[320]{0:T(512)S(1)}, s32[320]{0:T(512)S(1)}, u32[]{:S(2)}, u32[]{:S(2)}) collective-permute-start(s32[320]{0:T(512)S(1)} %copy-done.86), channel_id=1, source_target_pairs={{0,8},{8,0},{16,24},{24,16},{1,9},{9,1},{17,25},{25,17},{2,10},{10... | collective-permute-start | bytes 3848 | tf_op jit(solution)/shard_map/ppermute | solution.py:765
  219.2 3.0 collective-permute-start.7
  222.6 2.8 collective-permute-start.8
  223.0 3.8 collective-permute-start.10
  255.0 104.6 %all-to-all-start.1 = ((bf16[8,320,384]{2,1,0:T(8,128)(2,1)}), bf16[8,320,384]{2,1,0:T(8,128)(2,1)S(1)}, u32[]{:S(2)}, u32[]{:S(2)}) async-start(bf16[8,320,384]{2,1,0:T(8,128)(2,1)} %copy-done.21), calls=%async_computation.1 | async-start | bytes 3932160 | tf_op jit(solution)/shard_map/all_to_all | solution.py:1107
  261.2 102.7 %collective-permute-start.14 = (bf16[320,1536]{1,0:T(8,128)(2,1)}, bf16[320,1536]{1,0:T(8,128)(2,1)}, u32[]{:S(2)}, u32[]{:S(2)}) collective-permute-start(bf16[320,1536]{1,0:T(8,128)(2,1)} %get-tuple-element.256), channel_id=1, source_target_pairs={{0,16},{8,24},{16,0},{24,8},{1,17},{9,25},{17,1},{25,9},{2,18},{10... | collective-permute-start | bytes 2949128 | tf_op jit(solution)/shard_map/ppermute | solution.py:765
  359.6 72.8 %copy-start.8 = (bf16[8,320,384]{2,1,0:T(8,128)(2,1)}, bf16[8,320,384]{2,1,0:T(8,128)(2,1)S(1)}, u32[]{:S(2)}) copy-start(bf16[8,320,384]{2,1,0:T(8,128)(2,1)S(1)} %all-to-all-done.1) | copy-start | bytes 5898244
  359.8 21.2 %collective-permute-start.11 = (bf16[1280,384]{1,0:T(8,128)(2,1)S(1)}, bf16[1280,384]{1,0:T(8,128)(2,1)S(1)}, u32[]{:S(2)}, u32[]{:S(2)}) collective-permute-start(bf16[1280,384]{1,0:T(8,128)(2,1)S(1)} %bitcast.94), channel_id=1, source_target_pairs={{0,2},{1,3},{2,4},{3,5},{4,6},{5,7},{8,10},{9,11},{10,12},{11,13},... | collective-permute-start | bytes 2949128 | tf_op jit(solution)/shard_map/ppermute | solution.py:1125
  361.2 30.8 %collective-permute-start.12 = (bf16[1280,384]{1,0:T(8,128)(2,1)S(1)}, bf16[1280,384]{1,0:T(8,128)(2,1)S(1)}, u32[]{:S(2)}, u32[]{:S(2)}) collective-permute-start(bf16[1280,384]{1,0:T(8,128)(2,1)S(1)} %bitcast.93), channel_id=1, source_target_pairs={{2,0},{3,1},{4,2},{5,3},{6,4},{7,5},{10,8},{11,9},{12,10},{13,11},... | collective-permute-start | bytes 2949128 | tf_op jit(solution)/shard_map/ppermute | solution.py:1125
  362.5 37.7 %collective-permute-start.13 = (bf16[320,1536]{1,0:T(8,128)(2,1)}, bf16[320,1536]{1,0:T(8,128)(2,1)}, u32[]{:S(2)}, u32[]{:S(2)}) collective-permute-start(bf16[320,1536]{1,0:T(8,128)(2,1)} %get-tuple-element.256), channel_id=1, source_target_pairs={{0,8},{8,0},{16,24},{24,16},{1,9},{9,1},{17,25},{25,17},{2,10},{10... | collective-permute-start | bytes 2949128 | tf_op jit(solution)/shard_map/ppermute | solution.py:765
  363.9 36.2 %collective-permute-start.15 = (bf16[320,1536]{1,0:T(8,128)(2,1)}, bf16[320,1536]{1,0:T(8,128)(2,1)}, u32[]{:S(2)}, u32[]{:S(2)}) collective-permute-start(bf16[320,1536]{1,0:T(8,128)(2,1)} %collective-permute-done.14), channel_id=1, source_target_pairs={{0,8},{8,0},{16,24},{24,16},{1,9},{9,1},{17,25},{25,17},{2,10},{10... | collective-permute-start | bytes 2949128 | tf_op jit(solution)/shard_map/ppermute | solution.py:765
  395.4 32.1 %all-to-all-start.2 = ((bf16[8,320,192]{1,2,0:T(8,128)(2,1)}), bf16[8,320,192]{1,2,0:T(8,128)(2,1)}, u32[]{:S(2)}, u32[]{:S(2)}) async-start(bf16[8,320,192]{1,2,0:T(8,128)(2,1)} %copy.104), calls=%async_computation.2 | async-start | bytes 2359296 | tf_op jit(solution)/shard_map/all_to_all | solution.py:1107
  400.1 269.9 %all-gather.7.cloned.1.call-start = ((), (), s32[]{:S(2)}) async-start(), calls=%async_computation.15 | async-start | bytes 10616832 | tf_op jit(solution)/shard_map/all_gather | solution.py:798
  429.9 426.5 %reduce-scatter.4.cloned.1.call-start = ((), (), s32[]{:S(2)}) async-start(), calls=%async_computation.11 | async-start | bytes 10616832 | tf_op jit(solution)/shard_map/reduce_scatter | solution.py:966
  431.9 46.7 %copy-start.32 = (s32[10]{0:T(128)}, s32[10]{0:T(128)S(1)}, u32[]{:S(2)}) copy-start(s32[10]{0:T(128)S(1)} %fusion.60.hi_ref) | copy-start | bytes 124
  432.0 46.7 %copy-start.33 = (s32[10]{0:T(128)}, s32[10]{0:T(128)S(1)}, u32[]{:S(2)}) copy-start(s32[10]{0:T(128)S(1)} %fusion.61.lo_ref) | copy-start | bytes 124
  482.8 67.0 %copy-start = (bf16[8,2,192,384]{3,2,1,0:T(8,128)(2,1)S(1)}, bf16[8,2,192,384]{3,2,1,0:T(8,128)(2,1)}, u32[]{:S(2)}) copy-start(bf16[8,2,192,384]{3,2,1,0:T(8,128)(2,1)} %get-tuple-element.101) | copy-start | bytes 7077892
  560.5 7.3 collective-permute-start.17
  565.6 3.8 collective-permute-start.16
  568.0 23.1 %collective-permute-start.18 = (bf16[320,1536]{1,0:T(8,128)(2,1)S(1)}, bf16[320,1536]{1,0:T(8,128)(2,1)S(1)}, u32[]{:S(2)}, u32[]{:S(2)}) collective-permute-start(bf16[320,1536]{1,0:T(8,128)(2,1)S(1)} %add_convert_fusion.6), channel_id=1, source_target_pairs={{0,16},{8,24},{16,0},{24,8},{1,17},{9,25},{17,1},{25,9},{2,18},{10... | collective-permute-start | bytes 2949128 | tf_op jit(solution)/shard_map/ppermute | solution.py:765
  596.0 22.2 %collective-permute-start.20 = (bf16[320,1536]{1,0:T(8,128)(2,1)S(1)}, bf16[320,1536]{1,0:T(8,128)(2,1)S(1)}, u32[]{:S(2)}, u32[]{:S(2)}) collective-permute-start(bf16[320,1536]{1,0:T(8,128)(2,1)S(1)} %add_convert_fusion.5), channel_id=1, source_target_pairs={{0,16},{8,24},{16,0},{24,8},{1,17},{9,25},{17,1},{25,9},{2,18},{10... | collective-permute-start | bytes 2949128 | tf_op jit(solution)/shard_map/ppermute | solution.py:765
  597.2 23.1 %collective-permute-start.19 = (bf16[320,1536]{1,0:T(8,128)(2,1)S(1)}, bf16[320,1536]{1,0:T(8,128)(2,1)S(1)}, u32[]{:S(2)}, u32[]{:S(2)}) collective-permute-start(bf16[320,1536]{1,0:T(8,128)(2,1)S(1)} %add_convert_fusion.5), channel_id=1, source_target_pairs={{0,8},{8,0},{16,24},{24,16},{1,9},{9,1},{17,25},{25,17},{2,10},{10... | collective-permute-start | bytes 2949128 | tf_op jit(solution)/shard_map/ppermute | solution.py:765
  618.2 4.2 collective-permute-start.21
  710.1 2.6 collective-permute-start.23
  710.4 27.1 %collective-permute-start.22 = (bf16[320,1536]{1,0:T(8,128)(2,1)}, bf16[320,1536]{1,0:T(8,128)(2,1)S(1)}, u32[]{:S(2)}, u32[]{:S(2)}) collective-permute-start(bf16[320,1536]{1,0:T(8,128)(2,1)} %get-tuple-element.212), channel_id=1, source_target_pairs={{0,8},{8,0},{16,24},{24,16},{1,9},{9,1},{17,25},{25,17},{2,10},{10... | collective-permute-start | bytes 2949128 | tf_op jit(solution)/shard_map/ppermute | solution.py:765
  712.9 24.6 %collective-permute-start.24 = (bf16[320,1536]{1,0:T(8,128)(2,1)S(1)}, bf16[320,1536]{1,0:T(8,128)(2,1)S(1)}, u32[]{:S(2)}, u32[]{:S(2)}) collective-permute-start(bf16[320,1536]{1,0:T(8,128)(2,1)S(1)} %add_convert_fusion.4), channel_id=1, source_target_pairs={{0,16},{8,24},{16,0},{24,8},{1,17},{9,25},{17,1},{25,9},{2,18},{10... | collective-permute-start | bytes 2949128 | tf_op jit(solution)/shard_map/ppermute | solution.py:765
  742.6 22.7 %collective-permute-start.26 = (bf16[320,1536]{1,0:T(8,128)(2,1)S(1)}, bf16[320,1536]{1,0:T(8,128)(2,1)S(1)}, u32[]{:S(2)}, u32[]{:S(2)}) collective-permute-start(bf16[320,1536]{1,0:T(8,128)(2,1)S(1)} %multiply_convert_fusion), channel_id=1, source_target_pairs={{0,16},{8,24},{16,0},{24,8},{1,17},{9,25},{17,1},{25,9},{2,18},{10... | collective-permute-start | bytes 2949128 | tf_op jit(solution)/shard_map/ppermute | solution.py:765
  743.1 23.7 %collective-permute-start.25 = (bf16[320,1536]{1,0:T(8,128)(2,1)S(1)}, bf16[320,1536]{1,0:T(8,128)(2,1)S(1)}, u32[]{:S(2)}, u32[]{:S(2)}) collective-permute-start(bf16[320,1536]{1,0:T(8,128)(2,1)S(1)} %multiply_convert_fusion), channel_id=1, source_target_pairs={{0,8},{8,0},{16,24},{24,16},{1,9},{9,1},{17,25},{25,17},{2,10},{10... | collective-permute-start | bytes 2949128 | tf_op jit(solution)/shard_map/ppermute | solution.py:765
  765.3 3.7 collective-permute-start.27
  783.8 60.9 %all-to-all-start.4 = ((bf16[8,320,192]{1,2,0:T(8,128)(2,1)}), bf16[8,320,192]{1,2,0:T(8,128)(2,1)}, u32[]{:S(2)}, u32[]{:S(2)}) async-start(bf16[8,320,192]{1,2,0:T(8,128)(2,1)} %copy.109), calls=%async_computation.4 | async-start | bytes 2359296 | tf_op jit(solution)/shard_map/all_to_all | solution.py:1107
  788.1 382.1 %reduce-scatter.6.cloned.1.call-start = ((), (), s32[]{:S(2)}) async-start(), calls=%async_computation.12 | async-start | bytes 5308416 | tf_op jit(solution)/shard_map/reduce_scatter | solution.py:966
  856.4 85.9 %collective-permute-start.28 = (bf16[2,768,384]{2,1,0:T(8,128)(2,1)}, bf16[2,768,384]{2,1,0:T(8,128)(2,1)}, u32[]{:S(2)}, u32[]{:S(2)}) collective-permute-start(bf16[2,768,384]{2,1,0:T(8,128)(2,1)} %reduce-scatter.4.cloned.1.call-done), channel_id=1, source_target_pairs={{0,0},{1,1},{2,8},{3,9},{4,16},{5,17},{6,24},{7,25},{8,2},{9,3},{1... | collective-permute-start | bytes 3538952 | tf_op jit(solution)/shard_map/ppermute | solution.py:794
  942.3 55.9 %collective-permute-start.29 = (bf16[1280,384]{1,0:T(8,128)(2,1)}, bf16[1280,384]{1,0:T(8,128)(2,1)}, u32[]{:S(2)}, u32[]{:S(2)}) collective-permute-start(bf16[1280,384]{1,0:T(8,128)(2,1)} %get-tuple-element.120), channel_id=1, source_target_pairs={{2,0},{3,1},{4,2},{5,3},{6,4},{7,5},{10,8},{11,9},{12,10},{13,11},... | collective-permute-start | bytes 2949128 | tf_op jit(solution)/shard_map/ppermute | solution.py:1125
  943.6 54.6 %collective-permute-start.30 = (bf16[1280,384]{1,0:T(8,128)(2,1)}, bf16[1280,384]{1,0:T(8,128)(2,1)}, u32[]{:S(2)}, u32[]{:S(2)}) collective-permute-start(bf16[1280,384]{1,0:T(8,128)(2,1)} %get-tuple-element.121), channel_id=1, source_target_pairs={{0,2},{1,3},{2,4},{3,5},{4,6},{5,7},{8,10},{9,11},{10,12},{11,13},... | collective-permute-start | bytes 2949128 | tf_op jit(solution)/shard_map/ppermute | solution.py:1125
  961.6 60.9 %all-to-all-start.6 = ((bf16[8,320,192]{1,2,0:T(8,128)(2,1)}), bf16[8,320,192]{1,2,0:T(8,128)(2,1)}, u32[]{:S(2)}, u32[]{:S(2)}) async-start(bf16[8,320,192]{1,2,0:T(8,128)(2,1)} %copy.112), calls=%async_computation.7 | async-start | bytes 2359296 | tf_op jit(solution)/shard_map/all_to_all | solution.py:1107
  1022.5 53.3 %all-to-all-start.5 = ((bf16[8,320,384]{2,1,0:T(8,128)(2,1)}), bf16[8,320,384]{2,1,0:T(8,128)(2,1)}, u32[]{:S(2)}, u32[]{:S(2)}) async-start(bf16[8,320,384]{2,1,0:T(8,128)(2,1)} %bitcast.87), calls=%async_computation.6 | async-start | bytes 3932160 | tf_op jit(solution)/shard_map/all_to_all | solution.py:1107
  1029.2 166.1 %reduce-scatter.8.cloned.1.call-start = ((), (), s32[]{:S(2)}) async-start(), calls=%async_computation.13 | async-start | bytes 5308416 | tf_op jit(solution)/shard_map/reduce_scatter | solution.py:966
  1105.2 2.6 collective-permute-start.35
  1107.1 29.2 %collective-permute-start.32 = (bf16[320,1536]{1,0:T(8,128)(2,1)}, bf16[320,1536]{1,0:T(8,128)(2,1)}, u32[]{:S(2)}, u32[]{:S(2)}) collective-permute-start(bf16[320,1536]{1,0:T(8,128)(2,1)} %get-tuple-element.211), channel_id=1, source_target_pairs={{0,8},{8,0},{16,24},{24,16},{1,9},{9,1},{17,25},{25,17},{2,10},{10... | collective-permute-start | bytes 2949128 | tf_op jit(solution)/shard_map/ppermute | solution.py:765
  1107.2 33.3 %collective-permute-start.34 = (bf16[320,1536]{1,0:T(8,128)(2,1)}, bf16[320,1536]{1,0:T(8,128)(2,1)}, u32[]{:S(2)}, u32[]{:S(2)}) collective-permute-start(bf16[320,1536]{1,0:T(8,128)(2,1)} %get-tuple-element.208), channel_id=1, source_target_pairs={{0,8},{8,0},{16,24},{24,16},{1,9},{9,1},{17,25},{25,17},{2,10},{10... | collective-permute-start | bytes 2949128 | tf_op jit(solution)/shard_map/ppermute | solution.py:765
  1110.5 30.0 %collective-permute-start.36 = (bf16[320,1536]{1,0:T(8,128)(2,1)}, bf16[320,1536]{1,0:T(8,128)(2,1)}, u32[]{:S(2)}, u32[]{:S(2)}) collective-permute-start(bf16[320,1536]{1,0:T(8,128)(2,1)} %add_convert_fusion.1), channel_id=1, source_target_pairs={{0,16},{8,24},{16,0},{24,8},{1,17},{9,25},{17,1},{25,9},{2,18},{10... | collective-permute-start | bytes 2949128 | tf_op jit(solution)/shard_map/ppermute | solution.py:765
  1117.3 36.6 %collective-permute-start.31 = (bf16[320,1536]{1,0:T(8,128)(2,1)}, bf16[320,1536]{1,0:T(8,128)(2,1)}, u32[]{:S(2)}, u32[]{:S(2)}) collective-permute-start(bf16[320,1536]{1,0:T(8,128)(2,1)} %get-tuple-element.210), channel_id=1, source_target_pairs={{0,8},{8,0},{16,24},{24,16},{1,9},{9,1},{17,25},{25,17},{2,10},{10... | collective-permute-start | bytes 2949128 | tf_op jit(solution)/shard_map/ppermute | solution.py:765
  1138.8 23.9 %collective-permute-start.33 = (bf16[320,1536]{1,0:T(8,128)(2,1)}, bf16[320,1536]{1,0:T(8,128)(2,1)}, u32[]{:S(2)}, u32[]{:S(2)}) collective-permute-start(bf16[320,1536]{1,0:T(8,128)(2,1)} %add_convert_fusion.3), channel_id=1, source_target_pairs={{0,16},{8,24},{16,0},{24,8},{1,17},{9,25},{17,1},{25,9},{2,18},{10... | collective-permute-start | bytes 2949128 | tf_op jit(solution)/shard_map/ppermute | solution.py:765
  1170.2 31.6 %copy-start.77 = (s32[32,2]{1,0:T(8,128)S(1)}, s32[32,2]{1,0:T(8,128)}, u32[]{:S(2)}) copy-start(s32[32,2]{1,0:T(8,128)} %copy-done.76) | copy-start | bytes 772
  1196.5 121.8 %all-to-all-start.7 = ((f32[32,4,2432]{2,1,0:T(4,128)}), f32[32,4,2432]{2,1,0:T(4,128)}, u32[]{:S(2)}, u32[]{:S(2)}) async-start(f32[32,4,2432]{2,1,0:T(4,128)} %bitcast.88), calls=%async_computation.10 | async-start | bytes 2490368 | tf_op jit(solution)/shard_map/all_to_all | solution.py:1261
  1205.9 108.1 %copy-start.58 = (f32[2,192,1536]{2,1,0:T(8,128)S(1)}, f32[2,192,1536]{2,1,0:T(8,128)}, u32[]{:S(2)}) copy-start(f32[2,192,1536]{2,1,0:T(8,128)} %param.37) | copy-start | bytes 7077892
  1205.9 108.1 %copy-start.68 = (f32[2,192,1536]{2,1,0:T(8,128)S(1)}, f32[2,192,1536]{2,1,0:T(8,128)}, u32[]{:S(2)}) copy-start(f32[2,192,1536]{2,1,0:T(8,128)} %param.38) | copy-start | bytes 7077892
  1205.9 108.1 %copy-start.69 = (f32[2,192,1536]{2,1,0:T(8,128)S(1)}, f32[2,192,1536]{2,1,0:T(8,128)}, u32[]{:S(2)}) copy-start(f32[2,192,1536]{2,1,0:T(8,128)} %param.39) | copy-start | bytes 7077892
  1205.9 108.1 %copy-start.72 = (bf16[1,192,1536]{2,1,0:T(8,128)(2,1)S(1)}, bf16[1,192,1536]{2,1,0:T(8,128)(2,1)}, u32[]{:S(2)}) copy-start(bf16[1,192,1536]{2,1,0:T(8,128)(2,1)} %reduce-scatter.6.cloned.1.call-done) | copy-start | bytes 1769476
  1205.9 108.1 %copy-start.73 = (bf16[1,192,1536]{2,1,0:T(8,128)(2,1)S(1)}, bf16[1,192,1536]{2,1,0:T(8,128)(2,1)}, u32[]{:S(2)}) copy-start(bf16[1,192,1536]{2,1,0:T(8,128)(2,1)} %reduce-scatter.8.cloned.1.call-done) | copy-start | bytes 1769476
  1320.5 33.8 %collective-permute-start.37 = (bf16[2,192,384]{2,1,0:T(8,128)(2,1)}, bf16[2,192,384]{2,1,0:T(8,128)(2,1)S(1)}, u32[]{:S(2)}, u32[]{:S(2)}) collective-permute-start(bf16[2,192,384]{2,1,0:T(8,128)(2,1)} %get-tuple-element.222), channel_id=1, source_target_pairs={{0,0},{8,24},{16,16},{24,8},{1,1},{9,25},{17,17},{25,9},{2,2},{10,... | collective-permute-start | bytes 884744 | tf_op jit(solution)/shard_map/ppermute | solution.py:765
  1323.6 30.7 %collective-permute-start.38 = (bf16[2,192,384]{2,1,0:T(8,128)(2,1)}, bf16[2,192,384]{2,1,0:T(8,128)(2,1)S(1)}, u32[]{:S(2)}, u32[]{:S(2)}) collective-permute-start(bf16[2,192,384]{2,1,0:T(8,128)(2,1)} %get-tuple-element.223), channel_id=1, source_target_pairs={{0,8},{8,0},{16,24},{24,16},{1,9},{9,1},{17,25},{25,17},{2,10},{10... | collective-permute-start | bytes 884744 | tf_op jit(solution)/shard_map/ppermute | solution.py:765
  1324.0 30.2 %collective-permute-start.39 = (bf16[2,192,384]{2,1,0:T(8,128)(2,1)}, bf16[2,192,384]{2,1,0:T(8,128)(2,1)}, u32[]{:S(2)}, u32[]{:S(2)}) collective-permute-start(bf16[2,192,384]{2,1,0:T(8,128)(2,1)} %get-tuple-element.224), channel_id=1, source_target_pairs={{0,16},{8,8},{16,0},{24,24},{1,17},{9,9},{17,1},{25,25},{2,18},{10... | collective-permute-start | bytes 884744 | tf_op jit(solution)/shard_map/ppermute | solution.py:765
  1334.3 18.3 %collective-permute-start.40 = (bf16[2,192,384]{2,1,0:T(8,128)(2,1)S(1)}, bf16[2,192,384]{2,1,0:T(8,128)(2,1)S(1)}, u32[]{:S(2)}, u32[]{:S(2)}) collective-permute-start(bf16[2,192,384]{2,1,0:T(8,128)(2,1)S(1)} %get-tuple-element.140), channel_id=1, source_target_pairs={{0,0},{1,1},{2,8},{3,9},{4,16},{5,17},{6,24},{7,25},{8,2},{9,3},{1... | collective-permute-start | bytes 884744 | tf_op jit(solution)/shard_map/ppermute | solution.py:794
  (81 other events, 599.7 us)
Sparse Core Ops, SparseCore 0:
  190.0 185.7 all-gather.4
  430.1 161.2 all-gather.6
  670.1 186.2 reduce-scatter.3
  859.9 148.9 reduce-scatter.5
  1102.6 92.7 reduce-scatter.7

commit v7 on v6

--- a/solution.py
+++ b/solution.py
@@ -360,11 +360,17 @@
             text_windows(spots, blocks, x_ref.shape[0], text)
 
 
+def both(weight):
+    return weight if isinstance(weight, tuple) else (weight, weight)
+
+
 def column_weights(weight, tile):
-    shards, _, rows, _ = weight.shape
+    pair = both(weight)
+    shards, _, rows, _ = pair[0].shape
+    places = [stream if pair[0].shape[1] == 2 else 0 for stream in range(2)]
     return [
-        pl.BlockSpec((shards, 1, rows, tile), lambda j, s, stream=stream: (0, stream, 0, j))
-        for stream in range(2)
+        pl.BlockSpec((shards, 1, rows, tile), lambda j, s, place=place: (0, place, 0, j))
+        for place in places
     ]
 
 
@@ -516,7 +522,7 @@
 
 def forward_product(spots, x, weight, image, gathers=False, gelu=False):
     blocks = (spots.shape[0] - 1) // 2
-    if weight.ndim == 5:
+    if both(weight)[0].ndim == 5:
         tiles, q, _, rows, tile = weight.shape
         weights = [
             pl.BlockSpec((1, q, 1, rows, tile), lambda j, s, stream=stream: (j, 0, stream, 0, 0))
@@ -524,8 +530,9 @@
         ]
         depth = q * rows
     else:
-        depth, tile = weight.shape[0] * weight.shape[2], COLS
-        tiles = weight.shape[3] // tile
+        shards, _, rows, width = both(weight)[0].shape
+        depth, tile = shards * rows, COLS
+        tiles = width // tile
         weights = column_weights(weight, tile)
     count = image.shape[0]
     column = pl.BlockSpec((count, tile), lambda j, s: (0, j))
@@ -551,7 +558,7 @@
             flops=count * depth // 4 * tiles * tile, bytes_accessed=4 << 20, transcendentals=0
         ),
         name="forward_product",
-    )(spots, x, weight, weight, image)
+    )(spots, x, *both(weight), image)
 
 
 def backward_kernel(blocks, turned, scaled, packs, spots, dy_ref, w0, w1, image_ref, *rest):
@@ -605,7 +612,7 @@
 
 def backward_product(spots, dy, weight, image, factor=None, packs=False):
     blocks = (spots.shape[0] - 1) // 2
-    turned = weight.ndim == 5
+    turned = both(weight)[0].ndim == 5
     count = image.shape[0]
     if turned:
         tiles, q, _, rows, tile = weight.shape
@@ -628,18 +635,18 @@
             ]
         depth = q * rows
     else:
-        shards, _, rows, width = weight.shape
+        shards, streams, rows, width = both(weight)[0].shape
         depth = shards * rows
         bunch = max(1, 768 // rows)
         step = bunch * rows
         grid = (depth // step,)
         weights = [
-            pl.BlockSpec((bunch, 1, rows, width), lambda j, s, stream=stream: (j, stream, 0, 0))
-            for stream in range(2)
+            pl.BlockSpec((bunch, 1, rows, width), lambda j, s, place=place: (j, place, 0, 0))
+            for place in (0, streams - 1)
         ]
     column = pl.BlockSpec((count, step), lambda j, s: (0, j))
     in_specs = [resident(dy.shape), *weights, resident(image.shape)]
-    operands = [spots, dy, weight, weight, image]
+    operands = [spots, dy, *both(weight), image]
     if factor is not None:
         in_specs.append(column)
         operands.append(factor)
@@ -1038,6 +1045,7 @@
     wanted = jnp.stack([firsts, seconds], axis=1)[:, :, None] + stream_offset
     hot = (wanted.reshape(-1, 1) == jnp.arange(2 * slot_count, dtype=jnp.int32)).astype(bf16)
     mod_sent = jnp.dot(hot, mod_terms, preferred_element_type=f32).astype(bf16)
+    mod_sent, out_turned = lax.optimization_barrier((mod_sent, turn(w_out.astype(bf16))))
     mod_got = lax.all_to_all(
         mod_sent.reshape(device_count, 4, mod_cols), ("rep", "shard"), 0, 0, tiled=True
     )
@@ -1064,9 +1072,7 @@
             for t in range(3)
         ]
 
-    out_turned, fc2_low = lax.optimization_barrier(
-        (turn(w_out.astype(bf16)), w_fc2.astype(bf16))
-    )
+    out_turned, fc2_low = lax.optimization_barrier((out_turned, w_fc2.astype(bf16)))
     fc2_turned = turn(fc2_low)
     qkv_weights, out_full = ring_gather(
         jnp.concatenate(rolled(chunks, turns), axis=2), out_turned
@@ -1075,7 +1081,7 @@
     qkv_weights, mod_rows, fc1_low, fc2_turned = lax.optimization_barrier(
         (qkv_weights, mod_rows, w_fc1.astype(bf16), fc2_turned)
     )
-    fc1_weights = gather_weight(fc1_low)
+    fc1_image_weights = gather_weight(fc1_low[:1])
     first_seq = seq_ids[0]
     second_seq = jnp.minimum(first_seq + 1, slot_count - 1)
     is_second = (seq_ids != first_seq)[:, None]
@@ -1125,14 +1131,16 @@
         return lax.ppermute(value, "shard", pairs)
 
     pair_own = exchange(pair_sent).reshape(stretch_rows, 2 * half_width)
+    pair_own, fc1_text_low = lax.optimization_barrier((pair_own, fc1_low[1:]))
     pair_before = stretch_shift(pair_own[-halo:], 1)
     pair_after = stretch_shift(pair_own[:halo], -1)
     query_sent, pair_before, pair_after = lax.optimization_barrier(
         (query_sent, pair_before, pair_after)
     )
+    fc1_text_weights = gather_weight(fc1_text_low)
     query_own = exchange(query_sent).reshape(stretch_rows, half_width)
-    fc2_turned, query_own, fc1_weights, d_down_group = lax.optimization_barrier(
-        (fc2_turned, query_own, fc1_weights, d_down_group)
+    fc2_turned, query_own, fc1_image_weights, d_down_group = lax.optimization_barrier(
+        (fc2_turned, query_own, fc1_image_weights, d_down_group)
     )
     fc2_weights = as_turned(gather_weight(fc2_turned))
     window_rows = stretch_rows + 2 * halo
@@ -1152,6 +1160,8 @@
     attended_own, logsum = attention(
         query_own, pair_own, pair_before, pair_after, lo, hi, qid, kid
     )
+    attended_own, fc1_text_weights = lax.optimization_barrier((attended_own, fc1_text_weights))
+    fc1_weights = (fc1_image_weights, fc1_text_weights)
     attended_came = exchange(attended_own.reshape(bunch, tok_rows, half_width))
 
     def split_group(value):
@@ -1178,7 +1188,7 @@
     d_mid = back_out + d_mid_norm
     d_branch = (gate_one * d_mid).astype(bf16)
     fc1_image, fc1_text = gradient(
-        spots, act_two_group, d_up, image, fc1_weights.shape, split=True
+        spots, act_two_group, d_up, image, (shards, 2, *w_fc1.shape[1:]), split=True
     )
     fc1_image, fc1_text, d_branch = lax.optimization_barrier((fc1_image, fc1_text, d_branch))
     fc1_image = scatter_weight(fc1_image)

time: 1370 us -> 1360 us (level)
  waiting for transfers between devices: 402 us -> 344 us
  blocking collectives: 64.6 us -> 122 us
  Pallas kernels: 591 us -> 569 us
    all_to_all x5 -> x4, waiting for transfers between devices: 207 us -> 121 us  [exchange(): lax.all_to_all(value, 'shard', 0, 0, axis_index_groups=None if bunches ==...]
    all_to_all x1 -> x2, blocking collectives: 64.6 us -> 122 us  [exchange(): lax.all_to_all(value, 'shard', 0, 0, axis_index_groups=None if bunches ==...]
    ppermute x33, waiting for transfers between devices: 101 us -> 118 us  [over_rep(): return lax.ppermute(value, 'rep', [(r, target(r)) for r in range(count)])]
    unnamed x188 -> x176, local copies, waits for them, and re-layouts: 38.4 us -> 34.9 us
  transfers between devices with their start and end apart: 53 -> 53, of which waited for: 23 -> 24; matrix products, arithmetic and copies ran while one was open for 9% -> 9% of each run, Pallas kernels for 43% -> 42%
where the time goes in v7:
time: 1360 us; the launch traced here: 1350 us
  Pallas kernels  569 us (42%)
  waiting for transfers between devices  344 us (25%)
  starting transfers between devices  124 us (9%)
  blocking collectives  122 us (9%)
  other arithmetic  89.7 us (7%)
  local copies, waits for them, and re-layouts  73.4 us (5%)
  between operations  16.3 us (1%)
    pallas_call x1, Pallas kernels, ring_gather(): pl.pallas_call(functools.partial(ring_kernel, shards, count), in_specs=[a...  141 us
    all_to_all x2, blocking collectives, exchange(): lax.all_to_all(value, 'shard', 0, 0, axis_index_groups=None if bunches ==...  122 us
    all_to_all x4, waiting for transfers between devices, exchange(): lax.all_to_all(value, 'shard', 0, 0, axis_index_groups=None if bunches ==...  121 us
    ppermute x33, waiting for transfers between devices, over_rep(): return lax.ppermute(value, 'rep', [(r, target(r)) for r in range(count)])  118 us
    pallas_call x1, Pallas kernels, ring_scatter(): pl.pallas_call(functools.partial(ring_scatter_kernel, count), in_specs=[w...  107 us
    pallas_call x1, Pallas kernels, attention_back(): pl.pallas_call(attend_back_kernel, grid_spec=pltpu.PrefetchScalarGridSpec...  86.4 us
    pallas_call x4, Pallas kernels, gradient(): pl.pallas_call(functools.partial(gradient_kernel, blocks), grid_spec=pltp...  63.6 us
    ppermute x4, waiting for transfers between devices, stretch_shift(): return lax.ppermute(value, 'shard', pairs)  59.6 us
  transfers between devices with their start and end apart: 53, of which 24 were waited for; matrix products, arithmetic and copies ran while one was open for 9% of the time, Pallas kernels for 42%

profile of v7, /device:TPU:1, one launch (start us, length us, event | category | flops | bytes accessed | tf_op | source)
XLA Modules:
  0.0 1348.5 jit_solution(6986507950270105811)
XLA Ops:
  9.0 4.6 collective-permute-start.3
  16.1 5.1 collective-permute-start
  21.3 3.8 collective-permute-start.2
  31.9 3.9 all-to-all-start
  37.9 2.8 convert_element_type.203
  41.2 3.5 collective-permute-start.4
  47.1 141.3 %ring_gather.1 = (bf16[8,2,192,1152]{3,2,1,0:T(8,128)(2,1)}, bf16[8,2,192,384]{3,2,1,0:T(8,128)(2,1)}) custom-call(bf16[2,192,1152]{2,1,0:T(8,128)(2,1)} %pad_maximum_fusion.5.refs_0_, bf16[2,192,384]{2,1,0:T(8,128)(2,1)} %collective-permute-done.3.refs_1_), custom_call_target="tpu_custom_call" | custom-call | flops 1048576 | bytes 268435456 | tf_op jit(solution)/shard_map/ring_gather/pallas_call | solution.py:875
  192.7 2.8 fusion.20
  199.8 17.4 %collective-permute-done.6 = s32[320]{0:T(512)S(1)} collective-permute-done((s32[320]{0:T(512)S(1)}, s32[320]{0:T(512)S(1)}, u32[]{:S(2)}, u32[]{:S(2)}) %collective-permute-start.6) | collective-permute-done | bytes 1312 | tf_op jit(solution)/shard_map/ppermute | solution.py:772
  227.1 20.2 %qkv_product.1 = (bf16[8,320,192]{2,1,0:T(8,128)(2,1)S(1)}, bf16[8,320,384]{2,1,0:T(8,128)(2,1)S(1)}, f32[1280,768]{1,0:T(8,128)S(1)}) custom-call(s32[9]{0:T(128)S(1)} %pad_add_fusion.1.spots, bf16[1280,1536]{1,0:T(8,128)(2,1)S(1)} %pad_maximum_fusion.x_ref, bf16[8,2,192,1152]{3,2,1,0:T(8,128)(2,1)} %get-tuple-element.100.w0.w1, ...), custom_call_target="tpu_custom_call" | custom-call | flops 1073741824 | bytes 4194304 | tf_op jit(solution)/shard_map/qkv_product/pallas_call | solution.py:386
  249.3 62.7 %all_to_all.40 = bf16[8,320,384]{2,1,0:T(8,128)(2,1)S(1)} all-to-all(bf16[8,320,384]{2,1,0:T(8,128)(2,1)S(1)} %get-tuple-element.102), channel_id=1, replica_groups=mesh['rep'=4,'shard'=8] {'shard'}, dimensions={0} | all-to-all | bytes 3932160 | tf_op jit(solution)/shard_map/all_to_all | solution.py:1113
  312.6 3.2 collective-permute-start.11
  319.3 14.6 %collective-permute-done.14 = bf16[320,1536]{1,0:T(8,128)(2,1)} collective-permute-done((bf16[320,1536]{1,0:T(8,128)(2,1)}, bf16[320,1536]{1,0:T(8,128)(2,1)}, u32[]{:S(2)}, u32[]{:S(2)}) %collective-permute-start.14) | collective-permute-done | bytes 983072 | tf_op jit(solution)/shard_map/ppermute | solution.py:772
  336.6 12.4 collective-permute-done.11.before_ref
  349.9 7.9 collective-permute-done.12.after_ref
  361.3 4.3 all-to-all-start.2
  365.6 4.0 pad_maximum_fusion.1.dy_ref
  369.7 55.5 %all-to-all-done.2 = bf16[8,320,192]{1,2,0:T(8,128)(2,1)} async-done(((bf16[8,320,192]{1,2,0:T(8,128)(2,1)}), bf16[8,320,192]{1,2,0:T(8,128)(2,1)}, u32[]{:S(2)}, u32[]{:S(2)}) %all-to-all-start.2) | async-done | bytes 983072 | tf_op jit(solution)/shard_map/all_to_all | solution.py:1113
  433.3 44.2 %attend.1 = (bf16[2560,192]{1,0:T(8,128)(2,1)S(1)}, f32[10,8,256]{2,1,0:T(8,128)S(1)}) custom-call(s32[10]{0:T(128)S(1)} %fusion.61.lo_ref, s32[10]{0:T(128)S(1)} %fusion.60.hi_ref, bf16[2560,192]{1,0:T(8,128)(2,1)S(1)} %bitcast.75, bf16[2560,384]{1,0:T(8,128)(2,1)S(1)} %bitcast.71, bf16[1280,384]{1,0:T(8,128)(2,1)S(1)} %copy-done.25, ...), custom_call_target="tpu_custom_call" | custom-call | flops 1073741824 | bytes 4194304 | tf_op jit(solution)/shard_map/attend/pallas_call | solution.py:197
  481.7 59.4 %all_to_all.41 = bf16[8,320,192]{1,2,0:T(8,128)(2,1)} all-to-all(bf16[8,320,192]{1,2,0:T(8,128)(2,1)} %copy.111), channel_id=1, replica_groups=mesh['rep'=4,'shard'=8] {'shard'}, dimensions={0} | all-to-all | bytes 1966080 | tf_op jit(solution)/shard_map/all_to_all | solution.py:1113
  544.9 7.3 forward_product.3
  553.3 7.3 collective-permute-start.17
  564.6 21.6 %collective-permute-done.18 = bf16[320,1536]{1,0:T(8,128)(2,1)S(1)} collective-permute-done((bf16[320,1536]{1,0:T(8,128)(2,1)S(1)}, bf16[320,1536]{1,0:T(8,128)(2,1)S(1)}, u32[]{:S(2)}, u32[]{:S(2)}) %collective-permute-start.18) | collective-permute-done | bytes 983072 | tf_op jit(solution)/shard_map/ppermute | solution.py:772
  587.6 3.4 add_convert_fusion.5
  593.7 19.6 %collective-permute-done.20 = bf16[320,1536]{1,0:T(8,128)(2,1)S(1)} collective-permute-done((bf16[320,1536]{1,0:T(8,128)(2,1)S(1)}, bf16[320,1536]{1,0:T(8,128)(2,1)S(1)}, u32[]{:S(2)}, u32[]{:S(2)}) %collective-permute-start.20) | collective-permute-done | bytes 983072 | tf_op jit(solution)/shard_map/ppermute | solution.py:772
  617.8 19.2 %forward_product.4 = (bf16[1280,1536]{1,0:T(8,128)(2,1)S(1)}, bf16[1280,1536]{1,0:T(8,128)(2,1)S(1)}) custom-call(s32[9]{0:T(128)S(1)} %pad_add_fusion.1.spots, bf16[1280,1536]{1,0:T(8,128)(2,1)S(1)} %pad_maximum_fusion.2.x_ref, bf16[8,1,192,1536]{3,2,1,0:T(8,128)(2,1)} %bitcast.83, bf16[8,1,192,1536]{3,2,1,0:T(8,128)(2,1)} %bitcast.85, ...), custom_call_target="tpu_custom_call" | custom-call | flops 754974720 | bytes 4194304 | tf_op jit(solution)/shard_map/forward_product/pallas_call | solution.py:547
  638.9 21.0 %gradient.4 = bf16[4,2,2,768,384]{4,3,2,1,0:T(8,128)(2,1)} custom-call(s32[9]{0:T(128)S(1)} %pad_add_fusion.1.spots, bf16[1280,1536]{1,0:T(8,128)(2,1)S(1)} %get-tuple-element.118.x_ref, bf16[1280,1536]{1,0:T(8,128)(2,1)} %pad_maximum_fusion.1.dy_ref, s32[1280,1]{1,0:T(8,128)S(1)} %convert_element_type.210.image_ref), custom_call_target="tpu_custom_call" | custom-call | flops 754974720 | bytes 4194304 | tf_op jit(solution)/shard_map/gradient/pallas_call | solution.py:744
  660.0 18.3 %backward_product.4.dy_ref = bf16[1280,1536]{1,0:T(8,128)(2,1)S(1)} custom-call(s32[9]{0:T(128)S(1)} %pad_add_fusion.1.spots, bf16[1280,1536]{1,0:T(8,128)(2,1)} %pad_maximum_fusion.1.dy_ref, bf16[4,2,2,768,384]{4,3,2,1,0:T(8,128)(2,1)} %bitcast.78, bf16[4,2,2,768,384]{4,3,2,1,0:T(8,128)(2,1)} %bitcast.79, s32[1280,1]{1,0:T(8,128)S(1)} %convert_element_type.210.image_ref, ...), custom_call_target="tpu_custom_call" | custom-call | flops 754974720 | bytes 4194304 | tf_op jit(solution)/shard_map/backward_product/pallas_call | solution.py:658
  680.2 15.0 %backward_product.5 = bf16[1280,1536]{1,0:T(8,128)(2,1)S(1)} custom-call(s32[9]{0:T(128)S(1)} %pad_add_fusion.1.spots, bf16[1280,1536]{1,0:T(8,128)(2,1)} %copy-done.2, bf16[8,1,192,1536]{3,2,1,0:T(8,128)(2,1)} %bitcast.84, bf16[8,1,192,1536]{3,2,1,0:T(8,128)(2,1)} %bitcast.86, s32[1280,1]{1,0:T(8,128)S(1)} %convert_element_type.210.image_ref), custom_call_target="tpu_custom_call" | custom-call | flops 754974720 | bytes 4194304 | tf_op jit(solution)/shard_map/backward_product/pallas_call | solution.py:658
  700.4 20.4 %gradient.5 = (bf16[8,1,192,1536]{3,2,1,0:T(8,128)(2,1)}, bf16[8,1,192,1536]{3,2,1,0:T(8,128)(2,1)}) custom-call(s32[9]{0:T(128)S(1)} %pad_add_fusion.1.spots, bf16[1280,1536]{1,0:T(8,128)(2,1)S(1)} %copy-done.4, bf16[1280,1536]{1,0:T(8,128)(2,1)} %copy-done.2, s32[1280,1]{1,0:T(8,128)S(1)} %convert_element_type.210.image_ref), custom_call_target="tpu_custom_call" | custom-call | flops 754974720 | bytes 4194304 | tf_op jit(solution)/shard_map/gradient/pallas_call | solution.py:744
  729.8 19.7 %collective-permute-done.26 = bf16[320,1536]{1,0:T(8,128)(2,1)S(1)} collective-permute-done((bf16[320,1536]{1,0:T(8,128)(2,1)S(1)}, bf16[320,1536]{1,0:T(8,128)(2,1)S(1)}, u32[]{:S(2)}, u32[]{:S(2)}) %collective-permute-start.26) | collective-permute-done | bytes 983072 | tf_op jit(solution)/shard_map/ppermute | solution.py:772
  755.6 8.8 backward_product.6
  767.9 4.3 all-to-all-start.4
  776.2 7.4 gradient.6
  783.7 37.1 %all-to-all-done.4 = bf16[8,320,192]{1,2,0:T(8,128)(2,1)} async-done(((bf16[8,320,192]{1,2,0:T(8,128)(2,1)}), bf16[8,320,192]{1,2,0:T(8,128)(2,1)}, u32[]{:S(2)}, u32[]{:S(2)}) %all-to-all-start.4) | async-done | bytes 983072 | tf_op jit(solution)/shard_map/all_to_all | solution.py:1113
  823.2 17.5 %reduce-scatter.4.cloned.1.call-done = bf16[2,768,384]{2,1,0:T(8,128)(2,1)} async-done(((bf16[16,768,384]{2,1,0:T(8,128)(2,1)}), bf16[2,768,384]{2,1,0:T(8,128)(2,1)}) %reduce-scatter.4.cloned.1.call-update) | async-done | bytes 1179664 | tf_op jit(solution)/shard_map/reduce_scatter | solution.py:973
  842.6 86.4 %attend_back.1 = (bf16[2560,192]{1,0:T(8,128)(2,1)}, bf16[1280,384]{1,0:T(8,128)(2,1)}, bf16[1280,384]{1,0:T(8,128)(2,1)}, f32[2560,384]{1,0:T(8,128)}) custom-call(s32[10]{0:T(128)} %copy-done.32, s32[10]{0:T(128)} %copy-done.31, bf16[2560,192]{1,0:T(8,128)(2,1)} %bitcast.74, bf16[2560,384]{1,0:T(8,128)(2,1)} %bitcast.72, bf16[1280,384]{1,0:T(8,128)(2,1)} %copy-done.24, ...), custom_call_target="tpu_custom_call" | custom-call | flops 25769803776 | bytes 8388608 | tf_op jit(solution)/shard_map/attend_back/pallas_call | solution.py:237
  930.3 17.4 %collective-permute-start.30 = (bf16[1280,384]{1,0:T(8,128)(2,1)}, bf16[1280,384]{1,0:T(8,128)(2,1)}, u32[]{:S(2)}, u32[]{:S(2)}) collective-permute-start(bf16[1280,384]{1,0:T(8,128)(2,1)} %get-tuple-element.133), channel_id=1, source_target_pairs={{0,2},{1,3},{2,4},{3,5},{4,6},{5,7},{8,10},{9,11},{10,12},{11,13},... | collective-permute-start | bytes 2949128 | tf_op jit(solution)/shard_map/ppermute | solution.py:1131
  950.2 4.3 all-to-all-start.6
  954.5 39.2 %collective-permute-done.29 = bf16[1280,384]{1,0:T(8,128)(2,1)} collective-permute-done((bf16[1280,384]{1,0:T(8,128)(2,1)}, bf16[1280,384]{1,0:T(8,128)(2,1)}, u32[]{:S(2)}, u32[]{:S(2)}) %collective-permute-start.29) | collective-permute-done | bytes 983072 | tf_op jit(solution)/shard_map/ppermute | solution.py:1131
  993.7 4.4 add_convert_fusion
  998.1 8.7 all-to-all-done.6
  1006.8 7.5 all-to-all-start.5
  1016.6 15.8 %forward_product.5 = bf16[1280,1536]{1,0:T(8,128)(2,1)S(1)} custom-call(s32[9]{0:T(128)S(1)} %pad_add_fusion.1.spots, bf16[1280,1536]{1,0:T(8,128)(2,1)S(1)} %copy-done.10, bf16[4,2,2,768,384]{4,3,2,1,0:T(8,128)(2,1)} %bitcast.80, bf16[4,2,2,768,384]{4,3,2,1,0:T(8,128)(2,1)} %bitcast.81, s32[1280,1]{1,0:T(8,128)S(1)} %convert_element_type.210.image_ref), custom_call_target="tpu_custom_call" | custom-call | flops 754974720 | bytes 4194304 | tf_op jit(solution)/shard_map/forward_product/pallas_call | solution.py:547
  1036.9 19.8 %all-to-all-done.5.kv_ref = bf16[8,320,384]{2,1,0:T(8,128)(2,1)} async-done(((bf16[8,320,384]{2,1,0:T(8,128)(2,1)}), bf16[8,320,384]{2,1,0:T(8,128)(2,1)}, u32[]{:S(2)}, u32[]{:S(2)}) %all-to-all-start.5) | async-done | bytes 1966112 | tf_op jit(solution)/shard_map/all_to_all | solution.py:1113
  1060.1 8.6 norm_back.1
  1068.7 13.2 backward_product.7
  1091.5 6.7 fusion.76
  1100.8 14.8 %gradient.7.refs_0_ = bf16[8,2,192,1152]{3,2,1,0:T(8,128)(2,1)} custom-call(s32[9]{0:T(128)S(1)} %pad_add_fusion.1.spots, bf16[1280,1536]{1,0:T(8,128)(2,1)} %copy-done.1, bf16[1280,1152]{1,0:T(8,128)(2,1)S(1)} %copy-done.15, s32[1280,1]{1,0:T(8,128)S(1)} %convert_element_type.210.image_ref), custom_call_target="tpu_custom_call" | custom-call | flops 566231040 | bytes 4194304 | tf_op jit(solution)/shard_map/gradient/pallas_call | solution.py:744
  1120.9 3.1 fusion.79
  1124.1 4.1 multiply_dynamic-update-slice_fusion.1
  1130.5 11.5 collective-permute-done.33
  1142.0 3.5 fusion.21
  1145.5 4.0 fusion.49
  1149.6 27.1 %reduce-scatter.8.cloned.1.call-done = bf16[1,192,1536]{2,1,0:T(8,128)(2,1)} async-done(((bf16[8,192,1536]{2,1,0:T(8,128)(2,1)}), bf16[1,192,1536]{2,1,0:T(8,128)(2,1)}) %reduce-scatter.8.cloned.1.call-update) | async-done | bytes 589840 | tf_op jit(solution)/shard_map/reduce_scatter | solution.py:973
  1177.9 5.3 all-to-all-start.7
  1184.3 3.0 copy-done.7
  1187.3 107.2 %ring_scatter.1 = (bf16[2,192,1152]{2,1,0:T(8,128)(2,1)S(1)}, bf16[2,192,384]{2,1,0:T(8,128)(2,1)S(1)}) custom-call(bf16[8,2,192,1152]{3,2,1,0:T(8,128)(2,1)S(1)} %copy-done.7, bf16[8,2,192,384]{3,2,1,0:T(8,128)(2,1)S(1)} %bitcast.73), custom_call_target="tpu_custom_call" | custom-call | flops 1048576 | bytes 268435456 | tf_op jit(solution)/shard_map/ring_scatter/pallas_call | solution.py:954
  1295.5 4.3 fusion.65
  1301.9 3.1 collective-permute-start.37
  1305.5 3.7 collective-permute-start.39
  1315.7 8.9 collective-permute-start.40
  1324.6 7.8 fusion.74
  1336.7 4.5 fusion.71
  (398 shorter events, 163.0 us)
Async XLA Ops:
  9.0 22.0 %collective-permute-start.3 = (bf16[2,192,384]{2,1,0:T(8,128)(2,1)}, bf16[2,192,384]{2,1,0:T(8,128)(2,1)}, u32[]{:S(2)}, u32[]{:S(2)}) collective-permute-start(bf16[2,192,384]{2,1,0:T(8,128)(2,1)} %convert_element_type.201), channel_id=1, source_target_pairs={{0,0},{1,1},{2,8},{3,9},{4,16},{5,17},{6,24},{7,25},{8,2},{9,3},{1... | collective-permute-start | bytes 884744 | tf_op jit(solution)/shard_map/ppermute | solution.py:801
  16.1 28.7 %collective-permute-start = (bf16[2,192,384]{2,1,0:T(8,128)(2,1)}, bf16[2,192,384]{2,1,0:T(8,128)(2,1)}, u32[]{:S(2)}, u32[]{:S(2)}) collective-permute-start(bf16[2,192,384]{2,1,0:T(8,128)(2,1)} %get-tuple-element.244), channel_id=1, source_target_pairs={{0,0},{8,24},{16,16},{24,8},{1,1},{9,25},{17,17},{25,9},{2,2},{10,... | collective-permute-start | bytes 884744 | tf_op jit(solution)/shard_map/ppermute | solution.py:772
  21.2 23.6 %collective-permute-start.1 = (bf16[2,192,384]{2,1,0:T(8,128)(2,1)}, bf16[2,192,384]{2,1,0:T(8,128)(2,1)}, u32[]{:S(2)}, u32[]{:S(2)}) collective-permute-start(bf16[2,192,384]{2,1,0:T(8,128)(2,1)} %get-tuple-element.242), channel_id=1, source_target_pairs={{0,8},{8,0},{16,24},{24,16},{1,9},{9,1},{17,25},{25,17},{2,10},{10... | collective-permute-start | bytes 884744 | tf_op jit(solution)/shard_map/ppermute | solution.py:772
  21.3 23.5 %collective-permute-start.2 = (bf16[2,192,384]{2,1,0:T(8,128)(2,1)}, bf16[2,192,384]{2,1,0:T(8,128)(2,1)}, u32[]{:S(2)}, u32[]{:S(2)}) collective-permute-start(bf16[2,192,384]{2,1,0:T(8,128)(2,1)} %get-tuple-element.243), channel_id=1, source_target_pairs={{0,16},{8,8},{16,0},{24,24},{1,17},{9,9},{17,1},{25,25},{2,18},{10... | collective-permute-start | bytes 884744 | tf_op jit(solution)/shard_map/ppermute | solution.py:772
  31.9 156.5 %all-to-all-start = ((bf16[32,4,2304]{2,1,0:T(4,128)(2,1)}), bf16[32,4,2304]{2,1,0:T(4,128)(2,1)S(1)}, u32[]{:S(2)}, u32[]{:S(2)}) async-start(bf16[32,4,2304]{2,1,0:T(4,128)(2,1)} %reshape.440), calls=%async_computation | async-start | bytes 1179648 | tf_op jit(solution)/shard_map/all_to_all | solution.py:1049
  35.8 391.8 %all-gather.7.cloned.1.call-start = ((), (), s32[]{:S(2)}) async-start(), calls=%async_computation.14 | async-start | bytes 5308416 | tf_op jit(solution)/shard_map/all_gather | solution.py:805
  41.2 147.5 %collective-permute-start.4 = (bf16[2,768,384]{2,1,0:T(8,128)(2,1)S(1)}, bf16[2,768,384]{2,1,0:T(8,128)(2,1)}, u32[]{:S(2)}, u32[]{:S(2)}) collective-permute-start(bf16[2,768,384]{2,1,0:T(8,128)(2,1)S(1)} %convert_element_type.202), channel_id=1, source_target_pairs={{0,0},{1,1},{2,8},{3,9},{4,16},{5,17},{6,24},{7,25},{8,2},{9,3},{1... | collective-permute-start | bytes 3538952 | tf_op jit(solution)/shard_map/ppermute | solution.py:801
  191.2 288.0 %all-gather.9.cloned.1.call-start = ((), (), s32[]{:S(2)}) async-start(), calls=%async_computation.15 | async-start | bytes 5308416 | tf_op jit(solution)/shard_map/all_gather | solution.py:805
  195.5 26.1 %collective-permute-start.9 = (bf16[320,1536]{1,0:T(8,128)(2,1)}, bf16[320,1536]{1,0:T(8,128)(2,1)S(1)}, u32[]{:S(2)}, u32[]{:S(2)}) collective-permute-start(bf16[320,1536]{1,0:T(8,128)(2,1)} %get-tuple-element.271), channel_id=1, source_target_pairs={{0,16},{8,24},{16,0},{24,8},{1,17},{9,25},{17,1},{25,9},{2,18},{10... | collective-permute-start | bytes 2949128 | tf_op jit(solution)/shard_map/ppermute | solution.py:772
  195.6 21.6 %collective-permute-start.6 = (s32[320]{0:T(512)S(1)}, s32[320]{0:T(512)S(1)}, u32[]{:S(2)}, u32[]{:S(2)}) collective-permute-start(s32[320]{0:T(512)S(1)} %copy-done.80), channel_id=1, source_target_pairs={{0,16},{8,24},{16,0},{24,8},{1,17},{9,25},{17,1},{25,9},{2,18},{10... | collective-permute-start | bytes 3848 | tf_op jit(solution)/shard_map/ppermute | solution.py:772
  197.0 23.0 %collective-permute-start.5 = (s32[320]{0:T(512)S(1)}, s32[320]{0:T(512)S(1)}, u32[]{:S(2)}, u32[]{:S(2)}) collective-permute-start(s32[320]{0:T(512)S(1)} %copy-done.80), channel_id=1, source_target_pairs={{0,8},{8,0},{16,24},{24,16},{1,9},{9,1},{17,25},{25,17},{2,10},{10... | collective-permute-start | bytes 3848 | tf_op jit(solution)/shard_map/ppermute | solution.py:772
  217.2 3.6 collective-permute-start.7
  221.2 2.8 collective-permute-start.8
  221.6 3.8 collective-permute-start.10
  249.3 62.7 %copy-start.22 = (bf16[8,320,192]{2,1,0:T(8,128)(2,1)}, bf16[8,320,192]{2,1,0:T(8,128)(2,1)S(1)}, u32[]{:S(2)}) copy-start(bf16[8,320,192]{2,1,0:T(8,128)(2,1)S(1)} %get-tuple-element.105) | copy-start | bytes 2949124
  312.0 118.1 %copy-start.8 = (bf16[8,320,384]{2,1,0:T(8,128)(2,1)}, bf16[8,320,384]{2,1,0:T(8,128)(2,1)S(1)}, u32[]{:S(2)}) copy-start(bf16[8,320,384]{2,1,0:T(8,128)(2,1)S(1)} %all_to_all.40) | copy-start | bytes 5898244
  312.0 21.9 %collective-permute-start.14 = (bf16[320,1536]{1,0:T(8,128)(2,1)}, bf16[320,1536]{1,0:T(8,128)(2,1)}, u32[]{:S(2)}, u32[]{:S(2)}) collective-permute-start(bf16[320,1536]{1,0:T(8,128)(2,1)} %get-tuple-element.270), channel_id=1, source_target_pairs={{0,16},{8,24},{16,0},{24,8},{1,17},{9,25},{17,1},{25,9},{2,18},{10... | collective-permute-start | bytes 2949128 | tf_op jit(solution)/shard_map/ppermute | solution.py:772
  312.6 36.4 %collective-permute-start.11 = (bf16[1280,384]{1,0:T(8,128)(2,1)S(1)}, bf16[1280,384]{1,0:T(8,128)(2,1)S(1)}, u32[]{:S(2)}, u32[]{:S(2)}) collective-permute-start(bf16[1280,384]{1,0:T(8,128)(2,1)S(1)} %get-tuple-element.231), channel_id=1, source_target_pairs={{0,2},{1,3},{2,4},{3,5},{4,6},{5,7},{8,10},{9,11},{10,12},{11,13},... | collective-permute-start | bytes 2949128 | tf_op jit(solution)/shard_map/ppermute | solution.py:1131
  315.8 42.1 %collective-permute-start.12 = (bf16[1280,384]{1,0:T(8,128)(2,1)S(1)}, bf16[1280,384]{1,0:T(8,128)(2,1)S(1)}, u32[]{:S(2)}, u32[]{:S(2)}) collective-permute-start(bf16[1280,384]{1,0:T(8,128)(2,1)S(1)} %get-tuple-element.230), channel_id=1, source_target_pairs={{2,0},{3,1},{4,2},{5,3},{6,4},{7,5},{10,8},{11,9},{12,10},{13,11},... | collective-permute-start | bytes 2949128 | tf_op jit(solution)/shard_map/ppermute | solution.py:1131
  317.1 48.5 %collective-permute-start.13 = (bf16[320,1536]{1,0:T(8,128)(2,1)}, bf16[320,1536]{1,0:T(8,128)(2,1)}, u32[]{:S(2)}, u32[]{:S(2)}) collective-permute-start(bf16[320,1536]{1,0:T(8,128)(2,1)} %get-tuple-element.270), channel_id=1, source_target_pairs={{0,8},{8,0},{16,24},{24,16},{1,9},{9,1},{17,25},{25,17},{2,10},{10... | collective-permute-start | bytes 2949128 | tf_op jit(solution)/shard_map/ppermute | solution.py:772
  333.9 31.7 %collective-permute-start.15 = (bf16[320,1536]{1,0:T(8,128)(2,1)}, bf16[320,1536]{1,0:T(8,128)(2,1)}, u32[]{:S(2)}, u32[]{:S(2)}) collective-permute-start(bf16[320,1536]{1,0:T(8,128)(2,1)} %collective-permute-done.14), channel_id=1, source_target_pairs={{0,8},{8,0},{16,24},{24,16},{1,9},{9,1},{17,25},{25,17},{2,10},{10... | collective-permute-start | bytes 2949128 | tf_op jit(solution)/shard_map/ppermute | solution.py:772
  361.3 63.9 %all-to-all-start.2 = ((bf16[8,320,192]{1,2,0:T(8,128)(2,1)}), bf16[8,320,192]{1,2,0:T(8,128)(2,1)}, u32[]{:S(2)}, u32[]{:S(2)}) async-start(bf16[8,320,192]{1,2,0:T(8,128)(2,1)} %copy.108), calls=%async_computation.2 | async-start | bytes 2359296 | tf_op jit(solution)/shard_map/all_to_all | solution.py:1113
  365.6 294.4 %all-gather.11.cloned.1.call-start = ((), (), s32[]{:S(2)}) async-start(), calls=%async_computation.16 | async-start | bytes 10616832 | tf_op jit(solution)/shard_map/all_gather | solution.py:805
  427.7 413.0 %reduce-scatter.4.cloned.1.call-start = ((), (), s32[]{:S(2)}) async-start(), calls=%async_computation.11 | async-start | bytes 10616832 | tf_op jit(solution)/shard_map/reduce_scatter | solution.py:973
  429.6 47.9 %copy-start.31 = (s32[10]{0:T(128)}, s32[10]{0:T(128)S(1)}, u32[]{:S(2)}) copy-start(s32[10]{0:T(128)S(1)} %fusion.60.hi_ref) | copy-start | bytes 124
  429.7 47.9 %copy-start.32 = (s32[10]{0:T(128)}, s32[10]{0:T(128)S(1)}, u32[]{:S(2)}) copy-start(s32[10]{0:T(128)S(1)} %fusion.61.lo_ref) | copy-start | bytes 124
  481.7 61.9 %copy-start = (bf16[8,2,192,384]{3,2,1,0:T(8,128)(2,1)S(1)}, bf16[8,2,192,384]{3,2,1,0:T(8,128)(2,1)}, u32[]{:S(2)}) copy-start(bf16[8,2,192,384]{3,2,1,0:T(8,128)(2,1)} %get-tuple-element.112) | copy-start | bytes 7077892
  553.3 9.5 collective-permute-start.17
  560.7 3.9 collective-permute-start.16
  563.1 23.1 %collective-permute-start.18 = (bf16[320,1536]{1,0:T(8,128)(2,1)S(1)}, bf16[320,1536]{1,0:T(8,128)(2,1)S(1)}, u32[]{:S(2)}, u32[]{:S(2)}) collective-permute-start(bf16[320,1536]{1,0:T(8,128)(2,1)S(1)} %add_convert_fusion.6), channel_id=1, source_target_pairs={{0,16},{8,24},{16,0},{24,8},{1,17},{9,25},{17,1},{25,9},{2,18},{10... | collective-permute-start | bytes 2949128 | tf_op jit(solution)/shard_map/ppermute | solution.py:772
  591.1 22.2 %collective-permute-start.20 = (bf16[320,1536]{1,0:T(8,128)(2,1)S(1)}, bf16[320,1536]{1,0:T(8,128)(2,1)S(1)}, u32[]{:S(2)}, u32[]{:S(2)}) collective-permute-start(bf16[320,1536]{1,0:T(8,128)(2,1)S(1)} %add_convert_fusion.5), channel_id=1, source_target_pairs={{0,16},{8,24},{16,0},{24,8},{1,17},{9,25},{17,1},{25,9},{2,18},{10... | collective-permute-start | bytes 2949128 | tf_op jit(solution)/shard_map/ppermute | solution.py:772
  592.3 23.0 %collective-permute-start.19 = (bf16[320,1536]{1,0:T(8,128)(2,1)S(1)}, bf16[320,1536]{1,0:T(8,128)(2,1)S(1)}, u32[]{:S(2)}, u32[]{:S(2)}) collective-permute-start(bf16[320,1536]{1,0:T(8,128)(2,1)S(1)} %add_convert_fusion.5), channel_id=1, source_target_pairs={{0,8},{8,0},{16,24},{24,16},{1,9},{9,1},{17,25},{25,17},{2,10},{10... | collective-permute-start | bytes 2949128 | tf_op jit(solution)/shard_map/ppermute | solution.py:772
  613.3 4.2 collective-permute-start.21
  696.3 2.6 collective-permute-start.23
  696.6 24.2 %collective-permute-start.22 = (bf16[320,1536]{1,0:T(8,128)(2,1)}, bf16[320,1536]{1,0:T(8,128)(2,1)S(1)}, u32[]{:S(2)}, u32[]{:S(2)}) collective-permute-start(bf16[320,1536]{1,0:T(8,128)(2,1)} %get-tuple-element.224), channel_id=1, source_target_pairs={{0,8},{8,0},{16,24},{24,16},{1,9},{9,1},{17,25},{25,17},{2,10},{10... | collective-permute-start | bytes 2949128 | tf_op jit(solution)/shard_map/ppermute | solution.py:772
  699.1 23.2 %collective-permute-start.24 = (bf16[320,1536]{1,0:T(8,128)(2,1)S(1)}, bf16[320,1536]{1,0:T(8,128)(2,1)S(1)}, u32[]{:S(2)}, u32[]{:S(2)}) collective-permute-start(bf16[320,1536]{1,0:T(8,128)(2,1)S(1)} %add_convert_fusion.4), channel_id=1, source_target_pairs={{0,16},{8,24},{16,0},{24,8},{1,17},{9,25},{17,1},{25,9},{2,18},{10... | collective-permute-start | bytes 2949128 | tf_op jit(solution)/shard_map/ppermute | solution.py:772
  727.3 22.2 %collective-permute-start.26 = (bf16[320,1536]{1,0:T(8,128)(2,1)S(1)}, bf16[320,1536]{1,0:T(8,128)(2,1)S(1)}, u32[]{:S(2)}, u32[]{:S(2)}) collective-permute-start(bf16[320,1536]{1,0:T(8,128)(2,1)S(1)} %multiply_convert_fusion), channel_id=1, source_target_pairs={{0,16},{8,24},{16,0},{24,8},{1,17},{9,25},{17,1},{25,9},{2,18},{10... | collective-permute-start | bytes 2949128 | tf_op jit(solution)/shard_map/ppermute | solution.py:772
  728.5 23.1 %collective-permute-start.25 = (bf16[320,1536]{1,0:T(8,128)(2,1)S(1)}, bf16[320,1536]{1,0:T(8,128)(2,1)S(1)}, u32[]{:S(2)}, u32[]{:S(2)}) collective-permute-start(bf16[320,1536]{1,0:T(8,128)(2,1)S(1)} %multiply_convert_fusion), channel_id=1, source_target_pairs={{0,8},{8,0},{16,24},{24,16},{1,9},{9,1},{17,25},{25,17},{2,10},{10... | collective-permute-start | bytes 2949128 | tf_op jit(solution)/shard_map/ppermute | solution.py:772
  749.5 4.2 collective-permute-start.27
  767.9 52.8 %all-to-all-start.4 = ((bf16[8,320,192]{1,2,0:T(8,128)(2,1)}), bf16[8,320,192]{1,2,0:T(8,128)(2,1)}, u32[]{:S(2)}, u32[]{:S(2)}) async-start(bf16[8,320,192]{1,2,0:T(8,128)(2,1)} %copy.113), calls=%async_computation.4 | async-start | bytes 2359296 | tf_op jit(solution)/shard_map/all_to_all | solution.py:1113
  772.2 377.4 %reduce-scatter.6.cloned.1.call-start = ((), (), s32[]{:S(2)}) async-start(), calls=%async_computation.12 | async-start | bytes 5308416 | tf_op jit(solution)/shard_map/reduce_scatter | solution.py:973
  840.7 88.3 %collective-permute-start.28 = (bf16[2,768,384]{2,1,0:T(8,128)(2,1)}, bf16[2,768,384]{2,1,0:T(8,128)(2,1)}, u32[]{:S(2)}, u32[]{:S(2)}) collective-permute-start(bf16[2,768,384]{2,1,0:T(8,128)(2,1)} %reduce-scatter.4.cloned.1.call-done), channel_id=1, source_target_pairs={{0,0},{1,1},{2,8},{3,9},{4,16},{5,17},{6,24},{7,25},{8,2},{9,3},{1... | collective-permute-start | bytes 3538952 | tf_op jit(solution)/shard_map/ppermute | solution.py:801
  929.0 64.7 %collective-permute-start.29 = (bf16[1280,384]{1,0:T(8,128)(2,1)}, bf16[1280,384]{1,0:T(8,128)(2,1)}, u32[]{:S(2)}, u32[]{:S(2)}) collective-permute-start(bf16[1280,384]{1,0:T(8,128)(2,1)} %get-tuple-element.132), channel_id=1, source_target_pairs={{2,0},{3,1},{4,2},{5,3},{6,4},{7,5},{10,8},{11,9},{12,10},{13,11},... | collective-permute-start | bytes 2949128 | tf_op jit(solution)/shard_map/ppermute | solution.py:1131
  930.3 63.4 %collective-permute-start.30 = (bf16[1280,384]{1,0:T(8,128)(2,1)}, bf16[1280,384]{1,0:T(8,128)(2,1)}, u32[]{:S(2)}, u32[]{:S(2)}) collective-permute-start(bf16[1280,384]{1,0:T(8,128)(2,1)} %get-tuple-element.133), channel_id=1, source_target_pairs={{0,2},{1,3},{2,4},{3,5},{4,6},{5,7},{8,10},{9,11},{10,12},{11,13},... | collective-permute-start | bytes 2949128 | tf_op jit(solution)/shard_map/ppermute | solution.py:1131
  950.2 56.6 %all-to-all-start.6 = ((bf16[8,320,192]{1,2,0:T(8,128)(2,1)}), bf16[8,320,192]{1,2,0:T(8,128)(2,1)}, u32[]{:S(2)}, u32[]{:S(2)}) async-start(bf16[8,320,192]{1,2,0:T(8,128)(2,1)} %copy.116), calls=%async_computation.7 | async-start | bytes 2359296 | tf_op jit(solution)/shard_map/all_to_all | solution.py:1113
  1006.8 49.9 %all-to-all-start.5 = ((bf16[8,320,384]{2,1,0:T(8,128)(2,1)}), bf16[8,320,384]{2,1,0:T(8,128)(2,1)}, u32[]{:S(2)}, u32[]{:S(2)}) async-start(bf16[8,320,384]{2,1,0:T(8,128)(2,1)} %bitcast.87), calls=%async_computation.6 | async-start | bytes 3932160 | tf_op jit(solution)/shard_map/all_to_all | solution.py:1113
  1014.3 162.5 %reduce-scatter.8.cloned.1.call-start = ((), (), s32[]{:S(2)}) async-start(), calls=%async_computation.13 | async-start | bytes 5308416 | tf_op jit(solution)/shard_map/reduce_scatter | solution.py:973
  1084.7 2.6 collective-permute-start.35
  1086.1 29.6 %collective-permute-start.32 = (bf16[320,1536]{1,0:T(8,128)(2,1)}, bf16[320,1536]{1,0:T(8,128)(2,1)}, u32[]{:S(2)}, u32[]{:S(2)}) collective-permute-start(bf16[320,1536]{1,0:T(8,128)(2,1)} %get-tuple-element.223), channel_id=1, source_target_pairs={{0,8},{8,0},{16,24},{24,16},{1,9},{9,1},{17,25},{25,17},{2,10},{10... | collective-permute-start | bytes 2949128 | tf_op jit(solution)/shard_map/ppermute | solution.py:772
  1086.6 31.6 %collective-permute-start.34 = (bf16[320,1536]{1,0:T(8,128)(2,1)}, bf16[320,1536]{1,0:T(8,128)(2,1)}, u32[]{:S(2)}, u32[]{:S(2)}) collective-permute-start(bf16[320,1536]{1,0:T(8,128)(2,1)} %get-tuple-element.220), channel_id=1, source_target_pairs={{0,8},{8,0},{16,24},{24,16},{1,9},{9,1},{17,25},{25,17},{2,10},{10... | collective-permute-start | bytes 2949128 | tf_op jit(solution)/shard_map/ppermute | solution.py:772
  1089.6 28.7 %collective-permute-start.36 = (bf16[320,1536]{1,0:T(8,128)(2,1)}, bf16[320,1536]{1,0:T(8,128)(2,1)}, u32[]{:S(2)}, u32[]{:S(2)}) collective-permute-start(bf16[320,1536]{1,0:T(8,128)(2,1)} %add_convert_fusion.1), channel_id=1, source_target_pairs={{0,16},{8,24},{16,0},{24,8},{1,17},{9,25},{17,1},{25,9},{2,18},{10... | collective-permute-start | bytes 2949128 | tf_op jit(solution)/shard_map/ppermute | solution.py:772
  1098.3 32.2 %collective-permute-start.31 = (bf16[320,1536]{1,0:T(8,128)(2,1)}, bf16[320,1536]{1,0:T(8,128)(2,1)}, u32[]{:S(2)}, u32[]{:S(2)}) collective-permute-start(bf16[320,1536]{1,0:T(8,128)(2,1)} %get-tuple-element.222), channel_id=1, source_target_pairs={{0,8},{8,0},{16,24},{24,16},{1,9},{9,1},{17,25},{25,17},{2,10},{10... | collective-permute-start | bytes 2949128 | tf_op jit(solution)/shard_map/ppermute | solution.py:772
  1118.3 23.7 %collective-permute-start.33 = (bf16[320,1536]{1,0:T(8,128)(2,1)}, bf16[320,1536]{1,0:T(8,128)(2,1)}, u32[]{:S(2)}, u32[]{:S(2)}) collective-permute-start(bf16[320,1536]{1,0:T(8,128)(2,1)} %add_convert_fusion.3), channel_id=1, source_target_pairs={{0,16},{8,24},{16,0},{24,8},{1,17},{9,25},{17,1},{25,9},{2,18},{10... | collective-permute-start | bytes 2949128 | tf_op jit(solution)/shard_map/ppermute | solution.py:772
  1149.6 33.7 %copy-start.71 = (s32[32,2]{1,0:T(8,128)S(1)}, s32[32,2]{1,0:T(8,128)}, u32[]{:S(2)}) copy-start(s32[32,2]{1,0:T(8,128)} %copy-done.70) | copy-start | bytes 772
  1177.9 121.8 %all-to-all-start.7 = ((f32[32,4,2432]{2,1,0:T(4,128)}), f32[32,4,2432]{2,1,0:T(4,128)}, u32[]{:S(2)}, u32[]{:S(2)}) async-start(f32[32,4,2432]{2,1,0:T(4,128)} %bitcast.88), calls=%async_computation.10 | async-start | bytes 2490368 | tf_op jit(solution)/shard_map/all_to_all | solution.py:1271
  1187.3 108.1 %copy-start.55 = (f32[2,192,1536]{2,1,0:T(8,128)S(1)}, f32[2,192,1536]{2,1,0:T(8,128)}, u32[]{:S(2)}) copy-start(f32[2,192,1536]{2,1,0:T(8,128)} %param.37) | copy-start | bytes 7077892
  1187.3 108.1 %copy-start.62 = (f32[2,192,1536]{2,1,0:T(8,128)S(1)}, f32[2,192,1536]{2,1,0:T(8,128)}, u32[]{:S(2)}) copy-start(f32[2,192,1536]{2,1,0:T(8,128)} %param.38) | copy-start | bytes 7077892
  1187.3 108.1 %copy-start.63 = (f32[2,192,1536]{2,1,0:T(8,128)S(1)}, f32[2,192,1536]{2,1,0:T(8,128)}, u32[]{:S(2)}) copy-start(f32[2,192,1536]{2,1,0:T(8,128)} %param.39) | copy-start | bytes 7077892
  1187.3 108.1 %copy-start.66 = (bf16[1,192,1536]{2,1,0:T(8,128)(2,1)S(1)}, bf16[1,192,1536]{2,1,0:T(8,128)(2,1)}, u32[]{:S(2)}) copy-start(bf16[1,192,1536]{2,1,0:T(8,128)(2,1)} %reduce-scatter.6.cloned.1.call-done) | copy-start | bytes 1769476
  1187.3 108.1 %copy-start.67 = (bf16[1,192,1536]{2,1,0:T(8,128)(2,1)S(1)}, bf16[1,192,1536]{2,1,0:T(8,128)(2,1)}, u32[]{:S(2)}) copy-start(bf16[1,192,1536]{2,1,0:T(8,128)(2,1)} %reduce-scatter.8.cloned.1.call-done) | copy-start | bytes 1769476
  1301.9 33.7 %collective-permute-start.37 = (bf16[2,192,384]{2,1,0:T(8,128)(2,1)}, bf16[2,192,384]{2,1,0:T(8,128)(2,1)S(1)}, u32[]{:S(2)}, u32[]{:S(2)}) collective-permute-start(bf16[2,192,384]{2,1,0:T(8,128)(2,1)} %get-tuple-element.236), channel_id=1, source_target_pairs={{0,0},{8,24},{16,16},{24,8},{1,1},{9,25},{17,17},{25,9},{2,2},{10,... | collective-permute-start | bytes 884744 | tf_op jit(solution)/shard_map/ppermute | solution.py:772
  1305.0 30.6 %collective-permute-start.38 = (bf16[2,192,384]{2,1,0:T(8,128)(2,1)}, bf16[2,192,384]{2,1,0:T(8,128)(2,1)S(1)}, u32[]{:S(2)}, u32[]{:S(2)}) collective-permute-start(bf16[2,192,384]{2,1,0:T(8,128)(2,1)} %get-tuple-element.237), channel_id=1, source_target_pairs={{0,8},{8,0},{16,24},{24,16},{1,9},{9,1},{17,25},{25,17},{2,10},{10... | collective-permute-start | bytes 884744 | tf_op jit(solution)/shard_map/ppermute | solution.py:772
  1305.5 30.1 %collective-permute-start.39 = (bf16[2,192,384]{2,1,0:T(8,128)(2,1)}, bf16[2,192,384]{2,1,0:T(8,128)(2,1)}, u32[]{:S(2)}, u32[]{:S(2)}) collective-permute-start(bf16[2,192,384]{2,1,0:T(8,128)(2,1)} %get-tuple-element.238), channel_id=1, source_target_pairs={{0,16},{8,8},{16,0},{24,24},{1,17},{9,9},{17,1},{25,25},{2,18},{10... | collective-permute-start | bytes 884744 | tf_op jit(solution)/shard_map/ppermute | solution.py:772
  1315.7 18.3 %collective-permute-start.40 = (bf16[2,192,384]{2,1,0:T(8,128)(2,1)S(1)}, bf16[2,192,384]{2,1,0:T(8,128)(2,1)S(1)}, u32[]{:S(2)}, u32[]{:S(2)}) collective-permute-start(bf16[2,192,384]{2,1,0:T(8,128)(2,1)S(1)} %get-tuple-element.152), channel_id=1, source_target_pairs={{0,0},{1,1},{2,8},{3,9},{4,16},{5,17},{6,24},{7,25},{8,2},{9,3},{1... | collective-permute-start | bytes 884744 | tf_op jit(solution)/shard_map/ppermute | solution.py:801
  (75 other events, 571.0 us)
Sparse Core Ops, SparseCore 0:
  191.3 100.3 all-gather.6
  312.2 119.3 all-gather.8
  433.8 158.8 all-gather.10
  660.1 180.5 reduce-scatter.3
  844.2 154.5 reduce-scatter.5
  1082.0 94.6 reduce-scatter.7

commit v8 on v7

--- a/solution.py
+++ b/solution.py
@@ -964,7 +964,7 @@
         compiler_params=pltpu.CompilerParams(
             collective_id=1, has_side_effects=True, vmem_limit_bytes=36 << 20
         ),
-        cost_estimate=pl.CostEstimate(flops=1 << 20, bytes_accessed=256 << 20, transcendentals=0),
+        cost_estimate=pl.CostEstimate(flops=1 << 20, bytes_accessed=8 << 20, transcendentals=0),
         name="ring_scatter",
     )(*terms)
 
@@ -1264,8 +1264,8 @@
         ]
     )
     up_fc2 = adam_step(w_fc2, m_fc2, v_fc2, g_fc2.astype(f32), rate_fc2)
-    qkv_terms, out_terms, fc1_image, fc1_text, up_fc2, leaving = lax.optimization_barrier(
-        (qkv_terms, out_terms, fc1_image, fc1_text, up_fc2, leaving)
+    qkv_terms, out_terms, fc1_image, up_fc2, leaving = lax.optimization_barrier(
+        (qkv_terms, out_terms, fc1_image, up_fc2, leaving)
     )
     leaving = jnp.broadcast_to(leaving[:, None], (reps, shards, *leaving.shape[1:]))
     came = lax.all_to_all(
@@ -1273,7 +1273,9 @@
     )
     out_terms = out_terms.reshape(shards, 2, -1, out_terms.shape[-1])
     g_qkv_group, g_out = ring_scatter(qkv_terms, out_terms)
-    g_qkv_group, g_out, came = lax.optimization_barrier((g_qkv_group, g_out, came))
+    g_qkv_group, g_out, came, fc1_text = lax.optimization_barrier(
+        (g_qkv_group, g_out, came, fc1_text)
+    )
     g_out = turn(g_out)
     g_fc1 = jnp.concatenate([fc1_image, fc1_text], axis=0)
     g_parts = [

time: 1360 us -> 1360 us (level)
  waiting for transfers between devices: 344 us -> 316 us
  Pallas kernels: 569 us -> 595 us
    reduce_scatter x3, waiting for transfers between devices: 44.6 us -> 20 us  [scatter_weight(): lax.psum_scatter(terms.reshape(-1, *terms.shape[-2:]), 'shard', scatter_d...]
    pallas_call x1, Pallas kernels: 107 us -> 126 us  [ring_scatter(): pl.pallas_call(functools.partial(ring_scatter_kernel, count), in_specs=[w...]
  transfers between devices with their start and end apart: 53 -> 53, of which waited for: 24 -> 23; matrix products, arithmetic and copies ran while one was open for 9% -> 9% of each run, Pallas kernels for 42% -> 44%
where the time goes in v8:
time: 1360 us; the launch traced here: 1350 us
  Pallas kernels  595 us (44%)
  waiting for transfers between devices  316 us (23%)
  blocking collectives  127 us (9%)
  starting transfers between devices  117 us (9%)
  other arithmetic  88.9 us (7%)
  local copies, waits for them, and re-layouts  74.9 us (6%)
  between operations  16.3 us (1%)
    pallas_call x1, Pallas kernels, ring_gather(): pl.pallas_call(functools.partial(ring_kernel, shards, count), in_specs=[a...  141 us
    all_to_all x4, waiting for transfers between devices, exchange(): lax.all_to_all(value, 'shard', 0, 0, axis_index_groups=None if bunches ==...  131 us
    all_to_all x2, blocking collectives, exchange(): lax.all_to_all(value, 'shard', 0, 0, axis_index_groups=None if bunches ==...  127 us
    pallas_call x1, Pallas kernels, ring_scatter(): pl.pallas_call(functools.partial(ring_scatter_kernel, count), in_specs=[w...  126 us
    ppermute x33, waiting for transfers between devices, over_rep(): return lax.ppermute(value, 'rep', [(r, target(r)) for r in range(count)])  117 us
    pallas_call x1, Pallas kernels, attention_back(): pl.pallas_call(attend_back_kernel, grid_spec=pltpu.PrefetchScalarGridSpec...  91 us
    pallas_call x4, Pallas kernels, gradient(): pl.pallas_call(functools.partial(gradient_kernel, blocks), grid_spec=pltp...  63.3 us
    pallas_call x4, Pallas kernels, backward_product(): pl.pallas_call(functools.partial(backward_kernel, blocks, turned, factor...  55.9 us
  transfers between devices with their start and end apart: 53, of which 23 were waited for; matrix products, arithmetic and copies ran while one was open for 9% of the time, Pallas kernels for 44%

profile of v8, /device:TPU:1, one launch (start us, length us, event | category | flops | bytes accessed | tf_op | source)
XLA Modules:
  0.0 1347.0 jit_solution(13530885388263877461)
XLA Ops:
  9.0 4.6 collective-permute-start.3
  16.1 5.1 collective-permute-start
  21.3 3.8 collective-permute-start.2
  31.9 3.9 all-to-all-start
  37.9 2.8 convert_element_type.203
  41.2 3.5 collective-permute-start.4
  47.1 141.3 %ring_gather.1 = (bf16[8,2,192,1152]{3,2,1,0:T(8,128)(2,1)}, bf16[8,2,192,384]{3,2,1,0:T(8,128)(2,1)}) custom-call(bf16[2,192,1152]{2,1,0:T(8,128)(2,1)} %pad_maximum_fusion.5.refs_0_, bf16[2,192,384]{2,1,0:T(8,128)(2,1)} %collective-permute-done.3.refs_1_), custom_call_target="tpu_custom_call" | custom-call | flops 1048576 | bytes 268435456 | tf_op jit(solution)/shard_map/ring_gather/pallas_call | solution.py:875
  192.7 2.8 fusion.20
  199.8 17.4 %collective-permute-done.6 = s32[320]{0:T(512)S(1)} collective-permute-done((s32[320]{0:T(512)S(1)}, s32[320]{0:T(512)S(1)}, u32[]{:S(2)}, u32[]{:S(2)}) %collective-permute-start.6) | collective-permute-done | bytes 1312 | tf_op jit(solution)/shard_map/ppermute | solution.py:772
  217.2 2.8 collective-permute-start.7
  227.1 20.2 %qkv_product.1 = (bf16[8,320,192]{2,1,0:T(8,128)(2,1)S(1)}, bf16[8,320,384]{2,1,0:T(8,128)(2,1)S(1)}, f32[1280,768]{1,0:T(8,128)S(1)}) custom-call(s32[9]{0:T(128)S(1)} %pad_add_fusion.1.spots, bf16[1280,1536]{1,0:T(8,128)(2,1)S(1)} %pad_maximum_fusion.x_ref, bf16[8,2,192,1152]{3,2,1,0:T(8,128)(2,1)} %get-tuple-element.100.w0.w1, ...), custom_call_target="tpu_custom_call" | custom-call | flops 1073741824 | bytes 4194304 | tf_op jit(solution)/shard_map/qkv_product/pallas_call | solution.py:386
  249.3 62.7 %all_to_all.40 = bf16[8,320,384]{2,1,0:T(8,128)(2,1)S(1)} all-to-all(bf16[8,320,384]{2,1,0:T(8,128)(2,1)S(1)} %get-tuple-element.102), channel_id=1, replica_groups=mesh['rep'=4,'shard'=8] {'shard'}, dimensions={0} | all-to-all | bytes 3932160 | tf_op jit(solution)/shard_map/all_to_all | solution.py:1113
  312.6 3.2 collective-permute-start.11
  319.3 14.6 %collective-permute-done.14 = bf16[320,1536]{1,0:T(8,128)(2,1)} collective-permute-done((bf16[320,1536]{1,0:T(8,128)(2,1)}, bf16[320,1536]{1,0:T(8,128)(2,1)}, u32[]{:S(2)}, u32[]{:S(2)}) %collective-permute-start.14) | collective-permute-done | bytes 983072 | tf_op jit(solution)/shard_map/ppermute | solution.py:772
  336.6 12.4 collective-permute-done.11.before_ref
  349.9 7.9 collective-permute-done.12.after_ref
  361.3 4.3 all-to-all-start.2
  365.6 4.0 pad_maximum_fusion.1.dy_ref
  369.6 55.5 %all-to-all-done.2 = bf16[8,320,192]{1,2,0:T(8,128)(2,1)} async-done(((bf16[8,320,192]{1,2,0:T(8,128)(2,1)}), bf16[8,320,192]{1,2,0:T(8,128)(2,1)}, u32[]{:S(2)}, u32[]{:S(2)}) %all-to-all-start.2) | async-done | bytes 983072 | tf_op jit(solution)/shard_map/all_to_all | solution.py:1113
  433.3 46.6 %attend.1 = (bf16[2560,192]{1,0:T(8,128)(2,1)S(1)}, f32[10,8,256]{2,1,0:T(8,128)S(1)}) custom-call(s32[10]{0:T(128)S(1)} %fusion.61.lo_ref, s32[10]{0:T(128)S(1)} %fusion.60.hi_ref, bf16[2560,192]{1,0:T(8,128)(2,1)S(1)} %bitcast.75, bf16[2560,384]{1,0:T(8,128)(2,1)S(1)} %bitcast.71, bf16[1280,384]{1,0:T(8,128)(2,1)S(1)} %copy-done.25, ...), custom_call_target="tpu_custom_call" | custom-call | flops 1073741824 | bytes 4194304 | tf_op jit(solution)/shard_map/attend/pallas_call | solution.py:197
  484.1 64.4 %all_to_all.41 = bf16[8,320,192]{1,2,0:T(8,128)(2,1)} all-to-all(bf16[8,320,192]{1,2,0:T(8,128)(2,1)} %copy.111), channel_id=1, replica_groups=mesh['rep'=4,'shard'=8] {'shard'}, dimensions={0} | all-to-all | bytes 1966080 | tf_op jit(solution)/shard_map/all_to_all | solution.py:1113
  552.4 7.3 forward_product.3
  566.3 21.8 %collective-permute-done.18 = bf16[320,1536]{1,0:T(8,128)(2,1)S(1)} collective-permute-done((bf16[320,1536]{1,0:T(8,128)(2,1)S(1)}, bf16[320,1536]{1,0:T(8,128)(2,1)S(1)}, u32[]{:S(2)}, u32[]{:S(2)}) %collective-permute-start.18) | collective-permute-done | bytes 983072 | tf_op jit(solution)/shard_map/ppermute | solution.py:772
  589.6 3.4 add_convert_fusion.5
  595.5 19.8 %collective-permute-done.20 = bf16[320,1536]{1,0:T(8,128)(2,1)S(1)} collective-permute-done((bf16[320,1536]{1,0:T(8,128)(2,1)S(1)}, bf16[320,1536]{1,0:T(8,128)(2,1)S(1)}, u32[]{:S(2)}, u32[]{:S(2)}) %collective-permute-start.20) | collective-permute-done | bytes 983072 | tf_op jit(solution)/shard_map/ppermute | solution.py:772
  619.7 19.2 %forward_product.4 = (bf16[1280,1536]{1,0:T(8,128)(2,1)S(1)}, bf16[1280,1536]{1,0:T(8,128)(2,1)S(1)}) custom-call(s32[9]{0:T(128)S(1)} %pad_add_fusion.1.spots, bf16[1280,1536]{1,0:T(8,128)(2,1)S(1)} %pad_maximum_fusion.2.x_ref, bf16[8,1,192,1536]{3,2,1,0:T(8,128)(2,1)} %bitcast.83, bf16[8,1,192,1536]{3,2,1,0:T(8,128)(2,1)} %bitcast.85, ...), custom_call_target="tpu_custom_call" | custom-call | flops 754974720 | bytes 4194304 | tf_op jit(solution)/shard_map/forward_product/pallas_call | solution.py:547
  640.9 21.0 %gradient.4 = bf16[4,2,2,768,384]{4,3,2,1,0:T(8,128)(2,1)} custom-call(s32[9]{0:T(128)S(1)} %pad_add_fusion.1.spots, bf16[1280,1536]{1,0:T(8,128)(2,1)S(1)} %get-tuple-element.118.x_ref, bf16[1280,1536]{1,0:T(8,128)(2,1)} %pad_maximum_fusion.1.dy_ref, s32[1280,1]{1,0:T(8,128)S(1)} %convert_element_type.210.image_ref), custom_call_target="tpu_custom_call" | custom-call | flops 754974720 | bytes 4194304 | tf_op jit(solution)/shard_map/gradient/pallas_call | solution.py:744
  661.9 18.3 %backward_product.4.dy_ref = bf16[1280,1536]{1,0:T(8,128)(2,1)S(1)} custom-call(s32[9]{0:T(128)S(1)} %pad_add_fusion.1.spots, bf16[1280,1536]{1,0:T(8,128)(2,1)} %pad_maximum_fusion.1.dy_ref, bf16[4,2,2,768,384]{4,3,2,1,0:T(8,128)(2,1)} %bitcast.78, bf16[4,2,2,768,384]{4,3,2,1,0:T(8,128)(2,1)} %bitcast.79, s32[1280,1]{1,0:T(8,128)S(1)} %convert_element_type.210.image_ref, ...), custom_call_target="tpu_custom_call" | custom-call | flops 754974720 | bytes 4194304 | tf_op jit(solution)/shard_map/backward_product/pallas_call | solution.py:658
  682.1 15.0 %backward_product.5 = bf16[1280,1536]{1,0:T(8,128)(2,1)S(1)} custom-call(s32[9]{0:T(128)S(1)} %pad_add_fusion.1.spots, bf16[1280,1536]{1,0:T(8,128)(2,1)} %copy-done.2, bf16[8,1,192,1536]{3,2,1,0:T(8,128)(2,1)} %bitcast.84, bf16[8,1,192,1536]{3,2,1,0:T(8,128)(2,1)} %bitcast.86, s32[1280,1]{1,0:T(8,128)S(1)} %convert_element_type.210.image_ref), custom_call_target="tpu_custom_call" | custom-call | flops 754974720 | bytes 4194304 | tf_op jit(solution)/shard_map/backward_product/pallas_call | solution.py:658
  702.2 20.2 %gradient.5 = (bf16[8,1,192,1536]{3,2,1,0:T(8,128)(2,1)}, bf16[8,1,192,1536]{3,2,1,0:T(8,128)(2,1)}) custom-call(s32[9]{0:T(128)S(1)} %pad_add_fusion.1.spots, bf16[1280,1536]{1,0:T(8,128)(2,1)S(1)} %copy-done.4, bf16[1280,1536]{1,0:T(8,128)(2,1)} %copy-done.2, s32[1280,1]{1,0:T(8,128)S(1)} %convert_element_type.210.image_ref), custom_call_target="tpu_custom_call" | custom-call | flops 754974720 | bytes 4194304 | tf_op jit(solution)/shard_map/gradient/pallas_call | solution.py:744
  731.6 19.9 %collective-permute-done.26 = bf16[320,1536]{1,0:T(8,128)(2,1)S(1)} collective-permute-done((bf16[320,1536]{1,0:T(8,128)(2,1)S(1)}, bf16[320,1536]{1,0:T(8,128)(2,1)S(1)}, u32[]{:S(2)}, u32[]{:S(2)}) %collective-permute-start.26) | collective-permute-done | bytes 983072 | tf_op jit(solution)/shard_map/ppermute | solution.py:772
  757.6 8.7 backward_product.6
  769.8 5.7 all-to-all-start.4
  780.3 7.4 gradient.6
  787.7 34.0 %all-to-all-done.4 = bf16[8,320,192]{1,2,0:T(8,128)(2,1)} async-done(((bf16[8,320,192]{1,2,0:T(8,128)(2,1)}), bf16[8,320,192]{1,2,0:T(8,128)(2,1)}, u32[]{:S(2)}, u32[]{:S(2)}) %all-to-all-start.4) | async-done | bytes 983072 | tf_op jit(solution)/shard_map/all_to_all | solution.py:1113
  824.2 19.9 %reduce-scatter.4.cloned.1.call-done = bf16[2,768,384]{2,1,0:T(8,128)(2,1)} async-done(((bf16[16,768,384]{2,1,0:T(8,128)(2,1)}), bf16[2,768,384]{2,1,0:T(8,128)(2,1)}) %reduce-scatter.4.cloned.1.call-update) | async-done | bytes 1179664 | tf_op jit(solution)/shard_map/reduce_scatter | solution.py:973
  846.0 91.0 %attend_back.1 = (bf16[2560,192]{1,0:T(8,128)(2,1)}, bf16[1280,384]{1,0:T(8,128)(2,1)}, bf16[1280,384]{1,0:T(8,128)(2,1)}, f32[2560,384]{1,0:T(8,128)}) custom-call(s32[10]{0:T(128)} %copy-done.32, s32[10]{0:T(128)} %copy-done.31, bf16[2560,192]{1,0:T(8,128)(2,1)} %bitcast.74, bf16[2560,384]{1,0:T(8,128)(2,1)} %bitcast.72, bf16[1280,384]{1,0:T(8,128)(2,1)} %copy-done.24, ...), custom_call_target="tpu_custom_call" | custom-call | flops 25769803776 | bytes 8388608 | tf_op jit(solution)/shard_map/attend_back/pallas_call | solution.py:237
  938.3 11.0 collective-permute-start.30
  951.8 4.3 all-to-all-start.6
  956.1 27.7 %collective-permute-done.29 = bf16[1280,384]{1,0:T(8,128)(2,1)} collective-permute-done((bf16[1280,384]{1,0:T(8,128)(2,1)}, bf16[1280,384]{1,0:T(8,128)(2,1)}, u32[]{:S(2)}, u32[]{:S(2)}) %collective-permute-start.29) | collective-permute-done | bytes 983072 | tf_op jit(solution)/shard_map/ppermute | solution.py:1131
  983.8 4.4 add_convert_fusion
  988.2 20.8 %all-to-all-done.6 = bf16[8,320,192]{1,2,0:T(8,128)(2,1)} async-done(((bf16[8,320,192]{1,2,0:T(8,128)(2,1)}), bf16[8,320,192]{1,2,0:T(8,128)(2,1)}, u32[]{:S(2)}, u32[]{:S(2)}) %all-to-all-start.6) | async-done | bytes 983072 | tf_op jit(solution)/shard_map/all_to_all | solution.py:1113
  1009.0 10.2 all-to-all-start.5
  1021.5 15.8 %forward_product.5 = bf16[1280,1536]{1,0:T(8,128)(2,1)S(1)} custom-call(s32[9]{0:T(128)S(1)} %pad_add_fusion.1.spots, bf16[1280,1536]{1,0:T(8,128)(2,1)S(1)} %copy-done.10, bf16[4,2,2,768,384]{4,3,2,1,0:T(8,128)(2,1)} %bitcast.80, bf16[4,2,2,768,384]{4,3,2,1,0:T(8,128)(2,1)} %bitcast.81, s32[1280,1]{1,0:T(8,128)S(1)} %convert_element_type.210.image_ref), custom_call_target="tpu_custom_call" | custom-call | flops 754974720 | bytes 4194304 | tf_op jit(solution)/shard_map/forward_product/pallas_call | solution.py:547
  1041.7 20.6 %all-to-all-done.5.kv_ref = bf16[8,320,384]{2,1,0:T(8,128)(2,1)} async-done(((bf16[8,320,384]{2,1,0:T(8,128)(2,1)}), bf16[8,320,384]{2,1,0:T(8,128)(2,1)}, u32[]{:S(2)}, u32[]{:S(2)}) %all-to-all-start.5) | async-done | bytes 1966112 | tf_op jit(solution)/shard_map/all_to_all | solution.py:1113
  1065.7 8.6 norm_back.1
  1074.3 13.9 %backward_product.7 = bf16[1280,1536]{1,0:T(8,128)(2,1)} custom-call(s32[9]{0:T(128)S(1)} %pad_add_fusion.1.spots, bf16[1280,1152]{1,0:T(8,128)(2,1)S(1)} %get-tuple-element.139.dy_ref, bf16[8,2,192,1152]{3,2,1,0:T(8,128)(2,1)} %get-tuple-element.100.w0.w1, bf16[8,2,192,1152]{3,2,1,0:T(8,128)(2,1)} %get-tuple-element.100.w0.w1, ...), custom_call_target="tpu_custom_call" | custom-call | flops 566231040 | bytes 4194304 | tf_op jit(solution)/shard_map/backward_product/pallas_call | solution.py:658
  1091.0 3.5 collective-permute-start.35
  1099.1 5.9 fusion.76
  1107.4 14.8 %gradient.7.refs_0_ = bf16[8,2,192,1152]{3,2,1,0:T(8,128)(2,1)} custom-call(s32[9]{0:T(128)S(1)} %pad_add_fusion.1.spots, bf16[1280,1536]{1,0:T(8,128)(2,1)} %copy-done.1, bf16[1280,1152]{1,0:T(8,128)(2,1)S(1)} %copy-done.15, s32[1280,1]{1,0:T(8,128)S(1)} %convert_element_type.210.image_ref), custom_call_target="tpu_custom_call" | custom-call | flops 566231040 | bytes 4194304 | tf_op jit(solution)/shard_map/gradient/pallas_call | solution.py:744
  1129.1 3.1 fusion.79
  1132.3 4.1 multiply_dynamic-update-slice_fusion.1
  1138.6 10.3 collective-permute-done.33
  1148.9 3.5 fusion.21
  1152.4 4.0 fusion.49
  1157.7 4.6 all-to-all-start.7
  1163.4 3.0 copy-done.7
  1166.4 126.2 %ring_scatter.1 = (bf16[2,192,1152]{2,1,0:T(8,128)(2,1)S(1)}, bf16[2,192,384]{2,1,0:T(8,128)(2,1)S(1)}) custom-call(bf16[8,2,192,1152]{3,2,1,0:T(8,128)(2,1)S(1)} %copy-done.7, bf16[8,2,192,384]{3,2,1,0:T(8,128)(2,1)S(1)} %bitcast.73), custom_call_target="tpu_custom_call" | custom-call | flops 1048576 | bytes 8388608 | tf_op jit(solution)/shard_map/ring_scatter/pallas_call | solution.py:954
  1295.7 3.1 collective-permute-start.37
  1299.3 3.7 collective-permute-start.39
  1309.4 8.8 collective-permute-start.40
  1318.3 6.2 fusion.65
  1324.9 5.9 fusion.74
  1335.1 4.5 fusion.71
  (398 shorter events, 161.8 us)
Async XLA Ops:
  9.0 22.0 %collective-permute-start.3 = (bf16[2,192,384]{2,1,0:T(8,128)(2,1)}, bf16[2,192,384]{2,1,0:T(8,128)(2,1)}, u32[]{:S(2)}, u32[]{:S(2)}) collective-permute-start(bf16[2,192,384]{2,1,0:T(8,128)(2,1)} %convert_element_type.201), channel_id=1, source_target_pairs={{0,0},{1,1},{2,8},{3,9},{4,16},{5,17},{6,24},{7,25},{8,2},{9,3},{1... | collective-permute-start | bytes 884744 | tf_op jit(solution)/shard_map/ppermute | solution.py:801
  16.1 28.7 %collective-permute-start = (bf16[2,192,384]{2,1,0:T(8,128)(2,1)}, bf16[2,192,384]{2,1,0:T(8,128)(2,1)}, u32[]{:S(2)}, u32[]{:S(2)}) collective-permute-start(bf16[2,192,384]{2,1,0:T(8,128)(2,1)} %get-tuple-element.244), channel_id=1, source_target_pairs={{0,0},{8,24},{16,16},{24,8},{1,1},{9,25},{17,17},{25,9},{2,2},{10,... | collective-permute-start | bytes 884744 | tf_op jit(solution)/shard_map/ppermute | solution.py:772
  21.2 23.6 %collective-permute-start.1 = (bf16[2,192,384]{2,1,0:T(8,128)(2,1)}, bf16[2,192,384]{2,1,0:T(8,128)(2,1)}, u32[]{:S(2)}, u32[]{:S(2)}) collective-permute-start(bf16[2,192,384]{2,1,0:T(8,128)(2,1)} %get-tuple-element.242), channel_id=1, source_target_pairs={{0,8},{8,0},{16,24},{24,16},{1,9},{9,1},{17,25},{25,17},{2,10},{10... | collective-permute-start | bytes 884744 | tf_op jit(solution)/shard_map/ppermute | solution.py:772
  21.3 23.5 %collective-permute-start.2 = (bf16[2,192,384]{2,1,0:T(8,128)(2,1)}, bf16[2,192,384]{2,1,0:T(8,128)(2,1)}, u32[]{:S(2)}, u32[]{:S(2)}) collective-permute-start(bf16[2,192,384]{2,1,0:T(8,128)(2,1)} %get-tuple-element.243), channel_id=1, source_target_pairs={{0,16},{8,8},{16,0},{24,24},{1,17},{9,9},{17,1},{25,25},{2,18},{10... | collective-permute-start | bytes 884744 | tf_op jit(solution)/shard_map/ppermute | solution.py:772
  31.9 156.5 %all-to-all-start = ((bf16[32,4,2304]{2,1,0:T(4,128)(2,1)}), bf16[32,4,2304]{2,1,0:T(4,128)(2,1)S(1)}, u32[]{:S(2)}, u32[]{:S(2)}) async-start(bf16[32,4,2304]{2,1,0:T(4,128)(2,1)} %reshape.440), calls=%async_computation | async-start | bytes 1179648 | tf_op jit(solution)/shard_map/all_to_all | solution.py:1049
  35.8 391.8 %all-gather.7.cloned.1.call-start = ((), (), s32[]{:S(2)}) async-start(), calls=%async_computation.14 | async-start | bytes 5308416 | tf_op jit(solution)/shard_map/all_gather | solution.py:805
  41.2 147.5 %collective-permute-start.4 = (bf16[2,768,384]{2,1,0:T(8,128)(2,1)S(1)}, bf16[2,768,384]{2,1,0:T(8,128)(2,1)}, u32[]{:S(2)}, u32[]{:S(2)}) collective-permute-start(bf16[2,768,384]{2,1,0:T(8,128)(2,1)S(1)} %convert_element_type.202), channel_id=1, source_target_pairs={{0,0},{1,1},{2,8},{3,9},{4,16},{5,17},{6,24},{7,25},{8,2},{9,3},{1... | collective-permute-start | bytes 3538952 | tf_op jit(solution)/shard_map/ppermute | solution.py:801
  191.2 290.5 %all-gather.9.cloned.1.call-start = ((), (), s32[]{:S(2)}) async-start(), calls=%async_computation.15 | async-start | bytes 5308416 | tf_op jit(solution)/shard_map/all_gather | solution.py:805
  195.5 26.1 %collective-permute-start.9 = (bf16[320,1536]{1,0:T(8,128)(2,1)}, bf16[320,1536]{1,0:T(8,128)(2,1)S(1)}, u32[]{:S(2)}, u32[]{:S(2)}) collective-permute-start(bf16[320,1536]{1,0:T(8,128)(2,1)} %get-tuple-element.271), channel_id=1, source_target_pairs={{0,16},{8,24},{16,0},{24,8},{1,17},{9,25},{17,1},{25,9},{2,18},{10... | collective-permute-start | bytes 2949128 | tf_op jit(solution)/shard_map/ppermute | solution.py:772
  195.6 21.6 %collective-permute-start.6 = (s32[320]{0:T(512)S(1)}, s32[320]{0:T(512)S(1)}, u32[]{:S(2)}, u32[]{:S(2)}) collective-permute-start(s32[320]{0:T(512)S(1)} %copy-done.80), channel_id=1, source_target_pairs={{0,16},{8,24},{16,0},{24,8},{1,17},{9,25},{17,1},{25,9},{2,18},{10... | collective-permute-start | bytes 3848 | tf_op jit(solution)/shard_map/ppermute | solution.py:772
  197.0 23.0 %collective-permute-start.5 = (s32[320]{0:T(512)S(1)}, s32[320]{0:T(512)S(1)}, u32[]{:S(2)}, u32[]{:S(2)}) collective-permute-start(s32[320]{0:T(512)S(1)} %copy-done.80), channel_id=1, source_target_pairs={{0,8},{8,0},{16,24},{24,16},{1,9},{9,1},{17,25},{25,17},{2,10},{10... | collective-permute-start | bytes 3848 | tf_op jit(solution)/shard_map/ppermute | solution.py:772
  217.2 3.6 collective-permute-start.7
  221.2 2.8 collective-permute-start.8
  221.6 3.8 collective-permute-start.10
  249.3 62.7 %copy-start.22 = (bf16[8,320,192]{2,1,0:T(8,128)(2,1)}, bf16[8,320,192]{2,1,0:T(8,128)(2,1)S(1)}, u32[]{:S(2)}) copy-start(bf16[8,320,192]{2,1,0:T(8,128)(2,1)S(1)} %get-tuple-element.105) | copy-start | bytes 2949124
  312.0 118.1 %copy-start.8 = (bf16[8,320,384]{2,1,0:T(8,128)(2,1)}, bf16[8,320,384]{2,1,0:T(8,128)(2,1)S(1)}, u32[]{:S(2)}) copy-start(bf16[8,320,384]{2,1,0:T(8,128)(2,1)S(1)} %all_to_all.40) | copy-start | bytes 5898244
  312.0 21.8 %collective-permute-start.14 = (bf16[320,1536]{1,0:T(8,128)(2,1)}, bf16[320,1536]{1,0:T(8,128)(2,1)}, u32[]{:S(2)}, u32[]{:S(2)}) collective-permute-start(bf16[320,1536]{1,0:T(8,128)(2,1)} %get-tuple-element.270), channel_id=1, source_target_pairs={{0,16},{8,24},{16,0},{24,8},{1,17},{9,25},{17,1},{25,9},{2,18},{10... | collective-permute-start | bytes 2949128 | tf_op jit(solution)/shard_map/ppermute | solution.py:772
  312.6 36.4 %collective-permute-start.11 = (bf16[1280,384]{1,0:T(8,128)(2,1)S(1)}, bf16[1280,384]{1,0:T(8,128)(2,1)S(1)}, u32[]{:S(2)}, u32[]{:S(2)}) collective-permute-start(bf16[1280,384]{1,0:T(8,128)(2,1)S(1)} %get-tuple-element.231), channel_id=1, source_target_pairs={{0,2},{1,3},{2,4},{3,5},{4,6},{5,7},{8,10},{9,11},{10,12},{11,13},... | collective-permute-start | bytes 2949128 | tf_op jit(solution)/shard_map/ppermute | solution.py:1131
  315.8 42.1 %collective-permute-start.12 = (bf16[1280,384]{1,0:T(8,128)(2,1)S(1)}, bf16[1280,384]{1,0:T(8,128)(2,1)S(1)}, u32[]{:S(2)}, u32[]{:S(2)}) collective-permute-start(bf16[1280,384]{1,0:T(8,128)(2,1)S(1)} %get-tuple-element.230), channel_id=1, source_target_pairs={{2,0},{3,1},{4,2},{5,3},{6,4},{7,5},{10,8},{11,9},{12,10},{13,11},... | collective-permute-start | bytes 2949128 | tf_op jit(solution)/shard_map/ppermute | solution.py:1131
  317.1 48.5 %collective-permute-start.13 = (bf16[320,1536]{1,0:T(8,128)(2,1)}, bf16[320,1536]{1,0:T(8,128)(2,1)}, u32[]{:S(2)}, u32[]{:S(2)}) collective-permute-start(bf16[320,1536]{1,0:T(8,128)(2,1)} %get-tuple-element.270), channel_id=1, source_target_pairs={{0,8},{8,0},{16,24},{24,16},{1,9},{9,1},{17,25},{25,17},{2,10},{10... | collective-permute-start | bytes 2949128 | tf_op jit(solution)/shard_map/ppermute | solution.py:772
  333.8 31.8 %collective-permute-start.15 = (bf16[320,1536]{1,0:T(8,128)(2,1)}, bf16[320,1536]{1,0:T(8,128)(2,1)}, u32[]{:S(2)}, u32[]{:S(2)}) collective-permute-start(bf16[320,1536]{1,0:T(8,128)(2,1)} %collective-permute-done.14), channel_id=1, source_target_pairs={{0,8},{8,0},{16,24},{24,16},{1,9},{9,1},{17,25},{25,17},{2,10},{10... | collective-permute-start | bytes 2949128 | tf_op jit(solution)/shard_map/ppermute | solution.py:772
  361.3 63.9 %all-to-all-start.2 = ((bf16[8,320,192]{1,2,0:T(8,128)(2,1)}), bf16[8,320,192]{1,2,0:T(8,128)(2,1)}, u32[]{:S(2)}, u32[]{:S(2)}) async-start(bf16[8,320,192]{1,2,0:T(8,128)(2,1)} %copy.108), calls=%async_computation.2 | async-start | bytes 2359296 | tf_op jit(solution)/shard_map/all_to_all | solution.py:1113
  365.6 296.3 %all-gather.11.cloned.1.call-start = ((), (), s32[]{:S(2)}) async-start(), calls=%async_computation.16 | async-start | bytes 10616832 | tf_op jit(solution)/shard_map/all_gather | solution.py:805
  427.6 416.4 %reduce-scatter.4.cloned.1.call-start = ((), (), s32[]{:S(2)}) async-start(), calls=%async_computation.11 | async-start | bytes 10616832 | tf_op jit(solution)/shard_map/reduce_scatter | solution.py:973
  429.6 50.3 %copy-start.31 = (s32[10]{0:T(128)}, s32[10]{0:T(128)S(1)}, u32[]{:S(2)}) copy-start(s32[10]{0:T(128)S(1)} %fusion.60.hi_ref) | copy-start | bytes 124
  429.7 50.3 %copy-start.32 = (s32[10]{0:T(128)}, s32[10]{0:T(128)S(1)}, u32[]{:S(2)}) copy-start(s32[10]{0:T(128)S(1)} %fusion.61.lo_ref) | copy-start | bytes 124
  484.1 66.9 %copy-start = (bf16[8,2,192,384]{3,2,1,0:T(8,128)(2,1)S(1)}, bf16[8,2,192,384]{3,2,1,0:T(8,128)(2,1)}, u32[]{:S(2)}) copy-start(bf16[8,2,192,384]{3,2,1,0:T(8,128)(2,1)} %get-tuple-element.112) | copy-start | bytes 7077892
  560.6 27.6 %copy-start.16 = (bf16[1280,1536]{1,0:T(8,128)(2,1)}, bf16[1280,1536]{1,0:T(8,128)(2,1)S(1)}, u32[]{:S(2)}) copy-start(bf16[1280,1536]{1,0:T(8,128)(2,1)S(1)} %get-tuple-element.113) | copy-start | bytes 11796484
  560.7 27.4 %copy-start.40 = (bf16[320,1536]{1,0:T(8,128)(2,1)S(1)}, bf16[320,1536]{1,0:T(8,128)(2,1)}, u32[]{:S(2)}) copy-start(bf16[320,1536]{1,0:T(8,128)(2,1)} %param.23) | copy-start | bytes 2949124
  560.8 4.0 collective-permute-start.17
  562.6 3.7 collective-permute-start.16
  565.0 23.1 %collective-permute-start.18 = (bf16[320,1536]{1,0:T(8,128)(2,1)S(1)}, bf16[320,1536]{1,0:T(8,128)(2,1)S(1)}, u32[]{:S(2)}, u32[]{:S(2)}) collective-permute-start(bf16[320,1536]{1,0:T(8,128)(2,1)S(1)} %add_convert_fusion.6), channel_id=1, source_target_pairs={{0,16},{8,24},{16,0},{24,8},{1,17},{9,25},{17,1},{25,9},{2,18},{10... | collective-permute-start | bytes 2949128 | tf_op jit(solution)/shard_map/ppermute | solution.py:772
  566.3 22.8 %copy-start.57 = (bf16[320,1536]{1,0:T(8,128)(2,1)}, bf16[320,1536]{1,0:T(8,128)(2,1)S(1)}, u32[]{:S(2)}) copy-start(bf16[320,1536]{1,0:T(8,128)(2,1)S(1)} %collective-permute-done.16) | copy-start | bytes 2949124
  593.0 22.2 %collective-permute-start.20 = (bf16[320,1536]{1,0:T(8,128)(2,1)S(1)}, bf16[320,1536]{1,0:T(8,128)(2,1)S(1)}, u32[]{:S(2)}, u32[]{:S(2)}) collective-permute-start(bf16[320,1536]{1,0:T(8,128)(2,1)S(1)} %add_convert_fusion.5), channel_id=1, source_target_pairs={{0,16},{8,24},{16,0},{24,8},{1,17},{9,25},{17,1},{25,9},{2,18},{10... | collective-permute-start | bytes 2949128 | tf_op jit(solution)/shard_map/ppermute | solution.py:772
  594.1 23.2 %collective-permute-start.19 = (bf16[320,1536]{1,0:T(8,128)(2,1)S(1)}, bf16[320,1536]{1,0:T(8,128)(2,1)S(1)}, u32[]{:S(2)}, u32[]{:S(2)}) collective-permute-start(bf16[320,1536]{1,0:T(8,128)(2,1)S(1)} %add_convert_fusion.5), channel_id=1, source_target_pairs={{0,8},{8,0},{16,24},{24,16},{1,9},{9,1},{17,25},{25,17},{2,10},{10... | collective-permute-start | bytes 2949128 | tf_op jit(solution)/shard_map/ppermute | solution.py:772
  615.2 4.2 collective-permute-start.21
  697.2 28.2 %copy-start.5 = (bf16[1280,1536]{1,0:T(8,128)(2,1)}, bf16[1280,1536]{1,0:T(8,128)(2,1)S(1)}, u32[]{:S(2)}) copy-start(bf16[1280,1536]{1,0:T(8,128)(2,1)S(1)} %backward_product.5) | copy-start | bytes 11796484
  698.3 2.6 collective-permute-start.23
  698.6 23.7 %collective-permute-start.22 = (bf16[320,1536]{1,0:T(8,128)(2,1)}, bf16[320,1536]{1,0:T(8,128)(2,1)S(1)}, u32[]{:S(2)}, u32[]{:S(2)}) collective-permute-start(bf16[320,1536]{1,0:T(8,128)(2,1)} %get-tuple-element.224), channel_id=1, source_target_pairs={{0,8},{8,0},{16,24},{24,16},{1,9},{9,1},{17,25},{25,17},{2,10},{10... | collective-permute-start | bytes 2949128 | tf_op jit(solution)/shard_map/ppermute | solution.py:772
  701.1 23.2 %copy-start.37 = (f32[320,1536]{1,0:T(8,128)S(1)}, f32[320,1536]{1,0:T(8,128)}, u32[]{:S(2)}) copy-start(f32[320,1536]{1,0:T(8,128)} %copy-done.36) | copy-start | bytes 5898244
  701.1 23.2 %collective-permute-start.24 = (bf16[320,1536]{1,0:T(8,128)(2,1)S(1)}, bf16[320,1536]{1,0:T(8,128)(2,1)S(1)}, u32[]{:S(2)}, u32[]{:S(2)}) collective-permute-start(bf16[320,1536]{1,0:T(8,128)(2,1)S(1)} %add_convert_fusion.4), channel_id=1, source_target_pairs={{0,16},{8,24},{16,0},{24,8},{1,17},{9,25},{17,1},{25,9},{2,18},{10... | collective-permute-start | bytes 2949128 | tf_op jit(solution)/shard_map/ppermute | solution.py:772
  729.2 22.3 %collective-permute-start.26 = (bf16[320,1536]{1,0:T(8,128)(2,1)S(1)}, bf16[320,1536]{1,0:T(8,128)(2,1)S(1)}, u32[]{:S(2)}, u32[]{:S(2)}) collective-permute-start(bf16[320,1536]{1,0:T(8,128)(2,1)S(1)} %multiply_convert_fusion), channel_id=1, source_target_pairs={{0,16},{8,24},{16,0},{24,8},{1,17},{9,25},{17,1},{25,9},{2,18},{10... | collective-permute-start | bytes 2949128 | tf_op jit(solution)/shard_map/ppermute | solution.py:772
  730.2 23.2 %collective-permute-start.25 = (bf16[320,1536]{1,0:T(8,128)(2,1)S(1)}, bf16[320,1536]{1,0:T(8,128)(2,1)S(1)}, u32[]{:S(2)}, u32[]{:S(2)}) collective-permute-start(bf16[320,1536]{1,0:T(8,128)(2,1)S(1)} %multiply_convert_fusion), channel_id=1, source_target_pairs={{0,8},{8,0},{16,24},{24,16},{1,9},{9,1},{17,25},{25,17},{2,10},{10... | collective-permute-start | bytes 2949128 | tf_op jit(solution)/shard_map/ppermute | solution.py:772
  751.5 4.1 collective-permute-start.27
  769.8 51.9 %all-to-all-start.4 = ((bf16[8,320,192]{1,2,0:T(8,128)(2,1)}), bf16[8,320,192]{1,2,0:T(8,128)(2,1)}, u32[]{:S(2)}, u32[]{:S(2)}) async-start(bf16[8,320,192]{1,2,0:T(8,128)(2,1)} %copy.113), calls=%async_computation.4 | async-start | bytes 2359296 | tf_op jit(solution)/shard_map/all_to_all | solution.py:1113
  775.6 381.0 %reduce-scatter.6.cloned.1.call-start = ((), (), s32[]{:S(2)}) async-start(), calls=%async_computation.12 | async-start | bytes 5308416 | tf_op jit(solution)/shard_map/reduce_scatter | solution.py:973
  844.1 92.9 %collective-permute-start.28 = (bf16[2,768,384]{2,1,0:T(8,128)(2,1)}, bf16[2,768,384]{2,1,0:T(8,128)(2,1)}, u32[]{:S(2)}, u32[]{:S(2)}) collective-permute-start(bf16[2,768,384]{2,1,0:T(8,128)(2,1)} %reduce-scatter.4.cloned.1.call-done), channel_id=1, source_target_pairs={{0,0},{1,1},{2,8},{3,9},{4,16},{5,17},{6,24},{7,25},{8,2},{9,3},{1... | collective-permute-start | bytes 3538952 | tf_op jit(solution)/shard_map/ppermute | solution.py:801
  937.0 46.8 %collective-permute-start.29 = (bf16[1280,384]{1,0:T(8,128)(2,1)}, bf16[1280,384]{1,0:T(8,128)(2,1)}, u32[]{:S(2)}, u32[]{:S(2)}) collective-permute-start(bf16[1280,384]{1,0:T(8,128)(2,1)} %get-tuple-element.132), channel_id=1, source_target_pairs={{2,0},{3,1},{4,2},{5,3},{6,4},{7,5},{10,8},{11,9},{12,10},{13,11},... | collective-permute-start | bytes 2949128 | tf_op jit(solution)/shard_map/ppermute | solution.py:1131
  938.3 45.5 %collective-permute-start.30 = (bf16[1280,384]{1,0:T(8,128)(2,1)}, bf16[1280,384]{1,0:T(8,128)(2,1)}, u32[]{:S(2)}, u32[]{:S(2)}) collective-permute-start(bf16[1280,384]{1,0:T(8,128)(2,1)} %get-tuple-element.133), channel_id=1, source_target_pairs={{0,2},{1,3},{2,4},{3,5},{4,6},{5,7},{8,10},{9,11},{10,12},{11,13},... | collective-permute-start | bytes 2949128 | tf_op jit(solution)/shard_map/ppermute | solution.py:1131
  951.8 57.2 %all-to-all-start.6 = ((bf16[8,320,192]{1,2,0:T(8,128)(2,1)}), bf16[8,320,192]{1,2,0:T(8,128)(2,1)}, u32[]{:S(2)}, u32[]{:S(2)}) async-start(bf16[8,320,192]{1,2,0:T(8,128)(2,1)} %copy.116), calls=%async_computation.7 | async-start | bytes 2359296 | tf_op jit(solution)/shard_map/all_to_all | solution.py:1113
  1009.0 53.3 %all-to-all-start.5 = ((bf16[8,320,384]{2,1,0:T(8,128)(2,1)}), bf16[8,320,384]{2,1,0:T(8,128)(2,1)}, u32[]{:S(2)}, u32[]{:S(2)}) async-start(bf16[8,320,384]{2,1,0:T(8,128)(2,1)} %bitcast.87), calls=%async_computation.6 | async-start | bytes 3932160 | tf_op jit(solution)/shard_map/all_to_all | solution.py:1113
  1019.2 274.4 %reduce-scatter.8.cloned.1.call-start = ((), (), s32[]{:S(2)}) async-start(), calls=%async_computation.13 | async-start | bytes 5308416 | tf_op jit(solution)/shard_map/reduce_scatter | solution.py:973
  1074.3 24.7 %copy-start.63 = (f32[2,768,384]{2,1,0:T(8,128)S(1)}, f32[2,768,384]{2,1,0:T(8,128)}, u32[]{:S(2)}) copy-start(f32[2,768,384]{2,1,0:T(8,128)} %param.42) | copy-start | bytes 7077892
  1091.0 5.7 collective-permute-start.35
  1096.0 26.3 %collective-permute-start.32 = (bf16[320,1536]{1,0:T(8,128)(2,1)}, bf16[320,1536]{1,0:T(8,128)(2,1)}, u32[]{:S(2)}, u32[]{:S(2)}) collective-permute-start(bf16[320,1536]{1,0:T(8,128)(2,1)} %get-tuple-element.223), channel_id=1, source_target_pairs={{0,8},{8,0},{16,24},{24,16},{1,9},{9,1},{17,25},{25,17},{2,10},{10... | collective-permute-start | bytes 2949128 | tf_op jit(solution)/shard_map/ppermute | solution.py:772
  1096.0 30.5 %collective-permute-start.34 = (bf16[320,1536]{1,0:T(8,128)(2,1)}, bf16[320,1536]{1,0:T(8,128)(2,1)}, u32[]{:S(2)}, u32[]{:S(2)}) collective-permute-start(bf16[320,1536]{1,0:T(8,128)(2,1)} %get-tuple-element.220), channel_id=1, source_target_pairs={{0,8},{8,0},{16,24},{24,16},{1,9},{9,1},{17,25},{25,17},{2,10},{10... | collective-permute-start | bytes 2949128 | tf_op jit(solution)/shard_map/ppermute | solution.py:772
  1099.1 27.4 %collective-permute-start.36 = (bf16[320,1536]{1,0:T(8,128)(2,1)}, bf16[320,1536]{1,0:T(8,128)(2,1)}, u32[]{:S(2)}, u32[]{:S(2)}) collective-permute-start(bf16[320,1536]{1,0:T(8,128)(2,1)} %add_convert_fusion.1), channel_id=1, source_target_pairs={{0,16},{8,24},{16,0},{24,8},{1,17},{9,25},{17,1},{25,9},{2,18},{10... | collective-permute-start | bytes 2949128 | tf_op jit(solution)/shard_map/ppermute | solution.py:772
  1105.1 33.5 %collective-permute-start.31 = (bf16[320,1536]{1,0:T(8,128)(2,1)}, bf16[320,1536]{1,0:T(8,128)(2,1)}, u32[]{:S(2)}, u32[]{:S(2)}) collective-permute-start(bf16[320,1536]{1,0:T(8,128)(2,1)} %get-tuple-element.222), channel_id=1, source_target_pairs={{0,8},{8,0},{16,24},{24,16},{1,9},{9,1},{17,25},{25,17},{2,10},{10... | collective-permute-start | bytes 2949128 | tf_op jit(solution)/shard_map/ppermute | solution.py:772
  1124.8 24.1 %collective-permute-start.33 = (bf16[320,1536]{1,0:T(8,128)(2,1)}, bf16[320,1536]{1,0:T(8,128)(2,1)}, u32[]{:S(2)}, u32[]{:S(2)}) collective-permute-start(bf16[320,1536]{1,0:T(8,128)(2,1)} %add_convert_fusion.3), channel_id=1, source_target_pairs={{0,16},{8,24},{16,0},{24,8},{1,17},{9,25},{17,1},{25,9},{2,18},{10... | collective-permute-start | bytes 2949128 | tf_op jit(solution)/shard_map/ppermute | solution.py:772
  1157.7 135.8 %all-to-all-start.7 = ((f32[32,4,2432]{2,1,0:T(4,128)}), f32[32,4,2432]{2,1,0:T(4,128)}, u32[]{:S(2)}, u32[]{:S(2)}) async-start(f32[32,4,2432]{2,1,0:T(4,128)} %bitcast.88), calls=%async_computation.9 | async-start | bytes 2490368 | tf_op jit(solution)/shard_map/all_to_all | solution.py:1271
  1295.7 38.3 %collective-permute-start.37 = (bf16[2,192,384]{2,1,0:T(8,128)(2,1)}, bf16[2,192,384]{2,1,0:T(8,128)(2,1)S(1)}, u32[]{:S(2)}, u32[]{:S(2)}) collective-permute-start(bf16[2,192,384]{2,1,0:T(8,128)(2,1)} %get-tuple-element.236), channel_id=1, source_target_pairs={{0,0},{8,24},{16,16},{24,8},{1,1},{9,25},{17,17},{25,9},{2,2},{10,... | collective-permute-start | bytes 884744 | tf_op jit(solution)/shard_map/ppermute | solution.py:772
  1298.8 35.2 %collective-permute-start.38 = (bf16[2,192,384]{2,1,0:T(8,128)(2,1)}, bf16[2,192,384]{2,1,0:T(8,128)(2,1)S(1)}, u32[]{:S(2)}, u32[]{:S(2)}) collective-permute-start(bf16[2,192,384]{2,1,0:T(8,128)(2,1)} %get-tuple-element.237), channel_id=1, source_target_pairs={{0,8},{8,0},{16,24},{24,16},{1,9},{9,1},{17,25},{25,17},{2,10},{10... | collective-permute-start | bytes 884744 | tf_op jit(solution)/shard_map/ppermute | solution.py:772
  1299.3 34.7 %collective-permute-start.39 = (bf16[2,192,384]{2,1,0:T(8,128)(2,1)}, bf16[2,192,384]{2,1,0:T(8,128)(2,1)}, u32[]{:S(2)}, u32[]{:S(2)}) collective-permute-start(bf16[2,192,384]{2,1,0:T(8,128)(2,1)} %get-tuple-element.238), channel_id=1, source_target_pairs={{0,16},{8,8},{16,0},{24,24},{1,17},{9,9},{17,1},{25,25},{2,18},{10... | collective-permute-start | bytes 884744 | tf_op jit(solution)/shard_map/ppermute | solution.py:772
  1309.4 22.9 %collective-permute-start.40 = (bf16[2,192,384]{2,1,0:T(8,128)(2,1)S(1)}, bf16[2,192,384]{2,1,0:T(8,128)(2,1)S(1)}, u32[]{:S(2)}, u32[]{:S(2)}) collective-permute-start(bf16[2,192,384]{2,1,0:T(8,128)(2,1)S(1)} %get-tuple-element.152), channel_id=1, source_target_pairs={{0,0},{1,1},{2,8},{3,9},{4,16},{5,17},{6,24},{7,25},{8,2},{9,3},{1... | collective-permute-start | bytes 884744 | tf_op jit(solution)/shard_map/ppermute | solution.py:801
  (75 other events, 397.8 us)
Sparse Core Ops, SparseCore 0:
  191.3 100.3 all-gather.6
  312.1 119.3 all-gather.8
  433.8 159.9 all-gather.10
  662.0 182.0 reduce-scatter.3
  847.6 148.8 reduce-scatter.5
  1105.6 121.2 reduce-scatter.7
